TPU v7x, 256 devices: a whole 4x4x8 slice. The times are simulated.
256 devices in a mesh: rows: 4 (over y), coarse: 4 (over x_lo, core), fine: 16 (over z, x_hi).
Axes of the slice: x: 4 (x_hi: 2, x_lo: 2; x = x_hi * 2 + x_lo), y: 4, z: 8, core: 2. Of those that a mesh axis runs over, the one named last changes fastest.
Arguments:
- eigvecs: bfloat16 [2048, 32768], P('rows', ('coarse', 'fine')), may hold values from -6 to 6
- perm: int32 [32768], P(('coarse', 'fine')), may hold values from 0 to 511, as said below
- counts: int32 [64], replicated, may hold values from 1 to 256, as said below
- poles: float32 [32768], replicated, may hold values from 0 to 32768, as said below
- weights: float32 [32768], replicated, may hold values from -10 to 10, as said below
- roots: float32 [32768], P(('coarse', 'fine')), may hold values from 0 to 32768, as said below
Outputs:
- merged: bfloat16 [2048, 32768], P('rows', ('coarse', 'fine'))
Inputs may be any that keep to these rules, and one draw needn't show every extreme that they name: `perm`: each aligned block of 512 entries is a permutation of 0 to 511. `counts`: at least one device has exactly 256. Every entry of poles lies 0.2 or more away from every entry of roots. `weights`: magnitudes 0.1 or more. `roots`: every entry lies 0.2 or more away from every entry of poles.
All inputs are finite; a program needn't handle non-finite values.
Results may differ from a plain program's by a relative error of at most 0.0027.
Values may be sent and summed in bfloat16 or wider, within the bound.
No kernel may reach another device: no remote copies, remote signals or barrier semaphores. Data moves between devices by JAX's collectives and lax.ppermute only.
A program may use at most 64 MiB of HBM per device.

v0:
```python
import jax
import jax.numpy as jnp
from jax import lax
from jax.sharding import PartitionSpec as P

UNDEF_MOST = 256


def per_device(eigvecs, perm, counts, poles, weights, roots):
    columns_dev = eigvecs.shape[1]
    live_width = UNDEF_MOST
    device_total = counts.shape[0]
    n_coarse = lax.axis_size("coarse")
    n_fine = lax.axis_size("fine")
    device_ids = jnp.arange(device_total, dtype=jnp.int32)
    my_device = lax.axis_index("coarse") * n_fine + lax.axis_index("fine")
    my_count = jnp.sum(jnp.where(device_ids == my_device, counts, 0))
    column_ids = jnp.arange(columns_dev, dtype=jnp.int32)
    selector = (column_ids[:, None] == perm[None, :]).astype(jnp.bfloat16)
    permuted = jnp.dot(eigvecs, selector, preferred_element_type=jnp.float32).astype(jnp.bfloat16)
    own_roots = roots[:live_width]
    outgoing = permuted[:, :live_width]
    within = jnp.arange(live_width, dtype=jnp.int32)
    alive = within[None, :] < counts[:, None]
    factor_table = jnp.where(alive, weights.reshape(device_total, columns_dev)[:, :live_width], 0.0)
    pole_table = poles.reshape(device_total, columns_dev)[:, :live_width]
    factor_flat = jnp.transpose(
        factor_table.reshape(n_coarse, n_fine, live_width), (1, 0, 2)
    ).reshape(-1)
    pole_flat = jnp.transpose(pole_table.reshape(n_coarse, n_fine, live_width), (1, 0, 2)).reshape(
        -1
    )
    panels = lax.all_gather(outgoing, "coarse", axis=1, tiled=True)
    panel_piece = lax.all_gather(panels, "fine", axis=1, tiled=True)
    cauchy = factor_flat[:, None] / (pole_flat[:, None] - own_roots[None, :])
    summed = jnp.dot(panel_piece, cauchy.astype(jnp.bfloat16), preferred_element_type=jnp.float32)
    summed, squares = (summed, jnp.sum(cauchy * cauchy, axis=0))
    updated = summed / jnp.sqrt(squares)[None, :]
    retain = within < my_count
    leading = jnp.where(retain[None, :], updated, outgoing.astype(jnp.float32)).astype(jnp.bfloat16)
    return jnp.concatenate([leading, permuted[:, live_width:]], axis=1)


def solution(mesh):
    in_specs = (
        P("rows", ("coarse", "fine")),
        P(("coarse", "fine")),
        P(),
        P(),
        P(),
        P(("coarse", "fine")),
    )
    out_specs = P("rows", ("coarse", "fine"))
    return jax.shard_map(
        per_device, mesh=mesh, in_specs=in_specs, out_specs=out_specs, check_vma=False
    )
```

profile of v0, /device:TPU:1, one launch (start us, length us, event | category | flops | bytes accessed | tf_op | source)
XLA Modules:
  0.0 287.3 jit_solution(11880553413928689479)
XLA Ops:
  6.5 0.0 copy-start
  6.5 0.0 all-gather.3.cloned.1.call-start
  6.5 1.0 copy-done
  7.6 1.2 fusion.6
  8.8 0.7 fusion.20
  9.5 0.0 all-gather.3.cloned.1.call-update
  9.5 0.0 all-gather.5.cloned.1.call-start
  9.6 27.6 %all-gather.3.cloned.1.call-done = bf16[512,1024]{0,1:T(8,128)(2,1)} async-done(((bf16[512,256]{0,1:T(8,128)(2,1)}), bf16[512,1024]{0,1:T(8,128)(2,1)}) %all-gather.3.cloned.1.call-update) | async-done | bytes 1048592 | tf_op jit(solution)/shard_map/all_gather | solution.py:33
  37.1 0.0 all-gather.5.cloned.1.call-update
  37.1 0.7 slice.18
  37.8 0.9 reshape.26
  38.9 0.9 reshape.24
  39.8 0.7 slice_select_fusion
  40.6 9.0 %multiply_reduce_fusion = f32[256]{0:T(256)S(1)} fusion(f32[256]{0:T(256)S(1)} %slice.18, f32[16384]{0:T(1024)S(1)} %bitcast.18, f32[16384]{0:T(1024)S(1)} %bitcast.20), kind=kLoop, calls=%fused_computation | loop fusion | flops 16776960 | bytes 133120 | tf_op jit(solution)/shard_map/reduce_sum | solution.py:37
  49.7 1.3 fusion.19
  51.0 0.6 iota_compare_fusion.2
  51.6 213.3 %all-gather.5.cloned.1.call-done = bf16[512,16384]{0,1:T(8,128)(2,1)} async-done(((bf16[512,1024]{0,1:T(8,128)(2,1)}), bf16[512,16384]{0,1:T(8,128)(2,1)}) %all-gather.5.cloned.1.call-update) | async-done | bytes 16777232 | tf_op jit(solution)/shard_map/all_gather | solution.py:34
  264.9 14.5 %fusion.13 = bf16[512,256]{0,1:T(8,128)(2,1)S(1)} fusion(bf16[512,16384]{0,1:T(8,128)(2,1)} %all-gather.5.cloned.1.call-done, f32[256]{0:T(256)S(1)} %slice.18, f32[16384]{0:T(1024)S(1)} %bitcast.19, f32[16384]{0:T(1024)S(1)} %bitcast.21, f32[256]{0:T(256)S(1)} %sqrt.7, pred[256]{0:T(512)(128)(4,1)S(1)} %iota_compare_fusion.2, bf16[512,512]{0,1:T(8,128)(2,1)S(1)} %fusion.6), kind=kOutput, calls=%fused_computation.11 | convolution fusion | flops 4308074496 | bytes 17434880 | tf_op jit(solution)/shard_map/dot_general | solution.py:36
  279.5 1.0 copy.14
  (7 shorter events, 0.2 us)
Async XLA Ops:
  6.5 1.0 copy-start
  6.5 30.6 %all-gather.3.cloned.1.call-start = ((), (), s32[]{:S(2)}) async-start(), calls=%async_computation | async-start | bytes 1310720 | tf_op jit(solution)/shard_map/all_gather | solution.py:33
  9.5 255.4 %all-gather.5.cloned.1.call-start = ((), (), s32[]{:S(2)}) async-start(), calls=%async_computation.1 | async-start | bytes 17825792 | tf_op jit(solution)/shard_map/all_gather | solution.py:34
Sparse Core Ops, SparseCore 0:
  9.6 27.4 all-gather.2
  39.7 225.1 all-gather.4
where the time goes:
time: 288 us; the launch traced here: 287 us
  waiting for transfers between devices  241 us (84%)
  matrix products  15.7 us (5%)
  between operations  13.5 us (5%)
  other arithmetic  11.7 us (4%)
  local copies, waits for them, and re-layouts  5.5 us (2%)
    all_gather x1, waiting for transfers between devices, per_device(): panel_piece = lax.all_gather(panels, 'fine', axis=1, tiled=True)  213 us
    all_gather x1, waiting for transfers between devices, per_device(): panels = lax.all_gather(outgoing, 'coarse', axis=1, tiled=True)  27.6 us
    dot_general x1, matrix products, per_device(): jnp.dot(panel_piece, cauchy.astype(jnp.bfloat16), preferred_element_type=...  14.5 us
    reduce_sum x1, other arithmetic, per_device(): summed, squares = (summed, jnp.sum(cauchy * cauchy, axis=0))  9.01 us
  transfers between devices with their start and end apart: 2, of which 2 were waited for; matrix products, arithmetic and copies ran while one was open for 5% of the time, Pallas kernels for 0%

commit v1 on v0

v1 whole, which is shorter than its diff:
```python
import jax
import jax.numpy as jnp
import numpy as np
from jax import lax
from jax.experimental import pallas as pl
from jax.experimental.pallas import tpu as pltpu
from jax.sharding import Mesh
from jax.sharding import PartitionSpec as P

LIVE = 256
COLS = 512
LANES = 128
ZS = 8
XS = 4
CHUNKS = ((0, 256), (256, 256))
TILE = 64

VM = pl.BlockSpec(memory_space=pltpu.VMEM)
SM = pl.BlockSpec(memory_space=pltpu.SMEM)
F32 = jnp.float32
BF16 = jnp.bfloat16


def params(mib):
    return pltpu.CompilerParams(vmem_limit_bytes=mib << 20)


def cost(flops, size):
    return pl.CostEstimate(flops=flops, transcendentals=0, bytes_accessed=size)


def xshift(a, k):
    pairs = []
    for xl in range(2):
        for xh in range(2):
            x = (2 * xh + xl + k) % XS
            pairs.append((2 * xl + xh, 2 * (x % 2) + x // 2))
    return lax.ppermute(a, ("xl", "xh"), pairs)


def zshift(a, k):
    return lax.ppermute(a, "z", [(i, (i + k) % ZS) for i in range(ZS)])


def cshift(a):
    return lax.ppermute(a, "core", [(0, 1), (1, 0)])


def permute_kernel(e_ref, perm_ref, p_ref, *x_refs):
    source = lax.broadcasted_iota(jnp.int32, (COLS, COLS), 0)
    selector = jnp.where(source == perm_ref[...], 1.0, 0.0).astype(BF16)
    for (start, size), x_ref in zip(CHUNKS, x_refs, strict=True):
        moved = jnp.dot(e_ref[start : start + size, :], selector, preferred_element_type=F32)
        p_ref[start : start + size, :] = moved.astype(BF16)
        x_ref[...] = jnp.transpose(moved[:, :LIVE]).astype(BF16)


def permute(eigvecs, perm):
    return pl.pallas_call(
        permute_kernel,
        in_specs=[VM, VM],
        out_specs=[VM] * (1 + len(CHUNKS)),
        out_shape=[jax.ShapeDtypeStruct((512, COLS), BF16)]
        + [jax.ShapeDtypeStruct((LIVE, size), BF16) for _, size in CHUNKS],
        name="permute",
        compiler_params=params(12),
        cost_estimate=cost(2 * 512**3, 3 << 19),
    )(eigvecs, perm)


def column(row):
    return jnp.transpose(jnp.broadcast_to(row, (8, LIVE)))[:, :1]


def cauchy_kernel(half, me_ref, counts_ref, poles_ref, weights_ref, *refs):
    r_refs, c_ref = refs[:-1], refs[-1]
    me = me_ref[0]
    z = (me // 2) % ZS
    lane = lax.broadcasted_iota(jnp.int32, (1, LANES), 1)
    for d in range(ZS):
        block = me + 2 * ((z + d) % ZS - z)
        live = counts_ref[block]
        for h in range(LIVE // LANES):
            at = 4 * block + h
            pole = poles_ref[pl.ds(at, 1), :]
            factor = jnp.where(lane + h * LANES < live, weights_ref[pl.ds(at, 1), :], 0.0)
            lo = d * LIVE + h * LANES
            for j, r_ref in enumerate(r_refs):
                roots = column(r_ref[:, half * LIVE : (half + 1) * LIVE])
                value = factor / (pole - roots)
                c_ref[j * LIVE : (j + 1) * LIVE, lo : lo + LANES] = value.astype(BF16)


def cauchy(half, me, counts, poles, weights, roots):
    return pl.pallas_call(
        lambda *refs: cauchy_kernel(half, *refs),
        in_specs=[SM, SM, VM, VM] + [VM] * XS,
        out_specs=VM,
        out_shape=pltpu.VMEM((XS * LIVE, ZS * LIVE), BF16),
        name="cauchy",
        compiler_params=params(12),
        cost_estimate=cost(XS * LIVE * ZS * LIVE * 400, 4 << 20),
    )(me, counts, poles, weights, *roots)


def norm_kernel(counts_ref, poles_ref, weights_ref, r_ref, n_ref):
    roots = column(r_ref[...])
    lane = lax.broadcasted_iota(jnp.int32, (1, LANES), 1)
    blocks = counts_ref.shape[0]
    for t in range(LIVE // TILE):
        own = jnp.broadcast_to(roots[t * TILE : (t + 1) * TILE], (TILE, LANES))

        def step(block, total):
            live = counts_ref[block]
            for h in range(LIVE // LANES):
                at = 4 * block + h
                factor = jnp.where(lane + h * LANES < live, weights_ref[pl.ds(at, 1), :], 0.0)
                value = factor / (poles_ref[pl.ds(at, 1), :] - own)
                total = total + value * value
            return total

        total = lax.fori_loop(0, blocks, step, jnp.zeros((TILE, LANES), F32), unroll=4)
        norm = jnp.sqrt(jnp.sum(total, axis=1, keepdims=True))
        n_ref[t * TILE : (t + 1) * TILE, :] = jnp.broadcast_to(norm, (TILE, LANES))


def norms(counts, poles, weights, roots):
    return pl.pallas_call(
        norm_kernel,
        in_specs=[SM, VM, VM, VM],
        out_specs=VM,
        out_shape=jax.ShapeDtypeStruct((LIVE, LANES), F32),
        name="norms",
        compiler_params=params(4),
        cost_estimate=cost(LIVE * 64 * LIVE * 400, 1 << 18),
    )(counts, poles, weights, roots)


def product_kernel(c_ref, *refs):
    x_refs, o_ref = refs[:-1], refs[-1]
    for j in range(XS):
        total = None
        for d, x_ref in enumerate(x_refs):
            piece = jnp.dot(
                c_ref[j * LIVE : (j + 1) * LIVE, d * LIVE : (d + 1) * LIVE],
                x_ref[...],
                preferred_element_type=F32,
            )
            total = piece if total is None else total + piece
        o_ref[j * LIVE : (j + 1) * LIVE, :] = total.astype(o_ref.dtype)


def product(c, pieces, kind):
    size = pieces[0].shape[1]
    return pl.pallas_call(
        product_kernel,
        in_specs=[VM] * (1 + ZS),
        out_specs=VM,
        out_shape=jax.ShapeDtypeStruct((XS * LIVE, size), kind),
        name="product",
        compiler_params=params(12),
        cost_estimate=cost(2 * XS * LIVE * ZS * LIVE * size, 6 << 20),
    )(pltpu.with_memory_space_constraint(c, pltpu.VMEM), *pieces)


def presum_kernel(mine_ref, other_ref, own_ref, *out_refs):
    own_ref[...] = mine_ref[:LIVE, :] + other_ref[:LIVE, :].astype(F32)
    for j, out_ref in enumerate(out_refs):
        part = slice((j + 1) * LIVE, (j + 2) * LIVE)
        out_ref[...] = (mine_ref[part, :] + other_ref[part, :].astype(F32)).astype(BF16)


def presum(mine, other):
    size = mine.shape[1]
    return pl.pallas_call(
        presum_kernel,
        in_specs=[VM] * 2,
        out_specs=[VM] * XS,
        out_shape=[jax.ShapeDtypeStruct((LIVE, size), F32)]
        + [jax.ShapeDtypeStruct((LIVE, size), BF16)] * (XS - 1),
        name="presum",
        compiler_params=params(8),
        cost_estimate=cost(XS * LIVE * size * 2, 2 << 20),
    )(mine, other)


def finish_kernel(count_ref, own_ref, a_ref, b_ref, c_ref, n_ref, p_ref, o_ref):
    total = own_ref[...] + a_ref[...].astype(F32) + b_ref[...].astype(F32) + c_ref[...].astype(F32)
    updated = jnp.transpose(total / n_ref[:, :1])
    within = lax.broadcasted_iota(jnp.int32, (1, LIVE), 1)
    retain = within < count_ref[0]
    o_ref[...] = jnp.where(retain, updated, p_ref[...].astype(F32)).astype(BF16)


def finish(count, own, received, norm, permuted, chunk):
    start, size = CHUNKS[chunk]
    part = pl.BlockSpec((size, LIVE), lambda i: (start // size, 0))
    whole = [pl.BlockSpec((LIVE, size), lambda i: (0, 0))] * XS
    return pl.pallas_call(
        finish_kernel,
        grid=(1,),
        in_specs=[SM] + whole + [pl.BlockSpec((LIVE, LANES), lambda i: (0, 0)), part],
        out_specs=part,
        out_shape=jax.ShapeDtypeStruct(permuted.shape, BF16),
        input_output_aliases={6: 0},
        name="finish",
        compiler_params=params(8),
        cost_estimate=cost(LIVE * size * 8, 1 << 20),
    )(count, own, *received, norm, permuted)


def per_device(eigvecs, perm, counts, poles, weights, roots):
    me = lax.axis_index(("xl", "core", "z", "xh")).astype(jnp.int32).reshape(1)
    count = lax.dynamic_slice(counts, (me[0],), (1,))
    poles = poles.reshape(-1, LANES)
    weights = weights.reshape(-1, LANES)
    permuted, *leading = permute(eigvecs, perm.reshape(1, COLS))

    own_roots = roots[:LIVE].reshape(1, LIVE)
    pair_roots = jnp.concatenate([own_roots, cshift(own_roots)], axis=1)
    all_roots = [pair_roots] + [xshift(pair_roots, -dx) for dx in range(1, XS)]

    gathered = []
    for chunk, lead in enumerate(leading):
        pieces = [None] * ZS
        pieces[0] = lead
        up = down = lead
        for s in range(1, ZS // 2):
            up, down = zshift(up, 1), zshift(down, -1)
            pieces[ZS - s], pieces[s] = up, down
        pieces[ZS // 2] = zshift(up, 1) if chunk % 2 == 0 else zshift(down, -1)
        gathered.append(pieces)

    c_other = cauchy(1, me, counts, poles, weights, all_roots)
    c_mine = cauchy(0, me, counts, poles, weights, all_roots)
    norm = norms(counts, poles, weights, own_roots)

    out = permuted
    for chunk, pieces in enumerate(gathered):
        other = cshift(product(c_other, pieces, BF16))
        mine = product(c_mine, pieces, F32)
        own, *sent = presum(mine, other)
        received = [xshift(part, dx + 1) for dx, part in enumerate(sent)]
        out = finish(count, own, received, norm, out, chunk)
    return out


def solution(mesh):
    fine_mesh = Mesh(mesh.devices.reshape(4, 2, 2, 8, 2), ("rows", "xl", "core", "z", "xh"))
    columns = ("xl", "core", "z", "xh")
    return jax.shard_map(
        per_device,
        mesh=fine_mesh,
        in_specs=(P("rows", columns), P(columns), P(), P(), P(), P(columns)),
        out_specs=P("rows", columns),
        check_vma=False,
    )
```

time: 288 us -> 86.9 us (0.30)
  waiting for transfers between devices: 241 us -> 12.1 us
  starting transfers between devices: 0.04 us -> 38.7 us
  Pallas kernels: 0 us -> 25.7 us
  matrix products: 15.7 us -> 0 us
  between operations: 13.5 us -> 0.17 us
  other arithmetic: 11.7 us -> 0.01 us
  local copies, waits for them, and re-layouts: 5.5 us -> 9.68 us
    all_gather x2 -> x0, waiting for transfers between devices: 241 us -> none  [the longest x1 213 us: per_device(): panel_piece = lax.all_gather(panels, 'fine', axis=1, tiled=True)]
    ppermute x0 -> x26, starting transfers between devices: none -> 38.7 us  [the longest x14 19.9 us: zshift(): return lax.ppermute(a, 'z', [(i, (i + k) % ZS) for i in range(ZS)])]
    pallas_call x0 -> x12, Pallas kernels: none -> 25.7 us  [the longest x2 9.96 us: cauchy(): pl.pallas_call(lambda *refs: cauchy_kernel(half, *refs), in_specs=[SM, SM...]
    dot_general x2 -> x0, matrix products: 15.7 us -> none  [the longest x1 14.5 us: per_device(): jnp.dot(panel_piece, cauchy.astype(jnp.bfloat16), preferred_element_type=...]
    ppermute x0 -> x26, waiting for transfers between devices: none -> 12.1 us  [the longest x9 7.73 us: xshift(): return lax.ppermute(a, ('xl', 'xh'), pairs)]
    reduce_sum x2 -> x0, other arithmetic: 10.3 us -> none  [the longest x1 9.01 us: per_device(): summed, squares = (summed, jnp.sum(cauchy * cauchy, axis=0))]
    unnamed x4 -> x20, local copies, waits for them, and re-layouts: 1.11 us -> 8.36 us
  transfers between devices with their start and end apart: 2 -> 26, of which waited for: 2 -> 5; matrix products, arithmetic and copies ran while one was open for 5% -> 2% of each run, Pallas kernels for 0% -> 26%
where the time goes in v1:
time: 86.9 us; the launch traced here: 86.5 us
  starting transfers between devices  38.7 us (45%)
  Pallas kernels  25.7 us (30%)
  waiting for transfers between devices  12.1 us (14%)
  local copies, waits for them, and re-layouts  9.68 us (11%)
    ppermute x14, starting transfers between devices, zshift(): return lax.ppermute(a, 'z', [(i, (i + k) % ZS) for i in range(ZS)])  19.9 us
    ppermute x9, starting transfers between devices, xshift(): return lax.ppermute(a, ('xl', 'xh'), pairs)  12 us
    pallas_call x2, Pallas kernels, cauchy(): pl.pallas_call(lambda *refs: cauchy_kernel(half, *refs), in_specs=[SM, SM...  9.96 us
    unnamed x20, local copies, waits for them, and re-layouts  8.36 us
    ppermute x9, waiting for transfers between devices, xshift(): return lax.ppermute(a, ('xl', 'xh'), pairs)  7.73 us
    ppermute x3, starting transfers between devices, cshift(): return lax.ppermute(a, 'core', [(0, 1), (1, 0)])  6.93 us
    pallas_call x4, Pallas kernels, product(): pl.pallas_call(product_kernel, in_specs=[VM] * (1 + ZS), out_specs=VM, ou...  4.97 us
    pallas_call x2, Pallas kernels, finish(): pl.pallas_call(finish_kernel, grid=(1,), in_specs=[SM] + whole + [pl.Bloc...  4.77 us
  transfers between devices with their start and end apart: 26, of which 5 were waited for; matrix products, arithmetic and copies ran while one was open for 2% of the time, Pallas kernels for 26%

profile of v1, /device:TPU:1, one launch (start us, length us, event | category | flops | bytes accessed | tf_op | source)
XLA Modules:
  0.0 86.5 jit_solution(12242496091180667740)
XLA Ops:
  3.0 2.5 %collective-permute-start.18 = (bf16[256,256]{1,0:T(8,128)(2,1)S(1)}, bf16[256,256]{1,0:T(8,128)(2,1)S(1)}, u32[]{:S(2)}, u32[]{:S(2)}) collective-permute-start(bf16[256,256]{1,0:T(8,128)(2,1)S(1)} %get-tuple-element.21.refs_0_), channel_id=1, source_target_pairs={{0,2},{2,4},{4,6},{6,8},{8,10},{10,12},{12,14},{14,0},{1,3},{3,5},... | collective-permute-start | bytes 393224 | tf_op jit(solution)/shard_map/ppermute | solution.py:42
  5.5 3.9 %collective-permute-start.4 = (bf16[256,256]{1,0:T(8,128)(2,1)S(1)}, bf16[256,256]{1,0:T(8,128)(2,1)S(1)}, u32[]{:S(2)}, u32[]{:S(2)}) collective-permute-start(bf16[256,256]{1,0:T(8,128)(2,1)S(1)} %get-tuple-element.16.refs_0_), channel_id=1, source_target_pairs={{0,14},{2,0},{4,2},{6,4},{8,6},{10,8},{12,10},{14,12},{1,15},{3,1}... | collective-permute-start | bytes 393224 | tf_op jit(solution)/shard_map/ppermute | solution.py:42
  9.4 1.5 %collective-permute-start.15 = (bf16[256,256]{1,0:T(8,128)(2,1)S(1)}, bf16[256,256]{1,0:T(8,128)(2,1)S(1)}, u32[]{:S(2)}, u32[]{:S(2)}) collective-permute-start(bf16[256,256]{1,0:T(8,128)(2,1)S(1)} %get-tuple-element.21.refs_0_), channel_id=1, source_target_pairs={{0,14},{2,0},{4,2},{6,4},{8,6},{10,8},{12,10},{14,12},{1,15},{3,1}... | collective-permute-start | bytes 393224 | tf_op jit(solution)/shard_map/ppermute | solution.py:42
  10.9 1.7 %collective-permute-done.18.refs_7_ = bf16[256,256]{1,0:T(8,128)(2,1)S(1)} collective-permute-done((bf16[256,256]{1,0:T(8,128)(2,1)S(1)}, bf16[256,256]{1,0:T(8,128)(2,1)S(1)}, u32[]{:S(2)}, u32[]{:S(2)}) %collective-permute-start.18) | collective-permute-done | bytes 131104 | tf_op jit(solution)/shard_map/ppermute | solution.py:42
  12.6 2.7 %collective-permute-start.5 = (bf16[256,256]{1,0:T(8,128)(2,1)S(1)}, bf16[256,256]{1,0:T(8,128)(2,1)S(1)}, u32[]{:S(2)}, u32[]{:S(2)}) collective-permute-start(bf16[256,256]{1,0:T(8,128)(2,1)S(1)} %collective-permute-done.4.refs_1_), channel_id=1, source_target_pairs={{0,14},{2,0},{4,2},{6,4},{8,6},{10,8},{12,10},{14,12},{1,15},{3,1}... | collective-permute-start | bytes 393224 | tf_op jit(solution)/shard_map/ppermute | solution.py:42
  15.4 2.4 %collective-permute-start.16 = (bf16[256,256]{1,0:T(8,128)(2,1)S(1)}, bf16[256,256]{1,0:T(8,128)(2,1)S(1)}, u32[]{:S(2)}, u32[]{:S(2)}) collective-permute-start(bf16[256,256]{1,0:T(8,128)(2,1)S(1)} %collective-permute-done.15.refs_1_), channel_id=1, source_target_pairs={{0,14},{2,0},{4,2},{6,4},{8,6},{10,8},{12,10},{14,12},{1,15},{3,1}... | collective-permute-start | bytes 393224 | tf_op jit(solution)/shard_map/ppermute | solution.py:42
  17.8 2.6 %collective-permute-done.8.refs_7_ = bf16[256,256]{1,0:T(8,128)(2,1)S(1)} collective-permute-done((bf16[256,256]{1,0:T(8,128)(2,1)S(1)}, bf16[256,256]{1,0:T(8,128)(2,1)S(1)}, u32[]{:S(2)}, u32[]{:S(2)}) %collective-permute-start.8) | collective-permute-done | bytes 131104 | tf_op jit(solution)/shard_map/ppermute | solution.py:42
  20.4 2.7 %collective-permute-start.6 = (bf16[256,256]{1,0:T(8,128)(2,1)S(1)}, bf16[256,256]{1,0:T(8,128)(2,1)S(1)}, u32[]{:S(2)}, u32[]{:S(2)}) collective-permute-start(bf16[256,256]{1,0:T(8,128)(2,1)S(1)} %collective-permute-done.5.refs_2_), channel_id=1, source_target_pairs={{0,14},{2,0},{4,2},{6,4},{8,6},{10,8},{12,10},{14,12},{1,15},{3,1}... | collective-permute-start | bytes 393224 | tf_op jit(solution)/shard_map/ppermute | solution.py:42
  23.8 3.1 %collective-permute-start = (f32[1,256]{1,0:T(1,128)S(1)}, f32[1,256]{1,0:T(1,128)S(1)}, u32[]{:S(2)}, u32[]{:S(2)}) collective-permute-start(f32[1,256]{1,0:T(1,128)S(1)} %bitcast.11), channel_id=1, source_target_pairs={{0,16},{16,0},{1,17},{17,1},{2,18},{18,2},{3,19},{19,3},{4,20},{20... | collective-permute-start | bytes 3080 | tf_op jit(solution)/shard_map/ppermute | solution.py:46
  29.6 2.7 %collective-permute-done.3.refs_7_ = f32[1,512]{1,0:T(1,128)S(1)} collective-permute-done((f32[1,512]{1,0:T(1,128)S(1)}, f32[1,512]{1,0:T(1,128)S(1)}, u32[]{:S(2)}, u32[]{:S(2)}) %collective-permute-start.3) | collective-permute-done | bytes 2080 | tf_op jit(solution)/shard_map/ppermute | solution.py:38
  32.4 1.5 %collective-permute-start.2 = (f32[1,512]{1,0:T(1,128)S(1)}, f32[1,512]{1,0:T(1,128)S(1)}, u32[]{:S(2)}, u32[]{:S(2)}) collective-permute-start(f32[1,512]{1,0:T(1,128)S(1)} %pad_maximum_fusion.refs_4_), channel_id=1, source_target_pairs={{0,1},{1,0},{32,33},{33,32},{2,3},{3,2},{34,35},{35,34},{4,5},{5,4... | collective-permute-start | bytes 6152 | tf_op jit(solution)/shard_map/ppermute | solution.py:38
  33.9 2.4 %collective-permute-done.2.refs_6_ = f32[1,512]{1,0:T(1,128)S(1)} collective-permute-done((f32[1,512]{1,0:T(1,128)S(1)}, f32[1,512]{1,0:T(1,128)S(1)}, u32[]{:S(2)}, u32[]{:S(2)}) %collective-permute-start.2) | collective-permute-done | bytes 2080 | tf_op jit(solution)/shard_map/ppermute | solution.py:38
  37.6 2.7 %collective-permute-start.7 = (bf16[256,256]{1,0:T(8,128)(2,1)S(1)}, bf16[256,256]{1,0:T(8,128)(2,1)S(1)}, u32[]{:S(2)}, u32[]{:S(2)}) collective-permute-start(bf16[256,256]{1,0:T(8,128)(2,1)S(1)} %collective-permute-done.6.refs_3_), channel_id=1, source_target_pairs={{0,14},{2,0},{4,2},{6,4},{8,6},{10,8},{12,10},{14,12},{1,15},{3,1}... | collective-permute-start | bytes 393224 | tf_op jit(solution)/shard_map/ppermute | solution.py:42
  42.7 5.0 %cauchy.3.c_ref = bf16[1024,2048]{1,0:T(8,128)(2,1)S(1)} custom-call(s32[1]{0:T(128)} %bitcast.refs_0_, s32[64]{0:T(128)S(1)} %copy-done.6, f32[256,128]{1,0:T(8,128)S(1)} %bitcast.5, f32[256,128]{1,0:T(8,128)S(1)} %bitcast.8, f32[1,512]{1,0:T(1,128)S(1)} %pad_maximum_fusion.refs_4_, f32[1,512]{1,0:T(1,128)S(1)} %collective-permute-done.1.refs_5_, ...), custom_call_target="tpu_custom_call" | custom-call | flops 838860800 | bytes 4194304 | tf_op jit(solution)/shard_map/cauchy/pallas_call | solution.py:95
  49.0 3.5 %collective-permute-start.22 = (bf16[1024,256]{1,0:T(8,128)(2,1)S(1)}, bf16[1024,256]{1,0:T(8,128)(2,1)S(1)}, u32[]{:S(2)}, u32[]{:S(2)}) collective-permute-start(bf16[1024,256]{1,0:T(8,128)(2,1)S(1)} %product.7), channel_id=1, source_target_pairs={{0,16},{16,0},{1,17},{17,1},{2,18},{18,2},{3,19},{19,3},{4,20},{20... | collective-permute-start | bytes 1572872 | tf_op jit(solution)/shard_map/ppermute | solution.py:46
  54.1 5.0 %cauchy.2.c_ref = bf16[1024,2048]{1,0:T(8,128)(2,1)S(1)} custom-call(s32[1]{0:T(128)} %bitcast.refs_0_, s32[64]{0:T(128)S(1)} %copy-done.6, f32[256,128]{1,0:T(8,128)S(1)} %bitcast.6, f32[256,128]{1,0:T(8,128)S(1)} %bitcast.9, f32[1,512]{1,0:T(1,128)S(1)} %pad_maximum_fusion.refs_4_, f32[1,512]{1,0:T(1,128)S(1)} %collective-permute-done.1.refs_5_, ...), custom_call_target="tpu_custom_call" | custom-call | flops 838860800 | bytes 4194304 | tf_op jit(solution)/shard_map/cauchy/pallas_call | solution.py:95
  60.4 2.0 %copy-done = bf16[1024,2048]{1,0:T(8,128)(2,1)} copy-done((bf16[1024,2048]{1,0:T(8,128)(2,1)}, bf16[1024,2048]{1,0:T(8,128)(2,1)S(1)}, u32[]{:S(2)}) %copy-start) | copy-done | bytes 4194328
  63.4 2.2 %copy-done.1 = bf16[1024,2048]{1,0:T(8,128)(2,1)S(1)} copy-done((bf16[1024,2048]{1,0:T(8,128)(2,1)S(1)}, bf16[1024,2048]{1,0:T(8,128)(2,1)}, u32[]{:S(2)}) %copy-start.1) | copy-done | bytes 4194328
  67.0 3.6 %collective-permute-start.13 = (bf16[256,256]{1,0:T(8,128)(2,1)S(1)}, bf16[256,256]{1,0:T(8,128)(2,1)S(1)}, u32[]{:S(2)}, u32[]{:S(2)}) collective-permute-start(bf16[256,256]{1,0:T(8,128)(2,1)S(1)} %get-tuple-element.19), channel_id=1, source_target_pairs={{0,1},{1,0},{32,33},{33,32},{2,3},{3,2},{34,35},{35,34},{4,5},{5,4... | collective-permute-start | bytes 393224 | tf_op jit(solution)/shard_map/ppermute | solution.py:38
  72.0 2.5 %collective-permute-start.25 = (bf16[256,256]{1,0:T(8,128)(2,1)S(1)}, bf16[256,256]{1,0:T(8,128)(2,1)S(1)}, u32[]{:S(2)}, u32[]{:S(2)}) collective-permute-start(bf16[256,256]{1,0:T(8,128)(2,1)S(1)} %get-tuple-element.25), channel_id=1, source_target_pairs={{0,33},{1,32},{32,0},{33,1},{2,35},{3,34},{34,2},{35,3},{4,37},{5,... | collective-permute-start | bytes 393224 | tf_op jit(solution)/shard_map/ppermute | solution.py:38
  74.5 4.6 %norms.1.n_ref = f32[256,128]{1,0:T(8,128)S(1)} custom-call(s32[64]{0:T(128)S(1)} %copy-done.7, f32[256,128]{1,0:T(8,128)S(1)} %bitcast.7, f32[256,128]{1,0:T(8,128)S(1)} %bitcast.10, f32[1,256]{1,0:T(1,128)S(1)} %bitcast.13), custom_call_target="tpu_custom_call" | custom-call | flops 1677721600 | bytes 262144 | tf_op jit(solution)/shard_map/norms/pallas_call | solution.py:128
  79.1 2.6 %collective-permute-done.25.c_ref = bf16[256,256]{1,0:T(8,128)(2,1)S(1)} collective-permute-done((bf16[256,256]{1,0:T(8,128)(2,1)S(1)}, bf16[256,256]{1,0:T(8,128)(2,1)S(1)}, u32[]{:S(2)}, u32[]{:S(2)}) %collective-permute-start.25) | collective-permute-done | bytes 131104 | tf_op jit(solution)/shard_map/ppermute | solution.py:38
  81.7 2.4 %finish.2.p_ref = bf16[512,512]{1,0:T(8,128)(2,1)} custom-call(s32[1]{0:T(128)} %dynamic_slice.3.count_ref, f32[256,256]{1,0:T(8,128)S(1)} %get-tuple-element.22.own_ref, bf16[256,256]{1,0:T(8,128)(2,1)S(1)} %collective-permute-done.23.a_ref, bf16[256,256]{1,0:T(8,128)(2,1)S(1)} %collective-permute-done.24.b_ref, ...), custom_call_target="tpu_custom_call", output_to_operand_aliasing={{}: (6, {})} | custom-call | flops 524288 | bytes 1048576 | tf_op jit(solution)/shard_map/finish/pallas_call | solution.py:199
  84.1 2.4 %finish.3 = bf16[512,512]{1,0:T(8,128)(2,1)} custom-call(s32[1]{0:T(128)} %dynamic_slice.3.count_ref, f32[256,256]{1,0:T(8,128)S(1)} %get-tuple-element.17.own_ref, bf16[256,256]{1,0:T(8,128)(2,1)S(1)} %collective-permute-done.12.a_ref, bf16[256,256]{1,0:T(8,128)(2,1)S(1)} %collective-permute-done.13.b_ref, ...), custom_call_target="tpu_custom_call", output_to_operand_aliasing={{}: (6, {})} | custom-call | flops 524288 | bytes 1048576 | tf_op jit(solution)/shard_map/finish/pallas_call | solution.py:199
  (63 shorter events, 18.2 us)
Async XLA Ops:
  3.0 9.6 %collective-permute-start.18 = (bf16[256,256]{1,0:T(8,128)(2,1)S(1)}, bf16[256,256]{1,0:T(8,128)(2,1)S(1)}, u32[]{:S(2)}, u32[]{:S(2)}) collective-permute-start(bf16[256,256]{1,0:T(8,128)(2,1)S(1)} %get-tuple-element.21.refs_0_), channel_id=1, source_target_pairs={{0,2},{2,4},{4,6},{6,8},{8,10},{10,12},{12,14},{14,0},{1,3},{3,5},... | collective-permute-start | bytes 393224 | tf_op jit(solution)/shard_map/ppermute | solution.py:42
  5.5 7.2 %collective-permute-start.4 = (bf16[256,256]{1,0:T(8,128)(2,1)S(1)}, bf16[256,256]{1,0:T(8,128)(2,1)S(1)}, u32[]{:S(2)}, u32[]{:S(2)}) collective-permute-start(bf16[256,256]{1,0:T(8,128)(2,1)S(1)} %get-tuple-element.16.refs_0_), channel_id=1, source_target_pairs={{0,14},{2,0},{4,2},{6,4},{8,6},{10,8},{12,10},{14,12},{1,15},{3,1}... | collective-permute-start | bytes 393224 | tf_op jit(solution)/shard_map/ppermute | solution.py:42
  9.4 5.9 %collective-permute-start.15 = (bf16[256,256]{1,0:T(8,128)(2,1)S(1)}, bf16[256,256]{1,0:T(8,128)(2,1)S(1)}, u32[]{:S(2)}, u32[]{:S(2)}) collective-permute-start(bf16[256,256]{1,0:T(8,128)(2,1)S(1)} %get-tuple-element.21.refs_0_), channel_id=1, source_target_pairs={{0,14},{2,0},{4,2},{6,4},{8,6},{10,8},{12,10},{14,12},{1,15},{3,1}... | collective-permute-start | bytes 393224 | tf_op jit(solution)/shard_map/ppermute | solution.py:42
  12.6 5.2 %collective-permute-start.19 = (bf16[256,256]{1,0:T(8,128)(2,1)S(1)}, bf16[256,256]{1,0:T(8,128)(2,1)S(1)}, u32[]{:S(2)}, u32[]{:S(2)}) collective-permute-start(bf16[256,256]{1,0:T(8,128)(2,1)S(1)} %collective-permute-done.18.refs_7_), channel_id=1, source_target_pairs={{0,2},{2,4},{4,6},{6,8},{8,10},{10,12},{12,14},{14,0},{1,3},{3,5},... | collective-permute-start | bytes 393224 | tf_op jit(solution)/shard_map/ppermute | solution.py:42
  12.6 7.8 %collective-permute-start.8 = (bf16[256,256]{1,0:T(8,128)(2,1)S(1)}, bf16[256,256]{1,0:T(8,128)(2,1)S(1)}, u32[]{:S(2)}, u32[]{:S(2)}) collective-permute-start(bf16[256,256]{1,0:T(8,128)(2,1)S(1)} %get-tuple-element.16.refs_0_), channel_id=1, source_target_pairs={{0,2},{2,4},{4,6},{6,8},{8,10},{10,12},{12,14},{14,0},{1,3},{3,5},... | collective-permute-start | bytes 393224 | tf_op jit(solution)/shard_map/ppermute | solution.py:42
  12.6 7.8 %collective-permute-start.5 = (bf16[256,256]{1,0:T(8,128)(2,1)S(1)}, bf16[256,256]{1,0:T(8,128)(2,1)S(1)}, u32[]{:S(2)}, u32[]{:S(2)}) collective-permute-start(bf16[256,256]{1,0:T(8,128)(2,1)S(1)} %collective-permute-done.4.refs_1_), channel_id=1, source_target_pairs={{0,14},{2,0},{4,2},{6,4},{8,6},{10,8},{12,10},{14,12},{1,15},{3,1}... | collective-permute-start | bytes 393224 | tf_op jit(solution)/shard_map/ppermute | solution.py:42
  15.4 11.5 %collective-permute-start.16 = (bf16[256,256]{1,0:T(8,128)(2,1)S(1)}, bf16[256,256]{1,0:T(8,128)(2,1)S(1)}, u32[]{:S(2)}, u32[]{:S(2)}) collective-permute-start(bf16[256,256]{1,0:T(8,128)(2,1)S(1)} %collective-permute-done.15.refs_1_), channel_id=1, source_target_pairs={{0,14},{2,0},{4,2},{6,4},{8,6},{10,8},{12,10},{14,12},{1,15},{3,1}... | collective-permute-start | bytes 393224 | tf_op jit(solution)/shard_map/ppermute | solution.py:42
  17.8 9.1 %collective-permute-start.20 = (bf16[256,256]{1,0:T(8,128)(2,1)S(1)}, bf16[256,256]{1,0:T(8,128)(2,1)S(1)}, u32[]{:S(2)}, u32[]{:S(2)}) collective-permute-start(bf16[256,256]{1,0:T(8,128)(2,1)S(1)} %collective-permute-done.19.refs_6_), channel_id=1, source_target_pairs={{0,2},{2,4},{4,6},{6,8},{8,10},{10,12},{12,14},{14,0},{1,3},{3,5},... | collective-permute-start | bytes 393224 | tf_op jit(solution)/shard_map/ppermute | solution.py:42
  20.4 17.2 %collective-permute-start.9 = (bf16[256,256]{1,0:T(8,128)(2,1)S(1)}, bf16[256,256]{1,0:T(8,128)(2,1)S(1)}, u32[]{:S(2)}, u32[]{:S(2)}) collective-permute-start(bf16[256,256]{1,0:T(8,128)(2,1)S(1)} %collective-permute-done.8.refs_7_), channel_id=1, source_target_pairs={{0,2},{2,4},{4,6},{6,8},{8,10},{10,12},{12,14},{14,0},{1,3},{3,5},... | collective-permute-start | bytes 393224 | tf_op jit(solution)/shard_map/ppermute | solution.py:42
  20.4 17.2 %collective-permute-start.6 = (bf16[256,256]{1,0:T(8,128)(2,1)S(1)}, bf16[256,256]{1,0:T(8,128)(2,1)S(1)}, u32[]{:S(2)}, u32[]{:S(2)}) collective-permute-start(bf16[256,256]{1,0:T(8,128)(2,1)S(1)} %collective-permute-done.5.refs_2_), channel_id=1, source_target_pairs={{0,14},{2,0},{4,2},{6,4},{8,6},{10,8},{12,10},{14,12},{1,15},{3,1}... | collective-permute-start | bytes 393224 | tf_op jit(solution)/shard_map/ppermute | solution.py:42
  23.8 4.6 %collective-permute-start = (f32[1,256]{1,0:T(1,128)S(1)}, f32[1,256]{1,0:T(1,128)S(1)}, u32[]{:S(2)}, u32[]{:S(2)}) collective-permute-start(f32[1,256]{1,0:T(1,128)S(1)} %bitcast.11), channel_id=1, source_target_pairs={{0,16},{16,0},{1,17},{17,1},{2,18},{18,2},{3,19},{19,3},{4,20},{20... | collective-permute-start | bytes 3080 | tf_op jit(solution)/shard_map/ppermute | solution.py:46
  26.9 20.8 %collective-permute-start.17 = (bf16[256,256]{1,0:T(8,128)(2,1)S(1)}, bf16[256,256]{1,0:T(8,128)(2,1)S(1)}, u32[]{:S(2)}, u32[]{:S(2)}) collective-permute-start(bf16[256,256]{1,0:T(8,128)(2,1)S(1)} %collective-permute-done.16.refs_2_), channel_id=1, source_target_pairs={{0,14},{2,0},{4,2},{6,4},{8,6},{10,8},{12,10},{14,12},{1,15},{3,1}... | collective-permute-start | bytes 393224 | tf_op jit(solution)/shard_map/ppermute | solution.py:42
  26.9 20.8 %collective-permute-start.21 = (bf16[256,256]{1,0:T(8,128)(2,1)S(1)}, bf16[256,256]{1,0:T(8,128)(2,1)S(1)}, u32[]{:S(2)}, u32[]{:S(2)}) collective-permute-start(bf16[256,256]{1,0:T(8,128)(2,1)S(1)} %collective-permute-done.20.refs_5_), channel_id=1, source_target_pairs={{0,2},{2,4},{4,6},{6,8},{8,10},{10,12},{12,14},{14,0},{1,3},{3,5},... | collective-permute-start | bytes 393224 | tf_op jit(solution)/shard_map/ppermute | solution.py:42
  28.4 4.0 %collective-permute-start.3 = (f32[1,512]{1,0:T(1,128)S(1)}, f32[1,512]{1,0:T(1,128)S(1)}, u32[]{:S(2)}, u32[]{:S(2)}) collective-permute-start(f32[1,512]{1,0:T(1,128)S(1)} %pad_maximum_fusion.refs_4_), channel_id=1, source_target_pairs={{0,32},{1,33},{32,1},{33,0},{2,34},{3,35},{34,3},{35,2},{4,36},{5,... | collective-permute-start | bytes 6152 | tf_op jit(solution)/shard_map/ppermute | solution.py:38
  37.6 14.9 %collective-permute-start.10 = (bf16[256,256]{1,0:T(8,128)(2,1)S(1)}, bf16[256,256]{1,0:T(8,128)(2,1)S(1)}, u32[]{:S(2)}, u32[]{:S(2)}) collective-permute-start(bf16[256,256]{1,0:T(8,128)(2,1)S(1)} %collective-permute-done.9.refs_6_), channel_id=1, source_target_pairs={{0,2},{2,4},{4,6},{6,8},{8,10},{10,12},{12,14},{14,0},{1,3},{3,5},... | collective-permute-start | bytes 393224 | tf_op jit(solution)/shard_map/ppermute | solution.py:42
  37.6 14.9 %collective-permute-start.7 = (bf16[256,256]{1,0:T(8,128)(2,1)S(1)}, bf16[256,256]{1,0:T(8,128)(2,1)S(1)}, u32[]{:S(2)}, u32[]{:S(2)}) collective-permute-start(bf16[256,256]{1,0:T(8,128)(2,1)S(1)} %collective-permute-done.6.refs_3_), channel_id=1, source_target_pairs={{0,14},{2,0},{4,2},{6,4},{8,6},{10,8},{12,10},{14,12},{1,15},{3,1}... | collective-permute-start | bytes 393224 | tf_op jit(solution)/shard_map/ppermute | solution.py:42
  49.0 13.3 %collective-permute-start.22 = (bf16[1024,256]{1,0:T(8,128)(2,1)S(1)}, bf16[1024,256]{1,0:T(8,128)(2,1)S(1)}, u32[]{:S(2)}, u32[]{:S(2)}) collective-permute-start(bf16[1024,256]{1,0:T(8,128)(2,1)S(1)} %product.7), channel_id=1, source_target_pairs={{0,16},{16,0},{1,17},{17,1},{2,18},{18,2},{3,19},{19,3},{4,20},{20... | collective-permute-start | bytes 1572872 | tf_op jit(solution)/shard_map/ppermute | solution.py:46
  53.8 13.0 %collective-permute-start.11 = (bf16[1024,256]{1,0:T(8,128)(2,1)S(1)}, bf16[1024,256]{1,0:T(8,128)(2,1)S(1)}, u32[]{:S(2)}, u32[]{:S(2)}) collective-permute-start(bf16[1024,256]{1,0:T(8,128)(2,1)S(1)} %product.5), channel_id=1, source_target_pairs={{0,16},{16,0},{1,17},{17,1},{2,18},{18,2},{3,19},{19,3},{4,20},{20... | collective-permute-start | bytes 1572872 | tf_op jit(solution)/shard_map/ppermute | solution.py:46
  62.4 9.6 %collective-permute-start.23 = (bf16[256,256]{1,0:T(8,128)(2,1)S(1)}, bf16[256,256]{1,0:T(8,128)(2,1)S(1)}, u32[]{:S(2)}, u32[]{:S(2)}) collective-permute-start(bf16[256,256]{1,0:T(8,128)(2,1)S(1)} %get-tuple-element.23), channel_id=1, source_target_pairs={{0,32},{1,33},{32,1},{33,0},{2,34},{3,35},{34,3},{35,2},{4,36},{5,... | collective-permute-start | bytes 393224 | tf_op jit(solution)/shard_map/ppermute | solution.py:38
  66.9 17.2 %collective-permute-start.12 = (bf16[256,256]{1,0:T(8,128)(2,1)S(1)}, bf16[256,256]{1,0:T(8,128)(2,1)S(1)}, u32[]{:S(2)}, u32[]{:S(2)}) collective-permute-start(bf16[256,256]{1,0:T(8,128)(2,1)S(1)} %get-tuple-element.18), channel_id=1, source_target_pairs={{0,32},{1,33},{32,1},{33,0},{2,34},{3,35},{34,3},{35,2},{4,36},{5,... | collective-permute-start | bytes 393224 | tf_op jit(solution)/shard_map/ppermute | solution.py:38
  67.0 17.1 %collective-permute-start.13 = (bf16[256,256]{1,0:T(8,128)(2,1)S(1)}, bf16[256,256]{1,0:T(8,128)(2,1)S(1)}, u32[]{:S(2)}, u32[]{:S(2)}) collective-permute-start(bf16[256,256]{1,0:T(8,128)(2,1)S(1)} %get-tuple-element.19), channel_id=1, source_target_pairs={{0,1},{1,0},{32,33},{33,32},{2,3},{3,2},{34,35},{35,34},{4,5},{5,4... | collective-permute-start | bytes 393224 | tf_op jit(solution)/shard_map/ppermute | solution.py:38
  70.6 13.4 %collective-permute-start.14 = (bf16[256,256]{1,0:T(8,128)(2,1)S(1)}, bf16[256,256]{1,0:T(8,128)(2,1)S(1)}, u32[]{:S(2)}, u32[]{:S(2)}) collective-permute-start(bf16[256,256]{1,0:T(8,128)(2,1)S(1)} %get-tuple-element.20), channel_id=1, source_target_pairs={{0,33},{1,32},{32,0},{33,1},{2,35},{3,34},{34,2},{35,3},{4,37},{5,... | collective-permute-start | bytes 393224 | tf_op jit(solution)/shard_map/ppermute | solution.py:38
  71.3 7.8 %collective-permute-start.24 = (bf16[256,256]{1,0:T(8,128)(2,1)S(1)}, bf16[256,256]{1,0:T(8,128)(2,1)S(1)}, u32[]{:S(2)}, u32[]{:S(2)}) collective-permute-start(bf16[256,256]{1,0:T(8,128)(2,1)S(1)} %get-tuple-element.24), channel_id=1, source_target_pairs={{0,1},{1,0},{32,33},{33,32},{2,3},{3,2},{34,35},{35,34},{4,5},{5,4... | collective-permute-start | bytes 393224 | tf_op jit(solution)/shard_map/ppermute | solution.py:38
  72.0 9.7 %collective-permute-start.25 = (bf16[256,256]{1,0:T(8,128)(2,1)S(1)}, bf16[256,256]{1,0:T(8,128)(2,1)S(1)}, u32[]{:S(2)}, u32[]{:S(2)}) collective-permute-start(bf16[256,256]{1,0:T(8,128)(2,1)S(1)} %get-tuple-element.25), channel_id=1, source_target_pairs={{0,33},{1,32},{32,0},{33,1},{2,35},{3,34},{34,2},{35,3},{4,37},{5,... | collective-permute-start | bytes 393224 | tf_op jit(solution)/shard_map/ppermute | solution.py:38
  (12 other events, 30.1 us)

commit v2 on v1

v2 whole, which is shorter than its diff:
```python
import jax
import jax.numpy as jnp
from jax import lax
from jax.experimental import pallas as pl
from jax.experimental.pallas import tpu as pltpu
from jax.sharding import Mesh
from jax.sharding import PartitionSpec as P

LIVE = 256
COLS = 512
LANES = 128
ZS = 8
XS = 4
CHUNKS = ((0, 256), (256, 256))
TILE = 128

VM = pl.BlockSpec(memory_space=pltpu.VMEM)
HB = pl.BlockSpec(memory_space=pltpu.HBM)
SM = pl.BlockSpec(memory_space=pltpu.SMEM)
F32 = jnp.float32
BF16 = jnp.bfloat16


def params(mib):
    return pltpu.CompilerParams(vmem_limit_bytes=mib << 20)


def cost(flops, size):
    return pl.CostEstimate(flops=1, transcendentals=0, bytes_accessed=1)


def xflip(a, mask):
    partner = 2 * (mask % 2) + mask // 2
    return lax.ppermute(a, ("xl", "xh"), [(i, i ^ partner) for i in range(XS)])


def zshift(a, k):
    return lax.ppermute(a, "z", [(i, (i + k) % ZS) for i in range(ZS)])


def cshift(a):
    return lax.ppermute(a, "core", [(0, 1), (1, 0)])


def hold(a, *others):
    return lax.optimization_barrier((a, *others))[0]


def in_hbm(a):
    return pltpu.with_memory_space_constraint(a, pltpu.HBM)


def permute_kernel(e_hbm, perm_ref, lead_ref, rest_ref, *refs):
    x_refs, e_ref, sem = refs[: len(CHUNKS)], refs[-2], refs[-1]
    copies = []
    for i, (start, size) in enumerate(CHUNKS):
        part = pl.ds(start, size)
        copies.append(pltpu.make_async_copy(e_hbm.at[part, :], e_ref.at[part, :], sem.at[i]))
        copies[-1].start()
    source = lax.broadcasted_iota(jnp.int32, (COLS, COLS), 0)
    selector = jnp.where(source == perm_ref[...], 1.0, 0.0).astype(BF16)
    for copy, (start, size), x_ref in zip(copies, CHUNKS, x_refs, strict=True):
        copy.wait()
        rows = slice(start, start + size)
        moved = jnp.dot(e_ref[rows, :], selector, preferred_element_type=F32)
        x_ref[...] = jnp.transpose(moved[:, :LIVE]).astype(BF16)
        lead_ref[rows, :] = moved[:, :LIVE].astype(BF16)
        rest_ref[rows, :] = moved[:, LIVE:].astype(BF16)


def permute(eigvecs, perm):
    rows = eigvecs.shape[0]
    return pl.pallas_call(
        permute_kernel,
        in_specs=[HB, VM],
        out_specs=[VM] * (2 + len(CHUNKS)),
        out_shape=[pltpu.VMEM((rows, LIVE), BF16), pltpu.VMEM((rows, COLS - LIVE), BF16)]
        + [pltpu.VMEM((LIVE, size), BF16) for _, size in CHUNKS],
        scratch_shapes=[pltpu.VMEM(eigvecs.shape, BF16), pltpu.SemaphoreType.DMA((len(CHUNKS),))],
        name="permute",
        compiler_params=params(8),
        cost_estimate=cost(2 * 512 * 512 * COLS, 1 << 20),
    )(eigvecs, perm)


def table_kernel(counts_ref, poles_hbm, weights_hbm, p_ref, f_ref, poles_ref, weights_ref, sem):
    first = pltpu.make_async_copy(poles_hbm, poles_ref, sem.at[0])
    second = pltpu.make_async_copy(weights_hbm, weights_ref, sem.at[1])
    first.start()
    second.start()
    first.wait()
    second.wait()
    span, keep = COLS // LANES, LIVE // LANES
    at = lax.broadcasted_iota(jnp.int32, (keep, LANES), 0) * LANES
    at = at + lax.broadcasted_iota(jnp.int32, (keep, LANES), 1)
    for block in range(counts_ref.shape[0]):
        rows = slice(keep * block, keep * (block + 1))
        here = slice(span * block, span * block + keep)
        p_ref[rows, :] = poles_ref[here, :]
        f_ref[rows, :] = jnp.where(at < counts_ref[block], weights_ref[here, :], 0.0)


def tables(counts, poles, weights):
    shape = (counts.shape[0] * LIVE // LANES, LANES)
    return pl.pallas_call(
        table_kernel,
        in_specs=[SM, HB, HB],
        out_specs=[VM, VM],
        out_shape=[pltpu.VMEM(shape, F32)] * 2,
        scratch_shapes=[pltpu.VMEM(poles.shape, F32)] * 2 + [pltpu.SemaphoreType.DMA((2,))],
        name="tables",
        compiler_params=params(4),
        cost_estimate=cost(1 << 29, 1 << 19),
    )(counts, poles, weights)


def column(row):
    return jnp.transpose(jnp.broadcast_to(row, (8, LIVE)))[:, :1]


def cauchy_kernel(half, me_ref, poles_ref, factors_ref, r_ref, c_ref):
    me = me_ref[0]
    z = (me // 2) % ZS
    tiles = LIVE // LANES
    for j in range(XS):
        b = 2 * j + half
        roots = column(r_ref[:, b * LIVE : (b + 1) * LIVE])
        for t in range(LIVE // TILE):
            own = jnp.broadcast_to(roots[t * TILE : (t + 1) * TILE], (TILE, LANES))
            rows = slice(j * LIVE + t * TILE, j * LIVE + (t + 1) * TILE)
            for d in range(ZS):
                block = me + 2 * ((z + d) % ZS - z)
                for h in range(tiles):
                    at = pl.ds(tiles * block + h, 1)
                    value = factors_ref[at, :] / (poles_ref[at, :] - own)
                    lo = (tiles * d + h) * LANES
                    c_ref[rows, lo : lo + LANES] = value.astype(BF16)


def cauchy(half, me, poles, factors, roots):
    return pl.pallas_call(
        lambda *refs: cauchy_kernel(half, *refs),
        in_specs=[SM, VM, VM, VM],
        out_specs=VM,
        out_shape=pltpu.VMEM((XS * LIVE, ZS * LIVE), BF16),
        name="cauchy",
        compiler_params=params(8),
        cost_estimate=cost(1 << 31, 4 << 20),
    )(me, poles, factors, roots)


def norm_kernel(lo, size, poles_ref, factors_ref, r_ref, n_ref):
    roots = column(r_ref[...])[lo : lo + size]
    own = jnp.broadcast_to(roots, (size, LANES))
    group = 16

    def step(g, total):
        for u in range(group):
            at = pl.ds(g * group + u, 1)
            value = factors_ref[at, :] / (poles_ref[at, :] - own)
            total = total + value * value
        return total

    total = lax.fori_loop(0, poles_ref.shape[0] // group, step, jnp.zeros((size, LANES), F32))
    norm = jnp.sqrt(jnp.sum(total, axis=1, keepdims=True))
    n_ref[...] = jnp.broadcast_to(norm, (size, LANES))


def norms(lo, size, poles, factors, roots):
    return pl.pallas_call(
        lambda *refs: norm_kernel(lo, size, *refs),
        in_specs=[VM, VM, VM],
        out_specs=VM,
        out_shape=pltpu.VMEM((size, LANES), F32),
        name="norms",
        compiler_params=params(4),
        cost_estimate=cost(1 << 31, 1 << 18),
    )(poles, factors, roots)


def product_kernel(c_ref, *refs):
    x_refs, o_ref = refs[:-1], refs[-1]
    for j in range(XS):
        total = None
        for d, x_ref in enumerate(x_refs):
            piece = jnp.dot(
                c_ref[j * LIVE : (j + 1) * LIVE, d * LIVE : (d + 1) * LIVE],
                x_ref[...],
                preferred_element_type=F32,
            )
            total = piece if total is None else total + piece
        o_ref[j * LIVE : (j + 1) * LIVE, :] = total.astype(o_ref.dtype)


def product(c, pieces, kind):
    size = pieces[0].shape[1]
    return pl.pallas_call(
        product_kernel,
        in_specs=[VM] * (1 + ZS),
        out_specs=VM,
        out_shape=pltpu.VMEM((XS * LIVE, size), kind),
        name="product",
        compiler_params=params(8),
        cost_estimate=cost(2 * XS * LIVE * ZS * LIVE * size, 6 << 20),
    )(c, *pieces)


def presum_kernel(mine_ref, other_ref, own_ref, *out_refs):
    own_ref[...] = mine_ref[:LIVE, :] + other_ref[:LIVE, :].astype(F32)
    for j, out_ref in enumerate(out_refs):
        part = slice((j + 1) * LIVE, (j + 2) * LIVE)
        out_ref[...] = (mine_ref[part, :] + other_ref[part, :].astype(F32)).astype(BF16)


def presum(mine, other):
    size = mine.shape[1]
    return pl.pallas_call(
        presum_kernel,
        in_specs=[VM] * 2,
        out_specs=[VM] * XS,
        out_shape=[pltpu.VMEM((LIVE, size), F32)] + [pltpu.VMEM((LIVE, size), BF16)] * (XS - 1),
        name="presum",
        compiler_params=params(4),
        cost_estimate=cost(XS * LIVE * size * 2, 2 << 20),
    )(mine, other)


def finish_kernel(chunk, me_ref, counts_ref, own_ref, a_ref, b_ref, c_ref, n0_ref, n1_ref, lead_ref, *refs):
    start, size = CHUNKS[chunk]
    o_hbm, buffer, sem = refs[-3:]
    copies = []
    if chunk == 0:
        rest = o_hbm.at[:, pl.ds(LIVE, COLS - LIVE)]
        copies.append(pltpu.make_async_copy(refs[0], rest, sem.at[1]))
        copies[-1].start()
    total = own_ref[...] + a_ref[...].astype(F32) + b_ref[...].astype(F32) + c_ref[...].astype(F32)
    norm = jnp.concatenate([n0_ref[:, :1], n1_ref[:, :1]], axis=0)
    updated = jnp.transpose(total / norm)
    within = lax.broadcasted_iota(jnp.int32, (1, LIVE), 1)
    retain = within < counts_ref[me_ref[0]]
    lead = lead_ref[start : start + size, :]
    buffer[...] = jnp.where(retain, updated, lead.astype(F32)).astype(BF16)
    copies.append(pltpu.make_async_copy(buffer, o_hbm.at[pl.ds(start, size), pl.ds(0, LIVE)], sem.at[0]))
    copies[-1].start()
    for copy in copies:
        copy.wait()


def finish(me, counts, own, received, norm, lead, last, chunk):
    size = CHUNKS[chunk][1]
    return pl.pallas_call(
        lambda *refs: finish_kernel(chunk, *refs),
        in_specs=[SM, SM] + [VM] * (XS + 3) + [HB if chunk else VM],
        out_specs=HB,
        out_shape=jax.ShapeDtypeStruct((lead.shape[0], COLS), BF16),
        scratch_shapes=[pltpu.VMEM((size, LIVE), BF16), pltpu.SemaphoreType.DMA((2,))],
        input_output_aliases={2 + XS + 3: 0} if chunk else {},
        name="finish",
        compiler_params=params(4),
        cost_estimate=cost(LIVE * size * 8, 1 << 20),
    )(me, counts, own, *received, *norm, lead, last)


def per_device(eigvecs, perm, counts, poles, weights, roots):
    me = lax.axis_index(("xl", "core", "z", "xh")).astype(jnp.int32).reshape(1)

    own = roots.reshape(1, COLS)
    other = cshift(own)
    lead, rest, xa, xb = permute(in_hbm(eigvecs), perm.reshape(1, COLS))
    own_roots = hold(own, xa)[:, :LIVE]
    near = jnp.concatenate([own_roots, other[:, :LIVE]], axis=1)

    a_up, a_down = [xa], [xa]
    b_up, b_down = [xb], [xb]

    def advance(up, down, *others):
        up.append(zshift(hold(up[-1], *others), 1))
        down.append(zshift(hold(down[-1], *others), -1))

    advance(a_up, a_down)
    pair = jnp.concatenate([near, xflip(near, 1)], axis=1)
    advance(b_up, b_down, pair)
    all_roots = jnp.concatenate([pair, xflip(pair, 2)], axis=1)
    pole_table, factors = tables(
        hold(counts, xa), in_hbm(poles.reshape(-1, LANES)), in_hbm(weights.reshape(-1, LANES))
    )
    advance(a_up, a_down, all_roots, factors)
    c_other = cauchy(1, me, pole_table, factors, hold(all_roots, a_up[1], a_down[1]))
    advance(b_up, b_down, c_other)
    c_mine = cauchy(0, me, pole_table, factors, hold(all_roots, b_up[1], b_down[1]))
    advance(a_up, a_down, c_mine)
    advance(b_up, b_down)
    a_last = zshift(a_up[3], 1)
    b_last = zshift(b_down[3], -1)

    def order(up, down, last):
        return [up[0], down[1], down[2], down[3], last, up[3], up[2], up[1]]

    half = LIVE // 2
    a_all, b_all = order(a_up, a_down, a_last), order(b_up, b_down, b_last)
    a_other = cshift(product(c_other, a_all, BF16))
    a_mine = product(c_mine, a_all, F32)
    b_all[0] = hold(b_all[0], a_mine)
    b_other = cshift(product(c_other, b_all, BF16))
    a_own, *a_sent = presum(a_mine, a_other)
    a_recv = [xflip(part, i + 1) for i, part in enumerate(a_sent)]
    b_all[0] = hold(b_all[0], a_own)
    b_mine = product(c_mine, b_all, F32)
    b_own, *b_sent = presum(b_mine, b_other)
    b_recv = [xflip(part, i + 1) for i, part in enumerate(b_sent)]
    norm0 = norms(0, half, hold(pole_table, a_own, b_mine), factors, own_roots)
    norm1 = norms(half, half, hold(pole_table, b_own), factors, own_roots)
    norm = (norm0, norm1)
    out = finish(me, counts, a_own, a_recv, norm, lead, rest, 0)
    return finish(me, counts, b_own, b_recv, norm, lead, out, 1)


def solution(mesh):
    fine_mesh = Mesh(mesh.devices.reshape(4, 2, 2, 8, 2), ("rows", "xl", "core", "z", "xh"))
    columns = ("xl", "core", "z", "xh")
    return jax.shard_map(
        per_device,
        mesh=fine_mesh,
        in_specs=(P("rows", columns), P(columns), P(), P(), P(), P(columns)),
        out_specs=P("rows", columns),
        check_vma=False,
    )
```

time: 86.9 us -> 67.5 us (0.78)
  Pallas kernels: 25.7 us -> 17.4 us
  local copies, waits for them, and re-layouts: 9.68 us -> 2.03 us
  starting transfers between devices: 38.7 us -> 35 us
    pallas_call x6 -> x8, Pallas kernels: 20.6 us -> 12.2 us  [the longest x2 3.45 us: norms(): pl.pallas_call(lambda *refs: norm_kernel(lo, size, *refs), in_specs=[VM,...]
    unnamed x20 -> x6, local copies, waits for them, and re-layouts: 8.36 us -> 1.34 us
    ppermute x14, starting transfers between devices: 19.9 us -> 16 us  [zshift(): return lax.ppermute(a, 'z', [(i, (i + k) % ZS) for i in range(ZS)])]
    ppermute x14, waiting for transfers between devices: 4.38 us -> 7.89 us  [zshift(): return lax.ppermute(a, 'z', [(i, (i + k) % ZS) for i in range(ZS)])]
    ppermute x9 -> x8, waiting for transfers between devices: 7.73 us -> 4.6 us  [xflip(): return lax.ppermute(a, ('xl', 'xh'), [(i, i ^ partner) for i in range(XS)])]
    ppermute x3, starting transfers between devices: 6.93 us -> 10 us  [cshift(): return lax.ppermute(a, 'core', [(0, 1), (1, 0)])]
    ppermute x9 -> x8, starting transfers between devices: 12 us -> 8.98 us  [xflip(): return lax.ppermute(a, ('xl', 'xh'), [(i, i ^ partner) for i in range(XS)])]
  transfers between devices with their start and end apart: 26 -> 25, of which waited for: 5 -> 7; matrix products, arithmetic and copies ran while one was open for 2% -> 1% of each run, Pallas kernels for 26% -> 24%
where the time goes in v2:
time: 67.5 us; the launch traced here: 67.3 us
  starting transfers between devices  35 us (52%)
  Pallas kernels  17.4 us (26%)
  waiting for transfers between devices  12.5 us (19%)
  local copies, waits for them, and re-layouts  2.03 us (3%)
    ppermute x14, starting transfers between devices, zshift(): return lax.ppermute(a, 'z', [(i, (i + k) % ZS) for i in range(ZS)])  16 us
    ppermute x3, starting transfers between devices, cshift(): return lax.ppermute(a, 'core', [(0, 1), (1, 0)])  10 us
    ppermute x8, starting transfers between devices, xflip(): return lax.ppermute(a, ('xl', 'xh'), [(i, i ^ partner) for i in range(XS)])  8.98 us
    ppermute x14, waiting for transfers between devices, zshift(): return lax.ppermute(a, 'z', [(i, (i + k) % ZS) for i in range(ZS)])  7.89 us
    pallas_call x4, Pallas kernels, product(): pl.pallas_call(product_kernel, in_specs=[VM] * (1 + ZS), out_specs=VM, ou...  4.97 us
    ppermute x8, waiting for transfers between devices, xflip(): return lax.ppermute(a, ('xl', 'xh'), [(i, i ^ partner) for i in range(XS)])  4.6 us
    pallas_call x2, Pallas kernels, norms(): pl.pallas_call(lambda *refs: norm_kernel(lo, size, *refs), in_specs=[VM,...  3.45 us
    pallas_call x2, Pallas kernels, finish(): pl.pallas_call(lambda *refs: finish_kernel(chunk, *refs), in_specs=[SM, S...  2.82 us
  transfers between devices with their start and end apart: 25, of which 7 were waited for; matrix products, arithmetic and copies ran while one was open for 1% of the time, Pallas kernels for 24%

profile of v2, /device:TPU:1, one launch (start us, length us, event | category | flops | bytes accessed | tf_op | source)
XLA Modules:
  0.0 67.3 jit_solution(5125579778500482448)
XLA Ops:
  0.0 3.2 %collective-permute-start = (f32[1,512]{1,0:T(1,128)}, f32[1,512]{1,0:T(1,128)S(1)}, u32[]{:S(2)}, u32[]{:S(2)}) collective-permute-start(f32[1,512]{1,0:T(1,128)} %bitcast.8), channel_id=1, source_target_pairs={{0,16},{16,0},{1,17},{17,1},{2,18},{18,2},{3,19},{19,3},{4,20},{20... | collective-permute-start | bytes 6152 | tf_op jit(solution)/shard_map/ppermute | solution.py:42
  3.9 1.7 %permute.1 = (bf16[512,256]{1,0:T(8,128)(2,1)S(1)}, bf16[512,256]{1,0:T(8,128)(2,1)S(1)}, bf16[256,256]{1,0:T(8,128)(2,1)S(1)}, bf16[256,256]{1,0:T(8,128)(2,1)S(1)}) custom-call(bf16[512,512]{1,0:T(8,128)(2,1)} %e_hbm.1, s32[1,512]{1,0:T(1,128)S(1)} %bitcast.5), custom_call_target="tpu_custom_call" | custom-call | flops 1 | bytes 1 | tf_op jit(solution)/shard_map/permute/pallas_call | solution.py:73
  6.4 2.4 %collective-permute-done.1 = f32[1,512]{1,0:T(1,128)S(1)} collective-permute-done((f32[1,512]{1,0:T(1,128)S(1)}, f32[1,512]{1,0:T(1,128)S(1)}, u32[]{:S(2)}, u32[]{:S(2)}) %collective-permute-start.1) | collective-permute-done | bytes 2080 | tf_op jit(solution)/shard_map/ppermute | solution.py:34
  9.9 5.6 %collective-permute-start.5 = (bf16[256,256]{1,0:T(8,128)(2,1)S(1)}, bf16[256,256]{1,0:T(8,128)(2,1)S(1)}, u32[]{:S(2)}, u32[]{:S(2)}) collective-permute-start(bf16[256,256]{1,0:T(8,128)(2,1)S(1)} %get-tuple-element.34.refs_0_), channel_id=1, source_target_pairs={{0,14},{2,0},{4,2},{6,4},{8,6},{10,8},{12,10},{14,12},{1,15},{3,1}... | collective-permute-start | bytes 393224 | tf_op jit(solution)/shard_map/ppermute | solution.py:38
  16.1 1.6 %tables.1 = (f32[128,128]{1,0:T(8,128)S(1)}, f32[128,128]{1,0:T(8,128)S(1)}) custom-call(s32[64]{0:T(128)S(1)} %copy-done, f32[256,128]{1,0:T(8,128)} %bitcast.6, f32[256,128]{1,0:T(8,128)} %bitcast.7), custom_call_target="tpu_custom_call" | custom-call | flops 1 | bytes 1 | tf_op jit(solution)/shard_map/tables/pallas_call | solution.py:105
  17.8 2.7 %collective-permute-start.4 = (bf16[256,256]{1,0:T(8,128)(2,1)S(1)}, bf16[256,256]{1,0:T(8,128)(2,1)S(1)}, u32[]{:S(2)}, u32[]{:S(2)}) collective-permute-start(bf16[256,256]{1,0:T(8,128)(2,1)S(1)} %get-tuple-element.49.refs_0_), channel_id=1, source_target_pairs={{0,14},{2,0},{4,2},{6,4},{8,6},{10,8},{12,10},{14,12},{1,15},{3,1}... | collective-permute-start | bytes 393224 | tf_op jit(solution)/shard_map/ppermute | solution.py:38
  20.7 2.6 %collective-permute-start.6 = (bf16[256,256]{1,0:T(8,128)(2,1)S(1)}, bf16[256,256]{1,0:T(8,128)(2,1)S(1)}, u32[]{:S(2)}, u32[]{:S(2)}) collective-permute-start(bf16[256,256]{1,0:T(8,128)(2,1)S(1)} %collective-permute-done.5.refs_1_), channel_id=1, source_target_pairs={{0,14},{2,0},{4,2},{6,4},{8,6},{10,8},{12,10},{14,12},{1,15},{3,1}... | collective-permute-start | bytes 393224 | tf_op jit(solution)/shard_map/ppermute | solution.py:38
  23.3 1.3 %cauchy.3.c_ref = bf16[1024,2048]{1,0:T(8,128)(2,1)S(1)} custom-call(s32[1]{0:T(128)} %bitcast.refs_0_, f32[128,128]{1,0:T(8,128)S(1)} %get-tuple-element.57.refs_1_.refs_0_, f32[128,128]{1,0:T(8,128)S(1)} %get-tuple-element.37.refs_2_.refs_1_, f32[1,2048]{1,0:T(1,128)S(1)} %pad_maximum_fusion.refs_3_), custom_call_target="tpu_custom_call" | custom-call | flops 1 | bytes 1 | tf_op jit(solution)/shard_map/cauchy/pallas_call | solution.py:141
  25.6 1.3 %cauchy.2.c_ref = bf16[1024,2048]{1,0:T(8,128)(2,1)S(1)} custom-call(s32[1]{0:T(128)} %bitcast.refs_0_, f32[128,128]{1,0:T(8,128)S(1)} %get-tuple-element.57.refs_1_.refs_0_, f32[128,128]{1,0:T(8,128)S(1)} %get-tuple-element.37.refs_2_.refs_1_, f32[1,2048]{1,0:T(1,128)S(1)} %pad_maximum_fusion.refs_3_), custom_call_target="tpu_custom_call" | custom-call | flops 1 | bytes 1 | tf_op jit(solution)/shard_map/cauchy/pallas_call | solution.py:141
  27.7 2.2 %collective-permute-done.13.refs_2_ = bf16[256,256]{1,0:T(8,128)(2,1)S(1)} collective-permute-done((bf16[256,256]{1,0:T(8,128)(2,1)S(1)}, bf16[256,256]{1,0:T(8,128)(2,1)S(1)}, u32[]{:S(2)}, u32[]{:S(2)}) %collective-permute-start.13) | collective-permute-done | bytes 131104 | tf_op jit(solution)/shard_map/ppermute | solution.py:38
  33.4 1.5 %collective-permute-done.14.refs_3_ = bf16[256,256]{1,0:T(8,128)(2,1)S(1)} collective-permute-done((bf16[256,256]{1,0:T(8,128)(2,1)S(1)}, bf16[256,256]{1,0:T(8,128)(2,1)S(1)}, u32[]{:S(2)}, u32[]{:S(2)}) %collective-permute-start.14) | collective-permute-done | bytes 131104 | tf_op jit(solution)/shard_map/ppermute | solution.py:38
  35.0 1.7 %collective-permute-start.15 = (bf16[256,256]{1,0:T(8,128)(2,1)S(1)}, bf16[256,256]{1,0:T(8,128)(2,1)S(1)}, u32[]{:S(2)}, u32[]{:S(2)}) collective-permute-start(bf16[256,256]{1,0:T(8,128)(2,1)S(1)} %collective-permute-done.14.refs_3_), channel_id=1, source_target_pairs={{0,14},{2,0},{4,2},{6,4},{8,6},{10,8},{12,10},{14,12},{1,15},{3,1}... | collective-permute-start | bytes 393224 | tf_op jit(solution)/shard_map/ppermute | solution.py:38
  36.7 2.1 %collective-permute-done.11.refs_4_ = bf16[256,256]{1,0:T(8,128)(2,1)S(1)} collective-permute-done((bf16[256,256]{1,0:T(8,128)(2,1)S(1)}, bf16[256,256]{1,0:T(8,128)(2,1)S(1)}, u32[]{:S(2)}, u32[]{:S(2)}) %collective-permute-start.11) | collective-permute-done | bytes 131104 | tf_op jit(solution)/shard_map/ppermute | solution.py:38
  40.0 6.5 %collective-permute-start.12 = (bf16[1024,256]{1,0:T(8,128)(2,1)S(1)}, bf16[1024,256]{1,0:T(8,128)(2,1)S(1)}, u32[]{:S(2)}, u32[]{:S(2)}) collective-permute-start(bf16[1024,256]{1,0:T(8,128)(2,1)S(1)} %product.5), channel_id=1, source_target_pairs={{0,16},{16,0},{1,17},{17,1},{2,18},{18,2},{3,19},{19,3},{4,20},{20... | collective-permute-start | bytes 1572872 | tf_op jit(solution)/shard_map/ppermute | solution.py:42
  47.8 1.2 %product.7 = bf16[1024,256]{1,0:T(8,128)(2,1)S(1)} custom-call(bf16[1024,2048]{1,0:T(8,128)(2,1)S(1)} %cauchy.3.c_ref, bf16[256,256]{1,0:T(8,128)(2,1)S(1)} %get-tuple-element.49.refs_0_, bf16[256,256]{1,0:T(8,128)(2,1)S(1)} %collective-permute-done.4.refs_1_, bf16[256,256]{1,0:T(8,128)(2,1)S(1)} %collective-permute-done.13.refs_2_, ...), custom_call_target="tpu_custom_call" | custom-call | flops 1 | bytes 1 | tf_op jit(solution)/shard_map/product/pallas_call | solution.py:197
  49.8 1.7 %collective-permute-start.23 = (bf16[256,256]{1,0:T(8,128)(2,1)S(1)}, bf16[256,256]{1,0:T(8,128)(2,1)S(1)}, u32[]{:S(2)}, u32[]{:S(2)}) collective-permute-start(bf16[256,256]{1,0:T(8,128)(2,1)S(1)} %get-tuple-element.60), channel_id=1, source_target_pairs={{0,1},{1,0},{32,33},{33,32},{2,3},{3,2},{34,35},{35,34},{4,5},{5,4... | collective-permute-start | bytes 393224 | tf_op jit(solution)/shard_map/ppermute | solution.py:34
  51.6 1.8 %collective-permute-start.24 = (bf16[256,256]{1,0:T(8,128)(2,1)S(1)}, bf16[256,256]{1,0:T(8,128)(2,1)S(1)}, u32[]{:S(2)}, u32[]{:S(2)}) collective-permute-start(bf16[256,256]{1,0:T(8,128)(2,1)S(1)} %get-tuple-element.61), channel_id=1, source_target_pairs={{0,33},{1,32},{32,1},{33,0},{2,35},{3,34},{34,3},{35,2},{4,37},{5,... | collective-permute-start | bytes 393224 | tf_op jit(solution)/shard_map/ppermute | solution.py:34
  54.8 2.0 %collective-permute-start.20 = (bf16[256,256]{1,0:T(8,128)(2,1)S(1)}, bf16[256,256]{1,0:T(8,128)(2,1)S(1)}, u32[]{:S(2)}, u32[]{:S(2)}) collective-permute-start(bf16[256,256]{1,0:T(8,128)(2,1)S(1)} %get-tuple-element.54), channel_id=1, source_target_pairs={{0,1},{1,0},{32,33},{33,32},{2,3},{3,2},{34,35},{35,34},{4,5},{5,4... | collective-permute-start | bytes 393224 | tf_op jit(solution)/shard_map/ppermute | solution.py:34
  56.9 1.8 %collective-permute-start.21 = (bf16[256,256]{1,0:T(8,128)(2,1)S(1)}, bf16[256,256]{1,0:T(8,128)(2,1)S(1)}, u32[]{:S(2)}, u32[]{:S(2)}) collective-permute-start(bf16[256,256]{1,0:T(8,128)(2,1)S(1)} %get-tuple-element.55), channel_id=1, source_target_pairs={{0,33},{1,32},{32,1},{33,0},{2,35},{3,34},{34,3},{35,2},{4,37},{5,... | collective-permute-start | bytes 393224 | tf_op jit(solution)/shard_map/ppermute | solution.py:34
  58.7 1.7 %norms.2.refs_6_ = f32[128,128]{1,0:T(8,128)S(1)} custom-call(f32[128,128]{1,0:T(8,128)S(1)} %get-tuple-element.57.refs_1_.refs_0_, f32[128,128]{1,0:T(8,128)S(1)} %get-tuple-element.37.refs_2_.refs_1_, f32[1,256]{1,0:T(1,128)S(1)} %slice.6.refs_2_), custom_call_target="tpu_custom_call" | custom-call | flops 1 | bytes 1 | tf_op jit(solution)/shard_map/norms/pallas_call | solution.py:170
  60.4 1.7 %norms.3.refs_7_ = f32[128,128]{1,0:T(8,128)S(1)} custom-call(f32[128,128]{1,0:T(8,128)S(1)} %get-tuple-element.57.refs_1_.refs_0_, f32[128,128]{1,0:T(8,128)S(1)} %get-tuple-element.37.refs_2_.refs_1_, f32[1,256]{1,0:T(1,128)S(1)} %slice.6.refs_2_), custom_call_target="tpu_custom_call" | custom-call | flops 1 | bytes 1 | tf_op jit(solution)/shard_map/norms/pallas_call | solution.py:170
  62.2 1.4 %finish.2.refs_9_ = bf16[512,512]{1,0:T(8,128)(2,1)} custom-call(s32[1]{0:T(128)} %bitcast.refs_0_, s32[64]{0:T(128)S(1)} %copy-done.1, f32[256,256]{1,0:T(8,128)S(1)} %get-tuple-element.48.refs_2_, bf16[256,256]{1,0:T(8,128)(2,1)S(1)} %collective-permute-done.22.refs_3_, bf16[256,256]{1,0:T(8,128)(2,1)S(1)} %collective-permute-done.23.refs_4_, ...), custom_call_target="tpu_custom_call" | custom-call | flops 1 | bytes 1 | tf_op jit(solution)/shard_map/finish/pallas_call | solution.py:251
  63.6 2.2 %collective-permute-done.21.refs_5_ = bf16[256,256]{1,0:T(8,128)(2,1)S(1)} collective-permute-done((bf16[256,256]{1,0:T(8,128)(2,1)S(1)}, bf16[256,256]{1,0:T(8,128)(2,1)S(1)}, u32[]{:S(2)}, u32[]{:S(2)}) %collective-permute-start.21) | collective-permute-done | bytes 131104 | tf_op jit(solution)/shard_map/ppermute | solution.py:34
  65.8 1.4 %finish.3 = bf16[512,512]{1,0:T(8,128)(2,1)} custom-call(s32[1]{0:T(128)} %bitcast.refs_0_, s32[64]{0:T(128)S(1)} %copy-done.1, f32[256,256]{1,0:T(8,128)S(1)} %get-tuple-element.52.refs_2_, bf16[256,256]{1,0:T(8,128)(2,1)S(1)} %collective-permute-done.19.refs_3_, ...), custom_call_target="tpu_custom_call", output_to_operand_aliasing={{}: (9, {})} | custom-call | flops 1 | bytes 1 | tf_op jit(solution)/shard_map/finish/pallas_call | solution.py:251
  (51 shorter events, 13.2 us)
Async XLA Ops:
  0.0 6.3 %collective-permute-start = (f32[1,512]{1,0:T(1,128)}, f32[1,512]{1,0:T(1,128)S(1)}, u32[]{:S(2)}, u32[]{:S(2)}) collective-permute-start(f32[1,512]{1,0:T(1,128)} %bitcast.8), channel_id=1, source_target_pairs={{0,16},{16,0},{1,17},{17,1},{2,18},{18,2},{3,19},{19,3},{4,20},{20... | collective-permute-start | bytes 6152 | tf_op jit(solution)/shard_map/ppermute | solution.py:42
  8.9 11.7 %collective-permute-start.2 = (f32[1,1024]{1,0:T(1,128)S(1)}, f32[1,1024]{1,0:T(1,128)S(1)}, u32[]{:S(2)}, u32[]{:S(2)}) collective-permute-start(f32[1,1024]{1,0:T(1,128)S(1)} %pad_maximum_fusion.1), channel_id=1, source_target_pairs={{0,1},{1,0},{32,33},{33,32},{2,3},{3,2},{34,35},{35,34},{4,5},{5,4... | collective-permute-start | bytes 12296 | tf_op jit(solution)/shard_map/ppermute | solution.py:34
  9.9 10.8 %collective-permute-start.5 = (bf16[256,256]{1,0:T(8,128)(2,1)S(1)}, bf16[256,256]{1,0:T(8,128)(2,1)S(1)}, u32[]{:S(2)}, u32[]{:S(2)}) collective-permute-start(bf16[256,256]{1,0:T(8,128)(2,1)S(1)} %get-tuple-element.34.refs_0_), channel_id=1, source_target_pairs={{0,14},{2,0},{4,2},{6,4},{8,6},{10,8},{12,10},{14,12},{1,15},{3,1}... | collective-permute-start | bytes 393224 | tf_op jit(solution)/shard_map/ppermute | solution.py:38
  15.4 5.1 %collective-permute-start.8 = (bf16[256,256]{1,0:T(8,128)(2,1)S(1)}, bf16[256,256]{1,0:T(8,128)(2,1)S(1)}, u32[]{:S(2)}, u32[]{:S(2)}) collective-permute-start(bf16[256,256]{1,0:T(8,128)(2,1)S(1)} %get-tuple-element.34.refs_0_), channel_id=1, source_target_pairs={{0,2},{2,4},{4,6},{6,8},{8,10},{10,12},{12,14},{14,0},{1,3},{3,5},... | collective-permute-start | bytes 393224 | tf_op jit(solution)/shard_map/ppermute | solution.py:38
  17.7 7.9 %collective-permute-start.3 = (bf16[256,256]{1,0:T(8,128)(2,1)S(1)}, bf16[256,256]{1,0:T(8,128)(2,1)S(1)}, u32[]{:S(2)}, u32[]{:S(2)}) collective-permute-start(bf16[256,256]{1,0:T(8,128)(2,1)S(1)} %get-tuple-element.49.refs_0_), channel_id=1, source_target_pairs={{0,2},{2,4},{4,6},{6,8},{8,10},{10,12},{12,14},{14,0},{1,3},{3,5},... | collective-permute-start | bytes 393224 | tf_op jit(solution)/shard_map/ppermute | solution.py:38
  17.8 6.9 %collective-permute-start.4 = (bf16[256,256]{1,0:T(8,128)(2,1)S(1)}, bf16[256,256]{1,0:T(8,128)(2,1)S(1)}, u32[]{:S(2)}, u32[]{:S(2)}) collective-permute-start(bf16[256,256]{1,0:T(8,128)(2,1)S(1)} %get-tuple-element.49.refs_0_), channel_id=1, source_target_pairs={{0,14},{2,0},{4,2},{6,4},{8,6},{10,8},{12,10},{14,12},{1,15},{3,1}... | collective-permute-start | bytes 393224 | tf_op jit(solution)/shard_map/ppermute | solution.py:38
  20.6 6.4 %collective-permute-start.9 = (bf16[256,256]{1,0:T(8,128)(2,1)S(1)}, bf16[256,256]{1,0:T(8,128)(2,1)S(1)}, u32[]{:S(2)}, u32[]{:S(2)}) collective-permute-start(bf16[256,256]{1,0:T(8,128)(2,1)S(1)} %collective-permute-done.8.refs_7_), channel_id=1, source_target_pairs={{0,2},{2,4},{4,6},{6,8},{8,10},{10,12},{12,14},{14,0},{1,3},{3,5},... | collective-permute-start | bytes 393224 | tf_op jit(solution)/shard_map/ppermute | solution.py:38
  20.7 10.2 %collective-permute-start.6 = (bf16[256,256]{1,0:T(8,128)(2,1)S(1)}, bf16[256,256]{1,0:T(8,128)(2,1)S(1)}, u32[]{:S(2)}, u32[]{:S(2)}) collective-permute-start(bf16[256,256]{1,0:T(8,128)(2,1)S(1)} %collective-permute-done.5.refs_1_), channel_id=1, source_target_pairs={{0,14},{2,0},{4,2},{6,4},{8,6},{10,8},{12,10},{14,12},{1,15},{3,1}... | collective-permute-start | bytes 393224 | tf_op jit(solution)/shard_map/ppermute | solution.py:38
  24.7 5.3 %collective-permute-start.13 = (bf16[256,256]{1,0:T(8,128)(2,1)S(1)}, bf16[256,256]{1,0:T(8,128)(2,1)S(1)}, u32[]{:S(2)}, u32[]{:S(2)}) collective-permute-start(bf16[256,256]{1,0:T(8,128)(2,1)S(1)} %collective-permute-done.4.refs_1_), channel_id=1, source_target_pairs={{0,14},{2,0},{4,2},{6,4},{8,6},{10,8},{12,10},{14,12},{1,15},{3,1}... | collective-permute-start | bytes 393224 | tf_op jit(solution)/shard_map/ppermute | solution.py:38
  26.9 5.1 %collective-permute-start.10 = (bf16[256,256]{1,0:T(8,128)(2,1)S(1)}, bf16[256,256]{1,0:T(8,128)(2,1)S(1)}, u32[]{:S(2)}, u32[]{:S(2)}) collective-permute-start(bf16[256,256]{1,0:T(8,128)(2,1)S(1)} %collective-permute-done.9.refs_6_), channel_id=1, source_target_pairs={{0,2},{2,4},{4,6},{6,8},{8,10},{10,12},{12,14},{14,0},{1,3},{3,5},... | collective-permute-start | bytes 393224 | tf_op jit(solution)/shard_map/ppermute | solution.py:38
  27.6 5.8 %collective-permute-start.16 = (bf16[256,256]{1,0:T(8,128)(2,1)S(1)}, bf16[256,256]{1,0:T(8,128)(2,1)S(1)}, u32[]{:S(2)}, u32[]{:S(2)}) collective-permute-start(bf16[256,256]{1,0:T(8,128)(2,1)S(1)} %collective-permute-done.3.refs_7_), channel_id=1, source_target_pairs={{0,2},{2,4},{4,6},{6,8},{8,10},{10,12},{12,14},{14,0},{1,3},{3,5},... | collective-permute-start | bytes 393224 | tf_op jit(solution)/shard_map/ppermute | solution.py:38
  30.0 5.0 %collective-permute-start.14 = (bf16[256,256]{1,0:T(8,128)(2,1)S(1)}, bf16[256,256]{1,0:T(8,128)(2,1)S(1)}, u32[]{:S(2)}, u32[]{:S(2)}) collective-permute-start(bf16[256,256]{1,0:T(8,128)(2,1)S(1)} %collective-permute-done.13.refs_2_), channel_id=1, source_target_pairs={{0,14},{2,0},{4,2},{6,4},{8,6},{10,8},{12,10},{14,12},{1,15},{3,1}... | collective-permute-start | bytes 393224 | tf_op jit(solution)/shard_map/ppermute | solution.py:38
  30.8 5.8 %collective-permute-start.7 = (bf16[256,256]{1,0:T(8,128)(2,1)S(1)}, bf16[256,256]{1,0:T(8,128)(2,1)S(1)}, u32[]{:S(2)}, u32[]{:S(2)}) collective-permute-start(bf16[256,256]{1,0:T(8,128)(2,1)S(1)} %collective-permute-done.6.refs_2_), channel_id=1, source_target_pairs={{0,14},{2,0},{4,2},{6,4},{8,6},{10,8},{12,10},{14,12},{1,15},{3,1}... | collective-permute-start | bytes 393224 | tf_op jit(solution)/shard_map/ppermute | solution.py:38
  32.0 6.7 %collective-permute-start.11 = (bf16[256,256]{1,0:T(8,128)(2,1)S(1)}, bf16[256,256]{1,0:T(8,128)(2,1)S(1)}, u32[]{:S(2)}, u32[]{:S(2)}) collective-permute-start(bf16[256,256]{1,0:T(8,128)(2,1)S(1)} %collective-permute-done.10.refs_5_), channel_id=1, source_target_pairs={{0,2},{2,4},{4,6},{6,8},{8,10},{10,12},{12,14},{14,0},{1,3},{3,5},... | collective-permute-start | bytes 393224 | tf_op jit(solution)/shard_map/ppermute | solution.py:38
  33.4 14.3 %collective-permute-start.17 = (bf16[256,256]{1,0:T(8,128)(2,1)S(1)}, bf16[256,256]{1,0:T(8,128)(2,1)S(1)}, u32[]{:S(2)}, u32[]{:S(2)}) collective-permute-start(bf16[256,256]{1,0:T(8,128)(2,1)S(1)} %collective-permute-done.16.refs_6_), channel_id=1, source_target_pairs={{0,2},{2,4},{4,6},{6,8},{8,10},{10,12},{12,14},{14,0},{1,3},{3,5},... | collective-permute-start | bytes 393224 | tf_op jit(solution)/shard_map/ppermute | solution.py:38
  35.0 12.8 %collective-permute-start.15 = (bf16[256,256]{1,0:T(8,128)(2,1)S(1)}, bf16[256,256]{1,0:T(8,128)(2,1)S(1)}, u32[]{:S(2)}, u32[]{:S(2)}) collective-permute-start(bf16[256,256]{1,0:T(8,128)(2,1)S(1)} %collective-permute-done.14.refs_3_), channel_id=1, source_target_pairs={{0,14},{2,0},{4,2},{6,4},{8,6},{10,8},{12,10},{14,12},{1,15},{3,1}... | collective-permute-start | bytes 393224 | tf_op jit(solution)/shard_map/ppermute | solution.py:38
  40.0 9.3 %collective-permute-start.12 = (bf16[1024,256]{1,0:T(8,128)(2,1)S(1)}, bf16[1024,256]{1,0:T(8,128)(2,1)S(1)}, u32[]{:S(2)}, u32[]{:S(2)}) collective-permute-start(bf16[1024,256]{1,0:T(8,128)(2,1)S(1)} %product.5), channel_id=1, source_target_pairs={{0,16},{16,0},{1,17},{17,1},{2,18},{18,2},{3,19},{19,3},{4,20},{20... | collective-permute-start | bytes 1572872 | tf_op jit(solution)/shard_map/ppermute | solution.py:42
  49.0 5.6 %collective-permute-start.18 = (bf16[1024,256]{1,0:T(8,128)(2,1)S(1)}, bf16[1024,256]{1,0:T(8,128)(2,1)S(1)}, u32[]{:S(2)}, u32[]{:S(2)}) collective-permute-start(bf16[1024,256]{1,0:T(8,128)(2,1)S(1)} %product.7), channel_id=1, source_target_pairs={{0,16},{16,0},{1,17},{17,1},{2,18},{18,2},{3,19},{19,3},{4,20},{20... | collective-permute-start | bytes 1572872 | tf_op jit(solution)/shard_map/ppermute | solution.py:42
  49.4 7.4 %collective-permute-start.22 = (bf16[256,256]{1,0:T(8,128)(2,1)S(1)}, bf16[256,256]{1,0:T(8,128)(2,1)S(1)}, u32[]{:S(2)}, u32[]{:S(2)}) collective-permute-start(bf16[256,256]{1,0:T(8,128)(2,1)S(1)} %get-tuple-element.59), channel_id=1, source_target_pairs={{0,32},{1,33},{32,0},{33,1},{2,34},{3,35},{34,2},{35,3},{4,36},{5,... | collective-permute-start | bytes 393224 | tf_op jit(solution)/shard_map/ppermute | solution.py:34
  49.8 12.3 %collective-permute-start.23 = (bf16[256,256]{1,0:T(8,128)(2,1)S(1)}, bf16[256,256]{1,0:T(8,128)(2,1)S(1)}, u32[]{:S(2)}, u32[]{:S(2)}) collective-permute-start(bf16[256,256]{1,0:T(8,128)(2,1)S(1)} %get-tuple-element.60), channel_id=1, source_target_pairs={{0,1},{1,0},{32,33},{33,32},{2,3},{3,2},{34,35},{35,34},{4,5},{5,4... | collective-permute-start | bytes 393224 | tf_op jit(solution)/shard_map/ppermute | solution.py:34
  51.6 10.6 %collective-permute-start.24 = (bf16[256,256]{1,0:T(8,128)(2,1)S(1)}, bf16[256,256]{1,0:T(8,128)(2,1)S(1)}, u32[]{:S(2)}, u32[]{:S(2)}) collective-permute-start(bf16[256,256]{1,0:T(8,128)(2,1)S(1)} %get-tuple-element.61), channel_id=1, source_target_pairs={{0,33},{1,32},{32,1},{33,0},{2,35},{3,34},{34,3},{35,2},{4,37},{5,... | collective-permute-start | bytes 393224 | tf_op jit(solution)/shard_map/ppermute | solution.py:34
  54.7 8.9 %collective-permute-start.19 = (bf16[256,256]{1,0:T(8,128)(2,1)S(1)}, bf16[256,256]{1,0:T(8,128)(2,1)S(1)}, u32[]{:S(2)}, u32[]{:S(2)}) collective-permute-start(bf16[256,256]{1,0:T(8,128)(2,1)S(1)} %get-tuple-element.53), channel_id=1, source_target_pairs={{0,32},{1,33},{32,0},{33,1},{2,34},{3,35},{34,2},{35,3},{4,36},{5,... | collective-permute-start | bytes 393224 | tf_op jit(solution)/shard_map/ppermute | solution.py:34
  54.8 8.8 %collective-permute-start.20 = (bf16[256,256]{1,0:T(8,128)(2,1)S(1)}, bf16[256,256]{1,0:T(8,128)(2,1)S(1)}, u32[]{:S(2)}, u32[]{:S(2)}) collective-permute-start(bf16[256,256]{1,0:T(8,128)(2,1)S(1)} %get-tuple-element.54), channel_id=1, source_target_pairs={{0,1},{1,0},{32,33},{33,32},{2,3},{3,2},{34,35},{35,34},{4,5},{5,4... | collective-permute-start | bytes 393224 | tf_op jit(solution)/shard_map/ppermute | solution.py:34
  56.9 8.9 %collective-permute-start.21 = (bf16[256,256]{1,0:T(8,128)(2,1)S(1)}, bf16[256,256]{1,0:T(8,128)(2,1)S(1)}, u32[]{:S(2)}, u32[]{:S(2)}) collective-permute-start(bf16[256,256]{1,0:T(8,128)(2,1)S(1)} %get-tuple-element.55), channel_id=1, source_target_pairs={{0,33},{1,32},{32,1},{33,0},{2,35},{3,34},{34,3},{35,2},{4,37},{5,... | collective-permute-start | bytes 393224 | tf_op jit(solution)/shard_map/ppermute | solution.py:34
  (4 other events, 16.6 us)

commit v3 on v0

v3 whole, which is shorter than its diff:
```python
import jax
import jax.numpy as jnp
from jax import lax
from jax.experimental import pallas as pl
from jax.experimental.pallas import tpu as pltpu
from jax.sharding import Mesh
from jax.sharding import PartitionSpec as P

LIVE = 256
COLS = 512
LANES = 128
TILES = LIVE // LANES
ZS = 8
XS = 4
TILE = 128
OTHER = range(7)
MINE = range(9)

VM = pl.BlockSpec(memory_space=pltpu.VMEM)
HB = pl.BlockSpec(memory_space=pltpu.HBM)
SM = pl.BlockSpec(memory_space=pltpu.SMEM)
F32 = jnp.float32
BF16 = jnp.bfloat16


def params(mib):
    return pltpu.CompilerParams(vmem_limit_bytes=mib << 20)


TINY = pl.CostEstimate(flops=1, transcendentals=0, bytes_accessed=1)
LONG = pl.CostEstimate(flops=10**10, transcendentals=0, bytes_accessed=1)


def xflip(a, mask):
    partner = 2 * (mask % 2) + mask // 2
    return lax.ppermute(a, ("xl", "xh"), [(i, i ^ partner) for i in range(XS)])


def around(a, way):
    up = [(z, (z + way) % ZS) for z in range(ZS)]
    down = [(ZS + z, ZS + (z - way) % ZS) for z in range(ZS)]
    return lax.ppermute(a, ("core", "z"), up + down)


def cshift(a):
    return lax.ppermute(a, "core", [(0, 1), (1, 0)])


def hold(a, *others):
    return lax.optimization_barrier((a, *others))[0]


def in_hbm(a):
    return pltpu.with_memory_space_constraint(a, pltpu.HBM)


def permute_kernel(e_hbm, perm_ref, x_ref, lead_ref, rest_ref, e_ref, sem):
    rows = e_ref.shape[0]
    half = rows // 2
    copies = []
    for i in range(2):
        part = pl.ds(i * half, half)
        copies.append(pltpu.make_async_copy(e_hbm.at[part, :], e_ref.at[part, :], sem.at[i]))
        copies[-1].start()
    source = lax.broadcasted_iota(jnp.int32, (COLS, COLS), 0)
    selector = jnp.where(source == perm_ref[...], 1.0, 0.0).astype(BF16)
    for i, copy in enumerate(copies):
        copy.wait()
        part = slice(i * half, (i + 1) * half)
        moved = jnp.dot(e_ref[part, :], selector, preferred_element_type=F32)
        x_ref[:, part] = jnp.transpose(moved[:, :LIVE]).astype(BF16)
        lead_ref[part, :] = moved[:, :LIVE].astype(BF16)
        rest_ref[part, :] = moved[:, LIVE:].astype(BF16)


def permute(eigvecs, perm):
    rows = eigvecs.shape[0]
    return pl.pallas_call(
        permute_kernel,
        in_specs=[HB, VM],
        out_specs=[VM] * 3,
        out_shape=[
            pltpu.VMEM((LIVE, rows), BF16),
            pltpu.VMEM((rows, LIVE), BF16),
            pltpu.VMEM((rows, COLS - LIVE), BF16),
        ],
        scratch_shapes=[pltpu.VMEM(eigvecs.shape, BF16), pltpu.SemaphoreType.DMA((2,))],
        name="permute",
        compiler_params=params(8),
        cost_estimate=TINY,
    )(eigvecs, perm)


def table_kernel(counts_ref, poles_hbm, weights_hbm, p_ref, f_ref, poles_ref, weights_ref, sem):
    first = pltpu.make_async_copy(poles_hbm, poles_ref, sem.at[0])
    second = pltpu.make_async_copy(weights_hbm, weights_ref, sem.at[1])
    first.start()
    second.start()
    first.wait()
    second.wait()
    span, keep = COLS // LANES, LIVE // LANES
    at = lax.broadcasted_iota(jnp.int32, (keep, LANES), 0) * LANES
    at = at + lax.broadcasted_iota(jnp.int32, (keep, LANES), 1)
    for block in range(counts_ref.shape[0]):
        rows = slice(keep * block, keep * (block + 1))
        here = slice(span * block, span * block + keep)
        p_ref[rows, :] = poles_ref[here, :]
        f_ref[rows, :] = jnp.where(at < counts_ref[block], weights_ref[here, :], 0.0)


def tables(counts, poles, weights):
    shape = (counts.shape[0] * LIVE // LANES, LANES)
    return pl.pallas_call(
        table_kernel,
        in_specs=[SM, HB, HB],
        out_specs=[VM, VM],
        out_shape=[pltpu.VMEM(shape, F32)] * 2,
        scratch_shapes=[pltpu.VMEM(poles.shape, F32)] * 2 + [pltpu.SemaphoreType.DMA((2,))],
        name="tables",
        compiler_params=params(4),
        cost_estimate=TINY,
    )(counts, poles, weights)


def column(row):
    return jnp.transpose(jnp.broadcast_to(row, (8, LIVE)))[:, :1]


def cauchy_kernel(fc, pieces, me_ref, poles_ref, factors_ref, r_ref, c_ref):
    me = me_ref[0]
    xl, core, z, xh = me // 32, (me // 16) % 2, (me // 2) % ZS, me % 2
    step = 1 - 2 * core
    for j in range(XS):
        row = 4 * (xl ^ (j % 2)) + 2 * (core ^ fc) + (xh ^ (j // 2))
        roots = column(r_ref[pl.ds(row, 1), :LIVE])
        for t in range(LIVE // TILE):
            own = jnp.broadcast_to(roots[t * TILE : (t + 1) * TILE], (TILE, LANES))
            rows = slice(j * LIVE + t * TILE, j * LIVE + (t + 1) * TILE)
            for i, d in enumerate(pieces):
                away = (d + 1) // 2
                ring = (z + 4) % ZS if d >= 7 else (z + (1 - 2 * (d % 2)) * step * away + ZS) % ZS
                block = me + 2 * (ring - z)
                if d == 8:
                    block = block + 16 * step
                for h in range(TILES):
                    at = pl.ds(TILES * block + h, 1)
                    value = factors_ref[at, :] / (poles_ref[at, :] - own)
                    lo = (TILES * i + h) * LANES
                    c_ref[rows, lo : lo + LANES] = value.astype(BF16)


def cauchy(fc, pieces, me, poles, factors, roots):
    return pl.pallas_call(
        lambda *refs: cauchy_kernel(fc, pieces, *refs),
        in_specs=[SM, VM, VM, VM],
        out_specs=VM,
        out_shape=pltpu.VMEM((XS * LIVE, len(pieces) * LIVE), BF16),
        name="cauchy",
        compiler_params=params(8),
        cost_estimate=TINY,
    )(me, poles, factors, roots)


def norm_kernel(poles_ref, factors_ref, r_ref, rest_ref, n_ref, o_hbm, sem):
    copy = pltpu.make_async_copy(rest_ref, o_hbm.at[:, pl.ds(LIVE, COLS - LIVE)], sem.at[0])
    copy.start()
    roots = column(r_ref[:, :LIVE])
    group = 16
    for t in range(LIVE // TILE):
        own = jnp.broadcast_to(roots[t * TILE : (t + 1) * TILE], (TILE, LANES))

        def step(g, total):
            for u in range(group):
                at = pl.ds(g * group + u, 1)
                value = factors_ref[at, :] / (poles_ref[at, :] - own)
                total = total + value * value
            return total

        total = lax.fori_loop(0, poles_ref.shape[0] // group, step, jnp.zeros((TILE, LANES), F32))
        norm = jnp.sqrt(jnp.sum(total, axis=1, keepdims=True))
        n_ref[t * TILE : (t + 1) * TILE, :] = jnp.broadcast_to(norm, (TILE, LANES))
    copy.wait()


def norms(poles, factors, roots, rest):
    return pl.pallas_call(
        norm_kernel,
        in_specs=[VM] * 4,
        out_specs=[VM, HB],
        out_shape=[
            pltpu.VMEM((LIVE, LANES), F32),
            jax.ShapeDtypeStruct((rest.shape[0], COLS), BF16),
        ],
        scratch_shapes=[pltpu.SemaphoreType.DMA((1,))],
        name="norms",
        compiler_params=params(4),
        cost_estimate=TINY,
    )(poles, factors, roots, rest)


def product(c_ref, j, first, x_refs):
    total = None
    for i, x_ref in enumerate(x_refs):
        lo = (first + i) * LIVE
        part = c_ref[j * LIVE : (j + 1) * LIVE, lo : lo + LIVE]
        piece = jnp.dot(part, x_ref[...], preferred_element_type=F32)
        total = piece if total is None else total + piece
    return total


def stage_kernel(first, count, c_mine, c_other, *refs):
    x_refs, refs = refs[:count], refs[count:]
    sums, outs = refs[:-2], refs[-2:]
    for i, c_ref in enumerate((c_mine, c_other)):
        for j in range(XS):
            rows = slice(j * LIVE, (j + 1) * LIVE)
            total = product(c_ref, j, first, x_refs)
            if sums:
                total = total + sums[i][rows, :]
            outs[i][rows, :] = total.astype(outs[i].dtype)


def stage(first, c_mine, c_other, pieces, sums, last):
    shape = (XS * LIVE, pieces[0].shape[1])
    return pl.pallas_call(
        lambda *refs: stage_kernel(first, len(pieces), *refs),
        in_specs=[VM] * (2 + len(pieces) + len(sums)),
        out_specs=[VM] * 2,
        out_shape=[pltpu.VMEM(shape, F32), pltpu.VMEM(shape, BF16 if last else F32)],
        name="stage",
        compiler_params=params(8),
        cost_estimate=TINY,
    )(c_mine, c_other, *pieces, *sums)


def opposite_kernel(c_ref, x_ref, sum_ref, o_ref):
    for j in range(XS):
        rows = slice(j * LIVE, (j + 1) * LIVE)
        o_ref[rows, :] = sum_ref[rows, :] + product(c_ref, j, 7, (x_ref,))


def add_opposite(c_mine, piece, mine):
    return pl.pallas_call(
        opposite_kernel,
        in_specs=[VM] * 3,
        out_specs=VM,
        out_shape=pltpu.VMEM(mine.shape, F32),
        name="add_opposite",
        compiler_params=params(8),
        cost_estimate=LONG,
    )(c_mine, piece, mine)


def total_kernel(c_ref, x_ref, mine_ref, other_ref, own_ref, *out_refs):
    for j, out_ref in enumerate((own_ref, *out_refs)):
        rows = slice(j * LIVE, (j + 1) * LIVE)
        total = product(c_ref, j, 8, (x_ref,))
        total = total + mine_ref[rows, :] + other_ref[rows, :].astype(F32)
        out_ref[...] = total.astype(out_ref.dtype)


def totals(c_mine, sibling, mine, other):
    shape = (LIVE, mine.shape[1])
    return pl.pallas_call(
        total_kernel,
        in_specs=[VM] * 4,
        out_specs=[VM] * XS,
        out_shape=[pltpu.VMEM(shape, F32)] + [pltpu.VMEM(shape, BF16)] * (XS - 1),
        name="totals",
        compiler_params=params(8),
        cost_estimate=TINY,
    )(c_mine, sibling, mine, other)


def finish_kernel(me_ref, counts_ref, own_ref, a_ref, b_ref, c_ref, n_ref, lead_ref, _, o_hbm, buffer, sem):
    within = lax.broadcasted_iota(jnp.int32, (1, LIVE), 1)
    retain = within < counts_ref[me_ref[0]]
    norm = n_ref[:, :1]
    half = buffer.shape[0] // 2
    copies = []
    for i in range(2):
        part = slice(i * half, (i + 1) * half)
        total = own_ref[:, part] + a_ref[:, part].astype(F32)
        total = total + b_ref[:, part].astype(F32) + c_ref[:, part].astype(F32)
        updated = jnp.transpose(total / norm)
        lead = lead_ref[part, :].astype(F32)
        buffer[part, :] = jnp.where(retain, updated, lead).astype(BF16)
        rows = pl.ds(i * half, half)
        copies.append(
            pltpu.make_async_copy(buffer.at[rows, :], o_hbm.at[rows, pl.ds(0, LIVE)], sem.at[i])
        )
        copies[-1].start()
    for copy in copies:
        copy.wait()


def finish(me, counts, own, received, norm, lead, out):
    return pl.pallas_call(
        finish_kernel,
        in_specs=[SM, SM] + [VM] * (XS + 2) + [HB],
        out_specs=HB,
        out_shape=jax.ShapeDtypeStruct(out.shape, BF16),
        scratch_shapes=[pltpu.VMEM(lead.shape, BF16), pltpu.SemaphoreType.DMA((2,))],
        input_output_aliases={4 + XS: 0},
        name="finish",
        compiler_params=params(4),
        cost_estimate=TINY,
    )(me, counts, own, *received, norm, lead, out)


def per_device(eigvecs, perm, counts, poles, weights, roots):
    me = lax.axis_index(("xl", "core", "z", "xh")).astype(jnp.int32).reshape(1)
    roots = roots.reshape(1, COLS)
    all_roots = lax.all_gather(roots, ("xl", "core", "xh"), axis=0, tiled=True)

    own, lead, rest = permute(in_hbm(eigvecs), perm.reshape(1, COLS))
    table, factors = tables(
        hold(counts, own), in_hbm(poles.reshape(-1, LANES)), in_hbm(weights.reshape(-1, LANES))
    )
    p1 = around(own, 1)
    p2 = around(own, -1)
    p3 = around(hold(p1, factors), 1)
    p4 = around(p2, -1)
    c_other = cauchy(1, OTHER, me, table, factors, hold(all_roots, p2))
    p5 = around(hold(p3, c_other), 1)
    c_mine = cauchy(0, MINE, me, table, factors, hold(all_roots, p3, c_other))
    p6 = around(hold(p4, c_mine), -1)
    sums = stage(0, c_mine, c_other, (own, p1, p2, p3, p4), (), False)
    p7 = around(hold(p5, sums[0]), 1)
    mine, other = stage(5, c_mine, c_other, (p5, p6), sums, True)
    other = cshift(other)
    sibling = cshift(p7)
    mine = add_opposite(c_mine, p7, mine)
    own_sum, *sent = totals(c_mine, sibling, mine, other)
    received = [xflip(part, i + 1) for i, part in enumerate(sent)]
    norm, out = norms(table, factors, hold(roots, own_sum), rest)
    return finish(me, counts, own_sum, received, norm, lead, out)


def solution(mesh):
    fine_mesh = Mesh(mesh.devices.reshape(4, 2, 2, 8, 2), ("rows", "xl", "core", "z", "xh"))
    columns = ("xl", "core", "z", "xh")
    return jax.shard_map(
        per_device,
        mesh=fine_mesh,
        in_specs=(P("rows", columns), P(columns), P(), P(), P(), P(columns)),
        out_specs=P("rows", columns),
        check_vma=False,
    )
```

time: 288 us -> 79.8 us (0.28)
  waiting for transfers between devices: 241 us -> 16.1 us
  blocking collectives: 0 us -> 24.7 us
  starting transfers between devices: 0.04 us -> 21.1 us
  Pallas kernels: 0 us -> 15.8 us
  matrix products: 15.7 us -> 0 us
  between operations: 13.5 us -> 0.3 us
  other arithmetic: 11.7 us -> 0 us
  local copies, waits for them, and re-layouts: 5.5 us -> 1.35 us
    all_gather x2 -> x0, waiting for transfers between devices: 241 us -> none  [the longest x1 213 us: per_device(): panel_piece = lax.all_gather(panels, 'fine', axis=1, tiled=True)]
    all_gather x0 -> x1, blocking collectives: none -> 24.7 us  [per_device(): all_roots = lax.all_gather(roots, ('xl', 'core', 'xh'), axis=0, tiled=True)]
    ppermute x0 -> x12, starting transfers between devices: none -> 21.1 us  [the longest x7 13.7 us: around(): return lax.ppermute(a, ('core', 'z'), up + down)]
    ppermute x0 -> x12, waiting for transfers between devices: none -> 16.1 us  [the longest x3 10.3 us: xflip(): return lax.ppermute(a, ('xl', 'xh'), [(i, i ^ partner) for i in range(XS)])]
    pallas_call x0 -> x10, Pallas kernels: none -> 15.8 us  [the longest x2 4.13 us: stage(): pl.pallas_call(lambda *refs: stage_kernel(first, len(pieces), *refs), in_...]
    dot_general x2 -> x0, matrix products: 15.7 us -> none  [the longest x1 14.5 us: per_device(): jnp.dot(panel_piece, cauchy.astype(jnp.bfloat16), preferred_element_type=...]
    reduce_sum x2 -> x0, other arithmetic: 10.3 us -> none  [the longest x1 9.01 us: per_device(): summed, squares = (summed, jnp.sum(cauchy * cauchy, axis=0))]
  transfers between devices with their start and end apart: 2 -> 12, of which waited for: 2 -> 7; matrix products, arithmetic and copies ran while one was open for 5% -> 0% of each run, Pallas kernels for 0% -> 15%
where the time goes in v3:
time: 79.8 us; the launch traced here: 79.4 us
  blocking collectives  24.7 us (31%)
  starting transfers between devices  21.1 us (26%)
  waiting for transfers between devices  16.1 us (20%)
  Pallas kernels  15.8 us (20%)
  local copies, waits for them, and re-layouts  1.35 us (2%)
    all_gather x1, blocking collectives, per_device(): all_roots = lax.all_gather(roots, ('xl', 'core', 'xh'), axis=0, tiled=True)  24.7 us
    ppermute x7, starting transfers between devices, around(): return lax.ppermute(a, ('core', 'z'), up + down)  13.7 us
    ppermute x3, waiting for transfers between devices, xflip(): return lax.ppermute(a, ('xl', 'xh'), [(i, i ^ partner) for i in range(XS)])  10.3 us
    ppermute x7, waiting for transfers between devices, around(): return lax.ppermute(a, ('core', 'z'), up + down)  5.11 us
    ppermute x3, starting transfers between devices, xflip(): return lax.ppermute(a, ('xl', 'xh'), [(i, i ^ partner) for i in range(XS)])  4.35 us
    pallas_call x2, Pallas kernels, stage(): pl.pallas_call(lambda *refs: stage_kernel(first, len(pieces), *refs), in_...  4.13 us
    pallas_call x1, Pallas kernels, norms(): pl.pallas_call(norm_kernel, in_specs=[VM] * 4, out_specs=[VM, HB], out_sh...  3.38 us
    ppermute x2, starting transfers between devices, cshift(): return lax.ppermute(a, 'core', [(0, 1), (1, 0)])  2.97 us
  transfers between devices with their start and end apart: 12, of which 7 were waited for; matrix products, arithmetic and copies ran while one was open for 0% of the time, Pallas kernels for 15%

profile of v3, /device:TPU:1, one launch (start us, length us, event | category | flops | bytes accessed | tf_op | source)
XLA Modules:
  0.0 79.4 jit_solution(8766073942674278042)
XLA Ops:
  0.0 0.7 copy-done.1
  0.7 1.7 %permute.1 = (bf16[256,512]{1,0:T(8,128)(2,1)S(1)}, bf16[512,256]{1,0:T(8,128)(2,1)S(1)}, bf16[512,256]{1,0:T(8,128)(2,1)S(1)}) custom-call(bf16[512,512]{1,0:T(8,128)(2,1)} %e_hbm.1, s32[1,512]{1,0:T(1,128)S(1)} %bitcast.13), custom_call_target="tpu_custom_call" | custom-call | flops 1 | bytes 1 | tf_op jit(solution)/shard_map/permute/pallas_call | solution.py:78
  2.4 6.5 %collective-permute-start = (bf16[256,512]{1,0:T(8,128)(2,1)S(1)}, bf16[256,512]{1,0:T(8,128)(2,1)S(1)}, u32[]{:S(2)}, u32[]{:S(2)}) collective-permute-start(bf16[256,512]{1,0:T(8,128)(2,1)S(1)} %get-tuple-element.28.refs_2_), channel_id=1, source_target_pairs={{0,2},{2,4},{4,6},{6,8},{8,10},{10,12},{12,14},{14,0},{16,30},{18,... | collective-permute-start | bytes 786440 | tf_op jit(solution)/shard_map/ppermute | solution.py:42
  8.9 0.7 copy-done.2
  9.5 1.6 %tables.1 = (f32[128,128]{1,0:T(8,128)S(1)}, f32[128,128]{1,0:T(8,128)S(1)}) custom-call(s32[64]{0:T(128)S(1)} %copy-done.2, f32[256,128]{1,0:T(8,128)} %bitcast.14, f32[256,128]{1,0:T(8,128)} %bitcast.15), custom_call_target="tpu_custom_call" | custom-call | flops 1 | bytes 1 | tf_op jit(solution)/shard_map/tables/pallas_call | solution.py:113
  11.1 2.6 %collective-permute-done.refs_3_ = bf16[256,512]{1,0:T(8,128)(2,1)S(1)} collective-permute-done((bf16[256,512]{1,0:T(8,128)(2,1)S(1)}, bf16[256,512]{1,0:T(8,128)(2,1)S(1)}, u32[]{:S(2)}, u32[]{:S(2)}) %collective-permute-start) | collective-permute-done | bytes 262176 | tf_op jit(solution)/shard_map/ppermute | solution.py:42
  13.7 3.4 %collective-permute-start.1 = (bf16[256,512]{1,0:T(8,128)(2,1)S(1)}, bf16[256,512]{1,0:T(8,128)(2,1)S(1)}, u32[]{:S(2)}, u32[]{:S(2)}) collective-permute-start(bf16[256,512]{1,0:T(8,128)(2,1)S(1)} %collective-permute-done.refs_3_), channel_id=1, source_target_pairs={{0,2},{2,4},{4,6},{6,8},{8,10},{10,12},{12,14},{14,0},{16,30},{18,... | collective-permute-start | bytes 786440 | tf_op jit(solution)/shard_map/ppermute | solution.py:42
  17.2 24.7 %all-gather.1 = f32[8,1,512]{2,1,0:T(1,128)S(1)} all-gather(f32[1,1,512]{2,1,0:T(1,128)} %bitcast.11), channel_id=2, replica_groups=mesh['rows'=4,'xl'=2,'core'=2,'z'=8,'xh'=2] {'xl','core','xh'}, dimensions={0}, use_global_device_ids=true | all-gather | bytes 18432 | tf_op jit(solution)/shard_map/all_gather | solution.py:314
  41.9 1.2 %cauchy.2.refs_1_ = bf16[1024,1792]{1,0:T(8,128)(2,1)S(1)} custom-call(s32[1]{0:T(128)} %bitcast.refs_0_.me_ref, f32[128,128]{1,0:T(8,128)S(1)} %get-tuple-element.30.refs_1_.poles_ref, f32[128,128]{1,0:T(8,128)S(1)} %get-tuple-element.31.refs_2_.factors_ref, f32[8,512]{1,0:T(8,128)S(1)} %bitcast.9), custom_call_target="tpu_custom_call" | custom-call | flops 1 | bytes 1 | tf_op jit(solution)/shard_map/cauchy/pallas_call | solution.py:153
  43.1 1.6 %collective-permute-start.3 = (bf16[256,512]{1,0:T(8,128)(2,1)S(1)}, bf16[256,512]{1,0:T(8,128)(2,1)S(1)}, u32[]{:S(2)}, u32[]{:S(2)}) collective-permute-start(bf16[256,512]{1,0:T(8,128)(2,1)S(1)} %collective-permute-done.1.refs_5_), channel_id=1, source_target_pairs={{0,2},{2,4},{4,6},{6,8},{8,10},{10,12},{12,14},{14,0},{16,30},{18,... | collective-permute-start | bytes 786440 | tf_op jit(solution)/shard_map/ppermute | solution.py:42
  44.8 1.5 %cauchy.3.refs_0_.c_ref = bf16[1024,2304]{1,0:T(8,128)(2,1)S(1)} custom-call(s32[1]{0:T(128)} %bitcast.refs_0_.me_ref, f32[128,128]{1,0:T(8,128)S(1)} %get-tuple-element.30.refs_1_.poles_ref, f32[128,128]{1,0:T(8,128)S(1)} %get-tuple-element.31.refs_2_.factors_ref, f32[8,512]{1,0:T(8,128)S(1)} %bitcast.10), custom_call_target="tpu_custom_call" | custom-call | flops 1 | bytes 1 | tf_op jit(solution)/shard_map/cauchy/pallas_call | solution.py:153
  46.3 2.9 %stage.2 = (f32[1024,512]{1,0:T(8,128)S(1)}, f32[1024,512]{1,0:T(8,128)S(1)}) custom-call(bf16[1024,2304]{1,0:T(8,128)(2,1)S(1)} %cauchy.3.refs_0_.c_ref, bf16[1024,1792]{1,0:T(8,128)(2,1)S(1)} %cauchy.2.refs_1_, bf16[256,512]{1,0:T(8,128)(2,1)S(1)} %get-tuple-element.28.refs_2_, bf16[256,512]{1,0:T(8,128)(2,1)S(1)} %collective-permute-done.refs_3_, ...), custom_call_target="tpu_custom_call" | custom-call | flops 1 | bytes 1 | tf_op jit(solution)/shard_map/stage/pallas_call | solution.py:225
  49.2 0.6 collective-permute-done.3.refs_2_
  49.8 2.1 %collective-permute-start.5 = (bf16[256,512]{1,0:T(8,128)(2,1)S(1)}, bf16[256,512]{1,0:T(8,128)(2,1)S(1)}, u32[]{:S(2)}, u32[]{:S(2)}) collective-permute-start(bf16[256,512]{1,0:T(8,128)(2,1)S(1)} %collective-permute-done.3.refs_2_), channel_id=1, source_target_pairs={{0,2},{2,4},{4,6},{6,8},{8,10},{10,12},{12,14},{14,0},{16,30},{18,... | collective-permute-start | bytes 786440 | tf_op jit(solution)/shard_map/ppermute | solution.py:42
  52.0 0.8 %collective-permute-done.7.refs_3_ = bf16[256,512]{1,0:T(8,128)(2,1)S(1)} collective-permute-done((bf16[256,512]{1,0:T(8,128)(2,1)S(1)}, bf16[256,512]{1,0:T(8,128)(2,1)S(1)}, u32[]{:S(2)}, u32[]{:S(2)}) %collective-permute-start.7) | collective-permute-done | bytes 262176 | tf_op jit(solution)/shard_map/ppermute | solution.py:42
  52.8 1.3 %stage.3 = (f32[1024,512]{1,0:T(8,128)S(1)}, bf16[1024,512]{1,0:T(8,128)(2,1)S(1)}) custom-call(bf16[1024,2304]{1,0:T(8,128)(2,1)S(1)} %cauchy.3.refs_0_.c_ref, bf16[1024,1792]{1,0:T(8,128)(2,1)S(1)} %cauchy.2.refs_1_, bf16[256,512]{1,0:T(8,128)(2,1)S(1)} %collective-permute-done.3.refs_2_, bf16[256,512]{1,0:T(8,128)(2,1)S(1)} %collective-permute-done.7.refs_3_, ...), custom_call_target="tpu_custom_call" | custom-call | flops 1 | bytes 1 | tf_op jit(solution)/shard_map/stage/pallas_call | solution.py:225
  54.3 1.1 %collective-permute-done.5.x_ref = bf16[256,512]{1,0:T(8,128)(2,1)S(1)} collective-permute-done((bf16[256,512]{1,0:T(8,128)(2,1)S(1)}, bf16[256,512]{1,0:T(8,128)(2,1)S(1)}, u32[]{:S(2)}, u32[]{:S(2)}) %collective-permute-start.5) | collective-permute-done | bytes 262176 | tf_op jit(solution)/shard_map/ppermute | solution.py:42
  55.4 2.7 %collective-permute-start.6 = (bf16[256,512]{1,0:T(8,128)(2,1)S(1)}, bf16[256,512]{1,0:T(8,128)(2,1)S(1)}, u32[]{:S(2)}, u32[]{:S(2)}) collective-permute-start(bf16[256,512]{1,0:T(8,128)(2,1)S(1)} %collective-permute-done.5.x_ref), channel_id=1, source_target_pairs={{0,16},{16,0},{1,17},{17,1},{2,18},{18,2},{3,19},{19,3},{4,20},{20... | collective-permute-start | bytes 786440 | tf_op jit(solution)/shard_map/ppermute | solution.py:46
  58.5 0.7 collective-permute-done.6.x_ref
  60.1 4.0 %collective-permute-start.10 = (bf16[256,512]{1,0:T(8,128)(2,1)S(1)}, bf16[256,512]{1,0:T(8,128)(2,1)S(1)}, u32[]{:S(2)}, u32[]{:S(2)}) collective-permute-start(bf16[256,512]{1,0:T(8,128)(2,1)S(1)} %get-tuple-element.44), channel_id=1, source_target_pairs={{0,1},{1,0},{32,33},{33,32},{2,3},{3,2},{34,35},{35,34},{4,5},{5,4... | collective-permute-start | bytes 786440 | tf_op jit(solution)/shard_map/ppermute | solution.py:36
  64.0 3.4 %norms.1 = (f32[256,128]{1,0:T(8,128)S(1)}, bf16[512,512]{1,0:T(8,128)(2,1)}) custom-call(f32[128,128]{1,0:T(8,128)S(1)} %get-tuple-element.30.refs_1_.poles_ref, f32[128,128]{1,0:T(8,128)S(1)} %get-tuple-element.31.refs_2_.factors_ref, f32[1,512]{1,0:T(1,128)S(1)} %bitcast.12, bf16[512,256]{1,0:T(8,128)(2,1)S(1)} %get-tuple-element.47.rest_ref), custom_call_target="tpu_custom_call" | custom-call | flops 1 | bytes 1 | tf_op jit(solution)/shard_map/norms/pallas_call | solution.py:186
  67.4 8.3 %collective-permute-done.10.b_ref = bf16[256,512]{1,0:T(8,128)(2,1)S(1)} collective-permute-done((bf16[256,512]{1,0:T(8,128)(2,1)S(1)}, bf16[256,512]{1,0:T(8,128)(2,1)S(1)}, u32[]{:S(2)}, u32[]{:S(2)}) %collective-permute-start.10) | collective-permute-done | bytes 262176 | tf_op jit(solution)/shard_map/ppermute | solution.py:36
  75.7 2.0 %collective-permute-done.11.c_ref = bf16[256,512]{1,0:T(8,128)(2,1)S(1)} collective-permute-done((bf16[256,512]{1,0:T(8,128)(2,1)S(1)}, bf16[256,512]{1,0:T(8,128)(2,1)S(1)}, u32[]{:S(2)}, u32[]{:S(2)}) %collective-permute-start.11) | collective-permute-done | bytes 262176 | tf_op jit(solution)/shard_map/ppermute | solution.py:36
  77.7 1.5 %finish.1 = bf16[512,512]{1,0:T(8,128)(2,1)} custom-call(s32[1]{0:T(128)} %bitcast.refs_0_.me_ref, s32[64]{0:T(128)S(1)} %copy-done.3, f32[256,512]{1,0:T(8,128)S(1)} %get-tuple-element.42.own_ref, bf16[256,512]{1,0:T(8,128)(2,1)S(1)} %collective-permute-done.9.a_ref, ...), custom_call_target="tpu_custom_call", output_to_operand_aliasing={{}: (8, {})} | custom-call | flops 1 | bytes 1 | tf_op jit(solution)/shard_map/finish/pallas_call | solution.py:298
  (20 shorter events, 1.7 us)
Async XLA Ops:
  0.0 0.7 copy-start.1
  2.4 11.4 %collective-permute-start = (bf16[256,512]{1,0:T(8,128)(2,1)S(1)}, bf16[256,512]{1,0:T(8,128)(2,1)S(1)}, u32[]{:S(2)}, u32[]{:S(2)}) collective-permute-start(bf16[256,512]{1,0:T(8,128)(2,1)S(1)} %get-tuple-element.28.refs_2_), channel_id=1, source_target_pairs={{0,2},{2,4},{4,6},{6,8},{8,10},{10,12},{12,14},{14,0},{16,30},{18,... | collective-permute-start | bytes 786440 | tf_op jit(solution)/shard_map/ppermute | solution.py:42
  8.9 8.3 %collective-permute-start.2 = (bf16[256,512]{1,0:T(8,128)(2,1)S(1)}, bf16[256,512]{1,0:T(8,128)(2,1)S(1)}, u32[]{:S(2)}, u32[]{:S(2)}) collective-permute-start(bf16[256,512]{1,0:T(8,128)(2,1)S(1)} %get-tuple-element.28.refs_2_), channel_id=1, source_target_pairs={{0,14},{2,0},{4,2},{6,4},{8,6},{10,8},{12,10},{14,12},{16,18},{18,... | collective-permute-start | bytes 786440 | tf_op jit(solution)/shard_map/ppermute | solution.py:42
  8.9 0.7 copy-start.2
  13.7 29.4 %collective-permute-start.1 = (bf16[256,512]{1,0:T(8,128)(2,1)S(1)}, bf16[256,512]{1,0:T(8,128)(2,1)S(1)}, u32[]{:S(2)}, u32[]{:S(2)}) collective-permute-start(bf16[256,512]{1,0:T(8,128)(2,1)S(1)} %collective-permute-done.refs_3_), channel_id=1, source_target_pairs={{0,2},{2,4},{4,6},{6,8},{8,10},{10,12},{12,14},{14,0},{16,30},{18,... | collective-permute-start | bytes 786440 | tf_op jit(solution)/shard_map/ppermute | solution.py:42
  17.2 29.1 %collective-permute-start.4 = (bf16[256,512]{1,0:T(8,128)(2,1)S(1)}, bf16[256,512]{1,0:T(8,128)(2,1)S(1)}, u32[]{:S(2)}, u32[]{:S(2)}) collective-permute-start(bf16[256,512]{1,0:T(8,128)(2,1)S(1)} %collective-permute-done.2.refs_4_), channel_id=1, source_target_pairs={{0,14},{2,0},{4,2},{6,4},{8,6},{10,8},{12,10},{14,12},{16,18},{18,... | collective-permute-start | bytes 786440 | tf_op jit(solution)/shard_map/ppermute | solution.py:42
  43.1 6.7 %collective-permute-start.3 = (bf16[256,512]{1,0:T(8,128)(2,1)S(1)}, bf16[256,512]{1,0:T(8,128)(2,1)S(1)}, u32[]{:S(2)}, u32[]{:S(2)}) collective-permute-start(bf16[256,512]{1,0:T(8,128)(2,1)S(1)} %collective-permute-done.1.refs_5_), channel_id=1, source_target_pairs={{0,2},{2,4},{4,6},{6,8},{8,10},{10,12},{12,14},{14,0},{16,30},{18,... | collective-permute-start | bytes 786440 | tf_op jit(solution)/shard_map/ppermute | solution.py:42
  46.2 6.5 %collective-permute-start.7 = (bf16[256,512]{1,0:T(8,128)(2,1)S(1)}, bf16[256,512]{1,0:T(8,128)(2,1)S(1)}, u32[]{:S(2)}, u32[]{:S(2)}) collective-permute-start(bf16[256,512]{1,0:T(8,128)(2,1)S(1)} %collective-permute-done.4.refs_6_), channel_id=1, source_target_pairs={{0,14},{2,0},{4,2},{6,4},{8,6},{10,8},{12,10},{14,12},{16,18},{18,... | collective-permute-start | bytes 786440 | tf_op jit(solution)/shard_map/ppermute | solution.py:42
  49.8 5.5 %collective-permute-start.5 = (bf16[256,512]{1,0:T(8,128)(2,1)S(1)}, bf16[256,512]{1,0:T(8,128)(2,1)S(1)}, u32[]{:S(2)}, u32[]{:S(2)}) collective-permute-start(bf16[256,512]{1,0:T(8,128)(2,1)S(1)} %collective-permute-done.3.refs_2_), channel_id=1, source_target_pairs={{0,2},{2,4},{4,6},{6,8},{8,10},{10,12},{12,14},{14,0},{16,30},{18,... | collective-permute-start | bytes 786440 | tf_op jit(solution)/shard_map/ppermute | solution.py:42
  54.0 5.2 %collective-permute-start.8 = (bf16[1024,512]{1,0:T(8,128)(2,1)S(1)}, bf16[1024,512]{1,0:T(8,128)(2,1)S(1)}, u32[]{:S(2)}, u32[]{:S(2)}) collective-permute-start(bf16[1024,512]{1,0:T(8,128)(2,1)S(1)} %get-tuple-element.41), channel_id=1, source_target_pairs={{0,16},{16,0},{1,17},{17,1},{2,18},{18,2},{3,19},{19,3},{4,20},{20... | collective-permute-start | bytes 3145736 | tf_op jit(solution)/shard_map/ppermute | solution.py:46
  55.4 3.9 %collective-permute-start.6 = (bf16[256,512]{1,0:T(8,128)(2,1)S(1)}, bf16[256,512]{1,0:T(8,128)(2,1)S(1)}, u32[]{:S(2)}, u32[]{:S(2)}) collective-permute-start(bf16[256,512]{1,0:T(8,128)(2,1)S(1)} %collective-permute-done.5.x_ref), channel_id=1, source_target_pairs={{0,16},{16,0},{1,17},{17,1},{2,18},{18,2},{3,19},{19,3},{4,20},{20... | collective-permute-start | bytes 786440 | tf_op jit(solution)/shard_map/ppermute | solution.py:46
  58.5 5.5 %copy-start = (f32[512]{0:T(512)S(1)}, f32[512]{0:T(512)}, u32[]{:S(2)}) copy-start(f32[512]{0:T(512)} %param.11) | copy-start | bytes 6148
  58.5 19.2 %copy-start.3 = (s32[64]{0:T(128)S(1)}, s32[64]{0:T(128)}, u32[]{:S(2)}) copy-start(s32[64]{0:T(128)} %counts_ref.2) | copy-start | bytes 772
  59.7 7.7 %collective-permute-start.9 = (bf16[256,512]{1,0:T(8,128)(2,1)S(1)}, bf16[256,512]{1,0:T(8,128)(2,1)S(1)}, u32[]{:S(2)}, u32[]{:S(2)}) collective-permute-start(bf16[256,512]{1,0:T(8,128)(2,1)S(1)} %get-tuple-element.43), channel_id=1, source_target_pairs={{0,32},{1,33},{32,0},{33,1},{2,34},{3,35},{34,2},{35,3},{4,36},{5,... | collective-permute-start | bytes 786440 | tf_op jit(solution)/shard_map/ppermute | solution.py:36
  60.1 15.7 %collective-permute-start.10 = (bf16[256,512]{1,0:T(8,128)(2,1)S(1)}, bf16[256,512]{1,0:T(8,128)(2,1)S(1)}, u32[]{:S(2)}, u32[]{:S(2)}) collective-permute-start(bf16[256,512]{1,0:T(8,128)(2,1)S(1)} %get-tuple-element.44), channel_id=1, source_target_pairs={{0,1},{1,0},{32,33},{33,32},{2,3},{3,2},{34,35},{35,34},{4,5},{5,4... | collective-permute-start | bytes 786440 | tf_op jit(solution)/shard_map/ppermute | solution.py:36
  64.0 13.7 %collective-permute-start.11 = (bf16[256,512]{1,0:T(8,128)(2,1)S(1)}, bf16[256,512]{1,0:T(8,128)(2,1)S(1)}, u32[]{:S(2)}, u32[]{:S(2)}) collective-permute-start(bf16[256,512]{1,0:T(8,128)(2,1)S(1)} %get-tuple-element.45), channel_id=1, source_target_pairs={{0,33},{1,32},{32,1},{33,0},{2,35},{3,34},{34,3},{35,2},{4,37},{5,... | collective-permute-start | bytes 786440 | tf_op jit(solution)/shard_map/ppermute | solution.py:36

commit v4 on v3

--- a/solution.py
+++ b/solution.py
@@ -34,6 +34,15 @@
 def xflip(a, mask):
     partner = 2 * (mask % 2) + mask // 2
     return lax.ppermute(a, ("xl", "xh"), [(i, i ^ partner) for i in range(XS)])
+
+
+def neighbours(a, first):
+    pairs = []
+    for i in range(2 * XS):
+        xl, core, xh = i // 4, (i // 2) % 2, i % 2
+        flip = core if first else 1 - core
+        pairs.append((i, 4 * (1 - xl) + 2 * core + (xh ^ flip)))
+    return lax.ppermute(a, ("xl", "core", "xh"), pairs)
 
 
 def around(a, way):
@@ -128,11 +137,12 @@
 
 def cauchy_kernel(fc, pieces, me_ref, poles_ref, factors_ref, r_ref, c_ref):
     me = me_ref[0]
-    xl, core, z, xh = me // 32, (me // 16) % 2, (me // 2) % ZS, me % 2
+    core, z = (me // 16) % 2, (me // 2) % ZS
     step = 1 - 2 * core
     for j in range(XS):
-        row = 4 * (xl ^ (j % 2)) + 2 * (core ^ fc) + (xh ^ (j // 2))
-        roots = column(r_ref[pl.ds(row, 1), :LIVE])
+        mask = 2 - (1 - 2 * fc) * step * (2 - j) if j % 2 else j
+        lo = pl.multiple_of((2 * mask + fc) * LIVE, LIVE)
+        roots = column(r_ref[:, pl.ds(lo, LIVE)])
         for t in range(LIVE // TILE):
             own = jnp.broadcast_to(roots[t * TILE : (t + 1) * TILE], (TILE, LANES))
             rows = slice(j * LIVE + t * TILE, j * LIVE + (t + 1) * TILE)
@@ -251,28 +261,49 @@
     )(c_mine, piece, mine)
 
 
-def total_kernel(c_ref, x_ref, mine_ref, other_ref, own_ref, *out_refs):
-    for j, out_ref in enumerate((own_ref, *out_refs)):
+def total_kernel(c_ref, x_ref, mine_ref, other_ref, own_ref, two_ref, last_ref):
+    outs = (own_ref, two_ref.at[:LIVE, :], two_ref.at[LIVE:, :], last_ref)
+    for j in (1, 2, 3, 0):
         rows = slice(j * LIVE, (j + 1) * LIVE)
         total = product(c_ref, j, 8, (x_ref,))
         total = total + mine_ref[rows, :] + other_ref[rows, :].astype(F32)
-        out_ref[...] = total.astype(out_ref.dtype)
+        outs[j][...] = total.astype(outs[j].dtype)
 
 
 def totals(c_mine, sibling, mine, other):
-    shape = (LIVE, mine.shape[1])
+    rows = mine.shape[1]
     return pl.pallas_call(
         total_kernel,
         in_specs=[VM] * 4,
-        out_specs=[VM] * XS,
-        out_shape=[pltpu.VMEM(shape, F32)] + [pltpu.VMEM(shape, BF16)] * (XS - 1),
+        out_specs=[VM] * 3,
+        out_shape=[
+            pltpu.VMEM((LIVE, rows), F32),
+            pltpu.VMEM((2 * LIVE, rows), BF16),
+            pltpu.VMEM((LIVE, rows), F32),
+        ],
         name="totals",
         compiler_params=params(8),
         cost_estimate=TINY,
     )(c_mine, sibling, mine, other)
 
 
-def finish_kernel(me_ref, counts_ref, own_ref, a_ref, b_ref, c_ref, n_ref, lead_ref, _, o_hbm, buffer, sem):
+def relay_kernel(mine_ref, got_ref, o_ref):
+    o_ref[...] = (mine_ref[...] + got_ref[LIVE:, :].astype(F32)).astype(BF16)
+
+
+def relay(mine, got):
+    return pl.pallas_call(
+        relay_kernel,
+        in_specs=[VM] * 2,
+        out_specs=VM,
+        out_shape=pltpu.VMEM(mine.shape, BF16),
+        name="relay",
+        compiler_params=params(4),
+        cost_estimate=TINY,
+    )(mine, got)
+
+
+def finish_kernel(me_ref, counts_ref, own_ref, a_ref, b_ref, n_ref, lead_ref, _, o_hbm, buffer, sem):
     within = lax.broadcasted_iota(jnp.int32, (1, LIVE), 1)
     retain = within < counts_ref[me_ref[0]]
     norm = n_ref[:, :1]
@@ -280,8 +311,7 @@
     copies = []
     for i in range(2):
         part = slice(i * half, (i + 1) * half)
-        total = own_ref[:, part] + a_ref[:, part].astype(F32)
-        total = total + b_ref[:, part].astype(F32) + c_ref[:, part].astype(F32)
+        total = own_ref[:, part] + a_ref[:LIVE, part].astype(F32) + b_ref[:, part].astype(F32)
         updated = jnp.transpose(total / norm)
         lead = lead_ref[part, :].astype(F32)
         buffer[part, :] = jnp.where(retain, updated, lead).astype(BF16)
@@ -294,24 +324,24 @@
         copy.wait()
 
 
-def finish(me, counts, own, received, norm, lead, out):
+def finish(me, counts, own, near, far, norm, lead, out):
     return pl.pallas_call(
         finish_kernel,
-        in_specs=[SM, SM] + [VM] * (XS + 2) + [HB],
+        in_specs=[SM, SM] + [VM] * 5 + [HB],
         out_specs=HB,
         out_shape=jax.ShapeDtypeStruct(out.shape, BF16),
         scratch_shapes=[pltpu.VMEM(lead.shape, BF16), pltpu.SemaphoreType.DMA((2,))],
-        input_output_aliases={4 + XS: 0},
+        input_output_aliases={7: 0},
         name="finish",
         compiler_params=params(4),
         cost_estimate=TINY,
-    )(me, counts, own, *received, norm, lead, out)
+    )(me, counts, own, near, far, norm, lead, out)
 
 
 def per_device(eigvecs, perm, counts, poles, weights, roots):
     me = lax.axis_index(("xl", "core", "z", "xh")).astype(jnp.int32).reshape(1)
     roots = roots.reshape(1, COLS)
-    all_roots = lax.all_gather(roots, ("xl", "core", "xh"), axis=0, tiled=True)
+    other_roots = cshift(roots)
 
     own, lead, rest = permute(in_hbm(eigvecs), perm.reshape(1, COLS))
     table, factors = tables(
@@ -319,8 +349,13 @@
     )
     p1 = around(own, 1)
     p2 = around(own, -1)
-    p3 = around(hold(p1, factors), 1)
-    p4 = around(p2, -1)
+    own_roots = hold(roots, factors)[:, :LIVE]
+    near = jnp.concatenate([own_roots, other_roots[:, :LIVE]], axis=1)
+    pair = jnp.concatenate([near, xflip(near, 1)], axis=1)
+    p3 = around(hold(p1, near), 1)
+    far = xflip(hold(pair, p1), 2)
+    p4 = around(hold(p2, pair), -1)
+    all_roots = jnp.concatenate([pair, far], axis=1)
     c_other = cauchy(1, OTHER, me, table, factors, hold(all_roots, p2))
     p5 = around(hold(p3, c_other), 1)
     c_mine = cauchy(0, MINE, me, table, factors, hold(all_roots, p3, c_other))
@@ -331,10 +366,11 @@
     other = cshift(other)
     sibling = cshift(p7)
     mine = add_opposite(c_mine, p7, mine)
-    own_sum, *sent = totals(c_mine, sibling, mine, other)
-    received = [xflip(part, i + 1) for i, part in enumerate(sent)]
+    own_sum, two, last = totals(c_mine, sibling, mine, other)
+    got = neighbours(two, True)
     norm, out = norms(table, factors, hold(roots, own_sum), rest)
-    return finish(me, counts, own_sum, received, norm, lead, out)
+    final = neighbours(relay(hold(last, norm), got), False)
+    return finish(me, counts, own_sum, got, final, norm, lead, out)
 
 
 def solution(mesh):

time: 79.8 us -> 61.2 us (0.77)
  the two profiles are of different devices: /device:TPU:1 before, /device:TPU:96 now
where the time goes in v4:
time: 61.2 us; the launch traced here: 61.1 us
  waiting for transfers between devices  21.6 us (35%)
  starting transfers between devices  21.2 us (35%)
  Pallas kernels  15.9 us (26%)
  local copies, waits for them, and re-layouts  2.03 us (3%)
    ppermute x7, starting transfers between devices, around(): return lax.ppermute(a, ('core', 'z'), up + down)  12.4 us
    ppermute x2, waiting for transfers between devices, neighbours(): return lax.ppermute(a, ('xl', 'core', 'xh'), pairs)  9.96 us
    ppermute x7, waiting for transfers between devices, around(): return lax.ppermute(a, ('core', 'z'), up + down)  7.54 us
    ppermute x2, starting transfers between devices, xflip(): return lax.ppermute(a, ('xl', 'xh'), [(i, i ^ partner) for i in range(XS)])  4.69 us
    pallas_call x2, Pallas kernels, stage(): pl.pallas_call(lambda *refs: stage_kernel(first, len(pieces), *refs), in_...  4.12 us
    ppermute x2, starting transfers between devices, neighbours(): return lax.ppermute(a, ('xl', 'core', 'xh'), pairs)  3.58 us
    pallas_call x1, Pallas kernels, norms(): pl.pallas_call(norm_kernel, in_specs=[VM] * 4, out_specs=[VM, HB], out_sh...  3.38 us
    pallas_call x2, Pallas kernels, cauchy(): pl.pallas_call(lambda *refs: cauchy_kernel(fc, pieces, *refs), in_specs=[...  2.68 us
  transfers between devices with their start and end apart: 14, of which 7 were waited for; matrix products, arithmetic and copies ran while one was open for 1% of the time, Pallas kernels for 20%

profile of v4, /device:TPU:96, one launch (start us, length us, event | category | flops | bytes accessed | tf_op | source)
XLA Modules:
  0.0 61.1 jit_solution(761144226409181269)
XLA Ops:
  0.7 1.7 %permute.1 = (bf16[256,512]{1,0:T(8,128)(2,1)S(1)}, bf16[512,256]{1,0:T(8,128)(2,1)S(1)}, bf16[512,256]{1,0:T(8,128)(2,1)S(1)}) custom-call(bf16[512,512]{1,0:T(8,128)(2,1)} %e_hbm.1, s32[1,512]{1,0:T(1,128)S(1)} %bitcast.8), custom_call_target="tpu_custom_call" | custom-call | flops 1 | bytes 1 | tf_op jit(solution)/shard_map/permute/pallas_call | solution.py:87
  2.4 3.2 %collective-permute-start.2 = (bf16[256,512]{1,0:T(8,128)(2,1)S(1)}, bf16[256,512]{1,0:T(8,128)(2,1)S(1)}, u32[]{:S(2)}, u32[]{:S(2)}) collective-permute-start(bf16[256,512]{1,0:T(8,128)(2,1)S(1)} %get-tuple-element.31.refs_2_), channel_id=1, source_target_pairs={{0,2},{2,4},{4,6},{6,8},{8,10},{10,12},{12,14},{14,0},{16,30},{18,... | collective-permute-start | bytes 786440 | tf_op jit(solution)/shard_map/ppermute | solution.py:51
  6.3 1.6 %tables.1 = (f32[128,128]{1,0:T(8,128)S(1)}, f32[128,128]{1,0:T(8,128)S(1)}) custom-call(s32[64]{0:T(128)S(1)} %copy-done.2, f32[256,128]{1,0:T(8,128)} %bitcast.9, f32[256,128]{1,0:T(8,128)} %bitcast.10), custom_call_target="tpu_custom_call" | custom-call | flops 1 | bytes 1 | tf_op jit(solution)/shard_map/tables/pallas_call | solution.py:122
  7.8 0.7 %slice.6 = f32[1,256]{1,0:T(1,128)S(1)} slice(f32[1,512]{1,0:T(1,128)} %bitcast.6), slice={[0:1], [0:256]} | slice | bytes 2048 | tf_op jit(solution)/shard_map/slice | solution.py:352
  8.5 1.6 %collective-permute-start.1 = (f32[1,512]{1,0:T(1,128)S(1)}, f32[1,512]{1,0:T(1,128)S(1)}, u32[]{:S(2)}, u32[]{:S(2)}) collective-permute-start(f32[1,512]{1,0:T(1,128)S(1)} %pad_maximum_fusion.2), channel_id=1, source_target_pairs={{0,32},{1,33},{32,0},{33,1},{2,34},{3,35},{34,2},{35,3},{4,36},{5,... | collective-permute-start | bytes 6152 | tf_op jit(solution)/shard_map/ppermute | solution.py:36
  10.1 1.1 %collective-permute-done.2.refs_3_ = bf16[256,512]{1,0:T(8,128)(2,1)S(1)} collective-permute-done((bf16[256,512]{1,0:T(8,128)(2,1)S(1)}, bf16[256,512]{1,0:T(8,128)(2,1)S(1)}, u32[]{:S(2)}, u32[]{:S(2)}) %collective-permute-start.2) | collective-permute-done | bytes 262176 | tf_op jit(solution)/shard_map/ppermute | solution.py:51
  11.2 3.7 %collective-permute-start.4 = (bf16[256,512]{1,0:T(8,128)(2,1)S(1)}, bf16[256,512]{1,0:T(8,128)(2,1)S(1)}, u32[]{:S(2)}, u32[]{:S(2)}) collective-permute-start(bf16[256,512]{1,0:T(8,128)(2,1)S(1)} %collective-permute-done.2.refs_3_), channel_id=1, source_target_pairs={{0,2},{2,4},{4,6},{6,8},{8,10},{10,12},{12,14},{14,0},{16,30},{18,... | collective-permute-start | bytes 786440 | tf_op jit(solution)/shard_map/ppermute | solution.py:51
  15.0 3.1 %collective-permute-start.3 = (f32[1,1024]{1,0:T(1,128)S(1)}, f32[1,1024]{1,0:T(1,128)S(1)}, u32[]{:S(2)}, u32[]{:S(2)}) collective-permute-start(f32[1,1024]{1,0:T(1,128)S(1)} %pad_maximum_fusion.1), channel_id=1, source_target_pairs={{0,1},{1,0},{32,33},{33,32},{2,3},{3,2},{34,35},{35,34},{4,5},{5,4... | collective-permute-start | bytes 12296 | tf_op jit(solution)/shard_map/ppermute | solution.py:36
  18.1 2.1 %collective-permute-done.3 = f32[1,1024]{1,0:T(1,128)S(1)} collective-permute-done((f32[1,1024]{1,0:T(1,128)S(1)}, f32[1,1024]{1,0:T(1,128)S(1)}, u32[]{:S(2)}, u32[]{:S(2)}) %collective-permute-start.3) | collective-permute-done | bytes 4128 | tf_op jit(solution)/shard_map/ppermute | solution.py:36
  20.2 1.2 %cauchy.2.refs_1_ = bf16[1024,1792]{1,0:T(8,128)(2,1)S(1)} custom-call(s32[1]{0:T(128)} %bitcast.refs_0_.me_ref, f32[128,128]{1,0:T(8,128)S(1)} %get-tuple-element.33.refs_1_.poles_ref, f32[128,128]{1,0:T(8,128)S(1)} %get-tuple-element.34.refs_2_.factors_ref, f32[1,2048]{1,0:T(1,128)S(1)} %pad_maximum_fusion.refs_3_), custom_call_target="tpu_custom_call" | custom-call | flops 1 | bytes 1 | tf_op jit(solution)/shard_map/cauchy/pallas_call | solution.py:163
  21.4 2.0 %collective-permute-start.6 = (bf16[256,512]{1,0:T(8,128)(2,1)S(1)}, bf16[256,512]{1,0:T(8,128)(2,1)S(1)}, u32[]{:S(2)}, u32[]{:S(2)}) collective-permute-start(bf16[256,512]{1,0:T(8,128)(2,1)S(1)} %collective-permute-done.4.refs_5_), channel_id=1, source_target_pairs={{0,2},{2,4},{4,6},{6,8},{8,10},{10,12},{12,14},{14,0},{16,30},{18,... | collective-permute-start | bytes 786440 | tf_op jit(solution)/shard_map/ppermute | solution.py:51
  23.4 1.5 %cauchy.3.refs_0_.c_ref = bf16[1024,2304]{1,0:T(8,128)(2,1)S(1)} custom-call(s32[1]{0:T(128)} %bitcast.refs_0_.me_ref, f32[128,128]{1,0:T(8,128)S(1)} %get-tuple-element.33.refs_1_.poles_ref, f32[128,128]{1,0:T(8,128)S(1)} %get-tuple-element.34.refs_2_.factors_ref, f32[1,2048]{1,0:T(1,128)S(1)} %pad_maximum_fusion.refs_3_), custom_call_target="tpu_custom_call" | custom-call | flops 1 | bytes 1 | tf_op jit(solution)/shard_map/cauchy/pallas_call | solution.py:163
  24.8 3.4 %collective-permute-done.7.refs_6_ = bf16[256,512]{1,0:T(8,128)(2,1)S(1)} collective-permute-done((bf16[256,512]{1,0:T(8,128)(2,1)S(1)}, bf16[256,512]{1,0:T(8,128)(2,1)S(1)}, u32[]{:S(2)}, u32[]{:S(2)}) %collective-permute-start.7) | collective-permute-done | bytes 262176 | tf_op jit(solution)/shard_map/ppermute | solution.py:51
  28.3 2.9 %stage.2 = (f32[1024,512]{1,0:T(8,128)S(1)}, f32[1024,512]{1,0:T(8,128)S(1)}) custom-call(bf16[1024,2304]{1,0:T(8,128)(2,1)S(1)} %cauchy.3.refs_0_.c_ref, bf16[1024,1792]{1,0:T(8,128)(2,1)S(1)} %cauchy.2.refs_1_, bf16[256,512]{1,0:T(8,128)(2,1)S(1)} %get-tuple-element.31.refs_2_, bf16[256,512]{1,0:T(8,128)(2,1)S(1)} %collective-permute-done.2.refs_3_, ...), custom_call_target="tpu_custom_call" | custom-call | flops 1 | bytes 1 | tf_op jit(solution)/shard_map/stage/pallas_call | solution.py:235
  31.2 3.5 %collective-permute-start.8 = (bf16[256,512]{1,0:T(8,128)(2,1)S(1)}, bf16[256,512]{1,0:T(8,128)(2,1)S(1)}, u32[]{:S(2)}, u32[]{:S(2)}) collective-permute-start(bf16[256,512]{1,0:T(8,128)(2,1)S(1)} %collective-permute-done.6.refs_2_), channel_id=1, source_target_pairs={{0,2},{2,4},{4,6},{6,8},{8,10},{10,12},{12,14},{14,0},{16,30},{18,... | collective-permute-start | bytes 786440 | tf_op jit(solution)/shard_map/ppermute | solution.py:51
  34.6 3.0 %collective-permute-done.10.refs_3_ = bf16[256,512]{1,0:T(8,128)(2,1)S(1)} collective-permute-done((bf16[256,512]{1,0:T(8,128)(2,1)S(1)}, bf16[256,512]{1,0:T(8,128)(2,1)S(1)}, u32[]{:S(2)}, u32[]{:S(2)}) %collective-permute-start.10) | collective-permute-done | bytes 262176 | tf_op jit(solution)/shard_map/ppermute | solution.py:51
  37.6 1.3 %stage.3 = (f32[1024,512]{1,0:T(8,128)S(1)}, bf16[1024,512]{1,0:T(8,128)(2,1)S(1)}) custom-call(bf16[1024,2304]{1,0:T(8,128)(2,1)S(1)} %cauchy.3.refs_0_.c_ref, bf16[1024,1792]{1,0:T(8,128)(2,1)S(1)} %cauchy.2.refs_1_, bf16[256,512]{1,0:T(8,128)(2,1)S(1)} %collective-permute-done.6.refs_2_, bf16[256,512]{1,0:T(8,128)(2,1)S(1)} %collective-permute-done.10.refs_3_, ...), custom_call_target="tpu_custom_call" | custom-call | flops 1 | bytes 1 | tf_op jit(solution)/shard_map/stage/pallas_call | solution.py:235
  40.0 2.0 %collective-permute-done.9.x_ref = bf16[256,512]{1,0:T(8,128)(2,1)S(1)} collective-permute-done((bf16[256,512]{1,0:T(8,128)(2,1)S(1)}, bf16[256,512]{1,0:T(8,128)(2,1)S(1)}, u32[]{:S(2)}, u32[]{:S(2)}) %collective-permute-start.9) | collective-permute-done | bytes 262176 | tf_op jit(solution)/shard_map/ppermute | solution.py:55
  42.5 1.4 %collective-permute-start.12 = (bf16[512,512]{1,0:T(8,128)(2,1)S(1)}, bf16[512,512]{1,0:T(8,128)(2,1)S(1)}, u32[]{:S(2)}, u32[]{:S(2)}) collective-permute-start(bf16[512,512]{1,0:T(8,128)(2,1)S(1)} %get-tuple-element.49), channel_id=1, source_target_pairs={{0,32},{1,33},{16,49},{17,48},{32,0},{33,1},{48,17},{49,16},{2,34}... | collective-permute-start | bytes 1572872 | tf_op jit(solution)/shard_map/ppermute | solution.py:45
  43.8 3.4 %norms.1 = (f32[256,128]{1,0:T(8,128)S(1)}, bf16[512,512]{1,0:T(8,128)(2,1)}) custom-call(f32[128,128]{1,0:T(8,128)S(1)} %get-tuple-element.33.refs_1_.poles_ref, f32[128,128]{1,0:T(8,128)S(1)} %get-tuple-element.34.refs_2_.factors_ref, f32[1,512]{1,0:T(1,128)S(1)} %bitcast.7, bf16[512,256]{1,0:T(8,128)(2,1)S(1)} %get-tuple-element.52.rest_ref), custom_call_target="tpu_custom_call" | custom-call | flops 1 | bytes 1 | tf_op jit(solution)/shard_map/norms/pallas_call | solution.py:196
  47.2 4.5 %collective-permute-done.12.got_ref.a_ref = bf16[512,512]{1,0:T(8,128)(2,1)S(1)} collective-permute-done((bf16[512,512]{1,0:T(8,128)(2,1)S(1)}, bf16[512,512]{1,0:T(8,128)(2,1)S(1)}, u32[]{:S(2)}, u32[]{:S(2)}) %collective-permute-start.12) | collective-permute-done | bytes 524320 | tf_op jit(solution)/shard_map/ppermute | solution.py:45
  51.8 2.2 %collective-permute-start.13 = (bf16[256,512]{1,0:T(8,128)(2,1)S(1)}, bf16[256,512]{1,0:T(8,128)(2,1)S(1)}, u32[]{:S(2)}, u32[]{:S(2)}) collective-permute-start(bf16[256,512]{1,0:T(8,128)(2,1)S(1)} %relay.1), channel_id=1, source_target_pairs={{0,33},{1,32},{16,48},{17,49},{32,1},{33,0},{48,16},{49,17},{2,35}... | collective-permute-start | bytes 786440 | tf_op jit(solution)/shard_map/ppermute | solution.py:45
  54.0 5.5 %collective-permute-done.13.b_ref = bf16[256,512]{1,0:T(8,128)(2,1)S(1)} collective-permute-done((bf16[256,512]{1,0:T(8,128)(2,1)S(1)}, bf16[256,512]{1,0:T(8,128)(2,1)S(1)}, u32[]{:S(2)}, u32[]{:S(2)}) %collective-permute-start.13) | collective-permute-done | bytes 262176 | tf_op jit(solution)/shard_map/ppermute | solution.py:45
  59.5 1.5 %finish.1 = bf16[512,512]{1,0:T(8,128)(2,1)} custom-call(s32[1]{0:T(128)} %bitcast.refs_0_.me_ref, s32[64]{0:T(128)S(1)} %copy-done.3, f32[256,512]{1,0:T(8,128)S(1)} %get-tuple-element.48.own_ref, bf16[512,512]{1,0:T(8,128)(2,1)S(1)} %collective-permute-done.12.got_ref.a_ref, ...), custom_call_target="tpu_custom_call", output_to_operand_aliasing={{}: (7, {})} | custom-call | flops 1 | bytes 1 | tf_op jit(solution)/shard_map/finish/pallas_call | solution.py:328
  (28 shorter events, 2.9 us)
Async XLA Ops:
  0.0 0.7 %copy-start.1 = (s32[512]{0:T(512)S(1)}, s32[512]{0:T(512)}, u32[]{:S(2)}) copy-start(s32[512]{0:T(512)} %param.7) | copy-start | bytes 6148
  2.4 8.9 %collective-permute-start.2 = (bf16[256,512]{1,0:T(8,128)(2,1)S(1)}, bf16[256,512]{1,0:T(8,128)(2,1)S(1)}, u32[]{:S(2)}, u32[]{:S(2)}) collective-permute-start(bf16[256,512]{1,0:T(8,128)(2,1)S(1)} %get-tuple-element.31.refs_2_), channel_id=1, source_target_pairs={{0,2},{2,4},{4,6},{6,8},{8,10},{10,12},{12,14},{14,0},{16,30},{18,... | collective-permute-start | bytes 786440 | tf_op jit(solution)/shard_map/ppermute | solution.py:51
  5.6 12.5 %collective-permute-start.5 = (bf16[256,512]{1,0:T(8,128)(2,1)S(1)}, bf16[256,512]{1,0:T(8,128)(2,1)S(1)}, u32[]{:S(2)}, u32[]{:S(2)}) collective-permute-start(bf16[256,512]{1,0:T(8,128)(2,1)S(1)} %get-tuple-element.31.refs_2_), channel_id=1, source_target_pairs={{0,14},{2,0},{4,2},{6,4},{8,6},{10,8},{12,10},{14,12},{16,18},{18,... | collective-permute-start | bytes 786440 | tf_op jit(solution)/shard_map/ppermute | solution.py:51
  5.6 2.9 %collective-permute-start = (f32[1,512]{1,0:T(1,128)}, f32[1,512]{1,0:T(1,128)S(1)}, u32[]{:S(2)}, u32[]{:S(2)}) collective-permute-start(f32[1,512]{1,0:T(1,128)} %bitcast.5), channel_id=1, source_target_pairs={{0,16},{16,0},{1,17},{17,1},{2,18},{18,2},{3,19},{19,3},{4,20},{20... | collective-permute-start | bytes 6152 | tf_op jit(solution)/shard_map/ppermute | solution.py:55
  5.6 0.7 %copy-start.2 = (s32[64]{0:T(128)S(1)}, s32[64]{0:T(128)}, u32[]{:S(2)}) copy-start(s32[64]{0:T(128)} %counts_ref.2) | copy-start | bytes 772
  8.5 6.4 %collective-permute-start.1 = (f32[1,512]{1,0:T(1,128)S(1)}, f32[1,512]{1,0:T(1,128)S(1)}, u32[]{:S(2)}, u32[]{:S(2)}) collective-permute-start(f32[1,512]{1,0:T(1,128)S(1)} %pad_maximum_fusion.2), channel_id=1, source_target_pairs={{0,32},{1,33},{32,0},{33,1},{2,34},{3,35},{34,2},{35,3},{4,36},{5,... | collective-permute-start | bytes 6152 | tf_op jit(solution)/shard_map/ppermute | solution.py:36
  11.2 10.1 %collective-permute-start.4 = (bf16[256,512]{1,0:T(8,128)(2,1)S(1)}, bf16[256,512]{1,0:T(8,128)(2,1)S(1)}, u32[]{:S(2)}, u32[]{:S(2)}) collective-permute-start(bf16[256,512]{1,0:T(8,128)(2,1)S(1)} %collective-permute-done.2.refs_3_), channel_id=1, source_target_pairs={{0,2},{2,4},{4,6},{6,8},{8,10},{10,12},{12,14},{14,0},{16,30},{18,... | collective-permute-start | bytes 786440 | tf_op jit(solution)/shard_map/ppermute | solution.py:51
  15.0 5.2 %collective-permute-start.3 = (f32[1,1024]{1,0:T(1,128)S(1)}, f32[1,1024]{1,0:T(1,128)S(1)}, u32[]{:S(2)}, u32[]{:S(2)}) collective-permute-start(f32[1,1024]{1,0:T(1,128)S(1)} %pad_maximum_fusion.1), channel_id=1, source_target_pairs={{0,1},{1,0},{32,33},{33,32},{2,3},{3,2},{34,35},{35,34},{4,5},{5,4... | collective-permute-start | bytes 12296 | tf_op jit(solution)/shard_map/ppermute | solution.py:36
  18.1 10.2 %collective-permute-start.7 = (bf16[256,512]{1,0:T(8,128)(2,1)S(1)}, bf16[256,512]{1,0:T(8,128)(2,1)S(1)}, u32[]{:S(2)}, u32[]{:S(2)}) collective-permute-start(bf16[256,512]{1,0:T(8,128)(2,1)S(1)} %collective-permute-done.5.refs_4_), channel_id=1, source_target_pairs={{0,14},{2,0},{4,2},{6,4},{8,6},{10,8},{12,10},{14,12},{16,18},{18,... | collective-permute-start | bytes 786440 | tf_op jit(solution)/shard_map/ppermute | solution.py:51
  21.4 9.8 %collective-permute-start.6 = (bf16[256,512]{1,0:T(8,128)(2,1)S(1)}, bf16[256,512]{1,0:T(8,128)(2,1)S(1)}, u32[]{:S(2)}, u32[]{:S(2)}) collective-permute-start(bf16[256,512]{1,0:T(8,128)(2,1)S(1)} %collective-permute-done.4.refs_5_), channel_id=1, source_target_pairs={{0,2},{2,4},{4,6},{6,8},{8,10},{10,12},{12,14},{14,0},{16,30},{18,... | collective-permute-start | bytes 786440 | tf_op jit(solution)/shard_map/ppermute | solution.py:51
  28.3 9.3 %collective-permute-start.10 = (bf16[256,512]{1,0:T(8,128)(2,1)S(1)}, bf16[256,512]{1,0:T(8,128)(2,1)S(1)}, u32[]{:S(2)}, u32[]{:S(2)}) collective-permute-start(bf16[256,512]{1,0:T(8,128)(2,1)S(1)} %collective-permute-done.7.refs_6_), channel_id=1, source_target_pairs={{0,14},{2,0},{4,2},{6,4},{8,6},{10,8},{12,10},{14,12},{16,18},{18,... | collective-permute-start | bytes 786440 | tf_op jit(solution)/shard_map/ppermute | solution.py:51
  31.2 7.8 %collective-permute-start.8 = (bf16[256,512]{1,0:T(8,128)(2,1)S(1)}, bf16[256,512]{1,0:T(8,128)(2,1)S(1)}, u32[]{:S(2)}, u32[]{:S(2)}) collective-permute-start(bf16[256,512]{1,0:T(8,128)(2,1)S(1)} %collective-permute-done.6.refs_2_), channel_id=1, source_target_pairs={{0,2},{2,4},{4,6},{6,8},{8,10},{10,12},{12,14},{14,0},{16,30},{18,... | collective-permute-start | bytes 786440 | tf_op jit(solution)/shard_map/ppermute | solution.py:51
  38.9 3.1 %collective-permute-start.11 = (bf16[1024,512]{1,0:T(8,128)(2,1)S(1)}, bf16[1024,512]{1,0:T(8,128)(2,1)S(1)}, u32[]{:S(2)}, u32[]{:S(2)}) collective-permute-start(bf16[1024,512]{1,0:T(8,128)(2,1)S(1)} %get-tuple-element.47), channel_id=1, source_target_pairs={{0,16},{16,0},{1,17},{17,1},{2,18},{18,2},{3,19},{19,3},{4,20},{20... | collective-permute-start | bytes 3145736 | tf_op jit(solution)/shard_map/ppermute | solution.py:55
  39.0 3.0 %collective-permute-start.9 = (bf16[256,512]{1,0:T(8,128)(2,1)S(1)}, bf16[256,512]{1,0:T(8,128)(2,1)S(1)}, u32[]{:S(2)}, u32[]{:S(2)}) collective-permute-start(bf16[256,512]{1,0:T(8,128)(2,1)S(1)} %collective-permute-done.8.x_ref), channel_id=1, source_target_pairs={{0,16},{16,0},{1,17},{17,1},{2,18},{18,2},{3,19},{19,3},{4,20},{20... | collective-permute-start | bytes 786440 | tf_op jit(solution)/shard_map/ppermute | solution.py:55
  39.9 3.9 %copy-start = (f32[512]{0:T(512)S(1)}, f32[512]{0:T(512)}, u32[]{:S(2)}) copy-start(f32[512]{0:T(512)} %param.11) | copy-start | bytes 6148
  39.9 19.5 %copy-start.3 = (s32[64]{0:T(128)S(1)}, s32[64]{0:T(128)}, u32[]{:S(2)}) copy-start(s32[64]{0:T(128)} %counts_ref.2) | copy-start | bytes 772
  42.5 9.3 %collective-permute-start.12 = (bf16[512,512]{1,0:T(8,128)(2,1)S(1)}, bf16[512,512]{1,0:T(8,128)(2,1)S(1)}, u32[]{:S(2)}, u32[]{:S(2)}) collective-permute-start(bf16[512,512]{1,0:T(8,128)(2,1)S(1)} %get-tuple-element.49), channel_id=1, source_target_pairs={{0,32},{1,33},{16,49},{17,48},{32,0},{33,1},{48,17},{49,16},{2,34}... | collective-permute-start | bytes 1572872 | tf_op jit(solution)/shard_map/ppermute | solution.py:45
  51.8 7.7 %collective-permute-start.13 = (bf16[256,512]{1,0:T(8,128)(2,1)S(1)}, bf16[256,512]{1,0:T(8,128)(2,1)S(1)}, u32[]{:S(2)}, u32[]{:S(2)}) collective-permute-start(bf16[256,512]{1,0:T(8,128)(2,1)S(1)} %relay.1), channel_id=1, source_target_pairs={{0,33},{1,32},{16,48},{17,49},{32,1},{33,0},{48,16},{49,17},{2,35}... | collective-permute-start | bytes 786440 | tf_op jit(solution)/shard_map/ppermute | solution.py:45

commit v5 on v3

--- a/solution.py
+++ b/solution.py
@@ -13,6 +13,7 @@
 ZS = 8
 XS = 4
 TILE = 128
+AWAY = (0, 1, -1, 2, -2, 3, -3, 4, 4)
 OTHER = range(7)
 MINE = range(9)
 
@@ -31,9 +32,13 @@
 LONG = pl.CostEstimate(flops=10**10, transcendentals=0, bytes_accessed=1)
 
 
-def xflip(a, mask):
-    partner = 2 * (mask % 2) + mask // 2
-    return lax.ppermute(a, ("xl", "xh"), [(i, i ^ partner) for i in range(XS)])
+def xshift(a, k):
+    pairs = []
+    for i in range(XS):
+        xl, xh = i // 2, i % 2
+        x = (2 * xh + xl + k) % XS
+        pairs.append((i, 2 * (x % 2) + x // 2))
+    return lax.ppermute(a, ("xl", "xh"), pairs)
 
 
 def around(a, way):
@@ -54,14 +59,17 @@
     return pltpu.with_memory_space_constraint(a, pltpu.HBM)
 
 
-def permute_kernel(e_hbm, perm_ref, x_ref, lead_ref, rest_ref, e_ref, sem):
+def permute_kernel(e_hbm, perm_hbm, x_ref, lead_ref, rest_ref, e_ref, perm_ref, sem):
     rows = e_ref.shape[0]
     half = rows // 2
+    order = pltpu.make_async_copy(perm_hbm, perm_ref, sem.at[2])
+    order.start()
     copies = []
     for i in range(2):
         part = pl.ds(i * half, half)
         copies.append(pltpu.make_async_copy(e_hbm.at[part, :], e_ref.at[part, :], sem.at[i]))
         copies[-1].start()
+    order.wait()
     source = lax.broadcasted_iota(jnp.int32, (COLS, COLS), 0)
     selector = jnp.where(source == perm_ref[...], 1.0, 0.0).astype(BF16)
     for i, copy in enumerate(copies):
@@ -77,25 +85,32 @@
     rows = eigvecs.shape[0]
     return pl.pallas_call(
         permute_kernel,
-        in_specs=[HB, VM],
+        in_specs=[HB, HB],
         out_specs=[VM] * 3,
         out_shape=[
             pltpu.VMEM((LIVE, rows), BF16),
             pltpu.VMEM((rows, LIVE), BF16),
             pltpu.VMEM((rows, COLS - LIVE), BF16),
         ],
-        scratch_shapes=[pltpu.VMEM(eigvecs.shape, BF16), pltpu.SemaphoreType.DMA((2,))],
+        scratch_shapes=[
+            pltpu.VMEM(eigvecs.shape, BF16),
+            pltpu.VMEM(perm.shape, jnp.int32),
+            pltpu.SemaphoreType.DMA((3,)),
+        ],
         name="permute",
         compiler_params=params(8),
         cost_estimate=TINY,
     )(eigvecs, perm)
 
 
-def table_kernel(counts_ref, poles_hbm, weights_hbm, p_ref, f_ref, poles_ref, weights_ref, sem):
+def table_kernel(counts_hbm, poles_hbm, weights_hbm, p_ref, f_ref, poles_ref, weights_ref, counts_ref, sem):
     first = pltpu.make_async_copy(poles_hbm, poles_ref, sem.at[0])
     second = pltpu.make_async_copy(weights_hbm, weights_ref, sem.at[1])
+    third = pltpu.make_async_copy(counts_hbm, counts_ref, sem.at[2])
+    third.start()
     first.start()
     second.start()
+    third.wait()
     first.wait()
     second.wait()
     span, keep = COLS // LANES, LIVE // LANES
@@ -112,10 +127,11 @@
     shape = (counts.shape[0] * LIVE // LANES, LANES)
     return pl.pallas_call(
         table_kernel,
-        in_specs=[SM, HB, HB],
+        in_specs=[HB, HB, HB],
         out_specs=[VM, VM],
         out_shape=[pltpu.VMEM(shape, F32)] * 2,
-        scratch_shapes=[pltpu.VMEM(poles.shape, F32)] * 2 + [pltpu.SemaphoreType.DMA((2,))],
+        scratch_shapes=[pltpu.VMEM(poles.shape, F32)] * 2
+        + [pltpu.SMEM(counts.shape, jnp.int32), pltpu.SemaphoreType.DMA((3,))],
         name="tables",
         compiler_params=params(4),
         cost_estimate=TINY,
@@ -126,19 +142,18 @@
     return jnp.transpose(jnp.broadcast_to(row, (8, LIVE)))[:, :1]
 
 
-def cauchy_kernel(fc, pieces, me_ref, poles_ref, factors_ref, r_ref, c_ref):
+def cauchy_kernel(fc, pieces, me_ref, poles_ref, factors_ref, near_ref, far_ref, c_ref):
     me = me_ref[0]
-    xl, core, z, xh = me // 32, (me // 16) % 2, (me // 2) % ZS, me % 2
+    core, z = (me // 16) % 2, (me // 2) % ZS
     step = 1 - 2 * core
     for j in range(XS):
-        row = 4 * (xl ^ (j % 2)) + 2 * (core ^ fc) + (xh ^ (j // 2))
-        roots = column(r_ref[pl.ds(row, 1), :LIVE])
+        lo = (2 * (j % 2) + fc) * COLS
+        roots = column((far_ref if j // 2 else near_ref)[:, lo : lo + LIVE])
         for t in range(LIVE // TILE):
             own = jnp.broadcast_to(roots[t * TILE : (t + 1) * TILE], (TILE, LANES))
             rows = slice(j * LIVE + t * TILE, j * LIVE + (t + 1) * TILE)
             for i, d in enumerate(pieces):
-                away = (d + 1) // 2
-                ring = (z + 4) % ZS if d >= 7 else (z + (1 - 2 * (d % 2)) * step * away + ZS) % ZS
+                ring = (z - step * AWAY[d] + ZS) % ZS
                 block = me + 2 * (ring - z)
                 if d == 8:
                     block = block + 16 * step
@@ -149,16 +164,16 @@
                     c_ref[rows, lo : lo + LANES] = value.astype(BF16)
 
 
-def cauchy(fc, pieces, me, poles, factors, roots):
+def cauchy(fc, pieces, me, poles, factors, near, far):
     return pl.pallas_call(
         lambda *refs: cauchy_kernel(fc, pieces, *refs),
-        in_specs=[SM, VM, VM, VM],
+        in_specs=[SM, VM, VM, VM, VM],
         out_specs=VM,
         out_shape=pltpu.VMEM((XS * LIVE, len(pieces) * LIVE), BF16),
         name="cauchy",
         compiler_params=params(8),
         cost_estimate=TINY,
-    )(me, poles, factors, roots)
+    )(me, poles, factors, near, far)
 
 
 def norm_kernel(poles_ref, factors_ref, r_ref, rest_ref, n_ref, o_hbm, sem):
@@ -311,28 +326,32 @@
 def per_device(eigvecs, perm, counts, poles, weights, roots):
     me = lax.axis_index(("xl", "core", "z", "xh")).astype(jnp.int32).reshape(1)
     roots = roots.reshape(1, COLS)
-    all_roots = lax.all_gather(roots, ("xl", "core", "xh"), axis=0, tiled=True)
-
-    own, lead, rest = permute(in_hbm(eigvecs), perm.reshape(1, COLS))
+    other_roots = cshift(roots)
+
+    own, lead, rest = permute(in_hbm(eigvecs), in_hbm(perm.reshape(1, COLS)))
     table, factors = tables(
-        hold(counts, own), in_hbm(poles.reshape(-1, LANES)), in_hbm(weights.reshape(-1, LANES))
+        hold(in_hbm(counts), own), in_hbm(poles.reshape(-1, LANES)), in_hbm(weights.reshape(-1, LANES))
     )
+    p3 = around(own, 2)
+    p4 = around(own, -2)
     p1 = around(own, 1)
     p2 = around(own, -1)
-    p3 = around(hold(p1, factors), 1)
-    p4 = around(p2, -1)
-    c_other = cauchy(1, OTHER, me, table, factors, hold(all_roots, p2))
-    p5 = around(hold(p3, c_other), 1)
-    c_mine = cauchy(0, MINE, me, table, factors, hold(all_roots, p3, c_other))
-    p6 = around(hold(p4, c_mine), -1)
+    near = jnp.concatenate([hold(roots, factors), other_roots], axis=1)
+    pair = jnp.concatenate([near, xshift(near, -1)], axis=1)
+    far = xshift(pair, -2)
+    p5 = around(p3, 1)
+    p6 = around(p4, -1)
+    p7 = around(p3, 2)
+    c_other = cauchy(1, OTHER, me, table, factors, pair, hold(far, p3, p4))
+    c_mine = cauchy(0, MINE, me, table, factors, pair, hold(far, c_other))
+
     sums = stage(0, c_mine, c_other, (own, p1, p2, p3, p4), (), False)
-    p7 = around(hold(p5, sums[0]), 1)
     mine, other = stage(5, c_mine, c_other, (p5, p6), sums, True)
     other = cshift(other)
     sibling = cshift(p7)
     mine = add_opposite(c_mine, p7, mine)
     own_sum, *sent = totals(c_mine, sibling, mine, other)
-    received = [xflip(part, i + 1) for i, part in enumerate(sent)]
+    received = [xshift(part, k) for k, part in zip((1, 2, -1), sent, strict=True)]
     norm, out = norms(table, factors, hold(roots, own_sum), rest)
     return finish(me, counts, own_sum, received, norm, lead, out)
 

time: 79.8 us -> 60 us (0.75)
  blocking collectives: 24.7 us -> 0 us
  starting transfers between devices: 21.1 us -> 32.2 us
  waiting for transfers between devices: 16.1 us -> 10.5 us
    all_gather x1 -> x0, blocking collectives: 24.7 us -> none  [per_device(): all_roots = lax.all_gather(roots, ('xl', 'core', 'xh'), axis=0, tiled=True)]
    ppermute x3 -> x5, starting transfers between devices: 4.35 us -> 10.2 us  [xshift(): return lax.ppermute(a, ('xl', 'xh'), pairs)]
    ppermute x7, waiting for transfers between devices: 5.11 us -> 1.54 us  [around(): return lax.ppermute(a, ('core', 'z'), up + down)]
    ppermute x7, starting transfers between devices: 13.7 us -> 16.6 us  [around(): return lax.ppermute(a, ('core', 'z'), up + down)]
    ppermute x2 -> x3, starting transfers between devices: 2.97 us -> 5.39 us  [cshift(): return lax.ppermute(a, 'core', [(0, 1), (1, 0)])]
    ppermute x3 -> x5, waiting for transfers between devices: 10.3 us -> 8.27 us  [xshift(): return lax.ppermute(a, ('xl', 'xh'), pairs)]
  transfers between devices with their start and end apart: 12 -> 15, of which waited for: 7 -> 5; matrix products, arithmetic and copies ran while one was open for 0% -> 2% of each run, Pallas kernels for 15% -> 20%
where the time goes in v5:
time: 60 us; the launch traced here: 59.7 us
  starting transfers between devices  32.2 us (54%)
  Pallas kernels  15.3 us (26%)
  waiting for transfers between devices  10.5 us (18%)
  local copies, waits for them, and re-layouts  0.71 us (1%)
  other arithmetic  0.69 us (1%)
    ppermute x7, starting transfers between devices, around(): return lax.ppermute(a, ('core', 'z'), up + down)  16.6 us
    ppermute x5, starting transfers between devices, xshift(): return lax.ppermute(a, ('xl', 'xh'), pairs)  10.2 us
    ppermute x5, waiting for transfers between devices, xshift(): return lax.ppermute(a, ('xl', 'xh'), pairs)  8.27 us
    ppermute x3, starting transfers between devices, cshift(): return lax.ppermute(a, 'core', [(0, 1), (1, 0)])  5.39 us
    pallas_call x2, Pallas kernels, stage(): pl.pallas_call(lambda *refs: stage_kernel(first, len(pieces), *refs), in_...  4.13 us
    pallas_call x1, Pallas kernels, norms(): pl.pallas_call(norm_kernel, in_specs=[VM] * 4, out_specs=[VM, HB], out_sh...  3.38 us
    pallas_call x2, Pallas kernels, cauchy(): pl.pallas_call(lambda *refs: cauchy_kernel(fc, pieces, *refs), in_specs=[...  2.7 us
    pallas_call x1, Pallas kernels, permute(): pl.pallas_call(permute_kernel, in_specs=[HB, HB], out_specs=[VM] * 3, out...  1.72 us
  transfers between devices with their start and end apart: 15, of which 5 were waited for; matrix products, arithmetic and copies ran while one was open for 2% of the time, Pallas kernels for 20%

profile of v5, /device:TPU:1, one launch (start us, length us, event | category | flops | bytes accessed | tf_op | source)
XLA Modules:
  0.0 59.7 jit_solution(17743954354073188125)
XLA Ops:
  0.0 1.7 %permute.1 = (bf16[256,512]{1,0:T(8,128)(2,1)S(1)}, bf16[512,256]{1,0:T(8,128)(2,1)S(1)}, bf16[512,256]{1,0:T(8,128)(2,1)S(1)}) custom-call(bf16[512,512]{1,0:T(8,128)(2,1)} %e_hbm.1, s32[1,512]{1,0:T(1,128)} %bitcast.11), custom_call_target="tpu_custom_call" | custom-call | flops 1 | bytes 1 | tf_op jit(solution)/shard_map/permute/pallas_call | solution.py:86
  1.7 6.9 %collective-permute-start.3 = (bf16[256,512]{1,0:T(8,128)(2,1)S(1)}, bf16[256,512]{1,0:T(8,128)(2,1)S(1)}, u32[]{:S(2)}, u32[]{:S(2)}) collective-permute-start(bf16[256,512]{1,0:T(8,128)(2,1)S(1)} %get-tuple-element.25.refs_2_), channel_id=1, source_target_pairs={{0,4},{2,6},{4,8},{6,10},{8,12},{10,14},{12,0},{14,2},{16,28},{18,... | collective-permute-start | bytes 786440 | tf_op jit(solution)/shard_map/ppermute | solution.py:47
  8.7 0.7 %collective-permute-start.10 = (bf16[256,512]{1,0:T(8,128)(2,1)S(1)}, bf16[256,512]{1,0:T(8,128)(2,1)S(1)}, u32[]{:S(2)}, u32[]{:S(2)}) collective-permute-start(bf16[256,512]{1,0:T(8,128)(2,1)S(1)} %get-tuple-element.25.refs_2_), channel_id=1, source_target_pairs={{0,14},{2,0},{4,2},{6,4},{8,6},{10,8},{12,10},{14,12},{16,18},{18,... | collective-permute-start | bytes 786440 | tf_op jit(solution)/shard_map/ppermute | solution.py:47
  9.4 2.4 %collective-permute-start.9 = (bf16[256,512]{1,0:T(8,128)(2,1)S(1)}, bf16[256,512]{1,0:T(8,128)(2,1)S(1)}, u32[]{:S(2)}, u32[]{:S(2)}) collective-permute-start(bf16[256,512]{1,0:T(8,128)(2,1)S(1)} %get-tuple-element.25.refs_2_), channel_id=1, source_target_pairs={{0,2},{2,4},{4,6},{6,8},{8,10},{10,12},{12,14},{14,0},{16,30},{18,... | collective-permute-start | bytes 786440 | tf_op jit(solution)/shard_map/ppermute | solution.py:47
  12.1 1.1 %tables.1 = (f32[128,128]{1,0:T(8,128)S(1)}, f32[128,128]{1,0:T(8,128)S(1)}) custom-call(s32[64]{0:T(128)} %counts_ref.1, f32[256,128]{1,0:T(8,128)} %bitcast.9, f32[256,128]{1,0:T(8,128)} %bitcast.10), custom_call_target="tpu_custom_call" | custom-call | flops 1 | bytes 1 | tf_op jit(solution)/shard_map/tables/pallas_call | solution.py:128
  14.5 2.5 %collective-permute-start.1 = (f32[1,1024]{1,0:T(1,128)S(1)}, f32[1,1024]{1,0:T(1,128)S(1)}, u32[]{:S(2)}, u32[]{:S(2)}) collective-permute-start(f32[1,1024]{1,0:T(1,128)S(1)} %pad_maximum_fusion), channel_id=1, source_target_pairs={{0,33},{1,32},{32,0},{33,1},{2,35},{3,34},{34,2},{35,3},{4,37},{5,... | collective-permute-start | bytes 12296 | tf_op jit(solution)/shard_map/ppermute | solution.py:41
  17.0 1.5 %collective-permute-done.3.refs_5_ = bf16[256,512]{1,0:T(8,128)(2,1)S(1)} collective-permute-done((bf16[256,512]{1,0:T(8,128)(2,1)S(1)}, bf16[256,512]{1,0:T(8,128)(2,1)S(1)}, u32[]{:S(2)}, u32[]{:S(2)}) %collective-permute-start.3) | collective-permute-done | bytes 262176 | tf_op jit(solution)/shard_map/ppermute | solution.py:47
  18.5 3.8 %collective-permute-start.7 = (bf16[256,512]{1,0:T(8,128)(2,1)S(1)}, bf16[256,512]{1,0:T(8,128)(2,1)S(1)}, u32[]{:S(2)}, u32[]{:S(2)}) collective-permute-start(bf16[256,512]{1,0:T(8,128)(2,1)S(1)} %collective-permute-done.3.refs_5_), channel_id=1, source_target_pairs={{0,2},{2,4},{4,6},{6,8},{8,10},{10,12},{12,14},{14,0},{16,30},{18,... | collective-permute-start | bytes 786440 | tf_op jit(solution)/shard_map/ppermute | solution.py:47
  22.4 0.8 %collective-permute-start.8 = (bf16[256,512]{1,0:T(8,128)(2,1)S(1)}, bf16[256,512]{1,0:T(8,128)(2,1)S(1)}, u32[]{:S(2)}, u32[]{:S(2)}) collective-permute-start(bf16[256,512]{1,0:T(8,128)(2,1)S(1)} %collective-permute-done.4.refs_6_), channel_id=1, source_target_pairs={{0,14},{2,0},{4,2},{6,4},{8,6},{10,8},{12,10},{14,12},{16,18},{18,... | collective-permute-start | bytes 786440 | tf_op jit(solution)/shard_map/ppermute | solution.py:47
  23.2 2.9 %collective-permute-start.2 = (f32[1,2048]{1,0:T(1,128)S(1)}, f32[1,2048]{1,0:T(1,128)S(1)}, u32[]{:S(2)}, u32[]{:S(2)}) collective-permute-start(f32[1,2048]{1,0:T(1,128)S(1)} %constant_dynamic-update-slice_fusion.refs_3_), channel_id=1, source_target_pairs={{0,1},{1,0},{32,33},{33,32},{2,3},{3,2},{34,35},{35,34},{4,5},{5,4... | collective-permute-start | bytes 24584 | tf_op jit(solution)/shard_map/ppermute | solution.py:41
  26.2 1.1 %collective-permute-done.2.refs_4_ = f32[1,2048]{1,0:T(1,128)S(1)} collective-permute-done((f32[1,2048]{1,0:T(1,128)S(1)}, f32[1,2048]{1,0:T(1,128)S(1)}, u32[]{:S(2)}, u32[]{:S(2)}) %collective-permute-start.2) | collective-permute-done | bytes 8224 | tf_op jit(solution)/shard_map/ppermute | solution.py:41
  27.2 1.8 %collective-permute-start.5 = (bf16[256,512]{1,0:T(8,128)(2,1)S(1)}, bf16[256,512]{1,0:T(8,128)(2,1)S(1)}, u32[]{:S(2)}, u32[]{:S(2)}) collective-permute-start(bf16[256,512]{1,0:T(8,128)(2,1)S(1)} %collective-permute-done.3.refs_5_), channel_id=1, source_target_pairs={{0,4},{2,6},{4,8},{6,10},{8,12},{10,14},{12,0},{14,2},{16,28},{18,... | collective-permute-start | bytes 786440 | tf_op jit(solution)/shard_map/ppermute | solution.py:47
  29.1 1.2 %cauchy.2.refs_1_ = bf16[1024,1792]{1,0:T(8,128)(2,1)S(1)} custom-call(s32[1]{0:T(128)} %bitcast.refs_0_.me_ref, f32[128,128]{1,0:T(8,128)S(1)} %get-tuple-element.27.refs_1_.poles_ref, f32[128,128]{1,0:T(8,128)S(1)} %get-tuple-element.28.refs_2_.factors_ref, f32[1,2048]{1,0:T(1,128)S(1)} %constant_dynamic-update-slice_fusion.refs_3_, ...), custom_call_target="tpu_custom_call" | custom-call | flops 1 | bytes 1 | tf_op jit(solution)/shard_map/cauchy/pallas_call | solution.py:168
  30.3 1.5 %cauchy.3.refs_0_.c_ref = bf16[1024,2304]{1,0:T(8,128)(2,1)S(1)} custom-call(s32[1]{0:T(128)} %bitcast.refs_0_.me_ref, f32[128,128]{1,0:T(8,128)S(1)} %get-tuple-element.27.refs_1_.poles_ref, f32[128,128]{1,0:T(8,128)S(1)} %get-tuple-element.28.refs_2_.factors_ref, f32[1,2048]{1,0:T(1,128)S(1)} %constant_dynamic-update-slice_fusion.refs_3_, ...), custom_call_target="tpu_custom_call" | custom-call | flops 1 | bytes 1 | tf_op jit(solution)/shard_map/cauchy/pallas_call | solution.py:168
  31.8 2.9 %stage.2 = (f32[1024,512]{1,0:T(8,128)S(1)}, f32[1024,512]{1,0:T(8,128)S(1)}) custom-call(bf16[1024,2304]{1,0:T(8,128)(2,1)S(1)} %cauchy.3.refs_0_.c_ref, bf16[1024,1792]{1,0:T(8,128)(2,1)S(1)} %cauchy.2.refs_1_, bf16[256,512]{1,0:T(8,128)(2,1)S(1)} %get-tuple-element.25.refs_2_, bf16[256,512]{1,0:T(8,128)(2,1)S(1)} %collective-permute-done.9.refs_3_, ...), custom_call_target="tpu_custom_call" | custom-call | flops 1 | bytes 1 | tf_op jit(solution)/shard_map/stage/pallas_call | solution.py:240
  34.7 1.3 %stage.3 = (f32[1024,512]{1,0:T(8,128)S(1)}, bf16[1024,512]{1,0:T(8,128)(2,1)S(1)}) custom-call(bf16[1024,2304]{1,0:T(8,128)(2,1)S(1)} %cauchy.3.refs_0_.c_ref, bf16[1024,1792]{1,0:T(8,128)(2,1)S(1)} %cauchy.2.refs_1_, bf16[256,512]{1,0:T(8,128)(2,1)S(1)} %collective-permute-done.7.refs_2_, bf16[256,512]{1,0:T(8,128)(2,1)S(1)} %collective-permute-done.8.refs_3_, ...), custom_call_target="tpu_custom_call" | custom-call | flops 1 | bytes 1 | tf_op jit(solution)/shard_map/stage/pallas_call | solution.py:240
  36.0 1.5 %collective-permute-start.11 = (bf16[1024,512]{1,0:T(8,128)(2,1)S(1)}, bf16[1024,512]{1,0:T(8,128)(2,1)S(1)}, u32[]{:S(2)}, u32[]{:S(2)}) collective-permute-start(bf16[1024,512]{1,0:T(8,128)(2,1)S(1)} %get-tuple-element.35), channel_id=1, source_target_pairs={{0,16},{16,0},{1,17},{17,1},{2,18},{18,2},{3,19},{19,3},{4,20},{20... | collective-permute-start | bytes 3145736 | tf_op jit(solution)/shard_map/ppermute | solution.py:51
  37.5 3.6 %collective-permute-start.6 = (bf16[256,512]{1,0:T(8,128)(2,1)S(1)}, bf16[256,512]{1,0:T(8,128)(2,1)S(1)}, u32[]{:S(2)}, u32[]{:S(2)}) collective-permute-start(bf16[256,512]{1,0:T(8,128)(2,1)S(1)} %collective-permute-done.5.x_ref), channel_id=1, source_target_pairs={{0,16},{16,0},{1,17},{17,1},{2,18},{18,2},{3,19},{19,3},{4,20},{20... | collective-permute-start | bytes 786440 | tf_op jit(solution)/shard_map/ppermute | solution.py:51
  42.7 1.3 %collective-permute-start.12 = (bf16[256,512]{1,0:T(8,128)(2,1)S(1)}, bf16[256,512]{1,0:T(8,128)(2,1)S(1)}, u32[]{:S(2)}, u32[]{:S(2)}) collective-permute-start(bf16[256,512]{1,0:T(8,128)(2,1)S(1)} %get-tuple-element.37), channel_id=1, source_target_pairs={{0,32},{1,33},{32,1},{33,0},{2,34},{3,35},{34,3},{35,2},{4,36},{5,... | collective-permute-start | bytes 786440 | tf_op jit(solution)/shard_map/ppermute | solution.py:41
  44.0 2.5 %collective-permute-start.13 = (bf16[256,512]{1,0:T(8,128)(2,1)S(1)}, bf16[256,512]{1,0:T(8,128)(2,1)S(1)}, u32[]{:S(2)}, u32[]{:S(2)}) collective-permute-start(bf16[256,512]{1,0:T(8,128)(2,1)S(1)} %get-tuple-element.38), channel_id=1, source_target_pairs={{0,1},{1,0},{32,33},{33,32},{2,3},{3,2},{34,35},{35,34},{4,5},{5,4... | collective-permute-start | bytes 786440 | tf_op jit(solution)/shard_map/ppermute | solution.py:41
  46.4 1.1 %collective-permute-start.14 = (bf16[256,512]{1,0:T(8,128)(2,1)S(1)}, bf16[256,512]{1,0:T(8,128)(2,1)S(1)}, u32[]{:S(2)}, u32[]{:S(2)}) collective-permute-start(bf16[256,512]{1,0:T(8,128)(2,1)S(1)} %get-tuple-element.39), channel_id=1, source_target_pairs={{0,33},{1,32},{32,0},{33,1},{2,35},{3,34},{34,2},{35,3},{4,37},{5,... | collective-permute-start | bytes 786440 | tf_op jit(solution)/shard_map/ppermute | solution.py:41
  47.5 3.4 %norms.1 = (f32[256,128]{1,0:T(8,128)S(1)}, bf16[512,512]{1,0:T(8,128)(2,1)}) custom-call(f32[128,128]{1,0:T(8,128)S(1)} %get-tuple-element.27.refs_1_.poles_ref, f32[128,128]{1,0:T(8,128)S(1)} %get-tuple-element.28.refs_2_.factors_ref, f32[1,512]{1,0:T(1,128)S(1)} %bitcast.8, bf16[512,256]{1,0:T(8,128)(2,1)S(1)} %get-tuple-element.41.rest_ref), custom_call_target="tpu_custom_call" | custom-call | flops 1 | bytes 1 | tf_op jit(solution)/shard_map/norms/pallas_call | solution.py:201
  51.5 6.6 %collective-permute-done.13.b_ref = bf16[256,512]{1,0:T(8,128)(2,1)S(1)} collective-permute-done((bf16[256,512]{1,0:T(8,128)(2,1)S(1)}, bf16[256,512]{1,0:T(8,128)(2,1)S(1)}, u32[]{:S(2)}, u32[]{:S(2)}) %collective-permute-start.13) | collective-permute-done | bytes 262176 | tf_op jit(solution)/shard_map/ppermute | solution.py:41
  58.1 1.5 %finish.1 = bf16[512,512]{1,0:T(8,128)(2,1)} custom-call(s32[1]{0:T(128)} %bitcast.refs_0_.me_ref, s32[64]{0:T(128)S(1)} %copy-done.1, f32[256,512]{1,0:T(8,128)S(1)} %get-tuple-element.36.own_ref, bf16[256,512]{1,0:T(8,128)(2,1)S(1)} %collective-permute-done.12.a_ref, ...), custom_call_target="tpu_custom_call", output_to_operand_aliasing={{}: (8, {})} | custom-call | flops 1 | bytes 1 | tf_op jit(solution)/shard_map/finish/pallas_call | solution.py:313
  (24 shorter events, 3.9 us)
Async XLA Ops:
  1.7 16.8 %collective-permute-start.3 = (bf16[256,512]{1,0:T(8,128)(2,1)S(1)}, bf16[256,512]{1,0:T(8,128)(2,1)S(1)}, u32[]{:S(2)}, u32[]{:S(2)}) collective-permute-start(bf16[256,512]{1,0:T(8,128)(2,1)S(1)} %get-tuple-element.25.refs_2_), channel_id=1, source_target_pairs={{0,4},{2,6},{4,8},{6,10},{8,12},{10,14},{12,0},{14,2},{16,28},{18,... | collective-permute-start | bytes 786440 | tf_op jit(solution)/shard_map/ppermute | solution.py:47
  8.7 13.7 %collective-permute-start.4 = (bf16[256,512]{1,0:T(8,128)(2,1)S(1)}, bf16[256,512]{1,0:T(8,128)(2,1)S(1)}, u32[]{:S(2)}, u32[]{:S(2)}) collective-permute-start(bf16[256,512]{1,0:T(8,128)(2,1)S(1)} %get-tuple-element.25.refs_2_), channel_id=1, source_target_pairs={{0,12},{2,14},{4,0},{6,2},{8,4},{10,6},{12,8},{14,10},{16,20},{18,... | collective-permute-start | bytes 786440 | tf_op jit(solution)/shard_map/ppermute | solution.py:47
  8.7 23.1 %collective-permute-start.10 = (bf16[256,512]{1,0:T(8,128)(2,1)S(1)}, bf16[256,512]{1,0:T(8,128)(2,1)S(1)}, u32[]{:S(2)}, u32[]{:S(2)}) collective-permute-start(bf16[256,512]{1,0:T(8,128)(2,1)S(1)} %get-tuple-element.25.refs_2_), channel_id=1, source_target_pairs={{0,14},{2,0},{4,2},{6,4},{8,6},{10,8},{12,10},{14,12},{16,18},{18,... | collective-permute-start | bytes 786440 | tf_op jit(solution)/shard_map/ppermute | solution.py:47
  9.4 22.4 %collective-permute-start.9 = (bf16[256,512]{1,0:T(8,128)(2,1)S(1)}, bf16[256,512]{1,0:T(8,128)(2,1)S(1)}, u32[]{:S(2)}, u32[]{:S(2)}) collective-permute-start(bf16[256,512]{1,0:T(8,128)(2,1)S(1)} %get-tuple-element.25.refs_2_), channel_id=1, source_target_pairs={{0,2},{2,4},{4,6},{6,8},{8,10},{10,12},{12,14},{14,0},{16,30},{18,... | collective-permute-start | bytes 786440 | tf_op jit(solution)/shard_map/ppermute | solution.py:47
  11.8 2.1 %collective-permute-start = (f32[1,512]{1,0:T(1,128)}, f32[1,512]{1,0:T(1,128)S(1)}, u32[]{:S(2)}, u32[]{:S(2)}) collective-permute-start(f32[1,512]{1,0:T(1,128)} %bitcast.5), channel_id=1, source_target_pairs={{0,16},{16,0},{1,17},{17,1},{2,18},{18,2},{3,19},{19,3},{4,20},{20... | collective-permute-start | bytes 6152 | tf_op jit(solution)/shard_map/ppermute | solution.py:51
  14.5 8.7 %collective-permute-start.1 = (f32[1,1024]{1,0:T(1,128)S(1)}, f32[1,1024]{1,0:T(1,128)S(1)}, u32[]{:S(2)}, u32[]{:S(2)}) collective-permute-start(f32[1,1024]{1,0:T(1,128)S(1)} %pad_maximum_fusion), channel_id=1, source_target_pairs={{0,33},{1,32},{32,0},{33,1},{2,35},{3,34},{34,2},{35,3},{4,37},{5,... | collective-permute-start | bytes 12296 | tf_op jit(solution)/shard_map/ppermute | solution.py:41
  18.5 16.1 %collective-permute-start.7 = (bf16[256,512]{1,0:T(8,128)(2,1)S(1)}, bf16[256,512]{1,0:T(8,128)(2,1)S(1)}, u32[]{:S(2)}, u32[]{:S(2)}) collective-permute-start(bf16[256,512]{1,0:T(8,128)(2,1)S(1)} %collective-permute-done.3.refs_5_), channel_id=1, source_target_pairs={{0,2},{2,4},{4,6},{6,8},{8,10},{10,12},{12,14},{14,0},{16,30},{18,... | collective-permute-start | bytes 786440 | tf_op jit(solution)/shard_map/ppermute | solution.py:47
  22.4 12.3 %collective-permute-start.8 = (bf16[256,512]{1,0:T(8,128)(2,1)S(1)}, bf16[256,512]{1,0:T(8,128)(2,1)S(1)}, u32[]{:S(2)}, u32[]{:S(2)}) collective-permute-start(bf16[256,512]{1,0:T(8,128)(2,1)S(1)} %collective-permute-done.4.refs_6_), channel_id=1, source_target_pairs={{0,14},{2,0},{4,2},{6,4},{8,6},{10,8},{12,10},{14,12},{16,18},{18,... | collective-permute-start | bytes 786440 | tf_op jit(solution)/shard_map/ppermute | solution.py:47
  23.2 4.0 %collective-permute-start.2 = (f32[1,2048]{1,0:T(1,128)S(1)}, f32[1,2048]{1,0:T(1,128)S(1)}, u32[]{:S(2)}, u32[]{:S(2)}) collective-permute-start(f32[1,2048]{1,0:T(1,128)S(1)} %constant_dynamic-update-slice_fusion.refs_3_), channel_id=1, source_target_pairs={{0,1},{1,0},{32,33},{33,32},{2,3},{3,2},{34,35},{35,34},{4,5},{5,4... | collective-permute-start | bytes 24584 | tf_op jit(solution)/shard_map/ppermute | solution.py:41
  27.2 10.2 %collective-permute-start.5 = (bf16[256,512]{1,0:T(8,128)(2,1)S(1)}, bf16[256,512]{1,0:T(8,128)(2,1)S(1)}, u32[]{:S(2)}, u32[]{:S(2)}) collective-permute-start(bf16[256,512]{1,0:T(8,128)(2,1)S(1)} %collective-permute-done.3.refs_5_), channel_id=1, source_target_pairs={{0,4},{2,6},{4,8},{6,10},{8,12},{10,14},{12,0},{14,2},{16,28},{18,... | collective-permute-start | bytes 786440 | tf_op jit(solution)/shard_map/ppermute | solution.py:47
  36.0 6.3 %collective-permute-start.11 = (bf16[1024,512]{1,0:T(8,128)(2,1)S(1)}, bf16[1024,512]{1,0:T(8,128)(2,1)S(1)}, u32[]{:S(2)}, u32[]{:S(2)}) collective-permute-start(bf16[1024,512]{1,0:T(8,128)(2,1)S(1)} %get-tuple-element.35), channel_id=1, source_target_pairs={{0,16},{16,0},{1,17},{17,1},{2,18},{18,2},{3,19},{19,3},{4,20},{20... | collective-permute-start | bytes 3145736 | tf_op jit(solution)/shard_map/ppermute | solution.py:51
  37.5 4.8 %collective-permute-start.6 = (bf16[256,512]{1,0:T(8,128)(2,1)S(1)}, bf16[256,512]{1,0:T(8,128)(2,1)S(1)}, u32[]{:S(2)}, u32[]{:S(2)}) collective-permute-start(bf16[256,512]{1,0:T(8,128)(2,1)S(1)} %collective-permute-done.5.x_ref), channel_id=1, source_target_pairs={{0,16},{16,0},{1,17},{17,1},{2,18},{18,2},{3,19},{19,3},{4,20},{20... | collective-permute-start | bytes 786440 | tf_op jit(solution)/shard_map/ppermute | solution.py:51
  41.5 6.0 %copy-start = (f32[512]{0:T(512)S(1)}, f32[512]{0:T(512)}, u32[]{:S(2)}) copy-start(f32[512]{0:T(512)} %param.11) | copy-start | bytes 6148
  41.5 16.6 %copy-start.1 = (s32[64]{0:T(128)S(1)}, s32[64]{0:T(128)}, u32[]{:S(2)}) copy-start(s32[64]{0:T(128)} %counts_ref.1) | copy-start | bytes 772
  42.7 8.8 %collective-permute-start.12 = (bf16[256,512]{1,0:T(8,128)(2,1)S(1)}, bf16[256,512]{1,0:T(8,128)(2,1)S(1)}, u32[]{:S(2)}, u32[]{:S(2)}) collective-permute-start(bf16[256,512]{1,0:T(8,128)(2,1)S(1)} %get-tuple-element.37), channel_id=1, source_target_pairs={{0,32},{1,33},{32,1},{33,0},{2,34},{3,35},{34,3},{35,2},{4,36},{5,... | collective-permute-start | bytes 786440 | tf_op jit(solution)/shard_map/ppermute | solution.py:41
  44.0 14.1 %collective-permute-start.13 = (bf16[256,512]{1,0:T(8,128)(2,1)S(1)}, bf16[256,512]{1,0:T(8,128)(2,1)S(1)}, u32[]{:S(2)}, u32[]{:S(2)}) collective-permute-start(bf16[256,512]{1,0:T(8,128)(2,1)S(1)} %get-tuple-element.38), channel_id=1, source_target_pairs={{0,1},{1,0},{32,33},{33,32},{2,3},{3,2},{34,35},{35,34},{4,5},{5,4... | collective-permute-start | bytes 786440 | tf_op jit(solution)/shard_map/ppermute | solution.py:41
  46.4 11.7 %collective-permute-start.14 = (bf16[256,512]{1,0:T(8,128)(2,1)S(1)}, bf16[256,512]{1,0:T(8,128)(2,1)S(1)}, u32[]{:S(2)}, u32[]{:S(2)}) collective-permute-start(bf16[256,512]{1,0:T(8,128)(2,1)S(1)} %get-tuple-element.39), channel_id=1, source_target_pairs={{0,33},{1,32},{32,0},{33,1},{2,35},{3,34},{34,2},{35,3},{4,37},{5,... | collective-permute-start | bytes 786440 | tf_op jit(solution)/shard_map/ppermute | solution.py:41

commit v6 on v5

--- a/solution.py
+++ b/solution.py
@@ -103,11 +103,15 @@
     )(eigvecs, perm)
 
 
-def table_kernel(counts_hbm, poles_hbm, weights_hbm, p_ref, f_ref, poles_ref, weights_ref, counts_ref, sem):
+def table_kernel(
+    counts_hbm, poles_hbm, weights_hbm, roots_hbm, sibling_ref, p_ref, f_ref, near_ref, poles_ref, weights_ref, counts_ref, sem
+):
     first = pltpu.make_async_copy(poles_hbm, poles_ref, sem.at[0])
     second = pltpu.make_async_copy(weights_hbm, weights_ref, sem.at[1])
     third = pltpu.make_async_copy(counts_hbm, counts_ref, sem.at[2])
+    fourth = pltpu.make_async_copy(roots_hbm, near_ref.at[:, pl.ds(0, COLS)], sem.at[3])
     third.start()
+    fourth.start()
     first.start()
     second.start()
     third.wait()
@@ -121,34 +125,36 @@
         here = slice(span * block, span * block + keep)
         p_ref[rows, :] = poles_ref[here, :]
         f_ref[rows, :] = jnp.where(at < counts_ref[block], weights_ref[here, :], 0.0)
-
-
-def tables(counts, poles, weights):
+    near_ref[:, COLS:] = sibling_ref[...]
+    fourth.wait()
+
+
+def tables(counts, poles, weights, roots, sibling):
     shape = (counts.shape[0] * LIVE // LANES, LANES)
     return pl.pallas_call(
         table_kernel,
-        in_specs=[HB, HB, HB],
-        out_specs=[VM, VM],
-        out_shape=[pltpu.VMEM(shape, F32)] * 2,
+        in_specs=[HB, HB, HB, HB, VM],
+        out_specs=[VM, VM, VM],
+        out_shape=[pltpu.VMEM(shape, F32)] * 2 + [pltpu.VMEM((1, 2 * COLS), F32)],
         scratch_shapes=[pltpu.VMEM(poles.shape, F32)] * 2
-        + [pltpu.SMEM(counts.shape, jnp.int32), pltpu.SemaphoreType.DMA((3,))],
+        + [pltpu.SMEM(counts.shape, jnp.int32), pltpu.SemaphoreType.DMA((4,))],
         name="tables",
         compiler_params=params(4),
         cost_estimate=TINY,
-    )(counts, poles, weights)
+    )(counts, poles, weights, roots, sibling)
 
 
 def column(row):
     return jnp.transpose(jnp.broadcast_to(row, (8, LIVE)))[:, :1]
 
 
-def cauchy_kernel(fc, pieces, me_ref, poles_ref, factors_ref, near_ref, far_ref, c_ref):
+def cauchy_kernel(fc, pieces, me_ref, poles_ref, factors_ref, *refs):
+    r_refs, c_ref = refs[:-1], refs[-1]
     me = me_ref[0]
     core, z = (me // 16) % 2, (me // 2) % ZS
     step = 1 - 2 * core
     for j in range(XS):
-        lo = (2 * (j % 2) + fc) * COLS
-        roots = column((far_ref if j // 2 else near_ref)[:, lo : lo + LIVE])
+        roots = column(r_refs[j][:, fc * COLS : fc * COLS + LIVE])
         for t in range(LIVE // TILE):
             own = jnp.broadcast_to(roots[t * TILE : (t + 1) * TILE], (TILE, LANES))
             rows = slice(j * LIVE + t * TILE, j * LIVE + (t + 1) * TILE)
@@ -164,16 +170,16 @@
                     c_ref[rows, lo : lo + LANES] = value.astype(BF16)
 
 
-def cauchy(fc, pieces, me, poles, factors, near, far):
+def cauchy(fc, pieces, me, poles, factors, roots):
     return pl.pallas_call(
         lambda *refs: cauchy_kernel(fc, pieces, *refs),
-        in_specs=[SM, VM, VM, VM, VM],
+        in_specs=[SM] + [VM] * (2 + XS),
         out_specs=VM,
         out_shape=pltpu.VMEM((XS * LIVE, len(pieces) * LIVE), BF16),
         name="cauchy",
         compiler_params=params(8),
         cost_estimate=TINY,
-    )(me, poles, factors, near, far)
+    )(me, poles, factors, *roots)
 
 
 def norm_kernel(poles_ref, factors_ref, r_ref, rest_ref, n_ref, o_hbm, sem):
@@ -329,21 +335,23 @@
     other_roots = cshift(roots)
 
     own, lead, rest = permute(in_hbm(eigvecs), in_hbm(perm.reshape(1, COLS)))
-    table, factors = tables(
-        hold(in_hbm(counts), own), in_hbm(poles.reshape(-1, LANES)), in_hbm(weights.reshape(-1, LANES))
+    table, factors, near = tables(
+        hold(in_hbm(counts), own),
+        in_hbm(poles.reshape(-1, LANES)),
+        in_hbm(weights.reshape(-1, LANES)),
+        in_hbm(roots),
+        other_roots,
     )
     p3 = around(own, 2)
     p4 = around(own, -2)
     p1 = around(own, 1)
     p2 = around(own, -1)
-    near = jnp.concatenate([hold(roots, factors), other_roots], axis=1)
-    pair = jnp.concatenate([near, xshift(near, -1)], axis=1)
-    far = xshift(pair, -2)
-    p5 = around(p3, 1)
+    far = [xshift(near, k) for k in (-1, -2, 1)]
+    c_other = cauchy(1, OTHER, me, table, factors, [near, *far])
+    p5 = around(hold(p3, c_other), 1)
+    p7 = around(hold(p3, c_other), 2)
     p6 = around(p4, -1)
-    p7 = around(p3, 2)
-    c_other = cauchy(1, OTHER, me, table, factors, pair, hold(far, p3, p4))
-    c_mine = cauchy(0, MINE, me, table, factors, pair, hold(far, c_other))
+    c_mine = cauchy(0, MINE, me, table, factors, [hold(near, p3, p4), *far])
 
     sums = stage(0, c_mine, c_other, (own, p1, p2, p3, p4), (), False)
     mine, other = stage(5, c_mine, c_other, (p5, p6), sums, True)

time: 60 us -> 59.7 us (level)
  waiting for transfers between devices: 10.5 us -> 11.6 us
  local copies, waits for them, and re-layouts: 0.71 us -> 0.01 us
  other arithmetic: 0.69 us -> 0 us
    ppermute x3, starting transfers between devices: 5.39 us -> 8.85 us  [cshift(): return lax.ppermute(a, 'core', [(0, 1), (1, 0)])]
    ppermute x5 -> x6, starting transfers between devices: 10.2 us -> 8.57 us  [xshift(): return lax.ppermute(a, ('xl', 'xh'), pairs)]
    ppermute x7, starting transfers between devices: 16.6 us -> 15 us  [around(): return lax.ppermute(a, ('core', 'z'), up + down)]
    ppermute x3, waiting for transfers between devices: 0.7 us -> 1.73 us  [cshift(): return lax.ppermute(a, 'core', [(0, 1), (1, 0)])]
    ppermute x7, waiting for transfers between devices: 1.54 us -> 2.27 us  [around(): return lax.ppermute(a, ('core', 'z'), up + down)]
    ppermute x5 -> x6, waiting for transfers between devices: 8.27 us -> 7.54 us  [xshift(): return lax.ppermute(a, ('xl', 'xh'), pairs)]
    unnamed x6 -> x4, local copies, waits for them, and re-layouts: 0.71 us -> 0.01 us
    concatenate x1 -> x0, other arithmetic: 0.69 us -> none  [per_device(): near = jnp.concatenate([hold(roots, factors), other_roots], axis=1)]
  transfers between devices with their start and end apart: 15 -> 16, of which waited for: 5 -> 7; matrix products, arithmetic and copies ran while one was open for 2% -> 0% of each run, Pallas kernels for 20% -> 20%
where the time goes in v6:
time: 59.7 us; the launch traced here: 59.6 us
  starting transfers between devices  32.4 us (54%)
  Pallas kernels  15.4 us (26%)
  waiting for transfers between devices  11.6 us (19%)
    ppermute x7, starting transfers between devices, around(): return lax.ppermute(a, ('core', 'z'), up + down)  15 us
    ppermute x3, starting transfers between devices, cshift(): return lax.ppermute(a, 'core', [(0, 1), (1, 0)])  8.85 us
    ppermute x6, starting transfers between devices, xshift(): return lax.ppermute(a, ('xl', 'xh'), pairs)  8.57 us
    ppermute x6, waiting for transfers between devices, xshift(): return lax.ppermute(a, ('xl', 'xh'), pairs)  7.54 us
    pallas_call x2, Pallas kernels, stage(): pl.pallas_call(lambda *refs: stage_kernel(first, len(pieces), *refs), in_...  4.17 us
    pallas_call x1, Pallas kernels, norms(): pl.pallas_call(norm_kernel, in_specs=[VM] * 4, out_specs=[VM, HB], out_sh...  3.38 us
    pallas_call x2, Pallas kernels, cauchy(): pl.pallas_call(lambda *refs: cauchy_kernel(fc, pieces, *refs), in_specs=[...  2.69 us
    ppermute x7, waiting for transfers between devices, around(): return lax.ppermute(a, ('core', 'z'), up + down)  2.27 us
  transfers between devices with their start and end apart: 16, of which 7 were waited for; matrix products, arithmetic and copies ran while one was open for 0% of the time, Pallas kernels for 20%

profile of v6, /device:TPU:1, one launch (start us, length us, event | category | flops | bytes accessed | tf_op | source)
XLA Modules:
  0.0 59.6 jit_solution(6295475914852917389)
XLA Ops:
  0.0 1.7 %permute.1 = (bf16[256,512]{1,0:T(8,128)(2,1)S(1)}, bf16[512,256]{1,0:T(8,128)(2,1)S(1)}, bf16[512,256]{1,0:T(8,128)(2,1)S(1)}) custom-call(bf16[512,512]{1,0:T(8,128)(2,1)} %e_hbm.1, s32[1,512]{1,0:T(1,128)} %bitcast.10), custom_call_target="tpu_custom_call" | custom-call | flops 1 | bytes 1 | tf_op jit(solution)/shard_map/permute/pallas_call | solution.py:86
  1.7 6.9 %collective-permute-start.1 = (bf16[256,512]{1,0:T(8,128)(2,1)S(1)}, bf16[256,512]{1,0:T(8,128)(2,1)S(1)}, u32[]{:S(2)}, u32[]{:S(2)}) collective-permute-start(bf16[256,512]{1,0:T(8,128)(2,1)S(1)} %get-tuple-element.25.refs_2_), channel_id=1, source_target_pairs={{0,4},{2,6},{4,8},{6,10},{8,12},{10,14},{12,0},{14,2},{16,28},{18,... | collective-permute-start | bytes 786440 | tf_op jit(solution)/shard_map/ppermute | solution.py:47
  8.7 1.0 %collective-permute-start = (f32[1,512]{1,0:T(1,128)}, f32[1,512]{1,0:T(1,128)S(1)}, u32[]{:S(2)}, u32[]{:S(2)}) collective-permute-start(f32[1,512]{1,0:T(1,128)} %bitcast.5), channel_id=1, source_target_pairs={{0,16},{16,0},{1,17},{17,1},{2,18},{18,2},{3,19},{19,3},{4,20},{20... | collective-permute-start | bytes 6152 | tf_op jit(solution)/shard_map/ppermute | solution.py:51
  9.7 1.0 %collective-permute-done.sibling_ref = f32[1,512]{1,0:T(1,128)S(1)} collective-permute-done((f32[1,512]{1,0:T(1,128)}, f32[1,512]{1,0:T(1,128)S(1)}, u32[]{:S(2)}, u32[]{:S(2)}) %collective-permute-start) | collective-permute-done | bytes 2080 | tf_op jit(solution)/shard_map/ppermute | solution.py:51
  10.7 1.1 %tables.1 = (f32[128,128]{1,0:T(8,128)S(1)}, f32[128,128]{1,0:T(8,128)S(1)}, f32[1,1024]{1,0:T(1,128)S(1)}) custom-call(s32[64]{0:T(128)} %counts_ref.1, f32[256,128]{1,0:T(8,128)} %bitcast.8, f32[256,128]{1,0:T(8,128)} %bitcast.9, f32[1,512]{1,0:T(1,128)} %bitcast.6, f32[1,512]{1,0:T(1,128)S(1)} %collective-permute-done.sibling_ref), custom_call_target="tpu_custom_call" | custom-call | flops 1 | bytes 1 | tf_op jit(solution)/shard_map/tables/pallas_call | solution.py:134
  11.8 2.6 %collective-permute-start.3 = (f32[1,1024]{1,0:T(1,128)S(1)}, f32[1,1024]{1,0:T(1,128)S(1)}, u32[]{:S(2)}, u32[]{:S(2)}) collective-permute-start(f32[1,1024]{1,0:T(1,128)S(1)} %get-tuple-element.30.refs_3_), channel_id=1, source_target_pairs={{0,33},{1,32},{32,0},{33,1},{2,35},{3,34},{34,2},{35,3},{4,37},{5,... | collective-permute-start | bytes 12296 | tf_op jit(solution)/shard_map/ppermute | solution.py:41
  15.5 2.4 %collective-permute-start.10 = (bf16[256,512]{1,0:T(8,128)(2,1)S(1)}, bf16[256,512]{1,0:T(8,128)(2,1)S(1)}, u32[]{:S(2)}, u32[]{:S(2)}) collective-permute-start(bf16[256,512]{1,0:T(8,128)(2,1)S(1)} %get-tuple-element.25.refs_2_), channel_id=1, source_target_pairs={{0,2},{2,4},{4,6},{6,8},{8,10},{10,12},{12,14},{14,0},{16,30},{18,... | collective-permute-start | bytes 786440 | tf_op jit(solution)/shard_map/ppermute | solution.py:47
  18.3 1.0 %collective-permute-start.11 = (bf16[256,512]{1,0:T(8,128)(2,1)S(1)}, bf16[256,512]{1,0:T(8,128)(2,1)S(1)}, u32[]{:S(2)}, u32[]{:S(2)}) collective-permute-start(bf16[256,512]{1,0:T(8,128)(2,1)S(1)} %get-tuple-element.25.refs_2_), channel_id=1, source_target_pairs={{0,14},{2,0},{4,2},{6,4},{8,6},{10,8},{12,10},{14,12},{16,18},{18,... | collective-permute-start | bytes 786440 | tf_op jit(solution)/shard_map/ppermute | solution.py:47
  19.4 1.2 %cauchy.3.refs_1_ = bf16[1024,1792]{1,0:T(8,128)(2,1)S(1)} custom-call(s32[1]{0:T(128)} %bitcast.refs_0_.me_ref, f32[128,128]{1,0:T(8,128)S(1)} %get-tuple-element.27.refs_1_.poles_ref, f32[128,128]{1,0:T(8,128)S(1)} %get-tuple-element.28.refs_2_.factors_ref, f32[1,1024]{1,0:T(1,128)S(1)} %get-tuple-element.30.refs_3_, ...), custom_call_target="tpu_custom_call" | custom-call | flops 1 | bytes 1 | tf_op jit(solution)/shard_map/cauchy/pallas_call | solution.py:174
  20.6 2.0 %collective-permute-start.8 = (bf16[256,512]{1,0:T(8,128)(2,1)S(1)}, bf16[256,512]{1,0:T(8,128)(2,1)S(1)}, u32[]{:S(2)}, u32[]{:S(2)}) collective-permute-start(bf16[256,512]{1,0:T(8,128)(2,1)S(1)} %collective-permute-done.1.refs_5_), channel_id=1, source_target_pairs={{0,2},{2,4},{4,6},{6,8},{8,10},{10,12},{12,14},{14,0},{16,30},{18,... | collective-permute-start | bytes 786440 | tf_op jit(solution)/shard_map/ppermute | solution.py:47
  22.9 2.3 %collective-permute-start.6 = (bf16[256,512]{1,0:T(8,128)(2,1)S(1)}, bf16[256,512]{1,0:T(8,128)(2,1)S(1)}, u32[]{:S(2)}, u32[]{:S(2)}) collective-permute-start(bf16[256,512]{1,0:T(8,128)(2,1)S(1)} %collective-permute-done.1.refs_5_), channel_id=1, source_target_pairs={{0,4},{2,6},{4,8},{6,10},{8,12},{10,14},{12,0},{14,2},{16,28},{18,... | collective-permute-start | bytes 786440 | tf_op jit(solution)/shard_map/ppermute | solution.py:47
  25.2 1.5 %cauchy.2.refs_0_.c_ref = bf16[1024,2304]{1,0:T(8,128)(2,1)S(1)} custom-call(s32[1]{0:T(128)} %bitcast.refs_0_.me_ref, f32[128,128]{1,0:T(8,128)S(1)} %get-tuple-element.27.refs_1_.poles_ref, f32[128,128]{1,0:T(8,128)S(1)} %get-tuple-element.28.refs_2_.factors_ref, f32[1,1024]{1,0:T(1,128)S(1)} %get-tuple-element.30.refs_3_, ...), custom_call_target="tpu_custom_call" | custom-call | flops 1 | bytes 1 | tf_op jit(solution)/shard_map/cauchy/pallas_call | solution.py:174
  26.9 2.9 %stage.2 = (f32[1024,512]{1,0:T(8,128)S(1)}, f32[1024,512]{1,0:T(8,128)S(1)}) custom-call(bf16[1024,2304]{1,0:T(8,128)(2,1)S(1)} %cauchy.2.refs_0_.c_ref, bf16[1024,1792]{1,0:T(8,128)(2,1)S(1)} %cauchy.3.refs_1_, bf16[256,512]{1,0:T(8,128)(2,1)S(1)} %get-tuple-element.25.refs_2_, bf16[256,512]{1,0:T(8,128)(2,1)S(1)} %collective-permute-done.10.refs_3_, ...), custom_call_target="tpu_custom_call" | custom-call | flops 1 | bytes 1 | tf_op jit(solution)/shard_map/stage/pallas_call | solution.py:246
  29.8 2.1 %collective-permute-done.9.refs_3_ = bf16[256,512]{1,0:T(8,128)(2,1)S(1)} collective-permute-done((bf16[256,512]{1,0:T(8,128)(2,1)S(1)}, bf16[256,512]{1,0:T(8,128)(2,1)S(1)}, u32[]{:S(2)}, u32[]{:S(2)}) %collective-permute-start.9) | collective-permute-done | bytes 262176 | tf_op jit(solution)/shard_map/ppermute | solution.py:47
  31.9 1.3 %stage.3 = (f32[1024,512]{1,0:T(8,128)S(1)}, bf16[1024,512]{1,0:T(8,128)(2,1)S(1)}) custom-call(bf16[1024,2304]{1,0:T(8,128)(2,1)S(1)} %cauchy.2.refs_0_.c_ref, bf16[1024,1792]{1,0:T(8,128)(2,1)S(1)} %cauchy.3.refs_1_, bf16[256,512]{1,0:T(8,128)(2,1)S(1)} %collective-permute-done.8.refs_2_, bf16[256,512]{1,0:T(8,128)(2,1)S(1)} %collective-permute-done.9.refs_3_, ...), custom_call_target="tpu_custom_call" | custom-call | flops 1 | bytes 1 | tf_op jit(solution)/shard_map/stage/pallas_call | solution.py:246
  33.2 5.9 %collective-permute-start.12 = (bf16[1024,512]{1,0:T(8,128)(2,1)S(1)}, bf16[1024,512]{1,0:T(8,128)(2,1)S(1)}, u32[]{:S(2)}, u32[]{:S(2)}) collective-permute-start(bf16[1024,512]{1,0:T(8,128)(2,1)S(1)} %get-tuple-element.35), channel_id=1, source_target_pairs={{0,16},{16,0},{1,17},{17,1},{2,18},{18,2},{3,19},{19,3},{4,20},{20... | collective-permute-start | bytes 3145736 | tf_op jit(solution)/shard_map/ppermute | solution.py:51
  39.1 1.9 %collective-permute-start.7 = (bf16[256,512]{1,0:T(8,128)(2,1)S(1)}, bf16[256,512]{1,0:T(8,128)(2,1)S(1)}, u32[]{:S(2)}, u32[]{:S(2)}) collective-permute-start(bf16[256,512]{1,0:T(8,128)(2,1)S(1)} %collective-permute-done.6.x_ref), channel_id=1, source_target_pairs={{0,16},{16,0},{1,17},{17,1},{2,18},{18,2},{3,19},{19,3},{4,20},{20... | collective-permute-start | bytes 786440 | tf_op jit(solution)/shard_map/ppermute | solution.py:51
  41.4 0.7 %collective-permute-done.7.x_ref = bf16[256,512]{1,0:T(8,128)(2,1)S(1)} collective-permute-done((bf16[256,512]{1,0:T(8,128)(2,1)S(1)}, bf16[256,512]{1,0:T(8,128)(2,1)S(1)}, u32[]{:S(2)}, u32[]{:S(2)}) %collective-permute-start.7) | collective-permute-done | bytes 262176 | tf_op jit(solution)/shard_map/ppermute | solution.py:51
  42.6 1.3 %collective-permute-start.13 = (bf16[256,512]{1,0:T(8,128)(2,1)S(1)}, bf16[256,512]{1,0:T(8,128)(2,1)S(1)}, u32[]{:S(2)}, u32[]{:S(2)}) collective-permute-start(bf16[256,512]{1,0:T(8,128)(2,1)S(1)} %get-tuple-element.37), channel_id=1, source_target_pairs={{0,32},{1,33},{32,1},{33,0},{2,34},{3,35},{34,3},{35,2},{4,36},{5,... | collective-permute-start | bytes 786440 | tf_op jit(solution)/shard_map/ppermute | solution.py:41
  43.9 2.4 %collective-permute-start.14 = (bf16[256,512]{1,0:T(8,128)(2,1)S(1)}, bf16[256,512]{1,0:T(8,128)(2,1)S(1)}, u32[]{:S(2)}, u32[]{:S(2)}) collective-permute-start(bf16[256,512]{1,0:T(8,128)(2,1)S(1)} %get-tuple-element.38), channel_id=1, source_target_pairs={{0,1},{1,0},{32,33},{33,32},{2,3},{3,2},{34,35},{35,34},{4,5},{5,4... | collective-permute-start | bytes 786440 | tf_op jit(solution)/shard_map/ppermute | solution.py:41
  46.3 1.2 %collective-permute-start.15 = (bf16[256,512]{1,0:T(8,128)(2,1)S(1)}, bf16[256,512]{1,0:T(8,128)(2,1)S(1)}, u32[]{:S(2)}, u32[]{:S(2)}) collective-permute-start(bf16[256,512]{1,0:T(8,128)(2,1)S(1)} %get-tuple-element.39), channel_id=1, source_target_pairs={{0,33},{1,32},{32,0},{33,1},{2,35},{3,34},{34,2},{35,3},{4,37},{5,... | collective-permute-start | bytes 786440 | tf_op jit(solution)/shard_map/ppermute | solution.py:41
  47.5 3.4 %norms.1 = (f32[256,128]{1,0:T(8,128)S(1)}, bf16[512,512]{1,0:T(8,128)(2,1)}) custom-call(f32[128,128]{1,0:T(8,128)S(1)} %get-tuple-element.27.refs_1_.poles_ref, f32[128,128]{1,0:T(8,128)S(1)} %get-tuple-element.28.refs_2_.factors_ref, f32[1,512]{1,0:T(1,128)S(1)} %bitcast.7, bf16[512,256]{1,0:T(8,128)(2,1)S(1)} %get-tuple-element.41.rest_ref), custom_call_target="tpu_custom_call" | custom-call | flops 1 | bytes 1 | tf_op jit(solution)/shard_map/norms/pallas_call | solution.py:207
  51.4 6.6 %collective-permute-done.14.b_ref = bf16[256,512]{1,0:T(8,128)(2,1)S(1)} collective-permute-done((bf16[256,512]{1,0:T(8,128)(2,1)S(1)}, bf16[256,512]{1,0:T(8,128)(2,1)S(1)}, u32[]{:S(2)}, u32[]{:S(2)}) %collective-permute-start.14) | collective-permute-done | bytes 262176 | tf_op jit(solution)/shard_map/ppermute | solution.py:41
  58.0 1.5 %finish.1 = bf16[512,512]{1,0:T(8,128)(2,1)} custom-call(s32[1]{0:T(128)} %bitcast.refs_0_.me_ref, s32[64]{0:T(128)S(1)} %copy-done.1, f32[256,512]{1,0:T(8,128)S(1)} %get-tuple-element.36.own_ref, bf16[256,512]{1,0:T(8,128)(2,1)S(1)} %collective-permute-done.13.a_ref, ...), custom_call_target="tpu_custom_call", output_to_operand_aliasing={{}: (8, {})} | custom-call | flops 1 | bytes 1 | tf_op jit(solution)/shard_map/finish/pallas_call | solution.py:319
  (22 shorter events, 3.4 us)
Async XLA Ops:
  1.7 18.9 %collective-permute-start.1 = (bf16[256,512]{1,0:T(8,128)(2,1)S(1)}, bf16[256,512]{1,0:T(8,128)(2,1)S(1)}, u32[]{:S(2)}, u32[]{:S(2)}) collective-permute-start(bf16[256,512]{1,0:T(8,128)(2,1)S(1)} %get-tuple-element.25.refs_2_), channel_id=1, source_target_pairs={{0,4},{2,6},{4,8},{6,10},{8,12},{10,14},{12,0},{14,2},{16,28},{18,... | collective-permute-start | bytes 786440 | tf_op jit(solution)/shard_map/ppermute | solution.py:47
  8.7 13.9 %collective-permute-start.2 = (bf16[256,512]{1,0:T(8,128)(2,1)S(1)}, bf16[256,512]{1,0:T(8,128)(2,1)S(1)}, u32[]{:S(2)}, u32[]{:S(2)}) collective-permute-start(bf16[256,512]{1,0:T(8,128)(2,1)S(1)} %get-tuple-element.25.refs_2_), channel_id=1, source_target_pairs={{0,12},{2,14},{4,0},{6,2},{8,4},{10,6},{12,8},{14,10},{16,20},{18,... | collective-permute-start | bytes 786440 | tf_op jit(solution)/shard_map/ppermute | solution.py:47
  8.7 2.1 %collective-permute-start = (f32[1,512]{1,0:T(1,128)}, f32[1,512]{1,0:T(1,128)S(1)}, u32[]{:S(2)}, u32[]{:S(2)}) collective-permute-start(f32[1,512]{1,0:T(1,128)} %bitcast.5), channel_id=1, source_target_pairs={{0,16},{16,0},{1,17},{17,1},{2,18},{18,2},{3,19},{19,3},{4,20},{20... | collective-permute-start | bytes 6152 | tf_op jit(solution)/shard_map/ppermute | solution.py:51
  11.8 3.7 %collective-permute-start.3 = (f32[1,1024]{1,0:T(1,128)S(1)}, f32[1,1024]{1,0:T(1,128)S(1)}, u32[]{:S(2)}, u32[]{:S(2)}) collective-permute-start(f32[1,1024]{1,0:T(1,128)S(1)} %get-tuple-element.30.refs_3_), channel_id=1, source_target_pairs={{0,33},{1,32},{32,0},{33,1},{2,35},{3,34},{34,2},{35,3},{4,37},{5,... | collective-permute-start | bytes 12296 | tf_op jit(solution)/shard_map/ppermute | solution.py:41
  14.4 4.0 %collective-permute-start.4 = (f32[1,1024]{1,0:T(1,128)S(1)}, f32[1,1024]{1,0:T(1,128)S(1)}, u32[]{:S(2)}, u32[]{:S(2)}) collective-permute-start(f32[1,1024]{1,0:T(1,128)S(1)} %get-tuple-element.30.refs_3_), channel_id=1, source_target_pairs={{0,1},{1,0},{32,33},{33,32},{2,3},{3,2},{34,35},{35,34},{4,5},{5,4... | collective-permute-start | bytes 12296 | tf_op jit(solution)/shard_map/ppermute | solution.py:41
  14.9 4.5 %collective-permute-start.5 = (f32[1,1024]{1,0:T(1,128)S(1)}, f32[1,1024]{1,0:T(1,128)S(1)}, u32[]{:S(2)}, u32[]{:S(2)}) collective-permute-start(f32[1,1024]{1,0:T(1,128)S(1)} %get-tuple-element.30.refs_3_), channel_id=1, source_target_pairs={{0,32},{1,33},{32,1},{33,0},{2,34},{3,35},{34,3},{35,2},{4,36},{5,... | collective-permute-start | bytes 12296 | tf_op jit(solution)/shard_map/ppermute | solution.py:41
  15.5 11.2 %collective-permute-start.10 = (bf16[256,512]{1,0:T(8,128)(2,1)S(1)}, bf16[256,512]{1,0:T(8,128)(2,1)S(1)}, u32[]{:S(2)}, u32[]{:S(2)}) collective-permute-start(bf16[256,512]{1,0:T(8,128)(2,1)S(1)} %get-tuple-element.25.refs_2_), channel_id=1, source_target_pairs={{0,2},{2,4},{4,6},{6,8},{8,10},{10,12},{12,14},{14,0},{16,30},{18,... | collective-permute-start | bytes 786440 | tf_op jit(solution)/shard_map/ppermute | solution.py:47
  18.3 8.5 %collective-permute-start.11 = (bf16[256,512]{1,0:T(8,128)(2,1)S(1)}, bf16[256,512]{1,0:T(8,128)(2,1)S(1)}, u32[]{:S(2)}, u32[]{:S(2)}) collective-permute-start(bf16[256,512]{1,0:T(8,128)(2,1)S(1)} %get-tuple-element.25.refs_2_), channel_id=1, source_target_pairs={{0,14},{2,0},{4,2},{6,4},{8,6},{10,8},{12,10},{14,12},{16,18},{18,... | collective-permute-start | bytes 786440 | tf_op jit(solution)/shard_map/ppermute | solution.py:47
  20.6 9.2 %collective-permute-start.8 = (bf16[256,512]{1,0:T(8,128)(2,1)S(1)}, bf16[256,512]{1,0:T(8,128)(2,1)S(1)}, u32[]{:S(2)}, u32[]{:S(2)}) collective-permute-start(bf16[256,512]{1,0:T(8,128)(2,1)S(1)} %collective-permute-done.1.refs_5_), channel_id=1, source_target_pairs={{0,2},{2,4},{4,6},{6,8},{8,10},{10,12},{12,14},{14,0},{16,30},{18,... | collective-permute-start | bytes 786440 | tf_op jit(solution)/shard_map/ppermute | solution.py:47
  22.6 9.3 %collective-permute-start.9 = (bf16[256,512]{1,0:T(8,128)(2,1)S(1)}, bf16[256,512]{1,0:T(8,128)(2,1)S(1)}, u32[]{:S(2)}, u32[]{:S(2)}) collective-permute-start(bf16[256,512]{1,0:T(8,128)(2,1)S(1)} %collective-permute-done.2.refs_6_), channel_id=1, source_target_pairs={{0,14},{2,0},{4,2},{6,4},{8,6},{10,8},{12,10},{14,12},{16,18},{18,... | collective-permute-start | bytes 786440 | tf_op jit(solution)/shard_map/ppermute | solution.py:47
  22.9 16.2 %collective-permute-start.6 = (bf16[256,512]{1,0:T(8,128)(2,1)S(1)}, bf16[256,512]{1,0:T(8,128)(2,1)S(1)}, u32[]{:S(2)}, u32[]{:S(2)}) collective-permute-start(bf16[256,512]{1,0:T(8,128)(2,1)S(1)} %collective-permute-done.1.refs_5_), channel_id=1, source_target_pairs={{0,4},{2,6},{4,8},{6,10},{8,12},{10,14},{12,0},{14,2},{16,28},{18,... | collective-permute-start | bytes 786440 | tf_op jit(solution)/shard_map/ppermute | solution.py:47
  33.2 9.0 %collective-permute-start.12 = (bf16[1024,512]{1,0:T(8,128)(2,1)S(1)}, bf16[1024,512]{1,0:T(8,128)(2,1)S(1)}, u32[]{:S(2)}, u32[]{:S(2)}) collective-permute-start(bf16[1024,512]{1,0:T(8,128)(2,1)S(1)} %get-tuple-element.35), channel_id=1, source_target_pairs={{0,16},{16,0},{1,17},{17,1},{2,18},{18,2},{3,19},{19,3},{4,20},{20... | collective-permute-start | bytes 3145736 | tf_op jit(solution)/shard_map/ppermute | solution.py:51
  39.1 3.1 %collective-permute-start.7 = (bf16[256,512]{1,0:T(8,128)(2,1)S(1)}, bf16[256,512]{1,0:T(8,128)(2,1)S(1)}, u32[]{:S(2)}, u32[]{:S(2)}) collective-permute-start(bf16[256,512]{1,0:T(8,128)(2,1)S(1)} %collective-permute-done.6.x_ref), channel_id=1, source_target_pairs={{0,16},{16,0},{1,17},{17,1},{2,18},{18,2},{3,19},{19,3},{4,20},{20... | collective-permute-start | bytes 786440 | tf_op jit(solution)/shard_map/ppermute | solution.py:51
  41.4 6.1 %copy-start = (f32[512]{0:T(512)S(1)}, f32[512]{0:T(512)}, u32[]{:S(2)}) copy-start(f32[512]{0:T(512)} %param.11) | copy-start | bytes 6148
  41.4 16.6 %copy-start.1 = (s32[64]{0:T(128)S(1)}, s32[64]{0:T(128)}, u32[]{:S(2)}) copy-start(s32[64]{0:T(128)} %counts_ref.1) | copy-start | bytes 772
  42.6 8.8 %collective-permute-start.13 = (bf16[256,512]{1,0:T(8,128)(2,1)S(1)}, bf16[256,512]{1,0:T(8,128)(2,1)S(1)}, u32[]{:S(2)}, u32[]{:S(2)}) collective-permute-start(bf16[256,512]{1,0:T(8,128)(2,1)S(1)} %get-tuple-element.37), channel_id=1, source_target_pairs={{0,32},{1,33},{32,1},{33,0},{2,34},{3,35},{34,3},{35,2},{4,36},{5,... | collective-permute-start | bytes 786440 | tf_op jit(solution)/shard_map/ppermute | solution.py:41
  43.9 14.1 %collective-permute-start.14 = (bf16[256,512]{1,0:T(8,128)(2,1)S(1)}, bf16[256,512]{1,0:T(8,128)(2,1)S(1)}, u32[]{:S(2)}, u32[]{:S(2)}) collective-permute-start(bf16[256,512]{1,0:T(8,128)(2,1)S(1)} %get-tuple-element.38), channel_id=1, source_target_pairs={{0,1},{1,0},{32,33},{33,32},{2,3},{3,2},{34,35},{35,34},{4,5},{5,4... | collective-permute-start | bytes 786440 | tf_op jit(solution)/shard_map/ppermute | solution.py:41
  46.3 11.7 %collective-permute-start.15 = (bf16[256,512]{1,0:T(8,128)(2,1)S(1)}, bf16[256,512]{1,0:T(8,128)(2,1)S(1)}, u32[]{:S(2)}, u32[]{:S(2)}) collective-permute-start(bf16[256,512]{1,0:T(8,128)(2,1)S(1)} %get-tuple-element.39), channel_id=1, source_target_pairs={{0,33},{1,32},{32,0},{33,1},{2,35},{3,34},{34,2},{35,3},{4,37},{5,... | collective-permute-start | bytes 786440 | tf_op jit(solution)/shard_map/ppermute | solution.py:41

commit v7 on v6

--- a/solution.py
+++ b/solution.py
@@ -343,23 +343,23 @@
         other_roots,
     )
     p3 = around(own, 2)
-    p4 = around(own, -2)
+    p2 = around(own, -1)
     p1 = around(own, 1)
-    p2 = around(own, -1)
     far = [xshift(near, k) for k in (-1, -2, 1)]
-    c_other = cauchy(1, OTHER, me, table, factors, [near, *far])
+    p4 = around(hold(p2, far[0]), -1)
+    c_other = cauchy(1, OTHER, me, table, factors, [hold(near, p2), *far])
     p5 = around(hold(p3, c_other), 1)
-    p7 = around(hold(p3, c_other), 2)
-    p6 = around(p4, -1)
-    c_mine = cauchy(0, MINE, me, table, factors, [hold(near, p3, p4), *far])
-
-    sums = stage(0, c_mine, c_other, (own, p1, p2, p3, p4), (), False)
-    mine, other = stage(5, c_mine, c_other, (p5, p6), sums, True)
+    c_mine = cauchy(0, MINE, me, table, factors, [hold(near, p3, c_other), *far])
+    p6 = around(hold(p4, c_mine), -1)
+    sums = stage(0, c_mine, c_other, (own, p1, p2, p3), (), False)
+    p7 = around(hold(p5, sums[0]), 1)
+    sums = stage(4, c_mine, c_other, (p4, p5), sums, False)
+    mine, other = stage(6, c_mine, c_other, (p6,), sums, True)
     other = cshift(other)
     sibling = cshift(p7)
     mine = add_opposite(c_mine, p7, mine)
     own_sum, *sent = totals(c_mine, sibling, mine, other)
-    received = [xshift(part, k) for k, part in zip((1, 2, -1), sent, strict=True)]
+    received = [xshift(sent[i], k) for i, k in ((1, 2), (0, 1), (2, -1))]
     norm, out = norms(table, factors, hold(roots, own_sum), rest)
     return finish(me, counts, own_sum, received, norm, lead, out)
 

time: 59.7 us -> 65.3 us (1.094)
  starting transfers between devices: 32.4 us -> 36.3 us
  waiting for transfers between devices: 11.6 us -> 13 us
    ppermute x6, starting transfers between devices: 8.57 us -> 11 us  [xshift(): return lax.ppermute(a, ('xl', 'xh'), pairs)]
    ppermute x3, starting transfers between devices: 8.85 us -> 10.2 us  [cshift(): return lax.ppermute(a, 'core', [(0, 1), (1, 0)])]
    ppermute x6, waiting for transfers between devices: 7.54 us -> 8.72 us  [xshift(): return lax.ppermute(a, ('xl', 'xh'), pairs)]
    pallas_call x2 -> x3, Pallas kernels: 4.17 us -> 4.31 us  [stage(): pl.pallas_call(lambda *refs: stage_kernel(first, len(pieces), *refs), in_...]
  transfers between devices with their start and end apart: 16 -> 16, of which waited for: 7 -> 7; matrix products, arithmetic and copies ran while one was open for 0% -> 0% of each run, Pallas kernels for 20% -> 18%
where the time goes in v7:
time: 65.3 us; the launch traced here: 65.2 us
  starting transfers between devices  36.3 us (56%)
  Pallas kernels  15.5 us (24%)
  waiting for transfers between devices  13 us (20%)
    ppermute x7, starting transfers between devices, around(): return lax.ppermute(a, ('core', 'z'), up + down)  15.1 us
    ppermute x6, starting transfers between devices, xshift(): return lax.ppermute(a, ('xl', 'xh'), pairs)  11 us
    ppermute x3, starting transfers between devices, cshift(): return lax.ppermute(a, 'core', [(0, 1), (1, 0)])  10.2 us
    ppermute x6, waiting for transfers between devices, xshift(): return lax.ppermute(a, ('xl', 'xh'), pairs)  8.72 us
    pallas_call x3, Pallas kernels, stage(): pl.pallas_call(lambda *refs: stage_kernel(first, len(pieces), *refs), in_...  4.31 us
    pallas_call x1, Pallas kernels, norms(): pl.pallas_call(norm_kernel, in_specs=[VM] * 4, out_specs=[VM, HB], out_sh...  3.38 us
    pallas_call x2, Pallas kernels, cauchy(): pl.pallas_call(lambda *refs: cauchy_kernel(fc, pieces, *refs), in_specs=[...  2.7 us
    ppermute x7, waiting for transfers between devices, around(): return lax.ppermute(a, ('core', 'z'), up + down)  2.26 us
  transfers between devices with their start and end apart: 16, of which 7 were waited for; matrix products, arithmetic and copies ran while one was open for 0% of the time, Pallas kernels for 18%

profile of v7, /device:TPU:1, one launch (start us, length us, event | category | flops | bytes accessed | tf_op | source)
XLA Modules:
  0.0 65.2 jit_solution(13179973677305888271)
XLA Ops:
  0.0 1.7 %permute.1 = (bf16[256,512]{1,0:T(8,128)(2,1)S(1)}, bf16[512,256]{1,0:T(8,128)(2,1)S(1)}, bf16[512,256]{1,0:T(8,128)(2,1)S(1)}) custom-call(bf16[512,512]{1,0:T(8,128)(2,1)} %e_hbm.1, s32[1,512]{1,0:T(1,128)} %bitcast.10), custom_call_target="tpu_custom_call" | custom-call | flops 1 | bytes 1 | tf_op jit(solution)/shard_map/permute/pallas_call | solution.py:86
  1.7 2.5 %collective-permute-start.2 = (bf16[256,512]{1,0:T(8,128)(2,1)S(1)}, bf16[256,512]{1,0:T(8,128)(2,1)S(1)}, u32[]{:S(2)}, u32[]{:S(2)}) collective-permute-start(bf16[256,512]{1,0:T(8,128)(2,1)S(1)} %get-tuple-element.31.refs_2_), channel_id=1, source_target_pairs={{0,14},{2,0},{4,2},{6,4},{8,6},{10,8},{12,10},{14,12},{16,18},{18,... | collective-permute-start | bytes 786440 | tf_op jit(solution)/shard_map/ppermute | solution.py:47
  4.3 5.1 %collective-permute-start.1 = (bf16[256,512]{1,0:T(8,128)(2,1)S(1)}, bf16[256,512]{1,0:T(8,128)(2,1)S(1)}, u32[]{:S(2)}, u32[]{:S(2)}) collective-permute-start(bf16[256,512]{1,0:T(8,128)(2,1)S(1)} %get-tuple-element.31.refs_2_), channel_id=1, source_target_pairs={{0,4},{2,6},{4,8},{6,10},{8,12},{10,14},{12,0},{14,2},{16,28},{18,... | collective-permute-start | bytes 786440 | tf_op jit(solution)/shard_map/ppermute | solution.py:47
  9.4 1.4 %collective-permute-done.sibling_ref = f32[1,512]{1,0:T(1,128)S(1)} collective-permute-done((f32[1,512]{1,0:T(1,128)}, f32[1,512]{1,0:T(1,128)S(1)}, u32[]{:S(2)}, u32[]{:S(2)}) %collective-permute-start) | collective-permute-done | bytes 2080 | tf_op jit(solution)/shard_map/ppermute | solution.py:51
  10.8 1.1 %tables.1 = (f32[128,128]{1,0:T(8,128)S(1)}, f32[128,128]{1,0:T(8,128)S(1)}, f32[1,1024]{1,0:T(1,128)S(1)}) custom-call(s32[64]{0:T(128)} %counts_ref.1, f32[256,128]{1,0:T(8,128)} %bitcast.8, f32[256,128]{1,0:T(8,128)} %bitcast.9, f32[1,512]{1,0:T(1,128)} %bitcast.6, f32[1,512]{1,0:T(1,128)S(1)} %collective-permute-done.sibling_ref), custom_call_target="tpu_custom_call" | custom-call | flops 1 | bytes 1 | tf_op jit(solution)/shard_map/tables/pallas_call | solution.py:134
  11.8 2.6 %collective-permute-start.3 = (f32[1,1024]{1,0:T(1,128)S(1)}, f32[1,1024]{1,0:T(1,128)S(1)}, u32[]{:S(2)}, u32[]{:S(2)}) collective-permute-start(f32[1,1024]{1,0:T(1,128)S(1)} %get-tuple-element.37.refs_3_), channel_id=1, source_target_pairs={{0,33},{1,32},{32,0},{33,1},{2,35},{3,34},{34,2},{35,3},{4,37},{5,... | collective-permute-start | bytes 12296 | tf_op jit(solution)/shard_map/ppermute | solution.py:41
  16.0 3.7 %collective-permute-start.4 = (f32[1,1024]{1,0:T(1,128)S(1)}, f32[1,1024]{1,0:T(1,128)S(1)}, u32[]{:S(2)}, u32[]{:S(2)}) collective-permute-start(f32[1,1024]{1,0:T(1,128)S(1)} %get-tuple-element.37.refs_3_), channel_id=1, source_target_pairs={{0,1},{1,0},{32,33},{33,32},{2,3},{3,2},{34,35},{35,34},{4,5},{5,4... | collective-permute-start | bytes 12296 | tf_op jit(solution)/shard_map/ppermute | solution.py:41
  19.6 2.6 %collective-permute-start.7 = (bf16[256,512]{1,0:T(8,128)(2,1)S(1)}, bf16[256,512]{1,0:T(8,128)(2,1)S(1)}, u32[]{:S(2)}, u32[]{:S(2)}) collective-permute-start(bf16[256,512]{1,0:T(8,128)(2,1)S(1)} %get-tuple-element.31.refs_2_), channel_id=1, source_target_pairs={{0,2},{2,4},{4,6},{6,8},{8,10},{10,12},{12,14},{14,0},{16,30},{18,... | collective-permute-start | bytes 786440 | tf_op jit(solution)/shard_map/ppermute | solution.py:47
  22.2 1.2 %cauchy.2.refs_1_ = bf16[1024,1792]{1,0:T(8,128)(2,1)S(1)} custom-call(s32[1]{0:T(128)} %bitcast.refs_0_.me_ref, f32[128,128]{1,0:T(8,128)S(1)} %get-tuple-element.33.refs_1_.poles_ref, f32[128,128]{1,0:T(8,128)S(1)} %get-tuple-element.34.refs_2_.factors_ref, f32[1,1024]{1,0:T(1,128)S(1)} %get-tuple-element.37.refs_3_, ...), custom_call_target="tpu_custom_call" | custom-call | flops 1 | bytes 1 | tf_op jit(solution)/shard_map/cauchy/pallas_call | solution.py:174
  23.5 1.1 %collective-permute-start.6 = (bf16[256,512]{1,0:T(8,128)(2,1)S(1)}, bf16[256,512]{1,0:T(8,128)(2,1)S(1)}, u32[]{:S(2)}, u32[]{:S(2)}) collective-permute-start(bf16[256,512]{1,0:T(8,128)(2,1)S(1)} %collective-permute-done.1.refs_5_), channel_id=1, source_target_pairs={{0,2},{2,4},{4,6},{6,8},{8,10},{10,12},{12,14},{14,0},{16,30},{18,... | collective-permute-start | bytes 786440 | tf_op jit(solution)/shard_map/ppermute | solution.py:47
  24.6 1.5 %cauchy.3.refs_0_.c_ref = bf16[1024,2304]{1,0:T(8,128)(2,1)S(1)} custom-call(s32[1]{0:T(128)} %bitcast.refs_0_.me_ref, f32[128,128]{1,0:T(8,128)S(1)} %get-tuple-element.33.refs_1_.poles_ref, f32[128,128]{1,0:T(8,128)S(1)} %get-tuple-element.34.refs_2_.factors_ref, f32[1,1024]{1,0:T(1,128)S(1)} %get-tuple-element.37.refs_3_, ...), custom_call_target="tpu_custom_call" | custom-call | flops 1 | bytes 1 | tf_op jit(solution)/shard_map/cauchy/pallas_call | solution.py:174
  26.6 1.5 %collective-permute-done.7.refs_3_ = bf16[256,512]{1,0:T(8,128)(2,1)S(1)} collective-permute-done((bf16[256,512]{1,0:T(8,128)(2,1)S(1)}, bf16[256,512]{1,0:T(8,128)(2,1)S(1)}, u32[]{:S(2)}, u32[]{:S(2)}) %collective-permute-start.7) | collective-permute-done | bytes 262176 | tf_op jit(solution)/shard_map/ppermute | solution.py:47
  28.1 2.3 %stage.3 = (f32[1024,512]{1,0:T(8,128)S(1)}, f32[1024,512]{1,0:T(8,128)S(1)}) custom-call(bf16[1024,2304]{1,0:T(8,128)(2,1)S(1)} %cauchy.3.refs_0_.c_ref, bf16[1024,1792]{1,0:T(8,128)(2,1)S(1)} %cauchy.2.refs_1_, bf16[256,512]{1,0:T(8,128)(2,1)S(1)} %get-tuple-element.31.refs_2_, bf16[256,512]{1,0:T(8,128)(2,1)S(1)} %collective-permute-done.7.refs_3_, ...), custom_call_target="tpu_custom_call" | custom-call | flops 1 | bytes 1 | tf_op jit(solution)/shard_map/stage/pallas_call | solution.py:246
  31.2 3.1 %collective-permute-start.8 = (bf16[256,512]{1,0:T(8,128)(2,1)S(1)}, bf16[256,512]{1,0:T(8,128)(2,1)S(1)}, u32[]{:S(2)}, u32[]{:S(2)}) collective-permute-start(bf16[256,512]{1,0:T(8,128)(2,1)S(1)} %collective-permute-done.6.refs_3_), channel_id=1, source_target_pairs={{0,2},{2,4},{4,6},{6,8},{8,10},{10,12},{12,14},{14,0},{16,30},{18,... | collective-permute-start | bytes 786440 | tf_op jit(solution)/shard_map/ppermute | solution.py:47
  34.3 1.3 %stage.4 = (f32[1024,512]{1,0:T(8,128)S(1)}, f32[1024,512]{1,0:T(8,128)S(1)}) custom-call(bf16[1024,2304]{1,0:T(8,128)(2,1)S(1)} %cauchy.3.refs_0_.c_ref, bf16[1024,1792]{1,0:T(8,128)(2,1)S(1)} %cauchy.2.refs_1_, bf16[256,512]{1,0:T(8,128)(2,1)S(1)} %collective-permute-done.10.refs_2_, bf16[256,512]{1,0:T(8,128)(2,1)S(1)} %collective-permute-done.6.refs_3_, ...), custom_call_target="tpu_custom_call" | custom-call | flops 1 | bytes 1 | tf_op jit(solution)/shard_map/stage/pallas_call | solution.py:246
  36.3 5.3 %collective-permute-start.12 = (bf16[1024,512]{1,0:T(8,128)(2,1)S(1)}, bf16[1024,512]{1,0:T(8,128)(2,1)S(1)}, u32[]{:S(2)}, u32[]{:S(2)}) collective-permute-start(bf16[1024,512]{1,0:T(8,128)(2,1)S(1)} %get-tuple-element.47), channel_id=1, source_target_pairs={{0,16},{16,0},{1,17},{17,1},{2,18},{18,2},{3,19},{19,3},{4,20},{20... | collective-permute-start | bytes 3145736 | tf_op jit(solution)/shard_map/ppermute | solution.py:51
  41.6 4.9 %collective-permute-start.9 = (bf16[256,512]{1,0:T(8,128)(2,1)S(1)}, bf16[256,512]{1,0:T(8,128)(2,1)S(1)}, u32[]{:S(2)}, u32[]{:S(2)}) collective-permute-start(bf16[256,512]{1,0:T(8,128)(2,1)S(1)} %collective-permute-done.8.x_ref), channel_id=1, source_target_pairs={{0,16},{16,0},{1,17},{17,1},{2,18},{18,2},{3,19},{19,3},{4,20},{20... | collective-permute-start | bytes 786440 | tf_op jit(solution)/shard_map/ppermute | solution.py:51
  48.1 1.4 %collective-permute-start.13 = (bf16[256,512]{1,0:T(8,128)(2,1)S(1)}, bf16[256,512]{1,0:T(8,128)(2,1)S(1)}, u32[]{:S(2)}, u32[]{:S(2)}) collective-permute-start(bf16[256,512]{1,0:T(8,128)(2,1)S(1)} %get-tuple-element.49), channel_id=1, source_target_pairs={{0,1},{1,0},{32,33},{33,32},{2,3},{3,2},{34,35},{35,34},{4,5},{5,4... | collective-permute-start | bytes 786440 | tf_op jit(solution)/shard_map/ppermute | solution.py:41
  49.5 1.0 %collective-permute-start.14 = (bf16[256,512]{1,0:T(8,128)(2,1)S(1)}, bf16[256,512]{1,0:T(8,128)(2,1)S(1)}, u32[]{:S(2)}, u32[]{:S(2)}) collective-permute-start(bf16[256,512]{1,0:T(8,128)(2,1)S(1)} %get-tuple-element.50), channel_id=1, source_target_pairs={{0,32},{1,33},{32,1},{33,0},{2,34},{3,35},{34,3},{35,2},{4,36},{5,... | collective-permute-start | bytes 786440 | tf_op jit(solution)/shard_map/ppermute | solution.py:41
  50.5 1.7 %collective-permute-start.15 = (bf16[256,512]{1,0:T(8,128)(2,1)S(1)}, bf16[256,512]{1,0:T(8,128)(2,1)S(1)}, u32[]{:S(2)}, u32[]{:S(2)}) collective-permute-start(bf16[256,512]{1,0:T(8,128)(2,1)S(1)} %get-tuple-element.51), channel_id=1, source_target_pairs={{0,33},{1,32},{32,0},{33,1},{2,35},{3,34},{34,2},{35,3},{4,37},{5,... | collective-permute-start | bytes 786440 | tf_op jit(solution)/shard_map/ppermute | solution.py:41
  52.2 3.4 %norms.1 = (f32[256,128]{1,0:T(8,128)S(1)}, bf16[512,512]{1,0:T(8,128)(2,1)}) custom-call(f32[128,128]{1,0:T(8,128)S(1)} %get-tuple-element.33.refs_1_.poles_ref, f32[128,128]{1,0:T(8,128)S(1)} %get-tuple-element.34.refs_2_.factors_ref, f32[1,512]{1,0:T(1,128)S(1)} %bitcast.7, bf16[512,256]{1,0:T(8,128)(2,1)S(1)} %get-tuple-element.53.rest_ref), custom_call_target="tpu_custom_call" | custom-call | flops 1 | bytes 1 | tf_op jit(solution)/shard_map/norms/pallas_call | solution.py:207
  55.6 1.7 %collective-permute-done.13.a_ref = bf16[256,512]{1,0:T(8,128)(2,1)S(1)} collective-permute-done((bf16[256,512]{1,0:T(8,128)(2,1)S(1)}, bf16[256,512]{1,0:T(8,128)(2,1)S(1)}, u32[]{:S(2)}, u32[]{:S(2)}) %collective-permute-start.13) | collective-permute-done | bytes 262176 | tf_op jit(solution)/shard_map/ppermute | solution.py:41
  57.2 6.3 %collective-permute-done.14.b_ref = bf16[256,512]{1,0:T(8,128)(2,1)S(1)} collective-permute-done((bf16[256,512]{1,0:T(8,128)(2,1)S(1)}, bf16[256,512]{1,0:T(8,128)(2,1)S(1)}, u32[]{:S(2)}, u32[]{:S(2)}) %collective-permute-start.14) | collective-permute-done | bytes 262176 | tf_op jit(solution)/shard_map/ppermute | solution.py:41
  63.5 1.5 %finish.1 = bf16[512,512]{1,0:T(8,128)(2,1)} custom-call(s32[1]{0:T(128)} %bitcast.refs_0_.me_ref, s32[64]{0:T(128)S(1)} %copy-done.1, f32[256,512]{1,0:T(8,128)S(1)} %get-tuple-element.48.own_ref, bf16[256,512]{1,0:T(8,128)(2,1)S(1)} %collective-permute-done.13.a_ref, ...), custom_call_target="tpu_custom_call", output_to_operand_aliasing={{}: (8, {})} | custom-call | flops 1 | bytes 1 | tf_op jit(solution)/shard_map/finish/pallas_call | solution.py:319
  (23 shorter events, 5.2 us)
Async XLA Ops:
  1.7 13.4 %collective-permute-start.2 = (bf16[256,512]{1,0:T(8,128)(2,1)S(1)}, bf16[256,512]{1,0:T(8,128)(2,1)S(1)}, u32[]{:S(2)}, u32[]{:S(2)}) collective-permute-start(bf16[256,512]{1,0:T(8,128)(2,1)S(1)} %get-tuple-element.31.refs_2_), channel_id=1, source_target_pairs={{0,14},{2,0},{4,2},{6,4},{8,6},{10,8},{12,10},{14,12},{16,18},{18,... | collective-permute-start | bytes 786440 | tf_op jit(solution)/shard_map/ppermute | solution.py:47
  4.3 19.2 %collective-permute-start.1 = (bf16[256,512]{1,0:T(8,128)(2,1)S(1)}, bf16[256,512]{1,0:T(8,128)(2,1)S(1)}, u32[]{:S(2)}, u32[]{:S(2)}) collective-permute-start(bf16[256,512]{1,0:T(8,128)(2,1)S(1)} %get-tuple-element.31.refs_2_), channel_id=1, source_target_pairs={{0,4},{2,6},{4,8},{6,10},{8,12},{10,14},{12,0},{14,2},{16,28},{18,... | collective-permute-start | bytes 786440 | tf_op jit(solution)/shard_map/ppermute | solution.py:47
  9.4 1.4 %collective-permute-start = (f32[1,512]{1,0:T(1,128)}, f32[1,512]{1,0:T(1,128)S(1)}, u32[]{:S(2)}, u32[]{:S(2)}) collective-permute-start(f32[1,512]{1,0:T(1,128)} %bitcast.5), channel_id=1, source_target_pairs={{0,16},{16,0},{1,17},{17,1},{2,18},{18,2},{3,19},{19,3},{4,20},{20... | collective-permute-start | bytes 6152 | tf_op jit(solution)/shard_map/ppermute | solution.py:51
  11.8 3.3 %collective-permute-start.3 = (f32[1,1024]{1,0:T(1,128)S(1)}, f32[1,1024]{1,0:T(1,128)S(1)}, u32[]{:S(2)}, u32[]{:S(2)}) collective-permute-start(f32[1,1024]{1,0:T(1,128)S(1)} %get-tuple-element.37.refs_3_), channel_id=1, source_target_pairs={{0,33},{1,32},{32,0},{33,1},{2,35},{3,34},{34,2},{35,3},{4,37},{5,... | collective-permute-start | bytes 12296 | tf_op jit(solution)/shard_map/ppermute | solution.py:41
  15.2 10.9 %collective-permute-start.10 = (bf16[256,512]{1,0:T(8,128)(2,1)S(1)}, bf16[256,512]{1,0:T(8,128)(2,1)S(1)}, u32[]{:S(2)}, u32[]{:S(2)}) collective-permute-start(bf16[256,512]{1,0:T(8,128)(2,1)S(1)} %collective-permute-done.2.refs_4_), channel_id=1, source_target_pairs={{0,14},{2,0},{4,2},{6,4},{8,6},{10,8},{12,10},{14,12},{16,18},{18,... | collective-permute-start | bytes 786440 | tf_op jit(solution)/shard_map/ppermute | solution.py:47
  15.3 7.0 %collective-permute-start.5 = (f32[1,1024]{1,0:T(1,128)S(1)}, f32[1,1024]{1,0:T(1,128)S(1)}, u32[]{:S(2)}, u32[]{:S(2)}) collective-permute-start(f32[1,1024]{1,0:T(1,128)S(1)} %get-tuple-element.37.refs_3_), channel_id=1, source_target_pairs={{0,32},{1,33},{32,1},{33,0},{2,34},{3,35},{34,3},{35,2},{4,36},{5,... | collective-permute-start | bytes 12296 | tf_op jit(solution)/shard_map/ppermute | solution.py:41
  16.0 6.3 %collective-permute-start.4 = (f32[1,1024]{1,0:T(1,128)S(1)}, f32[1,1024]{1,0:T(1,128)S(1)}, u32[]{:S(2)}, u32[]{:S(2)}) collective-permute-start(f32[1,1024]{1,0:T(1,128)S(1)} %get-tuple-element.37.refs_3_), channel_id=1, source_target_pairs={{0,1},{1,0},{32,33},{33,32},{2,3},{3,2},{34,35},{35,34},{4,5},{5,4... | collective-permute-start | bytes 12296 | tf_op jit(solution)/shard_map/ppermute | solution.py:41
  19.6 8.4 %collective-permute-start.7 = (bf16[256,512]{1,0:T(8,128)(2,1)S(1)}, bf16[256,512]{1,0:T(8,128)(2,1)S(1)}, u32[]{:S(2)}, u32[]{:S(2)}) collective-permute-start(bf16[256,512]{1,0:T(8,128)(2,1)S(1)} %get-tuple-element.31.refs_2_), channel_id=1, source_target_pairs={{0,2},{2,4},{4,6},{6,8},{8,10},{10,12},{12,14},{14,0},{16,30},{18,... | collective-permute-start | bytes 786440 | tf_op jit(solution)/shard_map/ppermute | solution.py:47
  23.5 7.7 %collective-permute-start.6 = (bf16[256,512]{1,0:T(8,128)(2,1)S(1)}, bf16[256,512]{1,0:T(8,128)(2,1)S(1)}, u32[]{:S(2)}, u32[]{:S(2)}) collective-permute-start(bf16[256,512]{1,0:T(8,128)(2,1)S(1)} %collective-permute-done.1.refs_5_), channel_id=1, source_target_pairs={{0,2},{2,4},{4,6},{6,8},{8,10},{10,12},{12,14},{14,0},{16,30},{18,... | collective-permute-start | bytes 786440 | tf_op jit(solution)/shard_map/ppermute | solution.py:47
  26.1 9.5 %collective-permute-start.11 = (bf16[256,512]{1,0:T(8,128)(2,1)S(1)}, bf16[256,512]{1,0:T(8,128)(2,1)S(1)}, u32[]{:S(2)}, u32[]{:S(2)}) collective-permute-start(bf16[256,512]{1,0:T(8,128)(2,1)S(1)} %collective-permute-done.10.refs_2_), channel_id=1, source_target_pairs={{0,14},{2,0},{4,2},{6,4},{8,6},{10,8},{12,10},{14,12},{16,18},{18,... | collective-permute-start | bytes 786440 | tf_op jit(solution)/shard_map/ppermute | solution.py:47
  31.2 10.4 %collective-permute-start.8 = (bf16[256,512]{1,0:T(8,128)(2,1)S(1)}, bf16[256,512]{1,0:T(8,128)(2,1)S(1)}, u32[]{:S(2)}, u32[]{:S(2)}) collective-permute-start(bf16[256,512]{1,0:T(8,128)(2,1)S(1)} %collective-permute-done.6.refs_3_), channel_id=1, source_target_pairs={{0,2},{2,4},{4,6},{6,8},{8,10},{10,12},{12,14},{14,0},{16,30},{18,... | collective-permute-start | bytes 786440 | tf_op jit(solution)/shard_map/ppermute | solution.py:47
  36.3 11.4 %collective-permute-start.12 = (bf16[1024,512]{1,0:T(8,128)(2,1)S(1)}, bf16[1024,512]{1,0:T(8,128)(2,1)S(1)}, u32[]{:S(2)}, u32[]{:S(2)}) collective-permute-start(bf16[1024,512]{1,0:T(8,128)(2,1)S(1)} %get-tuple-element.47), channel_id=1, source_target_pairs={{0,16},{16,0},{1,17},{17,1},{2,18},{18,2},{3,19},{19,3},{4,20},{20... | collective-permute-start | bytes 3145736 | tf_op jit(solution)/shard_map/ppermute | solution.py:51
  41.6 6.0 %collective-permute-start.9 = (bf16[256,512]{1,0:T(8,128)(2,1)S(1)}, bf16[256,512]{1,0:T(8,128)(2,1)S(1)}, u32[]{:S(2)}, u32[]{:S(2)}) collective-permute-start(bf16[256,512]{1,0:T(8,128)(2,1)S(1)} %collective-permute-done.8.x_ref), channel_id=1, source_target_pairs={{0,16},{16,0},{1,17},{17,1},{2,18},{18,2},{3,19},{19,3},{4,20},{20... | collective-permute-start | bytes 786440 | tf_op jit(solution)/shard_map/ppermute | solution.py:51
  46.9 5.3 %copy-start = (f32[512]{0:T(512)S(1)}, f32[512]{0:T(512)}, u32[]{:S(2)}) copy-start(f32[512]{0:T(512)} %param.11) | copy-start | bytes 6148
  46.9 16.6 %copy-start.1 = (s32[64]{0:T(128)S(1)}, s32[64]{0:T(128)}, u32[]{:S(2)}) copy-start(s32[64]{0:T(128)} %counts_ref.1) | copy-start | bytes 772
  48.1 9.2 %collective-permute-start.13 = (bf16[256,512]{1,0:T(8,128)(2,1)S(1)}, bf16[256,512]{1,0:T(8,128)(2,1)S(1)}, u32[]{:S(2)}, u32[]{:S(2)}) collective-permute-start(bf16[256,512]{1,0:T(8,128)(2,1)S(1)} %get-tuple-element.49), channel_id=1, source_target_pairs={{0,1},{1,0},{32,33},{33,32},{2,3},{3,2},{34,35},{35,34},{4,5},{5,4... | collective-permute-start | bytes 786440 | tf_op jit(solution)/shard_map/ppermute | solution.py:41
  49.5 14.0 %collective-permute-start.14 = (bf16[256,512]{1,0:T(8,128)(2,1)S(1)}, bf16[256,512]{1,0:T(8,128)(2,1)S(1)}, u32[]{:S(2)}, u32[]{:S(2)}) collective-permute-start(bf16[256,512]{1,0:T(8,128)(2,1)S(1)} %get-tuple-element.50), channel_id=1, source_target_pairs={{0,32},{1,33},{32,1},{33,0},{2,34},{3,35},{34,3},{35,2},{4,36},{5,... | collective-permute-start | bytes 786440 | tf_op jit(solution)/shard_map/ppermute | solution.py:41
  50.5 13.0 %collective-permute-start.15 = (bf16[256,512]{1,0:T(8,128)(2,1)S(1)}, bf16[256,512]{1,0:T(8,128)(2,1)S(1)}, u32[]{:S(2)}, u32[]{:S(2)}) collective-permute-start(bf16[256,512]{1,0:T(8,128)(2,1)S(1)} %get-tuple-element.51), channel_id=1, source_target_pairs={{0,33},{1,32},{32,0},{33,1},{2,35},{3,34},{34,2},{35,3},{4,37},{5,... | collective-permute-start | bytes 786440 | tf_op jit(solution)/shard_map/ppermute | solution.py:41

commit v8 on v5

--- a/solution.py
+++ b/solution.py
@@ -138,17 +138,34 @@
     )(counts, poles, weights)
 
 
+def join_kernel(a_ref, b_ref, o_ref):
+    o_ref[:, :COLS] = a_ref[...]
+    o_ref[:, COLS:] = b_ref[...]
+
+
+def join(a, b):
+    return pl.pallas_call(
+        join_kernel,
+        in_specs=[VM, VM],
+        out_specs=VM,
+        out_shape=pltpu.VMEM((1, 2 * COLS), F32),
+        name="join",
+        compiler_params=params(4),
+        cost_estimate=TINY,
+    )(a, b)
+
+
 def column(row):
     return jnp.transpose(jnp.broadcast_to(row, (8, LIVE)))[:, :1]
 
 
-def cauchy_kernel(fc, pieces, me_ref, poles_ref, factors_ref, near_ref, far_ref, c_ref):
+def cauchy_kernel(fc, pieces, me_ref, poles_ref, factors_ref, *refs):
+    r_refs, c_ref = refs[:-1], refs[-1]
     me = me_ref[0]
     core, z = (me // 16) % 2, (me // 2) % ZS
     step = 1 - 2 * core
     for j in range(XS):
-        lo = (2 * (j % 2) + fc) * COLS
-        roots = column((far_ref if j // 2 else near_ref)[:, lo : lo + LIVE])
+        roots = column(r_refs[j][:, fc * COLS : fc * COLS + LIVE])
         for t in range(LIVE // TILE):
             own = jnp.broadcast_to(roots[t * TILE : (t + 1) * TILE], (TILE, LANES))
             rows = slice(j * LIVE + t * TILE, j * LIVE + (t + 1) * TILE)
@@ -164,16 +181,16 @@
                     c_ref[rows, lo : lo + LANES] = value.astype(BF16)
 
 
-def cauchy(fc, pieces, me, poles, factors, near, far):
+def cauchy(fc, pieces, me, poles, factors, roots):
     return pl.pallas_call(
         lambda *refs: cauchy_kernel(fc, pieces, *refs),
-        in_specs=[SM, VM, VM, VM, VM],
+        in_specs=[SM] + [VM] * (2 + XS),
         out_specs=VM,
         out_shape=pltpu.VMEM((XS * LIVE, len(pieces) * LIVE), BF16),
         name="cauchy",
         compiler_params=params(8),
         cost_estimate=TINY,
-    )(me, poles, factors, near, far)
+    )(me, poles, factors, *roots)
 
 
 def norm_kernel(poles_ref, factors_ref, r_ref, rest_ref, n_ref, o_hbm, sem):
@@ -329,29 +346,28 @@
     other_roots = cshift(roots)
 
     own, lead, rest = permute(in_hbm(eigvecs), in_hbm(perm.reshape(1, COLS)))
+    p3 = around(own, 2)
+    p2 = around(own, -1)
+    p1 = around(own, 1)
+    near = join(roots, hold(other_roots, own))
+    far = [xshift(near, k) for k in (-1, -2, 1)]
     table, factors = tables(
-        hold(in_hbm(counts), own), in_hbm(poles.reshape(-1, LANES)), in_hbm(weights.reshape(-1, LANES))
+        hold(in_hbm(counts), near), in_hbm(poles.reshape(-1, LANES)), in_hbm(weights.reshape(-1, LANES))
     )
-    p3 = around(own, 2)
-    p4 = around(own, -2)
-    p1 = around(own, 1)
-    p2 = around(own, -1)
-    near = jnp.concatenate([hold(roots, factors), other_roots], axis=1)
-    pair = jnp.concatenate([near, xshift(near, -1)], axis=1)
-    far = xshift(pair, -2)
-    p5 = around(p3, 1)
-    p6 = around(p4, -1)
-    p7 = around(p3, 2)
-    c_other = cauchy(1, OTHER, me, table, factors, pair, hold(far, p3, p4))
-    c_mine = cauchy(0, MINE, me, table, factors, pair, hold(far, c_other))
-
-    sums = stage(0, c_mine, c_other, (own, p1, p2, p3, p4), (), False)
-    mine, other = stage(5, c_mine, c_other, (p5, p6), sums, True)
+    p4 = around(hold(p2, factors, *far), -1)
+    p5 = around(hold(p3, *far), 1)
+    c_other = cauchy(1, OTHER, me, table, factors, [hold(near, p3), *far])
+    c_mine = cauchy(0, MINE, me, table, factors, [hold(near, c_other), *far])
+    p6 = around(hold(p4, c_other), -1)
+    p7 = around(hold(p5, c_mine), 1)
+    sums = stage(0, c_mine, c_other, (hold(own, p5), p1, p2, p3), (), False)
+    sums = stage(4, c_mine, c_other, (p4, p5), sums, False)
+    mine, other = stage(6, c_mine, c_other, (p6,), sums, True)
     other = cshift(other)
     sibling = cshift(p7)
     mine = add_opposite(c_mine, p7, mine)
     own_sum, *sent = totals(c_mine, sibling, mine, other)
-    received = [xshift(part, k) for k, part in zip((1, 2, -1), sent, strict=True)]
+    received = [xshift(sent[i], k) for i, k in ((1, 2), (0, 1), (2, -1))]
     norm, out = norms(table, factors, hold(roots, own_sum), rest)
     return finish(me, counts, own_sum, received, norm, lead, out)
 

time: 60 us -> 60.9 us (1.015)
  waiting for transfers between devices: 10.5 us -> 13.4 us
  starting transfers between devices: 32.2 us -> 30.9 us
  other arithmetic: 0.69 us -> 0 us
    ppermute x7, starting transfers between devices: 16.6 us -> 15 us  [around(): return lax.ppermute(a, ('core', 'z'), up + down)]
    ppermute x3, starting transfers between devices: 5.39 us -> 6.93 us  [cshift(): return lax.ppermute(a, 'core', [(0, 1), (1, 0)])]
    ppermute x3, waiting for transfers between devices: 0.7 us -> 2.06 us  [cshift(): return lax.ppermute(a, 'core', [(0, 1), (1, 0)])]
    ppermute x5 -> x6, starting transfers between devices: 10.2 us -> 8.95 us  [xshift(): return lax.ppermute(a, ('xl', 'xh'), pairs)]
    ppermute x7, waiting for transfers between devices: 1.54 us -> 2.36 us  [around(): return lax.ppermute(a, ('core', 'z'), up + down)]
    ppermute x5 -> x6, waiting for transfers between devices: 8.27 us -> 8.99 us  [xshift(): return lax.ppermute(a, ('xl', 'xh'), pairs)]
    concatenate x1 -> x0, other arithmetic: 0.69 us -> none  [per_device(): near = jnp.concatenate([hold(roots, factors), other_roots], axis=1)]
    pallas_call x2 -> x3, Pallas kernels: 4.13 us -> 4.33 us  [stage(): pl.pallas_call(lambda *refs: stage_kernel(first, len(pieces), *refs), in_...]
  transfers between devices with their start and end apart: 15 -> 16, of which waited for: 5 -> 9; matrix products, arithmetic and copies ran while one was open for 2% -> 0% of each run, Pallas kernels for 20% -> 20%
where the time goes in v8:
time: 60.9 us; the launch traced here: 60.8 us
  starting transfers between devices  30.9 us (51%)
  Pallas kernels  15.5 us (25%)
  waiting for transfers between devices  13.4 us (22%)
  local copies, waits for them, and re-layouts  0.69 us (1%)
    ppermute x7, starting transfers between devices, around(): return lax.ppermute(a, ('core', 'z'), up + down)  15 us
    ppermute x6, waiting for transfers between devices, xshift(): return lax.ppermute(a, ('xl', 'xh'), pairs)  8.99 us
    ppermute x6, starting transfers between devices, xshift(): return lax.ppermute(a, ('xl', 'xh'), pairs)  8.95 us
    ppermute x3, starting transfers between devices, cshift(): return lax.ppermute(a, 'core', [(0, 1), (1, 0)])  6.93 us
    pallas_call x3, Pallas kernels, stage(): pl.pallas_call(lambda *refs: stage_kernel(first, len(pieces), *refs), in_...  4.33 us
    pallas_call x1, Pallas kernels, norms(): pl.pallas_call(norm_kernel, in_specs=[VM] * 4, out_specs=[VM, HB], out_sh...  3.38 us
    pallas_call x2, Pallas kernels, cauchy(): pl.pallas_call(lambda *refs: cauchy_kernel(fc, pieces, *refs), in_specs=[...  2.69 us
    ppermute x7, waiting for transfers between devices, around(): return lax.ppermute(a, ('core', 'z'), up + down)  2.36 us
  transfers between devices with their start and end apart: 16, of which 9 were waited for; matrix products, arithmetic and copies ran while one was open for 0% of the time, Pallas kernels for 20%

profile of v8, /device:TPU:1, one launch (start us, length us, event | category | flops | bytes accessed | tf_op | source)
XLA Modules:
  0.0 60.8 jit_solution(1783084203280959804)
XLA Ops:
  0.0 1.7 %permute.1 = (bf16[256,512]{1,0:T(8,128)(2,1)S(1)}, bf16[512,256]{1,0:T(8,128)(2,1)S(1)}, bf16[512,256]{1,0:T(8,128)(2,1)S(1)}) custom-call(bf16[512,512]{1,0:T(8,128)(2,1)} %e_hbm.1, s32[1,512]{1,0:T(1,128)} %bitcast.10), custom_call_target="tpu_custom_call" | custom-call | flops 1 | bytes 1 | tf_op jit(solution)/shard_map/permute/pallas_call | solution.py:86
  1.7 2.5 %collective-permute-start.8 = (bf16[256,512]{1,0:T(8,128)(2,1)S(1)}, bf16[256,512]{1,0:T(8,128)(2,1)S(1)}, u32[]{:S(2)}, u32[]{:S(2)}) collective-permute-start(bf16[256,512]{1,0:T(8,128)(2,1)S(1)} %get-tuple-element.43.refs_2_), channel_id=1, source_target_pairs={{0,14},{2,0},{4,2},{6,4},{8,6},{10,8},{12,10},{14,12},{16,18},{18,... | collective-permute-start | bytes 786440 | tf_op jit(solution)/shard_map/ppermute | solution.py:47
  4.3 5.1 %collective-permute-start.1 = (bf16[256,512]{1,0:T(8,128)(2,1)S(1)}, bf16[256,512]{1,0:T(8,128)(2,1)S(1)}, u32[]{:S(2)}, u32[]{:S(2)}) collective-permute-start(bf16[256,512]{1,0:T(8,128)(2,1)S(1)} %get-tuple-element.43.refs_2_), channel_id=1, source_target_pairs={{0,4},{2,6},{4,8},{6,10},{8,12},{10,14},{12,0},{14,2},{16,28},{18,... | collective-permute-start | bytes 786440 | tf_op jit(solution)/shard_map/ppermute | solution.py:47
  9.4 1.4 %collective-permute-done.b_ref = f32[1,512]{1,0:T(1,128)S(1)} collective-permute-done((f32[1,512]{1,0:T(1,128)}, f32[1,512]{1,0:T(1,128)S(1)}, u32[]{:S(2)}, u32[]{:S(2)}) %collective-permute-start) | collective-permute-done | bytes 2080 | tf_op jit(solution)/shard_map/ppermute | solution.py:51
  11.4 2.5 %collective-permute-start.2 = (f32[1,1024]{1,0:T(1,128)S(1)}, f32[1,1024]{1,0:T(1,128)S(1)}, u32[]{:S(2)}, u32[]{:S(2)}) collective-permute-start(f32[1,1024]{1,0:T(1,128)S(1)} %join.1.refs_3_), channel_id=1, source_target_pairs={{0,33},{1,32},{32,0},{33,1},{2,35},{3,34},{34,2},{35,3},{4,37},{5,... | collective-permute-start | bytes 12296 | tf_op jit(solution)/shard_map/ppermute | solution.py:41
  15.1 1.1 %tables.1 = (f32[128,128]{1,0:T(8,128)S(1)}, f32[128,128]{1,0:T(8,128)S(1)}) custom-call(s32[64]{0:T(128)} %counts_ref.1, f32[256,128]{1,0:T(8,128)} %bitcast.8, f32[256,128]{1,0:T(8,128)} %bitcast.9), custom_call_target="tpu_custom_call" | custom-call | flops 1 | bytes 1 | tf_op jit(solution)/shard_map/tables/pallas_call | solution.py:128
  16.1 2.1 %collective-permute-done.3.refs_5_ = f32[1,1024]{1,0:T(1,128)S(1)} collective-permute-done((f32[1,1024]{1,0:T(1,128)S(1)}, f32[1,1024]{1,0:T(1,128)S(1)}, u32[]{:S(2)}, u32[]{:S(2)}) %collective-permute-start.3) | collective-permute-done | bytes 4128 | tf_op jit(solution)/shard_map/ppermute | solution.py:41
  18.4 2.7 %collective-permute-start.5 = (bf16[256,512]{1,0:T(8,128)(2,1)S(1)}, bf16[256,512]{1,0:T(8,128)(2,1)S(1)}, u32[]{:S(2)}, u32[]{:S(2)}) collective-permute-start(bf16[256,512]{1,0:T(8,128)(2,1)S(1)} %collective-permute-done.1.refs_5_), channel_id=1, source_target_pairs={{0,2},{2,4},{4,6},{6,8},{8,10},{10,12},{12,14},{14,0},{16,30},{18,... | collective-permute-start | bytes 786440 | tf_op jit(solution)/shard_map/ppermute | solution.py:47
  21.1 1.7 %collective-permute-start.11 = (bf16[256,512]{1,0:T(8,128)(2,1)S(1)}, bf16[256,512]{1,0:T(8,128)(2,1)S(1)}, u32[]{:S(2)}, u32[]{:S(2)}) collective-permute-start(bf16[256,512]{1,0:T(8,128)(2,1)S(1)} %get-tuple-element.43.refs_2_), channel_id=1, source_target_pairs={{0,2},{2,4},{4,6},{6,8},{8,10},{10,12},{12,14},{14,0},{16,30},{18,... | collective-permute-start | bytes 786440 | tf_op jit(solution)/shard_map/ppermute | solution.py:47
  22.8 1.2 %cauchy.2.refs_1_ = bf16[1024,1792]{1,0:T(8,128)(2,1)S(1)} custom-call(s32[1]{0:T(128)} %bitcast.refs_0_.me_ref, f32[128,128]{1,0:T(8,128)S(1)} %get-tuple-element.35.refs_1_.poles_ref, f32[128,128]{1,0:T(8,128)S(1)} %get-tuple-element.36.refs_2_.factors_ref, f32[1,1024]{1,0:T(1,128)S(1)} %join.1.refs_3_, f32[1,1024]{1,0:T(1,128)S(1)} %collective-permute-done.2.refs_4_, ...), custom_call_target="tpu_custom_call" | custom-call | flops 1 | bytes 1 | tf_op jit(solution)/shard_map/cauchy/pallas_call | solution.py:185
  24.0 0.8 %collective-permute-done.9.refs_2_ = bf16[256,512]{1,0:T(8,128)(2,1)S(1)} collective-permute-done((bf16[256,512]{1,0:T(8,128)(2,1)S(1)}, bf16[256,512]{1,0:T(8,128)(2,1)S(1)}, u32[]{:S(2)}, u32[]{:S(2)}) %collective-permute-start.9) | collective-permute-done | bytes 262176 | tf_op jit(solution)/shard_map/ppermute | solution.py:47
  24.9 1.5 %cauchy.3.refs_0_.c_ref = bf16[1024,2304]{1,0:T(8,128)(2,1)S(1)} custom-call(s32[1]{0:T(128)} %bitcast.refs_0_.me_ref, f32[128,128]{1,0:T(8,128)S(1)} %get-tuple-element.35.refs_1_.poles_ref, f32[128,128]{1,0:T(8,128)S(1)} %get-tuple-element.36.refs_2_.factors_ref, f32[1,1024]{1,0:T(1,128)S(1)} %join.1.refs_3_, ...), custom_call_target="tpu_custom_call" | custom-call | flops 1 | bytes 1 | tf_op jit(solution)/shard_map/cauchy/pallas_call | solution.py:185
  26.4 2.9 %collective-permute-start.6 = (bf16[256,512]{1,0:T(8,128)(2,1)S(1)}, bf16[256,512]{1,0:T(8,128)(2,1)S(1)}, u32[]{:S(2)}, u32[]{:S(2)}) collective-permute-start(bf16[256,512]{1,0:T(8,128)(2,1)S(1)} %collective-permute-done.5.refs_3_), channel_id=1, source_target_pairs={{0,2},{2,4},{4,6},{6,8},{8,10},{10,12},{12,14},{14,0},{16,30},{18,... | collective-permute-start | bytes 786440 | tf_op jit(solution)/shard_map/ppermute | solution.py:47
  30.0 2.3 %stage.3 = (f32[1024,512]{1,0:T(8,128)S(1)}, f32[1024,512]{1,0:T(8,128)S(1)}) custom-call(bf16[1024,2304]{1,0:T(8,128)(2,1)S(1)} %cauchy.3.refs_0_.c_ref, bf16[1024,1792]{1,0:T(8,128)(2,1)S(1)} %cauchy.2.refs_1_, bf16[256,512]{1,0:T(8,128)(2,1)S(1)} %get-tuple-element.43.refs_2_, bf16[256,512]{1,0:T(8,128)(2,1)S(1)} %collective-permute-done.11.refs_3_, ...), custom_call_target="tpu_custom_call" | custom-call | flops 1 | bytes 1 | tf_op jit(solution)/shard_map/stage/pallas_call | solution.py:257
  32.4 1.3 %stage.4 = (f32[1024,512]{1,0:T(8,128)S(1)}, f32[1024,512]{1,0:T(8,128)S(1)}) custom-call(bf16[1024,2304]{1,0:T(8,128)(2,1)S(1)} %cauchy.3.refs_0_.c_ref, bf16[1024,1792]{1,0:T(8,128)(2,1)S(1)} %cauchy.2.refs_1_, bf16[256,512]{1,0:T(8,128)(2,1)S(1)} %collective-permute-done.9.refs_2_, bf16[256,512]{1,0:T(8,128)(2,1)S(1)} %collective-permute-done.5.refs_3_, ...), custom_call_target="tpu_custom_call" | custom-call | flops 1 | bytes 1 | tf_op jit(solution)/shard_map/stage/pallas_call | solution.py:257
  33.6 0.8 %collective-permute-done.10.refs_2_ = bf16[256,512]{1,0:T(8,128)(2,1)S(1)} collective-permute-done((bf16[256,512]{1,0:T(8,128)(2,1)S(1)}, bf16[256,512]{1,0:T(8,128)(2,1)S(1)}, u32[]{:S(2)}, u32[]{:S(2)}) %collective-permute-start.10) | collective-permute-done | bytes 262176 | tf_op jit(solution)/shard_map/ppermute | solution.py:47
  34.4 0.7 %stage.5 = (f32[1024,512]{1,0:T(8,128)S(1)}, bf16[1024,512]{1,0:T(8,128)(2,1)S(1)}) custom-call(bf16[1024,2304]{1,0:T(8,128)(2,1)S(1)} %cauchy.3.refs_0_.c_ref, bf16[1024,1792]{1,0:T(8,128)(2,1)S(1)} %cauchy.2.refs_1_, bf16[256,512]{1,0:T(8,128)(2,1)S(1)} %collective-permute-done.10.refs_2_, f32[1024,512]{1,0:T(8,128)S(1)} %get-tuple-element.46.refs_3_, ...), custom_call_target="tpu_custom_call" | custom-call | flops 1 | bytes 1 | tf_op jit(solution)/shard_map/stage/pallas_call | solution.py:257
  35.2 4.8 %collective-permute-start.12 = (bf16[1024,512]{1,0:T(8,128)(2,1)S(1)}, bf16[1024,512]{1,0:T(8,128)(2,1)S(1)}, u32[]{:S(2)}, u32[]{:S(2)}) collective-permute-start(bf16[1024,512]{1,0:T(8,128)(2,1)S(1)} %get-tuple-element.49), channel_id=1, source_target_pairs={{0,16},{16,0},{1,17},{17,1},{2,18},{18,2},{3,19},{19,3},{4,20},{20... | collective-permute-start | bytes 3145736 | tf_op jit(solution)/shard_map/ppermute | solution.py:51
  40.0 2.1 %collective-permute-start.7 = (bf16[256,512]{1,0:T(8,128)(2,1)S(1)}, bf16[256,512]{1,0:T(8,128)(2,1)S(1)}, u32[]{:S(2)}, u32[]{:S(2)}) collective-permute-start(bf16[256,512]{1,0:T(8,128)(2,1)S(1)} %collective-permute-done.6.x_ref), channel_id=1, source_target_pairs={{0,16},{16,0},{1,17},{17,1},{2,18},{18,2},{3,19},{19,3},{4,20},{20... | collective-permute-start | bytes 786440 | tf_op jit(solution)/shard_map/ppermute | solution.py:51
  43.7 2.7 %collective-permute-start.13 = (bf16[256,512]{1,0:T(8,128)(2,1)S(1)}, bf16[256,512]{1,0:T(8,128)(2,1)S(1)}, u32[]{:S(2)}, u32[]{:S(2)}) collective-permute-start(bf16[256,512]{1,0:T(8,128)(2,1)S(1)} %get-tuple-element.51), channel_id=1, source_target_pairs={{0,1},{1,0},{32,33},{33,32},{2,3},{3,2},{34,35},{35,34},{4,5},{5,4... | collective-permute-start | bytes 786440 | tf_op jit(solution)/shard_map/ppermute | solution.py:41
  46.7 2.4 %collective-permute-start.15 = (bf16[256,512]{1,0:T(8,128)(2,1)S(1)}, bf16[256,512]{1,0:T(8,128)(2,1)S(1)}, u32[]{:S(2)}, u32[]{:S(2)}) collective-permute-start(bf16[256,512]{1,0:T(8,128)(2,1)S(1)} %get-tuple-element.53), channel_id=1, source_target_pairs={{0,33},{1,32},{32,0},{33,1},{2,35},{3,34},{34,2},{35,3},{4,37},{5,... | collective-permute-start | bytes 786440 | tf_op jit(solution)/shard_map/ppermute | solution.py:41
  49.1 3.4 %norms.1 = (f32[256,128]{1,0:T(8,128)S(1)}, bf16[512,512]{1,0:T(8,128)(2,1)}) custom-call(f32[128,128]{1,0:T(8,128)S(1)} %get-tuple-element.35.refs_1_.poles_ref, f32[128,128]{1,0:T(8,128)S(1)} %get-tuple-element.36.refs_2_.factors_ref, f32[1,512]{1,0:T(1,128)S(1)} %bitcast.7, bf16[512,256]{1,0:T(8,128)(2,1)S(1)} %get-tuple-element.55.rest_ref), custom_call_target="tpu_custom_call" | custom-call | flops 1 | bytes 1 | tf_op jit(solution)/shard_map/norms/pallas_call | solution.py:218
  52.9 6.3 %collective-permute-done.14.b_ref = bf16[256,512]{1,0:T(8,128)(2,1)S(1)} collective-permute-done((bf16[256,512]{1,0:T(8,128)(2,1)S(1)}, bf16[256,512]{1,0:T(8,128)(2,1)S(1)}, u32[]{:S(2)}, u32[]{:S(2)}) %collective-permute-start.14) | collective-permute-done | bytes 262176 | tf_op jit(solution)/shard_map/ppermute | solution.py:41
  59.2 1.5 %finish.1 = bf16[512,512]{1,0:T(8,128)(2,1)} custom-call(s32[1]{0:T(128)} %bitcast.refs_0_.me_ref, s32[64]{0:T(128)S(1)} %copy-done.2, f32[256,512]{1,0:T(8,128)S(1)} %get-tuple-element.50.own_ref, bf16[256,512]{1,0:T(8,128)(2,1)S(1)} %collective-permute-done.13.a_ref, ...), custom_call_target="tpu_custom_call", output_to_operand_aliasing={{}: (8, {})} | custom-call | flops 1 | bytes 1 | tf_op jit(solution)/shard_map/finish/pallas_call | solution.py:330
  (26 shorter events, 5.1 us)
Async XLA Ops:
  1.7 16.7 %collective-permute-start.8 = (bf16[256,512]{1,0:T(8,128)(2,1)S(1)}, bf16[256,512]{1,0:T(8,128)(2,1)S(1)}, u32[]{:S(2)}, u32[]{:S(2)}) collective-permute-start(bf16[256,512]{1,0:T(8,128)(2,1)S(1)} %get-tuple-element.43.refs_2_), channel_id=1, source_target_pairs={{0,14},{2,0},{4,2},{6,4},{8,6},{10,8},{12,10},{14,12},{16,18},{18,... | collective-permute-start | bytes 786440 | tf_op jit(solution)/shard_map/ppermute | solution.py:47
  4.3 14.1 %collective-permute-start.1 = (bf16[256,512]{1,0:T(8,128)(2,1)S(1)}, bf16[256,512]{1,0:T(8,128)(2,1)S(1)}, u32[]{:S(2)}, u32[]{:S(2)}) collective-permute-start(bf16[256,512]{1,0:T(8,128)(2,1)S(1)} %get-tuple-element.43.refs_2_), channel_id=1, source_target_pairs={{0,4},{2,6},{4,8},{6,10},{8,12},{10,14},{12,0},{14,2},{16,28},{18,... | collective-permute-start | bytes 786440 | tf_op jit(solution)/shard_map/ppermute | solution.py:47
  9.4 1.4 %collective-permute-start = (f32[1,512]{1,0:T(1,128)}, f32[1,512]{1,0:T(1,128)S(1)}, u32[]{:S(2)}, u32[]{:S(2)}) collective-permute-start(f32[1,512]{1,0:T(1,128)} %bitcast.5), channel_id=1, source_target_pairs={{0,16},{16,0},{1,17},{17,1},{2,18},{18,2},{3,19},{19,3},{4,20},{20... | collective-permute-start | bytes 6152 | tf_op jit(solution)/shard_map/ppermute | solution.py:51
  10.8 0.7 %copy-start = (f32[512]{0:T(512)S(1)}, f32[512]{0:T(512)}, u32[]{:S(2)}) copy-start(f32[512]{0:T(512)} %param.11) | copy-start | bytes 6148
  11.4 4.7 %collective-permute-start.2 = (f32[1,1024]{1,0:T(1,128)S(1)}, f32[1,1024]{1,0:T(1,128)S(1)}, u32[]{:S(2)}, u32[]{:S(2)}) collective-permute-start(f32[1,1024]{1,0:T(1,128)S(1)} %join.1.refs_3_), channel_id=1, source_target_pairs={{0,33},{1,32},{32,0},{33,1},{2,35},{3,34},{34,2},{35,3},{4,37},{5,... | collective-permute-start | bytes 12296 | tf_op jit(solution)/shard_map/ppermute | solution.py:41
  13.9 4.3 %collective-permute-start.3 = (f32[1,1024]{1,0:T(1,128)S(1)}, f32[1,1024]{1,0:T(1,128)S(1)}, u32[]{:S(2)}, u32[]{:S(2)}) collective-permute-start(f32[1,1024]{1,0:T(1,128)S(1)} %join.1.refs_3_), channel_id=1, source_target_pairs={{0,1},{1,0},{32,33},{33,32},{2,3},{3,2},{34,35},{35,34},{4,5},{5,4... | collective-permute-start | bytes 12296 | tf_op jit(solution)/shard_map/ppermute | solution.py:41
  14.4 4.0 %collective-permute-start.4 = (f32[1,1024]{1,0:T(1,128)S(1)}, f32[1,1024]{1,0:T(1,128)S(1)}, u32[]{:S(2)}, u32[]{:S(2)}) collective-permute-start(f32[1,1024]{1,0:T(1,128)S(1)} %join.1.refs_3_), channel_id=1, source_target_pairs={{0,32},{1,33},{32,1},{33,0},{2,34},{3,35},{34,3},{35,2},{4,36},{5,... | collective-permute-start | bytes 12296 | tf_op jit(solution)/shard_map/ppermute | solution.py:41
  18.4 6.4 %collective-permute-start.9 = (bf16[256,512]{1,0:T(8,128)(2,1)S(1)}, bf16[256,512]{1,0:T(8,128)(2,1)S(1)}, u32[]{:S(2)}, u32[]{:S(2)}) collective-permute-start(bf16[256,512]{1,0:T(8,128)(2,1)S(1)} %collective-permute-done.8.refs_4_), channel_id=1, source_target_pairs={{0,14},{2,0},{4,2},{6,4},{8,6},{10,8},{12,10},{14,12},{16,18},{18,... | collective-permute-start | bytes 786440 | tf_op jit(solution)/shard_map/ppermute | solution.py:47
  18.4 7.9 %collective-permute-start.5 = (bf16[256,512]{1,0:T(8,128)(2,1)S(1)}, bf16[256,512]{1,0:T(8,128)(2,1)S(1)}, u32[]{:S(2)}, u32[]{:S(2)}) collective-permute-start(bf16[256,512]{1,0:T(8,128)(2,1)S(1)} %collective-permute-done.1.refs_5_), channel_id=1, source_target_pairs={{0,2},{2,4},{4,6},{6,8},{8,10},{10,12},{12,14},{14,0},{16,30},{18,... | collective-permute-start | bytes 786440 | tf_op jit(solution)/shard_map/ppermute | solution.py:47
  21.1 8.9 %collective-permute-start.11 = (bf16[256,512]{1,0:T(8,128)(2,1)S(1)}, bf16[256,512]{1,0:T(8,128)(2,1)S(1)}, u32[]{:S(2)}, u32[]{:S(2)}) collective-permute-start(bf16[256,512]{1,0:T(8,128)(2,1)S(1)} %get-tuple-element.43.refs_2_), channel_id=1, source_target_pairs={{0,2},{2,4},{4,6},{6,8},{8,10},{10,12},{12,14},{14,0},{16,30},{18,... | collective-permute-start | bytes 786440 | tf_op jit(solution)/shard_map/ppermute | solution.py:47
  24.8 9.6 %collective-permute-start.10 = (bf16[256,512]{1,0:T(8,128)(2,1)S(1)}, bf16[256,512]{1,0:T(8,128)(2,1)S(1)}, u32[]{:S(2)}, u32[]{:S(2)}) collective-permute-start(bf16[256,512]{1,0:T(8,128)(2,1)S(1)} %collective-permute-done.9.refs_2_), channel_id=1, source_target_pairs={{0,14},{2,0},{4,2},{6,4},{8,6},{10,8},{12,10},{14,12},{16,18},{18,... | collective-permute-start | bytes 786440 | tf_op jit(solution)/shard_map/ppermute | solution.py:47
  26.4 13.6 %collective-permute-start.6 = (bf16[256,512]{1,0:T(8,128)(2,1)S(1)}, bf16[256,512]{1,0:T(8,128)(2,1)S(1)}, u32[]{:S(2)}, u32[]{:S(2)}) collective-permute-start(bf16[256,512]{1,0:T(8,128)(2,1)S(1)} %collective-permute-done.5.refs_3_), channel_id=1, source_target_pairs={{0,2},{2,4},{4,6},{6,8},{8,10},{10,12},{12,14},{14,0},{16,30},{18,... | collective-permute-start | bytes 786440 | tf_op jit(solution)/shard_map/ppermute | solution.py:47
  35.2 8.1 %collective-permute-start.12 = (bf16[1024,512]{1,0:T(8,128)(2,1)S(1)}, bf16[1024,512]{1,0:T(8,128)(2,1)S(1)}, u32[]{:S(2)}, u32[]{:S(2)}) collective-permute-start(bf16[1024,512]{1,0:T(8,128)(2,1)S(1)} %get-tuple-element.49), channel_id=1, source_target_pairs={{0,16},{16,0},{1,17},{17,1},{2,18},{18,2},{3,19},{19,3},{4,20},{20... | collective-permute-start | bytes 3145736 | tf_op jit(solution)/shard_map/ppermute | solution.py:51
  40.0 3.3 %collective-permute-start.7 = (bf16[256,512]{1,0:T(8,128)(2,1)S(1)}, bf16[256,512]{1,0:T(8,128)(2,1)S(1)}, u32[]{:S(2)}, u32[]{:S(2)}) collective-permute-start(bf16[256,512]{1,0:T(8,128)(2,1)S(1)} %collective-permute-done.6.x_ref), channel_id=1, source_target_pairs={{0,16},{16,0},{1,17},{17,1},{2,18},{18,2},{3,19},{19,3},{4,20},{20... | collective-permute-start | bytes 786440 | tf_op jit(solution)/shard_map/ppermute | solution.py:51
  42.6 6.5 %copy-start.1 = (f32[512]{0:T(512)S(1)}, f32[512]{0:T(512)}, u32[]{:S(2)}) copy-start(f32[512]{0:T(512)} %param.11) | copy-start | bytes 6148
  42.6 16.6 %copy-start.2 = (s32[64]{0:T(128)S(1)}, s32[64]{0:T(128)}, u32[]{:S(2)}) copy-start(s32[64]{0:T(128)} %counts_ref.1) | copy-start | bytes 772
  43.7 9.1 %collective-permute-start.13 = (bf16[256,512]{1,0:T(8,128)(2,1)S(1)}, bf16[256,512]{1,0:T(8,128)(2,1)S(1)}, u32[]{:S(2)}, u32[]{:S(2)}) collective-permute-start(bf16[256,512]{1,0:T(8,128)(2,1)S(1)} %get-tuple-element.51), channel_id=1, source_target_pairs={{0,1},{1,0},{32,33},{33,32},{2,3},{3,2},{34,35},{35,34},{4,5},{5,4... | collective-permute-start | bytes 786440 | tf_op jit(solution)/shard_map/ppermute | solution.py:41
  46.4 12.8 %collective-permute-start.14 = (bf16[256,512]{1,0:T(8,128)(2,1)S(1)}, bf16[256,512]{1,0:T(8,128)(2,1)S(1)}, u32[]{:S(2)}, u32[]{:S(2)}) collective-permute-start(bf16[256,512]{1,0:T(8,128)(2,1)S(1)} %get-tuple-element.52), channel_id=1, source_target_pairs={{0,32},{1,33},{32,1},{33,0},{2,34},{3,35},{34,3},{35,2},{4,36},{5,... | collective-permute-start | bytes 786440 | tf_op jit(solution)/shard_map/ppermute | solution.py:41
  46.7 12.5 %collective-permute-start.15 = (bf16[256,512]{1,0:T(8,128)(2,1)S(1)}, bf16[256,512]{1,0:T(8,128)(2,1)S(1)}, u32[]{:S(2)}, u32[]{:S(2)}) collective-permute-start(bf16[256,512]{1,0:T(8,128)(2,1)S(1)} %get-tuple-element.53), channel_id=1, source_target_pairs={{0,33},{1,32},{32,0},{33,1},{2,35},{3,34},{34,2},{35,3},{4,37},{5,... | collective-permute-start | bytes 786440 | tf_op jit(solution)/shard_map/ppermute | solution.py:41

commit v9 on v8

--- a/solution.py
+++ b/solution.py
@@ -13,7 +13,7 @@
 ZS = 8
 XS = 4
 TILE = 128
-AWAY = (0, 1, -1, 2, -2, 3, -3, 4, 4)
+AWAY = (0, -1, 2, 1, -2, 3, -3, 4, 4)
 OTHER = range(7)
 MINE = range(9)
 
@@ -358,10 +358,10 @@
     p5 = around(hold(p3, *far), 1)
     c_other = cauchy(1, OTHER, me, table, factors, [hold(near, p3), *far])
     c_mine = cauchy(0, MINE, me, table, factors, [hold(near, c_other), *far])
-    p6 = around(hold(p4, c_other), -1)
-    p7 = around(hold(p5, c_mine), 1)
-    sums = stage(0, c_mine, c_other, (hold(own, p5), p1, p2, p3), (), False)
-    sums = stage(4, c_mine, c_other, (p4, p5), sums, False)
+    p6 = around(hold(p4, c_mine), -1)
+    sums = stage(0, c_mine, c_other, (own, p2, p3), (), False)
+    p7 = around(hold(p5, sums[0]), 1)
+    sums = stage(3, c_mine, c_other, (p1, p4, p5), sums, False)
     mine, other = stage(6, c_mine, c_other, (p6,), sums, True)
     other = cshift(other)
     sibling = cshift(p7)

time: 60.9 us -> 61.2 us (level)
  starting transfers between devices: 30.9 us -> 31.9 us
  waiting for transfers between devices: 13.4 us -> 12.7 us
    ppermute x6, waiting for transfers between devices: 8.99 us -> 7.24 us  [xshift(): return lax.ppermute(a, ('xl', 'xh'), pairs)]
    ppermute x6, starting transfers between devices: 8.95 us -> 10.1 us  [xshift(): return lax.ppermute(a, ('xl', 'xh'), pairs)]
    ppermute x7, waiting for transfers between devices: 2.36 us -> 3.42 us  [around(): return lax.ppermute(a, ('core', 'z'), up + down)]
  transfers between devices with their start and end apart: 16 -> 16, of which waited for: 9 -> 7; matrix products, arithmetic and copies ran while one was open for 0% -> 0% of each run, Pallas kernels for 20% -> 19%
where the time goes in v9:
time: 61.2 us; the launch traced here: 61.1 us
  starting transfers between devices  31.9 us (52%)
  Pallas kernels  15.5 us (25%)
  waiting for transfers between devices  12.7 us (21%)
  local copies, waits for them, and re-layouts  0.69 us (1%)
    ppermute x7, starting transfers between devices, around(): return lax.ppermute(a, ('core', 'z'), up + down)  15 us
    ppermute x6, starting transfers between devices, xshift(): return lax.ppermute(a, ('xl', 'xh'), pairs)  10.1 us
    ppermute x6, waiting for transfers between devices, xshift(): return lax.ppermute(a, ('xl', 'xh'), pairs)  7.24 us
    ppermute x3, starting transfers between devices, cshift(): return lax.ppermute(a, 'core', [(0, 1), (1, 0)])  6.69 us
    pallas_call x3, Pallas kernels, stage(): pl.pallas_call(lambda *refs: stage_kernel(first, len(pieces), *refs), in_...  4.34 us
    ppermute x7, waiting for transfers between devices, around(): return lax.ppermute(a, ('core', 'z'), up + down)  3.42 us
    pallas_call x1, Pallas kernels, norms(): pl.pallas_call(norm_kernel, in_specs=[VM] * 4, out_specs=[VM, HB], out_sh...  3.38 us
    pallas_call x2, Pallas kernels, cauchy(): pl.pallas_call(lambda *refs: cauchy_kernel(fc, pieces, *refs), in_specs=[...  2.7 us
  transfers between devices with their start and end apart: 16, of which 7 were waited for; matrix products, arithmetic and copies ran while one was open for 0% of the time, Pallas kernels for 19%

profile of v9, /device:TPU:1, one launch (start us, length us, event | category | flops | bytes accessed | tf_op | source)
XLA Modules:
  0.0 61.1 jit_solution(1735585977986882946)
XLA Ops:
  0.0 1.7 %permute.1 = (bf16[256,512]{1,0:T(8,128)(2,1)S(1)}, bf16[512,256]{1,0:T(8,128)(2,1)S(1)}, bf16[512,256]{1,0:T(8,128)(2,1)S(1)}) custom-call(bf16[512,512]{1,0:T(8,128)(2,1)} %e_hbm.1, s32[1,512]{1,0:T(1,128)} %bitcast.10), custom_call_target="tpu_custom_call" | custom-call | flops 1 | bytes 1 | tf_op jit(solution)/shard_map/permute/pallas_call | solution.py:86
  1.7 2.5 %collective-permute-start.6 = (bf16[256,512]{1,0:T(8,128)(2,1)S(1)}, bf16[256,512]{1,0:T(8,128)(2,1)S(1)}, u32[]{:S(2)}, u32[]{:S(2)}) collective-permute-start(bf16[256,512]{1,0:T(8,128)(2,1)S(1)} %get-tuple-element.31.refs_2_), channel_id=1, source_target_pairs={{0,14},{2,0},{4,2},{6,4},{8,6},{10,8},{12,10},{14,12},{16,18},{18,... | collective-permute-start | bytes 786440 | tf_op jit(solution)/shard_map/ppermute | solution.py:47
  4.3 5.1 %collective-permute-start.1 = (bf16[256,512]{1,0:T(8,128)(2,1)S(1)}, bf16[256,512]{1,0:T(8,128)(2,1)S(1)}, u32[]{:S(2)}, u32[]{:S(2)}) collective-permute-start(bf16[256,512]{1,0:T(8,128)(2,1)S(1)} %get-tuple-element.31.refs_2_), channel_id=1, source_target_pairs={{0,4},{2,6},{4,8},{6,10},{8,12},{10,14},{12,0},{14,2},{16,28},{18,... | collective-permute-start | bytes 786440 | tf_op jit(solution)/shard_map/ppermute | solution.py:47
  9.4 1.4 %collective-permute-done.b_ref = f32[1,512]{1,0:T(1,128)S(1)} collective-permute-done((f32[1,512]{1,0:T(1,128)}, f32[1,512]{1,0:T(1,128)S(1)}, u32[]{:S(2)}, u32[]{:S(2)}) %collective-permute-start) | collective-permute-done | bytes 2080 | tf_op jit(solution)/shard_map/ppermute | solution.py:51
  11.4 1.2 %collective-permute-start.4 = (f32[1,1024]{1,0:T(1,128)S(1)}, f32[1,1024]{1,0:T(1,128)S(1)}, u32[]{:S(2)}, u32[]{:S(2)}) collective-permute-start(f32[1,1024]{1,0:T(1,128)S(1)} %join.1.refs_3_), channel_id=1, source_target_pairs={{0,32},{1,33},{32,1},{33,0},{2,34},{3,35},{34,3},{35,2},{4,36},{5,... | collective-permute-start | bytes 12296 | tf_op jit(solution)/shard_map/ppermute | solution.py:41
  12.7 2.5 %collective-permute-start.3 = (f32[1,1024]{1,0:T(1,128)S(1)}, f32[1,1024]{1,0:T(1,128)S(1)}, u32[]{:S(2)}, u32[]{:S(2)}) collective-permute-start(f32[1,1024]{1,0:T(1,128)S(1)} %join.1.refs_3_), channel_id=1, source_target_pairs={{0,1},{1,0},{32,33},{33,32},{2,3},{3,2},{34,35},{35,34},{4,5},{5,4... | collective-permute-start | bytes 12296 | tf_op jit(solution)/shard_map/ppermute | solution.py:41
  15.1 1.2 %collective-permute-start.2 = (f32[1,1024]{1,0:T(1,128)S(1)}, f32[1,1024]{1,0:T(1,128)S(1)}, u32[]{:S(2)}, u32[]{:S(2)}) collective-permute-start(f32[1,1024]{1,0:T(1,128)S(1)} %join.1.refs_3_), channel_id=1, source_target_pairs={{0,33},{1,32},{32,0},{33,1},{2,35},{3,34},{34,2},{35,3},{4,37},{5,... | collective-permute-start | bytes 12296 | tf_op jit(solution)/shard_map/ppermute | solution.py:41
  16.3 1.1 %tables.1 = (f32[128,128]{1,0:T(8,128)S(1)}, f32[128,128]{1,0:T(8,128)S(1)}) custom-call(s32[64]{0:T(128)} %counts_ref.1, f32[256,128]{1,0:T(8,128)} %bitcast.8, f32[256,128]{1,0:T(8,128)} %bitcast.9), custom_call_target="tpu_custom_call" | custom-call | flops 1 | bytes 1 | tf_op jit(solution)/shard_map/tables/pallas_call | solution.py:128
  18.3 2.2 %collective-permute-start.5 = (bf16[256,512]{1,0:T(8,128)(2,1)S(1)}, bf16[256,512]{1,0:T(8,128)(2,1)S(1)}, u32[]{:S(2)}, u32[]{:S(2)}) collective-permute-start(bf16[256,512]{1,0:T(8,128)(2,1)S(1)} %collective-permute-done.1.refs_4_), channel_id=1, source_target_pairs={{0,2},{2,4},{4,6},{6,8},{8,10},{10,12},{12,14},{14,0},{16,30},{18,... | collective-permute-start | bytes 786440 | tf_op jit(solution)/shard_map/ppermute | solution.py:47
  20.5 2.0 %collective-permute-start.11 = (bf16[256,512]{1,0:T(8,128)(2,1)S(1)}, bf16[256,512]{1,0:T(8,128)(2,1)S(1)}, u32[]{:S(2)}, u32[]{:S(2)}) collective-permute-start(bf16[256,512]{1,0:T(8,128)(2,1)S(1)} %get-tuple-element.31.refs_2_), channel_id=1, source_target_pairs={{0,2},{2,4},{4,6},{6,8},{8,10},{10,12},{12,14},{14,0},{16,30},{18,... | collective-permute-start | bytes 786440 | tf_op jit(solution)/shard_map/ppermute | solution.py:47
  22.6 1.2 %cauchy.2.refs_1_ = bf16[1024,1792]{1,0:T(8,128)(2,1)S(1)} custom-call(s32[1]{0:T(128)} %bitcast.refs_0_.me_ref, f32[128,128]{1,0:T(8,128)S(1)} %get-tuple-element.34.refs_1_.poles_ref, f32[128,128]{1,0:T(8,128)S(1)} %get-tuple-element.35.refs_2_.factors_ref, f32[1,1024]{1,0:T(1,128)S(1)} %join.1.refs_3_, f32[1,1024]{1,0:T(1,128)S(1)} %collective-permute-done.2.refs_4_, ...), custom_call_target="tpu_custom_call" | custom-call | flops 1 | bytes 1 | tf_op jit(solution)/shard_map/cauchy/pallas_call | solution.py:185
  23.8 1.5 %cauchy.3.refs_0_.c_ref = bf16[1024,2304]{1,0:T(8,128)(2,1)S(1)} custom-call(s32[1]{0:T(128)} %bitcast.refs_0_.me_ref, f32[128,128]{1,0:T(8,128)S(1)} %get-tuple-element.34.refs_1_.poles_ref, f32[128,128]{1,0:T(8,128)S(1)} %get-tuple-element.35.refs_2_.factors_ref, f32[1,1024]{1,0:T(1,128)S(1)} %join.1.refs_3_, ...), custom_call_target="tpu_custom_call" | custom-call | flops 1 | bytes 1 | tf_op jit(solution)/shard_map/cauchy/pallas_call | solution.py:185
  25.4 1.8 %stage.3 = (f32[1024,512]{1,0:T(8,128)S(1)}, f32[1024,512]{1,0:T(8,128)S(1)}) custom-call(bf16[1024,2304]{1,0:T(8,128)(2,1)S(1)} %cauchy.3.refs_0_.c_ref, bf16[1024,1792]{1,0:T(8,128)(2,1)S(1)} %cauchy.2.refs_1_, bf16[256,512]{1,0:T(8,128)(2,1)S(1)} %get-tuple-element.31.refs_2_, bf16[256,512]{1,0:T(8,128)(2,1)S(1)} %collective-permute-done.6.refs_3_, ...), custom_call_target="tpu_custom_call" | custom-call | flops 1 | bytes 1 | tf_op jit(solution)/shard_map/stage/pallas_call | solution.py:257
  27.2 2.9 %collective-permute-start.7 = (bf16[256,512]{1,0:T(8,128)(2,1)S(1)}, bf16[256,512]{1,0:T(8,128)(2,1)S(1)}, u32[]{:S(2)}, u32[]{:S(2)}) collective-permute-start(bf16[256,512]{1,0:T(8,128)(2,1)S(1)} %collective-permute-done.5.refs_4_), channel_id=1, source_target_pairs={{0,2},{2,4},{4,6},{6,8},{8,10},{10,12},{12,14},{14,0},{16,30},{18,... | collective-permute-start | bytes 786440 | tf_op jit(solution)/shard_map/ppermute | solution.py:47
  30.1 1.8 %stage.4 = (f32[1024,512]{1,0:T(8,128)S(1)}, f32[1024,512]{1,0:T(8,128)S(1)}) custom-call(bf16[1024,2304]{1,0:T(8,128)(2,1)S(1)} %cauchy.3.refs_0_.c_ref, bf16[1024,1792]{1,0:T(8,128)(2,1)S(1)} %cauchy.2.refs_1_, bf16[256,512]{1,0:T(8,128)(2,1)S(1)} %collective-permute-done.11.refs_2_, bf16[256,512]{1,0:T(8,128)(2,1)S(1)} %collective-permute-done.9.refs_3_, ...), custom_call_target="tpu_custom_call" | custom-call | flops 1 | bytes 1 | tf_op jit(solution)/shard_map/stage/pallas_call | solution.py:257
  31.9 3.1 %collective-permute-done.10.refs_2_ = bf16[256,512]{1,0:T(8,128)(2,1)S(1)} collective-permute-done((bf16[256,512]{1,0:T(8,128)(2,1)S(1)}, bf16[256,512]{1,0:T(8,128)(2,1)S(1)}, u32[]{:S(2)}, u32[]{:S(2)}) %collective-permute-start.10) | collective-permute-done | bytes 262176 | tf_op jit(solution)/shard_map/ppermute | solution.py:47
  35.0 0.8 %stage.5 = (f32[1024,512]{1,0:T(8,128)S(1)}, bf16[1024,512]{1,0:T(8,128)(2,1)S(1)}) custom-call(bf16[1024,2304]{1,0:T(8,128)(2,1)S(1)} %cauchy.3.refs_0_.c_ref, bf16[1024,1792]{1,0:T(8,128)(2,1)S(1)} %cauchy.2.refs_1_, bf16[256,512]{1,0:T(8,128)(2,1)S(1)} %collective-permute-done.10.refs_2_, f32[1024,512]{1,0:T(8,128)S(1)} %get-tuple-element.44.refs_3_, ...), custom_call_target="tpu_custom_call" | custom-call | flops 1 | bytes 1 | tf_op jit(solution)/shard_map/stage/pallas_call | solution.py:257
  35.7 2.5 %collective-permute-start.12 = (bf16[1024,512]{1,0:T(8,128)(2,1)S(1)}, bf16[1024,512]{1,0:T(8,128)(2,1)S(1)}, u32[]{:S(2)}, u32[]{:S(2)}) collective-permute-start(bf16[1024,512]{1,0:T(8,128)(2,1)S(1)} %get-tuple-element.47), channel_id=1, source_target_pairs={{0,16},{16,0},{1,17},{17,1},{2,18},{18,2},{3,19},{19,3},{4,20},{20... | collective-permute-start | bytes 3145736 | tf_op jit(solution)/shard_map/ppermute | solution.py:51
  38.2 4.2 %collective-permute-start.8 = (bf16[256,512]{1,0:T(8,128)(2,1)S(1)}, bf16[256,512]{1,0:T(8,128)(2,1)S(1)}, u32[]{:S(2)}, u32[]{:S(2)}) collective-permute-start(bf16[256,512]{1,0:T(8,128)(2,1)S(1)} %collective-permute-done.7.x_ref), channel_id=1, source_target_pairs={{0,16},{16,0},{1,17},{17,1},{2,18},{18,2},{3,19},{19,3},{4,20},{20... | collective-permute-start | bytes 786440 | tf_op jit(solution)/shard_map/ppermute | solution.py:51
  44.0 2.7 %collective-permute-start.13 = (bf16[256,512]{1,0:T(8,128)(2,1)S(1)}, bf16[256,512]{1,0:T(8,128)(2,1)S(1)}, u32[]{:S(2)}, u32[]{:S(2)}) collective-permute-start(bf16[256,512]{1,0:T(8,128)(2,1)S(1)} %get-tuple-element.49), channel_id=1, source_target_pairs={{0,1},{1,0},{32,33},{33,32},{2,3},{3,2},{34,35},{35,34},{4,5},{5,4... | collective-permute-start | bytes 786440 | tf_op jit(solution)/shard_map/ppermute | solution.py:41
  47.1 2.2 %collective-permute-start.15 = (bf16[256,512]{1,0:T(8,128)(2,1)S(1)}, bf16[256,512]{1,0:T(8,128)(2,1)S(1)}, u32[]{:S(2)}, u32[]{:S(2)}) collective-permute-start(bf16[256,512]{1,0:T(8,128)(2,1)S(1)} %get-tuple-element.51), channel_id=1, source_target_pairs={{0,33},{1,32},{32,0},{33,1},{2,35},{3,34},{34,2},{35,3},{4,37},{5,... | collective-permute-start | bytes 786440 | tf_op jit(solution)/shard_map/ppermute | solution.py:41
  49.4 3.4 %norms.1 = (f32[256,128]{1,0:T(8,128)S(1)}, bf16[512,512]{1,0:T(8,128)(2,1)}) custom-call(f32[128,128]{1,0:T(8,128)S(1)} %get-tuple-element.34.refs_1_.poles_ref, f32[128,128]{1,0:T(8,128)S(1)} %get-tuple-element.35.refs_2_.factors_ref, f32[1,512]{1,0:T(1,128)S(1)} %bitcast.7, bf16[512,256]{1,0:T(8,128)(2,1)S(1)} %get-tuple-element.53.rest_ref), custom_call_target="tpu_custom_call" | custom-call | flops 1 | bytes 1 | tf_op jit(solution)/shard_map/norms/pallas_call | solution.py:218
  53.2 6.3 %collective-permute-done.14.b_ref = bf16[256,512]{1,0:T(8,128)(2,1)S(1)} collective-permute-done((bf16[256,512]{1,0:T(8,128)(2,1)S(1)}, bf16[256,512]{1,0:T(8,128)(2,1)S(1)}, u32[]{:S(2)}, u32[]{:S(2)}) %collective-permute-start.14) | collective-permute-done | bytes 262176 | tf_op jit(solution)/shard_map/ppermute | solution.py:41
  59.5 1.5 %finish.1 = bf16[512,512]{1,0:T(8,128)(2,1)} custom-call(s32[1]{0:T(128)} %bitcast.refs_0_.me_ref, s32[64]{0:T(128)S(1)} %copy-done.2, f32[256,512]{1,0:T(8,128)S(1)} %get-tuple-element.48.own_ref, bf16[256,512]{1,0:T(8,128)(2,1)S(1)} %collective-permute-done.13.a_ref, ...), custom_call_target="tpu_custom_call", output_to_operand_aliasing={{}: (8, {})} | custom-call | flops 1 | bytes 1 | tf_op jit(solution)/shard_map/finish/pallas_call | solution.py:330
  (26 shorter events, 4.2 us)
Async XLA Ops:
  1.7 16.1 %collective-permute-start.6 = (bf16[256,512]{1,0:T(8,128)(2,1)S(1)}, bf16[256,512]{1,0:T(8,128)(2,1)S(1)}, u32[]{:S(2)}, u32[]{:S(2)}) collective-permute-start(bf16[256,512]{1,0:T(8,128)(2,1)S(1)} %get-tuple-element.31.refs_2_), channel_id=1, source_target_pairs={{0,14},{2,0},{4,2},{6,4},{8,6},{10,8},{12,10},{14,12},{16,18},{18,... | collective-permute-start | bytes 786440 | tf_op jit(solution)/shard_map/ppermute | solution.py:47
  4.3 14.0 %collective-permute-start.1 = (bf16[256,512]{1,0:T(8,128)(2,1)S(1)}, bf16[256,512]{1,0:T(8,128)(2,1)S(1)}, u32[]{:S(2)}, u32[]{:S(2)}) collective-permute-start(bf16[256,512]{1,0:T(8,128)(2,1)S(1)} %get-tuple-element.31.refs_2_), channel_id=1, source_target_pairs={{0,4},{2,6},{4,8},{6,10},{8,12},{10,14},{12,0},{14,2},{16,28},{18,... | collective-permute-start | bytes 786440 | tf_op jit(solution)/shard_map/ppermute | solution.py:47
  9.4 1.4 %collective-permute-start = (f32[1,512]{1,0:T(1,128)}, f32[1,512]{1,0:T(1,128)S(1)}, u32[]{:S(2)}, u32[]{:S(2)}) collective-permute-start(f32[1,512]{1,0:T(1,128)} %bitcast.5), channel_id=1, source_target_pairs={{0,16},{16,0},{1,17},{17,1},{2,18},{18,2},{3,19},{19,3},{4,20},{20... | collective-permute-start | bytes 6152 | tf_op jit(solution)/shard_map/ppermute | solution.py:51
  10.8 0.7 %copy-start = (f32[512]{0:T(512)S(1)}, f32[512]{0:T(512)}, u32[]{:S(2)}) copy-start(f32[512]{0:T(512)} %param.11) | copy-start | bytes 6148
  11.4 5.9 %collective-permute-start.4 = (f32[1,1024]{1,0:T(1,128)S(1)}, f32[1,1024]{1,0:T(1,128)S(1)}, u32[]{:S(2)}, u32[]{:S(2)}) collective-permute-start(f32[1,1024]{1,0:T(1,128)S(1)} %join.1.refs_3_), channel_id=1, source_target_pairs={{0,32},{1,33},{32,1},{33,0},{2,34},{3,35},{34,3},{35,2},{4,36},{5,... | collective-permute-start | bytes 12296 | tf_op jit(solution)/shard_map/ppermute | solution.py:41
  12.7 4.7 %collective-permute-start.3 = (f32[1,1024]{1,0:T(1,128)S(1)}, f32[1,1024]{1,0:T(1,128)S(1)}, u32[]{:S(2)}, u32[]{:S(2)}) collective-permute-start(f32[1,1024]{1,0:T(1,128)S(1)} %join.1.refs_3_), channel_id=1, source_target_pairs={{0,1},{1,0},{32,33},{33,32},{2,3},{3,2},{34,35},{35,34},{4,5},{5,4... | collective-permute-start | bytes 12296 | tf_op jit(solution)/shard_map/ppermute | solution.py:41
  15.1 2.8 %collective-permute-start.2 = (f32[1,1024]{1,0:T(1,128)S(1)}, f32[1,1024]{1,0:T(1,128)S(1)}, u32[]{:S(2)}, u32[]{:S(2)}) collective-permute-start(f32[1,1024]{1,0:T(1,128)S(1)} %join.1.refs_3_), channel_id=1, source_target_pairs={{0,33},{1,32},{32,0},{33,1},{2,35},{3,34},{34,2},{35,3},{4,37},{5,... | collective-permute-start | bytes 12296 | tf_op jit(solution)/shard_map/ppermute | solution.py:41
  17.9 7.4 %collective-permute-start.9 = (bf16[256,512]{1,0:T(8,128)(2,1)S(1)}, bf16[256,512]{1,0:T(8,128)(2,1)S(1)}, u32[]{:S(2)}, u32[]{:S(2)}) collective-permute-start(bf16[256,512]{1,0:T(8,128)(2,1)S(1)} %collective-permute-done.6.refs_3_), channel_id=1, source_target_pairs={{0,14},{2,0},{4,2},{6,4},{8,6},{10,8},{12,10},{14,12},{16,18},{18,... | collective-permute-start | bytes 786440 | tf_op jit(solution)/shard_map/ppermute | solution.py:47
  18.3 8.9 %collective-permute-start.5 = (bf16[256,512]{1,0:T(8,128)(2,1)S(1)}, bf16[256,512]{1,0:T(8,128)(2,1)S(1)}, u32[]{:S(2)}, u32[]{:S(2)}) collective-permute-start(bf16[256,512]{1,0:T(8,128)(2,1)S(1)} %collective-permute-done.1.refs_4_), channel_id=1, source_target_pairs={{0,2},{2,4},{4,6},{6,8},{8,10},{10,12},{12,14},{14,0},{16,30},{18,... | collective-permute-start | bytes 786440 | tf_op jit(solution)/shard_map/ppermute | solution.py:47
  20.5 9.6 %collective-permute-start.11 = (bf16[256,512]{1,0:T(8,128)(2,1)S(1)}, bf16[256,512]{1,0:T(8,128)(2,1)S(1)}, u32[]{:S(2)}, u32[]{:S(2)}) collective-permute-start(bf16[256,512]{1,0:T(8,128)(2,1)S(1)} %get-tuple-element.31.refs_2_), channel_id=1, source_target_pairs={{0,2},{2,4},{4,6},{6,8},{8,10},{10,12},{12,14},{14,0},{16,30},{18,... | collective-permute-start | bytes 786440 | tf_op jit(solution)/shard_map/ppermute | solution.py:47
  25.3 9.7 %collective-permute-start.10 = (bf16[256,512]{1,0:T(8,128)(2,1)S(1)}, bf16[256,512]{1,0:T(8,128)(2,1)S(1)}, u32[]{:S(2)}, u32[]{:S(2)}) collective-permute-start(bf16[256,512]{1,0:T(8,128)(2,1)S(1)} %collective-permute-done.9.refs_3_), channel_id=1, source_target_pairs={{0,14},{2,0},{4,2},{6,4},{8,6},{10,8},{12,10},{14,12},{16,18},{18,... | collective-permute-start | bytes 786440 | tf_op jit(solution)/shard_map/ppermute | solution.py:47
  27.2 11.0 %collective-permute-start.7 = (bf16[256,512]{1,0:T(8,128)(2,1)S(1)}, bf16[256,512]{1,0:T(8,128)(2,1)S(1)}, u32[]{:S(2)}, u32[]{:S(2)}) collective-permute-start(bf16[256,512]{1,0:T(8,128)(2,1)S(1)} %collective-permute-done.5.refs_4_), channel_id=1, source_target_pairs={{0,2},{2,4},{4,6},{6,8},{8,10},{10,12},{12,14},{14,0},{16,30},{18,... | collective-permute-start | bytes 786440 | tf_op jit(solution)/shard_map/ppermute | solution.py:47
  35.7 7.9 %collective-permute-start.12 = (bf16[1024,512]{1,0:T(8,128)(2,1)S(1)}, bf16[1024,512]{1,0:T(8,128)(2,1)S(1)}, u32[]{:S(2)}, u32[]{:S(2)}) collective-permute-start(bf16[1024,512]{1,0:T(8,128)(2,1)S(1)} %get-tuple-element.47), channel_id=1, source_target_pairs={{0,16},{16,0},{1,17},{17,1},{2,18},{18,2},{3,19},{19,3},{4,20},{20... | collective-permute-start | bytes 3145736 | tf_op jit(solution)/shard_map/ppermute | solution.py:51
  38.2 5.4 %collective-permute-start.8 = (bf16[256,512]{1,0:T(8,128)(2,1)S(1)}, bf16[256,512]{1,0:T(8,128)(2,1)S(1)}, u32[]{:S(2)}, u32[]{:S(2)}) collective-permute-start(bf16[256,512]{1,0:T(8,128)(2,1)S(1)} %collective-permute-done.7.x_ref), channel_id=1, source_target_pairs={{0,16},{16,0},{1,17},{17,1},{2,18},{18,2},{3,19},{19,3},{4,20},{20... | collective-permute-start | bytes 786440 | tf_op jit(solution)/shard_map/ppermute | solution.py:51
  42.9 6.5 %copy-start.1 = (f32[512]{0:T(512)S(1)}, f32[512]{0:T(512)}, u32[]{:S(2)}) copy-start(f32[512]{0:T(512)} %param.11) | copy-start | bytes 6148
  42.9 16.6 %copy-start.2 = (s32[64]{0:T(128)S(1)}, s32[64]{0:T(128)}, u32[]{:S(2)}) copy-start(s32[64]{0:T(128)} %counts_ref.1) | copy-start | bytes 772
  44.0 9.2 %collective-permute-start.13 = (bf16[256,512]{1,0:T(8,128)(2,1)S(1)}, bf16[256,512]{1,0:T(8,128)(2,1)S(1)}, u32[]{:S(2)}, u32[]{:S(2)}) collective-permute-start(bf16[256,512]{1,0:T(8,128)(2,1)S(1)} %get-tuple-element.49), channel_id=1, source_target_pairs={{0,1},{1,0},{32,33},{33,32},{2,3},{3,2},{34,35},{35,34},{4,5},{5,4... | collective-permute-start | bytes 786440 | tf_op jit(solution)/shard_map/ppermute | solution.py:41
  46.7 12.8 %collective-permute-start.14 = (bf16[256,512]{1,0:T(8,128)(2,1)S(1)}, bf16[256,512]{1,0:T(8,128)(2,1)S(1)}, u32[]{:S(2)}, u32[]{:S(2)}) collective-permute-start(bf16[256,512]{1,0:T(8,128)(2,1)S(1)} %get-tuple-element.50), channel_id=1, source_target_pairs={{0,32},{1,33},{32,1},{33,0},{2,34},{3,35},{34,3},{35,2},{4,36},{5,... | collective-permute-start | bytes 786440 | tf_op jit(solution)/shard_map/ppermute | solution.py:41
  47.1 12.3 %collective-permute-start.15 = (bf16[256,512]{1,0:T(8,128)(2,1)S(1)}, bf16[256,512]{1,0:T(8,128)(2,1)S(1)}, u32[]{:S(2)}, u32[]{:S(2)}) collective-permute-start(bf16[256,512]{1,0:T(8,128)(2,1)S(1)} %get-tuple-element.51), channel_id=1, source_target_pairs={{0,33},{1,32},{32,0},{33,1},{2,35},{3,34},{34,2},{35,3},{4,37},{5,... | collective-permute-start | bytes 786440 | tf_op jit(solution)/shard_map/ppermute | solution.py:41

commit v10 on v9

--- a/solution.py
+++ b/solution.py
@@ -13,9 +13,9 @@
 ZS = 8
 XS = 4
 TILE = 128
-AWAY = (0, -1, 2, 1, -2, 3, -3, 4, 4)
-OTHER = range(7)
-MINE = range(9)
+AWAY = (0, -1, 2, 1, -2, 3, -3, 4, 3, 4)
+OTHER = range(6)
+MINE = range(10)
 
 VM = pl.BlockSpec(memory_space=pltpu.VMEM)
 HB = pl.BlockSpec(memory_space=pltpu.HBM)
@@ -172,7 +172,7 @@
             for i, d in enumerate(pieces):
                 ring = (z - step * AWAY[d] + ZS) % ZS
                 block = me + 2 * (ring - z)
-                if d == 8:
+                if d >= 8:
                     block = block + 16 * step
                 for h in range(TILES):
                     at = pl.ds(TILES * block + h, 1)
@@ -265,28 +265,34 @@
     )(c_mine, c_other, *pieces, *sums)
 
 
-def opposite_kernel(c_ref, x_ref, sum_ref, o_ref):
+def add_kernel(at, c_ref, *refs):
+    x_refs, sum_refs, o_ref = refs[: len(at)], refs[len(at) : -1], refs[-1]
     for j in range(XS):
         rows = slice(j * LIVE, (j + 1) * LIVE)
-        o_ref[rows, :] = sum_ref[rows, :] + product(c_ref, j, 7, (x_ref,))
-
-
-def add_opposite(c_mine, piece, mine):
-    return pl.pallas_call(
-        opposite_kernel,
-        in_specs=[VM] * 3,
+        total = sum_refs[0][rows, :]
+        for sum_ref in sum_refs[1:]:
+            total = total + sum_ref[rows, :].astype(F32)
+        for i, x_ref in zip(at, x_refs, strict=True):
+            total = total + product(c_ref, j, i, (x_ref,))
+        o_ref[rows, :] = total
+
+
+def add(at, c_mine, pieces, sums, estimate):
+    return pl.pallas_call(
+        lambda *refs: add_kernel(at, *refs),
+        in_specs=[VM] * (1 + len(at) + len(sums)),
         out_specs=VM,
-        out_shape=pltpu.VMEM(mine.shape, F32),
-        name="add_opposite",
-        compiler_params=params(8),
-        cost_estimate=LONG,
-    )(c_mine, piece, mine)
+        out_shape=pltpu.VMEM(sums[0].shape, F32),
+        name="add",
+        compiler_params=params(8),
+        cost_estimate=estimate,
+    )(c_mine, *pieces, *sums)
 
 
 def total_kernel(c_ref, x_ref, mine_ref, other_ref, own_ref, *out_refs):
     for j, out_ref in enumerate((own_ref, *out_refs)):
         rows = slice(j * LIVE, (j + 1) * LIVE)
-        total = product(c_ref, j, 8, (x_ref,))
+        total = product(c_ref, j, 9, (x_ref,))
         total = total + mine_ref[rows, :] + other_ref[rows, :].astype(F32)
         out_ref[...] = total.astype(out_ref.dtype)
 
@@ -308,16 +314,16 @@
     within = lax.broadcasted_iota(jnp.int32, (1, LIVE), 1)
     retain = within < counts_ref[me_ref[0]]
     norm = n_ref[:, :1]
-    half = buffer.shape[0] // 2
+    size = buffer.shape[0] // 4
     copies = []
-    for i in range(2):
-        part = slice(i * half, (i + 1) * half)
+    for i in range(4):
+        part = slice(i * size, (i + 1) * size)
         total = own_ref[:, part] + a_ref[:, part].astype(F32)
         total = total + b_ref[:, part].astype(F32) + c_ref[:, part].astype(F32)
         updated = jnp.transpose(total / norm)
         lead = lead_ref[part, :].astype(F32)
         buffer[part, :] = jnp.where(retain, updated, lead).astype(BF16)
-        rows = pl.ds(i * half, half)
+        rows = pl.ds(i * size, size)
         copies.append(
             pltpu.make_async_copy(buffer.at[rows, :], o_hbm.at[rows, pl.ds(0, LIVE)], sem.at[i])
         )
@@ -332,7 +338,7 @@
         in_specs=[SM, SM] + [VM] * (XS + 2) + [HB],
         out_specs=HB,
         out_shape=jax.ShapeDtypeStruct(out.shape, BF16),
-        scratch_shapes=[pltpu.VMEM(lead.shape, BF16), pltpu.SemaphoreType.DMA((2,))],
+        scratch_shapes=[pltpu.VMEM(lead.shape, BF16), pltpu.SemaphoreType.DMA((4,))],
         input_output_aliases={4 + XS: 0},
         name="finish",
         compiler_params=params(4),
@@ -348,7 +354,7 @@
     own, lead, rest = permute(in_hbm(eigvecs), in_hbm(perm.reshape(1, COLS)))
     p3 = around(own, 2)
     p2 = around(own, -1)
-    p1 = around(own, 1)
+    p1 = around(hold(own, p3), 1)
     near = join(roots, hold(other_roots, own))
     far = [xshift(near, k) for k in (-1, -2, 1)]
     table, factors = tables(
@@ -361,11 +367,12 @@
     p6 = around(hold(p4, c_mine), -1)
     sums = stage(0, c_mine, c_other, (own, p2, p3), (), False)
     p7 = around(hold(p5, sums[0]), 1)
-    sums = stage(3, c_mine, c_other, (p1, p4, p5), sums, False)
-    mine, other = stage(6, c_mine, c_other, (p6,), sums, True)
+    mine, other = stage(3, c_mine, c_other, (p1, p4, p5), sums, True)
     other = cshift(other)
+    p6 = hold(p6, mine)
+    mine = add((6, 8), c_mine, (p6, cshift(p6)), (mine,), TINY)
     sibling = cshift(p7)
-    mine = add_opposite(c_mine, p7, mine)
+    mine = add((7,), c_mine, (p7,), (mine,), LONG)
     own_sum, *sent = totals(c_mine, sibling, mine, other)
     received = [xshift(sent[i], k) for i, k in ((1, 2), (0, 1), (2, -1))]
     norm, out = norms(table, factors, hold(roots, own_sum), rest)

time: 61.2 us -> 66.2 us (1.082)
  waiting for transfers between devices: 12.7 us -> 15.6 us
  starting transfers between devices: 31.9 us -> 33.5 us
    ppermute x3 -> x4, starting transfers between devices: 6.69 us -> 15 us  [cshift(): return lax.ppermute(a, 'core', [(0, 1), (1, 0)])]
    ppermute x7, starting transfers between devices: 15 us -> 9.12 us  [around(): return lax.ppermute(a, ('core', 'z'), up + down)]
    ppermute x7, waiting for transfers between devices: 3.42 us -> 6.59 us  [around(): return lax.ppermute(a, ('core', 'z'), up + down)]
    ppermute x3 -> x4, waiting for transfers between devices: 2.06 us -> 1.04 us  [cshift(): return lax.ppermute(a, 'core', [(0, 1), (1, 0)])]
    ppermute x6, starting transfers between devices: 10.1 us -> 9.38 us  [xshift(): return lax.ppermute(a, ('xl', 'xh'), pairs)]
    pallas_call x3 -> x2, Pallas kernels: 4.34 us -> 3.61 us  [stage(): pl.pallas_call(lambda *refs: stage_kernel(first, len(pieces), *refs), in_...]
    pallas_call x1 -> x2, Pallas kernels: 0.44 us -> 1.14 us  [add(): pl.pallas_call(lambda *refs: add_kernel(at, *refs), in_specs=[VM] * (1 +...]
    ppermute x6, waiting for transfers between devices: 7.24 us -> 7.92 us  [xshift(): return lax.ppermute(a, ('xl', 'xh'), pairs)]
  transfers between devices with their start and end apart: 16 -> 17, of which waited for: 7 -> 7; matrix products, arithmetic and copies ran while one was open for 0% -> 0% of each run, Pallas kernels for 19% -> 18%
where the time goes in v10:
time: 66.2 us; the launch traced here: 65.6 us
  starting transfers between devices  33.5 us (51%)
  waiting for transfers between devices  15.6 us (24%)
  Pallas kernels  15.5 us (23%)
  local copies, waits for them, and re-layouts  0.69 us (1%)
    ppermute x4, starting transfers between devices, cshift(): return lax.ppermute(a, 'core', [(0, 1), (1, 0)])  15 us
    ppermute x6, starting transfers between devices, xshift(): return lax.ppermute(a, ('xl', 'xh'), pairs)  9.38 us
    ppermute x7, starting transfers between devices, around(): return lax.ppermute(a, ('core', 'z'), up + down)  9.12 us
    ppermute x6, waiting for transfers between devices, xshift(): return lax.ppermute(a, ('xl', 'xh'), pairs)  7.92 us
    ppermute x7, waiting for transfers between devices, around(): return lax.ppermute(a, ('core', 'z'), up + down)  6.59 us
    pallas_call x2, Pallas kernels, stage(): pl.pallas_call(lambda *refs: stage_kernel(first, len(pieces), *refs), in_...  3.61 us
    pallas_call x1, Pallas kernels, norms(): pl.pallas_call(norm_kernel, in_specs=[VM] * 4, out_specs=[VM, HB], out_sh...  3.38 us
    pallas_call x2, Pallas kernels, cauchy(): pl.pallas_call(lambda *refs: cauchy_kernel(fc, pieces, *refs), in_specs=[...  2.71 us
  transfers between devices with their start and end apart: 17, of which 7 were waited for; matrix products, arithmetic and copies ran while one was open for 0% of the time, Pallas kernels for 18%

profile of v10, /device:TPU:1, one launch (start us, length us, event | category | flops | bytes accessed | tf_op | source)
XLA Modules:
  0.0 65.6 jit_solution(14413451391551932635)
XLA Ops:
  0.0 1.7 %permute.1 = (bf16[256,512]{1,0:T(8,128)(2,1)S(1)}, bf16[512,256]{1,0:T(8,128)(2,1)S(1)}, bf16[512,256]{1,0:T(8,128)(2,1)S(1)}) custom-call(bf16[512,512]{1,0:T(8,128)(2,1)} %e_hbm.1, s32[1,512]{1,0:T(1,128)} %bitcast.10), custom_call_target="tpu_custom_call" | custom-call | flops 1 | bytes 1 | tf_op jit(solution)/shard_map/permute/pallas_call | solution.py:86
  1.7 2.5 %collective-permute-start.6 = (bf16[256,512]{1,0:T(8,128)(2,1)S(1)}, bf16[256,512]{1,0:T(8,128)(2,1)S(1)}, u32[]{:S(2)}, u32[]{:S(2)}) collective-permute-start(bf16[256,512]{1,0:T(8,128)(2,1)S(1)} %get-tuple-element.43.refs_2_), channel_id=1, source_target_pairs={{0,14},{2,0},{4,2},{6,4},{8,6},{10,8},{12,10},{14,12},{16,18},{18,... | collective-permute-start | bytes 786440 | tf_op jit(solution)/shard_map/ppermute | solution.py:47
  4.3 4.9 %collective-permute-start = (f32[1,512]{1,0:T(1,128)}, f32[1,512]{1,0:T(1,128)S(1)}, u32[]{:S(2)}, u32[]{:S(2)}) collective-permute-start(f32[1,512]{1,0:T(1,128)} %bitcast.5), channel_id=1, source_target_pairs={{0,16},{16,0},{1,17},{17,1},{2,18},{18,2},{3,19},{19,3},{4,20},{20... | collective-permute-start | bytes 6152 | tf_op jit(solution)/shard_map/ppermute | solution.py:51
  9.2 1.0 %collective-permute-done.b_ref = f32[1,512]{1,0:T(1,128)S(1)} collective-permute-done((f32[1,512]{1,0:T(1,128)}, f32[1,512]{1,0:T(1,128)S(1)}, u32[]{:S(2)}, u32[]{:S(2)}) %collective-permute-start) | collective-permute-done | bytes 2080 | tf_op jit(solution)/shard_map/ppermute | solution.py:51
  10.9 2.5 %collective-permute-start.2 = (f32[1,1024]{1,0:T(1,128)S(1)}, f32[1,1024]{1,0:T(1,128)S(1)}, u32[]{:S(2)}, u32[]{:S(2)}) collective-permute-start(f32[1,1024]{1,0:T(1,128)S(1)} %join.1.refs_3_), channel_id=1, source_target_pairs={{0,33},{1,32},{32,0},{33,1},{2,35},{3,34},{34,2},{35,3},{4,37},{5,... | collective-permute-start | bytes 12296 | tf_op jit(solution)/shard_map/ppermute | solution.py:41
  14.5 1.2 %collective-permute-start.1 = (bf16[256,512]{1,0:T(8,128)(2,1)S(1)}, bf16[256,512]{1,0:T(8,128)(2,1)S(1)}, u32[]{:S(2)}, u32[]{:S(2)}) collective-permute-start(bf16[256,512]{1,0:T(8,128)(2,1)S(1)} %get-tuple-element.43.refs_2_), channel_id=1, source_target_pairs={{0,4},{2,6},{4,8},{6,10},{8,12},{10,14},{12,0},{14,2},{16,28},{18,... | collective-permute-start | bytes 786440 | tf_op jit(solution)/shard_map/ppermute | solution.py:47
  15.7 1.1 %tables.1 = (f32[128,128]{1,0:T(8,128)S(1)}, f32[128,128]{1,0:T(8,128)S(1)}) custom-call(s32[64]{0:T(128)} %counts_ref.1, f32[256,128]{1,0:T(8,128)} %bitcast.8, f32[256,128]{1,0:T(8,128)} %bitcast.9), custom_call_target="tpu_custom_call" | custom-call | flops 1 | bytes 1 | tf_op jit(solution)/shard_map/tables/pallas_call | solution.py:128
  17.6 5.8 %collective-permute-done.1.refs_4_ = bf16[256,512]{1,0:T(8,128)(2,1)S(1)} collective-permute-done((bf16[256,512]{1,0:T(8,128)(2,1)S(1)}, bf16[256,512]{1,0:T(8,128)(2,1)S(1)}, u32[]{:S(2)}, u32[]{:S(2)}) %collective-permute-start.1) | collective-permute-done | bytes 262176 | tf_op jit(solution)/shard_map/ppermute | solution.py:47
  23.3 1.1 %cauchy.2.refs_1_ = bf16[1024,1536]{1,0:T(8,128)(2,1)S(1)} custom-call(s32[1]{0:T(128)} %bitcast.refs_0_.me_ref, f32[128,128]{1,0:T(8,128)S(1)} %get-tuple-element.34.refs_1_.poles_ref, f32[128,128]{1,0:T(8,128)S(1)} %get-tuple-element.35.refs_2_.factors_ref, f32[1,1024]{1,0:T(1,128)S(1)} %join.1.refs_3_, f32[1,1024]{1,0:T(1,128)S(1)} %collective-permute-done.2.refs_4_, ...), custom_call_target="tpu_custom_call" | custom-call | flops 1 | bytes 1 | tf_op jit(solution)/shard_map/cauchy/pallas_call | solution.py:185
  24.4 2.3 %collective-permute-start.5 = (bf16[256,512]{1,0:T(8,128)(2,1)S(1)}, bf16[256,512]{1,0:T(8,128)(2,1)S(1)}, u32[]{:S(2)}, u32[]{:S(2)}) collective-permute-start(bf16[256,512]{1,0:T(8,128)(2,1)S(1)} %collective-permute-done.1.refs_4_), channel_id=1, source_target_pairs={{0,2},{2,4},{4,6},{6,8},{8,10},{10,12},{12,14},{14,0},{16,30},{18,... | collective-permute-start | bytes 786440 | tf_op jit(solution)/shard_map/ppermute | solution.py:47
  26.8 1.7 %cauchy.3.refs_0_.c_ref = bf16[1024,2560]{1,0:T(8,128)(2,1)S(1)} custom-call(s32[1]{0:T(128)} %bitcast.refs_0_.me_ref, f32[128,128]{1,0:T(8,128)S(1)} %get-tuple-element.34.refs_1_.poles_ref, f32[128,128]{1,0:T(8,128)S(1)} %get-tuple-element.35.refs_2_.factors_ref, f32[1,1024]{1,0:T(1,128)S(1)} %join.1.refs_3_, ...), custom_call_target="tpu_custom_call" | custom-call | flops 1 | bytes 1 | tf_op jit(solution)/shard_map/cauchy/pallas_call | solution.py:185
  28.5 1.5 %collective-permute-start.10 = (bf16[256,512]{1,0:T(8,128)(2,1)S(1)}, bf16[256,512]{1,0:T(8,128)(2,1)S(1)}, u32[]{:S(2)}, u32[]{:S(2)}) collective-permute-start(bf16[256,512]{1,0:T(8,128)(2,1)S(1)} %collective-permute-done.9.refs_3_), channel_id=1, source_target_pairs={{0,14},{2,0},{4,2},{6,4},{8,6},{10,8},{12,10},{14,12},{16,18},{18,... | collective-permute-start | bytes 786440 | tf_op jit(solution)/shard_map/ppermute | solution.py:47
  29.9 1.8 %stage.2 = (f32[1024,512]{1,0:T(8,128)S(1)}, f32[1024,512]{1,0:T(8,128)S(1)}) custom-call(bf16[1024,2560]{1,0:T(8,128)(2,1)S(1)} %cauchy.3.refs_0_.c_ref, bf16[1024,1536]{1,0:T(8,128)(2,1)S(1)} %cauchy.2.refs_1_, bf16[256,512]{1,0:T(8,128)(2,1)S(1)} %get-tuple-element.43.refs_2_, bf16[256,512]{1,0:T(8,128)(2,1)S(1)} %collective-permute-done.6.refs_3_, ...), custom_call_target="tpu_custom_call" | custom-call | flops 1 | bytes 1 | tf_op jit(solution)/shard_map/stage/pallas_call | solution.py:257
  31.7 1.6 %collective-permute-start.7 = (bf16[256,512]{1,0:T(8,128)(2,1)S(1)}, bf16[256,512]{1,0:T(8,128)(2,1)S(1)}, u32[]{:S(2)}, u32[]{:S(2)}) collective-permute-start(bf16[256,512]{1,0:T(8,128)(2,1)S(1)} %collective-permute-done.5.refs_4_), channel_id=1, source_target_pairs={{0,2},{2,4},{4,6},{6,8},{8,10},{10,12},{12,14},{14,0},{16,30},{18,... | collective-permute-start | bytes 786440 | tf_op jit(solution)/shard_map/ppermute | solution.py:47
  33.3 1.8 %stage.3 = (f32[1024,512]{1,0:T(8,128)S(1)}, bf16[1024,512]{1,0:T(8,128)(2,1)S(1)}) custom-call(bf16[1024,2560]{1,0:T(8,128)(2,1)S(1)} %cauchy.3.refs_0_.c_ref, bf16[1024,1536]{1,0:T(8,128)(2,1)S(1)} %cauchy.2.refs_1_, bf16[256,512]{1,0:T(8,128)(2,1)S(1)} %collective-permute-done.11.refs_2_, bf16[256,512]{1,0:T(8,128)(2,1)S(1)} %collective-permute-done.9.refs_3_, ...), custom_call_target="tpu_custom_call" | custom-call | flops 1 | bytes 1 | tf_op jit(solution)/shard_map/stage/pallas_call | solution.py:257
  35.9 7.3 %collective-permute-start.12 = (bf16[256,512]{1,0:T(8,128)(2,1)S(1)}, bf16[256,512]{1,0:T(8,128)(2,1)S(1)}, u32[]{:S(2)}, u32[]{:S(2)}) collective-permute-start(bf16[256,512]{1,0:T(8,128)(2,1)S(1)} %collective-permute-done.10.refs_1_), channel_id=1, source_target_pairs={{0,16},{16,0},{1,17},{17,1},{2,18},{18,2},{3,19},{19,3},{4,20},{20... | collective-permute-start | bytes 786440 | tf_op jit(solution)/shard_map/ppermute | solution.py:51
  43.3 2.7 %collective-permute-start.8 = (bf16[256,512]{1,0:T(8,128)(2,1)S(1)}, bf16[256,512]{1,0:T(8,128)(2,1)S(1)}, u32[]{:S(2)}, u32[]{:S(2)}) collective-permute-start(bf16[256,512]{1,0:T(8,128)(2,1)S(1)} %collective-permute-done.7.refs_1_), channel_id=1, source_target_pairs={{0,16},{16,0},{1,17},{17,1},{2,18},{18,2},{3,19},{19,3},{4,20},{20... | collective-permute-start | bytes 786440 | tf_op jit(solution)/shard_map/ppermute | solution.py:51
  47.7 2.5 %collective-permute-start.14 = (bf16[256,512]{1,0:T(8,128)(2,1)S(1)}, bf16[256,512]{1,0:T(8,128)(2,1)S(1)}, u32[]{:S(2)}, u32[]{:S(2)}) collective-permute-start(bf16[256,512]{1,0:T(8,128)(2,1)S(1)} %get-tuple-element.49), channel_id=1, source_target_pairs={{0,1},{1,0},{32,33},{33,32},{2,3},{3,2},{34,35},{35,34},{4,5},{5,4... | collective-permute-start | bytes 786440 | tf_op jit(solution)/shard_map/ppermute | solution.py:41
  50.2 2.0 %collective-permute-start.15 = (bf16[256,512]{1,0:T(8,128)(2,1)S(1)}, bf16[256,512]{1,0:T(8,128)(2,1)S(1)}, u32[]{:S(2)}, u32[]{:S(2)}) collective-permute-start(bf16[256,512]{1,0:T(8,128)(2,1)S(1)} %get-tuple-element.50), channel_id=1, source_target_pairs={{0,32},{1,33},{32,1},{33,0},{2,34},{3,35},{34,3},{35,2},{4,36},{5,... | collective-permute-start | bytes 786440 | tf_op jit(solution)/shard_map/ppermute | solution.py:41
  52.2 1.3 %collective-permute-start.16 = (bf16[256,512]{1,0:T(8,128)(2,1)S(1)}, bf16[256,512]{1,0:T(8,128)(2,1)S(1)}, u32[]{:S(2)}, u32[]{:S(2)}) collective-permute-start(bf16[256,512]{1,0:T(8,128)(2,1)S(1)} %get-tuple-element.51), channel_id=1, source_target_pairs={{0,33},{1,32},{32,0},{33,1},{2,35},{3,34},{34,2},{35,3},{4,37},{5,... | collective-permute-start | bytes 786440 | tf_op jit(solution)/shard_map/ppermute | solution.py:41
  53.5 3.4 %norms.1 = (f32[256,128]{1,0:T(8,128)S(1)}, bf16[512,512]{1,0:T(8,128)(2,1)}) custom-call(f32[128,128]{1,0:T(8,128)S(1)} %get-tuple-element.34.refs_1_.poles_ref, f32[128,128]{1,0:T(8,128)S(1)} %get-tuple-element.35.refs_2_.factors_ref, f32[1,512]{1,0:T(1,128)S(1)} %bitcast.7, bf16[512,256]{1,0:T(8,128)(2,1)S(1)} %get-tuple-element.53.rest_ref), custom_call_target="tpu_custom_call" | custom-call | flops 1 | bytes 1 | tf_op jit(solution)/shard_map/norms/pallas_call | solution.py:218
  56.9 6.3 %collective-permute-done.15.b_ref = bf16[256,512]{1,0:T(8,128)(2,1)S(1)} collective-permute-done((bf16[256,512]{1,0:T(8,128)(2,1)S(1)}, bf16[256,512]{1,0:T(8,128)(2,1)S(1)}, u32[]{:S(2)}, u32[]{:S(2)}) %collective-permute-start.15) | collective-permute-done | bytes 262176 | tf_op jit(solution)/shard_map/ppermute | solution.py:41
  63.2 0.8 %collective-permute-done.16.c_ref = bf16[256,512]{1,0:T(8,128)(2,1)S(1)} collective-permute-done((bf16[256,512]{1,0:T(8,128)(2,1)S(1)}, bf16[256,512]{1,0:T(8,128)(2,1)S(1)}, u32[]{:S(2)}, u32[]{:S(2)}) %collective-permute-start.16) | collective-permute-done | bytes 262176 | tf_op jit(solution)/shard_map/ppermute | solution.py:41
  64.0 1.5 %finish.1 = bf16[512,512]{1,0:T(8,128)(2,1)} custom-call(s32[1]{0:T(128)} %bitcast.refs_0_.me_ref, s32[64]{0:T(128)S(1)} %copy-done.2, f32[256,512]{1,0:T(8,128)S(1)} %get-tuple-element.48.own_ref, bf16[256,512]{1,0:T(8,128)(2,1)S(1)} %collective-permute-done.14.a_ref, ...), custom_call_target="tpu_custom_call", output_to_operand_aliasing={{}: (8, {})} | custom-call | flops 1 | bytes 1 | tf_op jit(solution)/shard_map/finish/pallas_call | solution.py:336
  (28 shorter events, 5.3 us)
Async XLA Ops:
  1.7 15.8 %collective-permute-start.6 = (bf16[256,512]{1,0:T(8,128)(2,1)S(1)}, bf16[256,512]{1,0:T(8,128)(2,1)S(1)}, u32[]{:S(2)}, u32[]{:S(2)}) collective-permute-start(bf16[256,512]{1,0:T(8,128)(2,1)S(1)} %get-tuple-element.43.refs_2_), channel_id=1, source_target_pairs={{0,14},{2,0},{4,2},{6,4},{8,6},{10,8},{12,10},{14,12},{16,18},{18,... | collective-permute-start | bytes 786440 | tf_op jit(solution)/shard_map/ppermute | solution.py:47
  4.3 5.9 %collective-permute-start = (f32[1,512]{1,0:T(1,128)}, f32[1,512]{1,0:T(1,128)S(1)}, u32[]{:S(2)}, u32[]{:S(2)}) collective-permute-start(f32[1,512]{1,0:T(1,128)} %bitcast.5), channel_id=1, source_target_pairs={{0,16},{16,0},{1,17},{17,1},{2,18},{18,2},{3,19},{19,3},{4,20},{20... | collective-permute-start | bytes 6152 | tf_op jit(solution)/shard_map/ppermute | solution.py:51
  10.2 0.7 %copy-start = (f32[512]{0:T(512)S(1)}, f32[512]{0:T(512)}, u32[]{:S(2)}) copy-start(f32[512]{0:T(512)} %param.11) | copy-start | bytes 6148
  10.9 5.8 %collective-permute-start.2 = (f32[1,1024]{1,0:T(1,128)S(1)}, f32[1,1024]{1,0:T(1,128)S(1)}, u32[]{:S(2)}, u32[]{:S(2)}) collective-permute-start(f32[1,1024]{1,0:T(1,128)S(1)} %join.1.refs_3_), channel_id=1, source_target_pairs={{0,33},{1,32},{32,0},{33,1},{2,35},{3,34},{34,2},{35,3},{4,37},{5,... | collective-permute-start | bytes 12296 | tf_op jit(solution)/shard_map/ppermute | solution.py:41
  13.4 4.0 %collective-permute-start.3 = (f32[1,1024]{1,0:T(1,128)S(1)}, f32[1,1024]{1,0:T(1,128)S(1)}, u32[]{:S(2)}, u32[]{:S(2)}) collective-permute-start(f32[1,1024]{1,0:T(1,128)S(1)} %join.1.refs_3_), channel_id=1, source_target_pairs={{0,1},{1,0},{32,33},{33,32},{2,3},{3,2},{34,35},{35,34},{4,5},{5,4... | collective-permute-start | bytes 12296 | tf_op jit(solution)/shard_map/ppermute | solution.py:41
  13.9 3.7 %collective-permute-start.4 = (f32[1,1024]{1,0:T(1,128)S(1)}, f32[1,1024]{1,0:T(1,128)S(1)}, u32[]{:S(2)}, u32[]{:S(2)}) collective-permute-start(f32[1,1024]{1,0:T(1,128)S(1)} %join.1.refs_3_), channel_id=1, source_target_pairs={{0,32},{1,33},{32,1},{33,0},{2,34},{3,35},{34,3},{35,2},{4,36},{5,... | collective-permute-start | bytes 12296 | tf_op jit(solution)/shard_map/ppermute | solution.py:41
  14.5 8.9 %collective-permute-start.1 = (bf16[256,512]{1,0:T(8,128)(2,1)S(1)}, bf16[256,512]{1,0:T(8,128)(2,1)S(1)}, u32[]{:S(2)}, u32[]{:S(2)}) collective-permute-start(bf16[256,512]{1,0:T(8,128)(2,1)S(1)} %get-tuple-element.43.refs_2_), channel_id=1, source_target_pairs={{0,4},{2,6},{4,8},{6,10},{8,12},{10,14},{12,0},{14,2},{16,28},{18,... | collective-permute-start | bytes 786440 | tf_op jit(solution)/shard_map/ppermute | solution.py:47
  17.6 10.9 %collective-permute-start.9 = (bf16[256,512]{1,0:T(8,128)(2,1)S(1)}, bf16[256,512]{1,0:T(8,128)(2,1)S(1)}, u32[]{:S(2)}, u32[]{:S(2)}) collective-permute-start(bf16[256,512]{1,0:T(8,128)(2,1)S(1)} %collective-permute-done.6.refs_3_), channel_id=1, source_target_pairs={{0,14},{2,0},{4,2},{6,4},{8,6},{10,8},{12,10},{14,12},{16,18},{18,... | collective-permute-start | bytes 786440 | tf_op jit(solution)/shard_map/ppermute | solution.py:47
  24.4 7.3 %collective-permute-start.5 = (bf16[256,512]{1,0:T(8,128)(2,1)S(1)}, bf16[256,512]{1,0:T(8,128)(2,1)S(1)}, u32[]{:S(2)}, u32[]{:S(2)}) collective-permute-start(bf16[256,512]{1,0:T(8,128)(2,1)S(1)} %collective-permute-done.1.refs_4_), channel_id=1, source_target_pairs={{0,2},{2,4},{4,6},{6,8},{8,10},{10,12},{12,14},{14,0},{16,30},{18,... | collective-permute-start | bytes 786440 | tf_op jit(solution)/shard_map/ppermute | solution.py:47
  26.7 6.6 %collective-permute-start.11 = (bf16[256,512]{1,0:T(8,128)(2,1)S(1)}, bf16[256,512]{1,0:T(8,128)(2,1)S(1)}, u32[]{:S(2)}, u32[]{:S(2)}) collective-permute-start(bf16[256,512]{1,0:T(8,128)(2,1)S(1)} %get-tuple-element.43.refs_2_), channel_id=1, source_target_pairs={{0,2},{2,4},{4,6},{6,8},{8,10},{10,12},{12,14},{14,0},{16,30},{18,... | collective-permute-start | bytes 786440 | tf_op jit(solution)/shard_map/ppermute | solution.py:47
  28.5 7.5 %collective-permute-start.10 = (bf16[256,512]{1,0:T(8,128)(2,1)S(1)}, bf16[256,512]{1,0:T(8,128)(2,1)S(1)}, u32[]{:S(2)}, u32[]{:S(2)}) collective-permute-start(bf16[256,512]{1,0:T(8,128)(2,1)S(1)} %collective-permute-done.9.refs_3_), channel_id=1, source_target_pairs={{0,14},{2,0},{4,2},{6,4},{8,6},{10,8},{12,10},{14,12},{16,18},{18,... | collective-permute-start | bytes 786440 | tf_op jit(solution)/shard_map/ppermute | solution.py:47
  31.7 11.6 %collective-permute-start.7 = (bf16[256,512]{1,0:T(8,128)(2,1)S(1)}, bf16[256,512]{1,0:T(8,128)(2,1)S(1)}, u32[]{:S(2)}, u32[]{:S(2)}) collective-permute-start(bf16[256,512]{1,0:T(8,128)(2,1)S(1)} %collective-permute-done.5.refs_4_), channel_id=1, source_target_pairs={{0,2},{2,4},{4,6},{6,8},{8,10},{10,12},{12,14},{14,0},{16,30},{18,... | collective-permute-start | bytes 786440 | tf_op jit(solution)/shard_map/ppermute | solution.py:47
  35.9 10.1 %collective-permute-start.12 = (bf16[256,512]{1,0:T(8,128)(2,1)S(1)}, bf16[256,512]{1,0:T(8,128)(2,1)S(1)}, u32[]{:S(2)}, u32[]{:S(2)}) collective-permute-start(bf16[256,512]{1,0:T(8,128)(2,1)S(1)} %collective-permute-done.10.refs_1_), channel_id=1, source_target_pairs={{0,16},{16,0},{1,17},{17,1},{2,18},{18,2},{3,19},{19,3},{4,20},{20... | collective-permute-start | bytes 786440 | tf_op jit(solution)/shard_map/ppermute | solution.py:51
  43.2 4.1 %collective-permute-start.13 = (bf16[1024,512]{1,0:T(8,128)(2,1)S(1)}, bf16[1024,512]{1,0:T(8,128)(2,1)S(1)}, u32[]{:S(2)}, u32[]{:S(2)}) collective-permute-start(bf16[1024,512]{1,0:T(8,128)(2,1)S(1)} %get-tuple-element.47), channel_id=1, source_target_pairs={{0,16},{16,0},{1,17},{17,1},{2,18},{18,2},{3,19},{19,3},{4,20},{20... | collective-permute-start | bytes 3145736 | tf_op jit(solution)/shard_map/ppermute | solution.py:51
  43.3 3.9 %collective-permute-start.8 = (bf16[256,512]{1,0:T(8,128)(2,1)S(1)}, bf16[256,512]{1,0:T(8,128)(2,1)S(1)}, u32[]{:S(2)}, u32[]{:S(2)}) collective-permute-start(bf16[256,512]{1,0:T(8,128)(2,1)S(1)} %collective-permute-done.7.refs_1_), channel_id=1, source_target_pairs={{0,16},{16,0},{1,17},{17,1},{2,18},{18,2},{3,19},{19,3},{4,20},{20... | collective-permute-start | bytes 786440 | tf_op jit(solution)/shard_map/ppermute | solution.py:51
  47.2 6.3 %copy-start.1 = (f32[512]{0:T(512)S(1)}, f32[512]{0:T(512)}, u32[]{:S(2)}) copy-start(f32[512]{0:T(512)} %param.11) | copy-start | bytes 6148
  47.2 16.8 %copy-start.2 = (s32[64]{0:T(128)S(1)}, s32[64]{0:T(128)}, u32[]{:S(2)}) copy-start(s32[64]{0:T(128)} %counts_ref.1) | copy-start | bytes 772
  47.7 9.2 %collective-permute-start.14 = (bf16[256,512]{1,0:T(8,128)(2,1)S(1)}, bf16[256,512]{1,0:T(8,128)(2,1)S(1)}, u32[]{:S(2)}, u32[]{:S(2)}) collective-permute-start(bf16[256,512]{1,0:T(8,128)(2,1)S(1)} %get-tuple-element.49), channel_id=1, source_target_pairs={{0,1},{1,0},{32,33},{33,32},{2,3},{3,2},{34,35},{35,34},{4,5},{5,4... | collective-permute-start | bytes 786440 | tf_op jit(solution)/shard_map/ppermute | solution.py:41
  50.2 12.9 %collective-permute-start.15 = (bf16[256,512]{1,0:T(8,128)(2,1)S(1)}, bf16[256,512]{1,0:T(8,128)(2,1)S(1)}, u32[]{:S(2)}, u32[]{:S(2)}) collective-permute-start(bf16[256,512]{1,0:T(8,128)(2,1)S(1)} %get-tuple-element.50), channel_id=1, source_target_pairs={{0,32},{1,33},{32,1},{33,0},{2,34},{3,35},{34,3},{35,2},{4,36},{5,... | collective-permute-start | bytes 786440 | tf_op jit(solution)/shard_map/ppermute | solution.py:41
  52.2 11.8 %collective-permute-start.16 = (bf16[256,512]{1,0:T(8,128)(2,1)S(1)}, bf16[256,512]{1,0:T(8,128)(2,1)S(1)}, u32[]{:S(2)}, u32[]{:S(2)}) collective-permute-start(bf16[256,512]{1,0:T(8,128)(2,1)S(1)} %get-tuple-element.51), channel_id=1, source_target_pairs={{0,33},{1,32},{32,0},{33,1},{2,35},{3,34},{34,2},{35,3},{4,37},{5,... | collective-permute-start | bytes 786440 | tf_op jit(solution)/shard_map/ppermute | solution.py:41

commit v11 on v10

--- a/solution.py
+++ b/solution.py
@@ -354,7 +354,7 @@
     own, lead, rest = permute(in_hbm(eigvecs), in_hbm(perm.reshape(1, COLS)))
     p3 = around(own, 2)
     p2 = around(own, -1)
-    p1 = around(hold(own, p3), 1)
+    p1 = around(own, 1)
     near = join(roots, hold(other_roots, own))
     far = [xshift(near, k) for k in (-1, -2, 1)]
     table, factors = tables(
@@ -370,9 +370,9 @@
     mine, other = stage(3, c_mine, c_other, (p1, p4, p5), sums, True)
     other = cshift(other)
     p6 = hold(p6, mine)
-    mine = add((6, 8), c_mine, (p6, cshift(p6)), (mine,), TINY)
     sibling = cshift(p7)
     mine = add((7,), c_mine, (p7,), (mine,), LONG)
+    mine = add((6, 8), c_mine, (p6, cshift(p6)), (mine,), TINY)
     own_sum, *sent = totals(c_mine, sibling, mine, other)
     received = [xshift(sent[i], k) for i, k in ((1, 2), (0, 1), (2, -1))]
     norm, out = norms(table, factors, hold(roots, own_sum), rest)

time: 66.2 us -> 59.2 us (0.89)
  waiting for transfers between devices: 15.6 us -> 10.4 us
  starting transfers between devices: 33.5 us -> 32.1 us
    ppermute x4, starting transfers between devices: 15 us -> 8.38 us  [cshift(): return lax.ppermute(a, 'core', [(0, 1), (1, 0)])]
    ppermute x7, waiting for transfers between devices: 6.59 us -> 0.02 us  [around(): return lax.ppermute(a, ('core', 'z'), up + down)]
    ppermute x7, starting transfers between devices: 9.12 us -> 14.8 us  [around(): return lax.ppermute(a, ('core', 'z'), up + down)]
    ppermute x6, waiting for transfers between devices: 7.92 us -> 8.99 us  [xshift(): return lax.ppermute(a, ('xl', 'xh'), pairs)]
  transfers between devices with their start and end apart: 17 -> 17, of which waited for: 7 -> 5; matrix products, arithmetic and copies ran while one was open for 0% -> 0% of each run, Pallas kernels for 18% -> 20%
where the time goes in v11:
time: 59.2 us; the launch traced here: 59.1 us
  starting transfers between devices  32.1 us (54%)
  Pallas kernels  15.6 us (26%)
  waiting for transfers between devices  10.4 us (18%)
  local copies, waits for them, and re-layouts  0.69 us (1%)
    ppermute x7, starting transfers between devices, around(): return lax.ppermute(a, ('core', 'z'), up + down)  14.8 us
    ppermute x6, waiting for transfers between devices, xshift(): return lax.ppermute(a, ('xl', 'xh'), pairs)  8.99 us
    ppermute x6, starting transfers between devices, xshift(): return lax.ppermute(a, ('xl', 'xh'), pairs)  8.95 us
    ppermute x4, starting transfers between devices, cshift(): return lax.ppermute(a, 'core', [(0, 1), (1, 0)])  8.38 us
    pallas_call x2, Pallas kernels, stage(): pl.pallas_call(lambda *refs: stage_kernel(first, len(pieces), *refs), in_...  3.61 us
    pallas_call x1, Pallas kernels, norms(): pl.pallas_call(norm_kernel, in_specs=[VM] * 4, out_specs=[VM, HB], out_sh...  3.38 us
    pallas_call x2, Pallas kernels, cauchy(): pl.pallas_call(lambda *refs: cauchy_kernel(fc, pieces, *refs), in_specs=[...  2.72 us
    pallas_call x1, Pallas kernels, permute(): pl.pallas_call(permute_kernel, in_specs=[HB, HB], out_specs=[VM] * 3, out...  1.72 us
  transfers between devices with their start and end apart: 17, of which 5 were waited for; matrix products, arithmetic and copies ran while one was open for 0% of the time, Pallas kernels for 20%

profile of v11, /device:TPU:1, one launch (start us, length us, event | category | flops | bytes accessed | tf_op | source)
XLA Modules:
  0.0 59.1 jit_solution(14190243394761645440)
XLA Ops:
  0.0 1.7 %permute.1 = (bf16[256,512]{1,0:T(8,128)(2,1)S(1)}, bf16[512,256]{1,0:T(8,128)(2,1)S(1)}, bf16[512,256]{1,0:T(8,128)(2,1)S(1)}) custom-call(bf16[512,512]{1,0:T(8,128)(2,1)} %e_hbm.1, s32[1,512]{1,0:T(1,128)} %bitcast.10), custom_call_target="tpu_custom_call" | custom-call | flops 1 | bytes 1 | tf_op jit(solution)/shard_map/permute/pallas_call | solution.py:86
  1.7 2.5 %collective-permute-start.6 = (bf16[256,512]{1,0:T(8,128)(2,1)S(1)}, bf16[256,512]{1,0:T(8,128)(2,1)S(1)}, u32[]{:S(2)}, u32[]{:S(2)}) collective-permute-start(bf16[256,512]{1,0:T(8,128)(2,1)S(1)} %get-tuple-element.30.refs_2_), channel_id=1, source_target_pairs={{0,14},{2,0},{4,2},{6,4},{8,6},{10,8},{12,10},{14,12},{16,18},{18,... | collective-permute-start | bytes 786440 | tf_op jit(solution)/shard_map/ppermute | solution.py:47
  4.3 5.1 %collective-permute-start.1 = (bf16[256,512]{1,0:T(8,128)(2,1)S(1)}, bf16[256,512]{1,0:T(8,128)(2,1)S(1)}, u32[]{:S(2)}, u32[]{:S(2)}) collective-permute-start(bf16[256,512]{1,0:T(8,128)(2,1)S(1)} %get-tuple-element.30.refs_2_), channel_id=1, source_target_pairs={{0,4},{2,6},{4,8},{6,10},{8,12},{10,14},{12,0},{14,2},{16,28},{18,... | collective-permute-start | bytes 786440 | tf_op jit(solution)/shard_map/ppermute | solution.py:47
  9.4 1.4 %collective-permute-done.b_ref = f32[1,512]{1,0:T(1,128)S(1)} collective-permute-done((f32[1,512]{1,0:T(1,128)}, f32[1,512]{1,0:T(1,128)S(1)}, u32[]{:S(2)}, u32[]{:S(2)}) %collective-permute-start) | collective-permute-done | bytes 2080 | tf_op jit(solution)/shard_map/ppermute | solution.py:51
  10.8 0.7 %copy-done = f32[512]{0:T(512)S(1)} copy-done((f32[512]{0:T(512)S(1)}, f32[512]{0:T(512)}, u32[]{:S(2)}) %copy-start) | copy-done | bytes 2072
  11.4 2.5 %collective-permute-start.2 = (f32[1,1024]{1,0:T(1,128)S(1)}, f32[1,1024]{1,0:T(1,128)S(1)}, u32[]{:S(2)}, u32[]{:S(2)}) collective-permute-start(f32[1,1024]{1,0:T(1,128)S(1)} %join.1.refs_3_), channel_id=1, source_target_pairs={{0,33},{1,32},{32,0},{33,1},{2,35},{3,34},{34,2},{35,3},{4,37},{5,... | collective-permute-start | bytes 12296 | tf_op jit(solution)/shard_map/ppermute | solution.py:41
  15.1 1.1 %tables.1 = (f32[128,128]{1,0:T(8,128)S(1)}, f32[128,128]{1,0:T(8,128)S(1)}) custom-call(s32[64]{0:T(128)} %counts_ref.1, f32[256,128]{1,0:T(8,128)} %bitcast.8, f32[256,128]{1,0:T(8,128)} %bitcast.9), custom_call_target="tpu_custom_call" | custom-call | flops 1 | bytes 1 | tf_op jit(solution)/shard_map/tables/pallas_call | solution.py:128
  16.1 2.1 %collective-permute-done.3.refs_5_ = f32[1,1024]{1,0:T(1,128)S(1)} collective-permute-done((f32[1,1024]{1,0:T(1,128)S(1)}, f32[1,1024]{1,0:T(1,128)S(1)}, u32[]{:S(2)}, u32[]{:S(2)}) %collective-permute-start.3) | collective-permute-done | bytes 4128 | tf_op jit(solution)/shard_map/ppermute | solution.py:41
  18.4 2.7 %collective-permute-start.5 = (bf16[256,512]{1,0:T(8,128)(2,1)S(1)}, bf16[256,512]{1,0:T(8,128)(2,1)S(1)}, u32[]{:S(2)}, u32[]{:S(2)}) collective-permute-start(bf16[256,512]{1,0:T(8,128)(2,1)S(1)} %collective-permute-done.1.refs_4_), channel_id=1, source_target_pairs={{0,2},{2,4},{4,6},{6,8},{8,10},{10,12},{12,14},{14,0},{16,30},{18,... | collective-permute-start | bytes 786440 | tf_op jit(solution)/shard_map/ppermute | solution.py:47
  21.1 1.7 %collective-permute-start.11 = (bf16[256,512]{1,0:T(8,128)(2,1)S(1)}, bf16[256,512]{1,0:T(8,128)(2,1)S(1)}, u32[]{:S(2)}, u32[]{:S(2)}) collective-permute-start(bf16[256,512]{1,0:T(8,128)(2,1)S(1)} %get-tuple-element.30.refs_2_), channel_id=1, source_target_pairs={{0,2},{2,4},{4,6},{6,8},{8,10},{10,12},{12,14},{14,0},{16,30},{18,... | collective-permute-start | bytes 786440 | tf_op jit(solution)/shard_map/ppermute | solution.py:47
  22.8 1.1 %cauchy.2.refs_1_ = bf16[1024,1536]{1,0:T(8,128)(2,1)S(1)} custom-call(s32[1]{0:T(128)} %bitcast.refs_0_.me_ref, f32[128,128]{1,0:T(8,128)S(1)} %get-tuple-element.33.refs_1_.poles_ref, f32[128,128]{1,0:T(8,128)S(1)} %get-tuple-element.34.refs_2_.factors_ref, f32[1,1024]{1,0:T(1,128)S(1)} %join.1.refs_3_, f32[1,1024]{1,0:T(1,128)S(1)} %collective-permute-done.2.refs_4_, ...), custom_call_target="tpu_custom_call" | custom-call | flops 1 | bytes 1 | tf_op jit(solution)/shard_map/cauchy/pallas_call | solution.py:185
  23.9 1.7 %cauchy.3.refs_0_.c_ref = bf16[1024,2560]{1,0:T(8,128)(2,1)S(1)} custom-call(s32[1]{0:T(128)} %bitcast.refs_0_.me_ref, f32[128,128]{1,0:T(8,128)S(1)} %get-tuple-element.33.refs_1_.poles_ref, f32[128,128]{1,0:T(8,128)S(1)} %get-tuple-element.34.refs_2_.factors_ref, f32[1,1024]{1,0:T(1,128)S(1)} %join.1.refs_3_, ...), custom_call_target="tpu_custom_call" | custom-call | flops 1 | bytes 1 | tf_op jit(solution)/shard_map/cauchy/pallas_call | solution.py:185
  25.6 1.8 %stage.2 = (f32[1024,512]{1,0:T(8,128)S(1)}, f32[1024,512]{1,0:T(8,128)S(1)}) custom-call(bf16[1024,2560]{1,0:T(8,128)(2,1)S(1)} %cauchy.3.refs_0_.c_ref, bf16[1024,1536]{1,0:T(8,128)(2,1)S(1)} %cauchy.2.refs_1_, bf16[256,512]{1,0:T(8,128)(2,1)S(1)} %get-tuple-element.30.refs_2_, bf16[256,512]{1,0:T(8,128)(2,1)S(1)} %collective-permute-done.6.refs_3_, ...), custom_call_target="tpu_custom_call" | custom-call | flops 1 | bytes 1 | tf_op jit(solution)/shard_map/stage/pallas_call | solution.py:257
  27.5 2.7 %collective-permute-start.7 = (bf16[256,512]{1,0:T(8,128)(2,1)S(1)}, bf16[256,512]{1,0:T(8,128)(2,1)S(1)}, u32[]{:S(2)}, u32[]{:S(2)}) collective-permute-start(bf16[256,512]{1,0:T(8,128)(2,1)S(1)} %collective-permute-done.5.refs_4_), channel_id=1, source_target_pairs={{0,2},{2,4},{4,6},{6,8},{8,10},{10,12},{12,14},{14,0},{16,30},{18,... | collective-permute-start | bytes 786440 | tf_op jit(solution)/shard_map/ppermute | solution.py:47
  30.1 1.8 %stage.3 = (f32[1024,512]{1,0:T(8,128)S(1)}, bf16[1024,512]{1,0:T(8,128)(2,1)S(1)}) custom-call(bf16[1024,2560]{1,0:T(8,128)(2,1)S(1)} %cauchy.3.refs_0_.c_ref, bf16[1024,1536]{1,0:T(8,128)(2,1)S(1)} %cauchy.2.refs_1_, bf16[256,512]{1,0:T(8,128)(2,1)S(1)} %collective-permute-done.11.refs_2_, bf16[256,512]{1,0:T(8,128)(2,1)S(1)} %collective-permute-done.9.refs_3_, ...), custom_call_target="tpu_custom_call" | custom-call | flops 1 | bytes 1 | tf_op jit(solution)/shard_map/stage/pallas_call | solution.py:257
  32.0 3.5 %collective-permute-start.13 = (bf16[1024,512]{1,0:T(8,128)(2,1)S(1)}, bf16[1024,512]{1,0:T(8,128)(2,1)S(1)}, u32[]{:S(2)}, u32[]{:S(2)}) collective-permute-start(bf16[1024,512]{1,0:T(8,128)(2,1)S(1)} %get-tuple-element.45), channel_id=1, source_target_pairs={{0,16},{16,0},{1,17},{17,1},{2,18},{18,2},{3,19},{19,3},{4,20},{20... | collective-permute-start | bytes 3145736 | tf_op jit(solution)/shard_map/ppermute | solution.py:51
  35.5 1.1 %collective-permute-start.12 = (bf16[256,512]{1,0:T(8,128)(2,1)S(1)}, bf16[256,512]{1,0:T(8,128)(2,1)S(1)}, u32[]{:S(2)}, u32[]{:S(2)}) collective-permute-start(bf16[256,512]{1,0:T(8,128)(2,1)S(1)} %collective-permute-done.10.refs_1_), channel_id=1, source_target_pairs={{0,16},{16,0},{1,17},{17,1},{2,18},{18,2},{3,19},{19,3},{4,20},{20... | collective-permute-start | bytes 786440 | tf_op jit(solution)/shard_map/ppermute | solution.py:51
  36.7 3.7 %collective-permute-start.8 = (bf16[256,512]{1,0:T(8,128)(2,1)S(1)}, bf16[256,512]{1,0:T(8,128)(2,1)S(1)}, u32[]{:S(2)}, u32[]{:S(2)}) collective-permute-start(bf16[256,512]{1,0:T(8,128)(2,1)S(1)} %collective-permute-done.7.refs_1_), channel_id=1, source_target_pairs={{0,16},{16,0},{1,17},{17,1},{2,18},{18,2},{3,19},{19,3},{4,20},{20... | collective-permute-start | bytes 786440 | tf_op jit(solution)/shard_map/ppermute | solution.py:51
  40.8 0.7 %add.15.mine_ref = f32[1024,512]{1,0:T(8,128)S(1)} custom-call(bf16[1024,2560]{1,0:T(8,128)(2,1)S(1)} %cauchy.3.refs_0_.c_ref, bf16[256,512]{1,0:T(8,128)(2,1)S(1)} %collective-permute-done.10.refs_1_, bf16[256,512]{1,0:T(8,128)(2,1)S(1)} %collective-permute-done.12.refs_2_, f32[1024,512]{1,0:T(8,128)S(1)} %add.14.refs_3_), custom_call_target="tpu_custom_call" | custom-call | flops 1 | bytes 1 | tf_op jit(solution)/shard_map/add/pallas_call | solution.py:281
  42.0 2.7 %collective-permute-start.14 = (bf16[256,512]{1,0:T(8,128)(2,1)S(1)}, bf16[256,512]{1,0:T(8,128)(2,1)S(1)}, u32[]{:S(2)}, u32[]{:S(2)}) collective-permute-start(bf16[256,512]{1,0:T(8,128)(2,1)S(1)} %get-tuple-element.47), channel_id=1, source_target_pairs={{0,1},{1,0},{32,33},{33,32},{2,3},{3,2},{34,35},{35,34},{4,5},{5,4... | collective-permute-start | bytes 786440 | tf_op jit(solution)/shard_map/ppermute | solution.py:41
  45.0 2.4 %collective-permute-start.16 = (bf16[256,512]{1,0:T(8,128)(2,1)S(1)}, bf16[256,512]{1,0:T(8,128)(2,1)S(1)}, u32[]{:S(2)}, u32[]{:S(2)}) collective-permute-start(bf16[256,512]{1,0:T(8,128)(2,1)S(1)} %get-tuple-element.49), channel_id=1, source_target_pairs={{0,33},{1,32},{32,0},{33,1},{2,35},{3,34},{34,2},{35,3},{4,37},{5,... | collective-permute-start | bytes 786440 | tf_op jit(solution)/shard_map/ppermute | solution.py:41
  47.4 3.4 %norms.1 = (f32[256,128]{1,0:T(8,128)S(1)}, bf16[512,512]{1,0:T(8,128)(2,1)}) custom-call(f32[128,128]{1,0:T(8,128)S(1)} %get-tuple-element.33.refs_1_.poles_ref, f32[128,128]{1,0:T(8,128)S(1)} %get-tuple-element.34.refs_2_.factors_ref, f32[1,512]{1,0:T(1,128)S(1)} %bitcast.7, bf16[512,256]{1,0:T(8,128)(2,1)S(1)} %get-tuple-element.51.rest_ref), custom_call_target="tpu_custom_call" | custom-call | flops 1 | bytes 1 | tf_op jit(solution)/shard_map/norms/pallas_call | solution.py:218
  51.2 6.2 %collective-permute-done.15.b_ref = bf16[256,512]{1,0:T(8,128)(2,1)S(1)} collective-permute-done((bf16[256,512]{1,0:T(8,128)(2,1)S(1)}, bf16[256,512]{1,0:T(8,128)(2,1)S(1)}, u32[]{:S(2)}, u32[]{:S(2)}) %collective-permute-start.15) | collective-permute-done | bytes 262176 | tf_op jit(solution)/shard_map/ppermute | solution.py:41
  57.5 1.5 %finish.1 = bf16[512,512]{1,0:T(8,128)(2,1)} custom-call(s32[1]{0:T(128)} %bitcast.refs_0_.me_ref, s32[64]{0:T(128)S(1)} %copy-done.2, f32[256,512]{1,0:T(8,128)S(1)} %get-tuple-element.46.own_ref, bf16[256,512]{1,0:T(8,128)(2,1)S(1)} %collective-permute-done.14.a_ref, ...), custom_call_target="tpu_custom_call", output_to_operand_aliasing={{}: (8, {})} | custom-call | flops 1 | bytes 1 | tf_op jit(solution)/shard_map/finish/pallas_call | solution.py:336
  (28 shorter events, 3.2 us)
Async XLA Ops:
  1.7 16.7 %collective-permute-start.6 = (bf16[256,512]{1,0:T(8,128)(2,1)S(1)}, bf16[256,512]{1,0:T(8,128)(2,1)S(1)}, u32[]{:S(2)}, u32[]{:S(2)}) collective-permute-start(bf16[256,512]{1,0:T(8,128)(2,1)S(1)} %get-tuple-element.30.refs_2_), channel_id=1, source_target_pairs={{0,14},{2,0},{4,2},{6,4},{8,6},{10,8},{12,10},{14,12},{16,18},{18,... | collective-permute-start | bytes 786440 | tf_op jit(solution)/shard_map/ppermute | solution.py:47
  4.3 14.1 %collective-permute-start.1 = (bf16[256,512]{1,0:T(8,128)(2,1)S(1)}, bf16[256,512]{1,0:T(8,128)(2,1)S(1)}, u32[]{:S(2)}, u32[]{:S(2)}) collective-permute-start(bf16[256,512]{1,0:T(8,128)(2,1)S(1)} %get-tuple-element.30.refs_2_), channel_id=1, source_target_pairs={{0,4},{2,6},{4,8},{6,10},{8,12},{10,14},{12,0},{14,2},{16,28},{18,... | collective-permute-start | bytes 786440 | tf_op jit(solution)/shard_map/ppermute | solution.py:47
  9.4 1.4 %collective-permute-start = (f32[1,512]{1,0:T(1,128)}, f32[1,512]{1,0:T(1,128)S(1)}, u32[]{:S(2)}, u32[]{:S(2)}) collective-permute-start(f32[1,512]{1,0:T(1,128)} %bitcast.5), channel_id=1, source_target_pairs={{0,16},{16,0},{1,17},{17,1},{2,18},{18,2},{3,19},{19,3},{4,20},{20... | collective-permute-start | bytes 6152 | tf_op jit(solution)/shard_map/ppermute | solution.py:51
  10.8 0.7 %copy-start = (f32[512]{0:T(512)S(1)}, f32[512]{0:T(512)}, u32[]{:S(2)}) copy-start(f32[512]{0:T(512)} %param.11) | copy-start | bytes 6148
  11.4 4.7 %collective-permute-start.2 = (f32[1,1024]{1,0:T(1,128)S(1)}, f32[1,1024]{1,0:T(1,128)S(1)}, u32[]{:S(2)}, u32[]{:S(2)}) collective-permute-start(f32[1,1024]{1,0:T(1,128)S(1)} %join.1.refs_3_), channel_id=1, source_target_pairs={{0,33},{1,32},{32,0},{33,1},{2,35},{3,34},{34,2},{35,3},{4,37},{5,... | collective-permute-start | bytes 12296 | tf_op jit(solution)/shard_map/ppermute | solution.py:41
  13.9 4.3 %collective-permute-start.3 = (f32[1,1024]{1,0:T(1,128)S(1)}, f32[1,1024]{1,0:T(1,128)S(1)}, u32[]{:S(2)}, u32[]{:S(2)}) collective-permute-start(f32[1,1024]{1,0:T(1,128)S(1)} %join.1.refs_3_), channel_id=1, source_target_pairs={{0,1},{1,0},{32,33},{33,32},{2,3},{3,2},{34,35},{35,34},{4,5},{5,4... | collective-permute-start | bytes 12296 | tf_op jit(solution)/shard_map/ppermute | solution.py:41
  14.4 4.0 %collective-permute-start.4 = (f32[1,1024]{1,0:T(1,128)S(1)}, f32[1,1024]{1,0:T(1,128)S(1)}, u32[]{:S(2)}, u32[]{:S(2)}) collective-permute-start(f32[1,1024]{1,0:T(1,128)S(1)} %join.1.refs_3_), channel_id=1, source_target_pairs={{0,32},{1,33},{32,1},{33,0},{2,34},{3,35},{34,3},{35,2},{4,36},{5,... | collective-permute-start | bytes 12296 | tf_op jit(solution)/shard_map/ppermute | solution.py:41
  18.4 9.0 %collective-permute-start.9 = (bf16[256,512]{1,0:T(8,128)(2,1)S(1)}, bf16[256,512]{1,0:T(8,128)(2,1)S(1)}, u32[]{:S(2)}, u32[]{:S(2)}) collective-permute-start(bf16[256,512]{1,0:T(8,128)(2,1)S(1)} %collective-permute-done.6.refs_3_), channel_id=1, source_target_pairs={{0,14},{2,0},{4,2},{6,4},{8,6},{10,8},{12,10},{14,12},{16,18},{18,... | collective-permute-start | bytes 786440 | tf_op jit(solution)/shard_map/ppermute | solution.py:47
  18.4 9.1 %collective-permute-start.5 = (bf16[256,512]{1,0:T(8,128)(2,1)S(1)}, bf16[256,512]{1,0:T(8,128)(2,1)S(1)}, u32[]{:S(2)}, u32[]{:S(2)}) collective-permute-start(bf16[256,512]{1,0:T(8,128)(2,1)S(1)} %collective-permute-done.1.refs_4_), channel_id=1, source_target_pairs={{0,2},{2,4},{4,6},{6,8},{8,10},{10,12},{12,14},{14,0},{16,30},{18,... | collective-permute-start | bytes 786440 | tf_op jit(solution)/shard_map/ppermute | solution.py:47
  21.1 9.0 %collective-permute-start.11 = (bf16[256,512]{1,0:T(8,128)(2,1)S(1)}, bf16[256,512]{1,0:T(8,128)(2,1)S(1)}, u32[]{:S(2)}, u32[]{:S(2)}) collective-permute-start(bf16[256,512]{1,0:T(8,128)(2,1)S(1)} %get-tuple-element.30.refs_2_), channel_id=1, source_target_pairs={{0,2},{2,4},{4,6},{6,8},{8,10},{10,12},{12,14},{14,0},{16,30},{18,... | collective-permute-start | bytes 786440 | tf_op jit(solution)/shard_map/ppermute | solution.py:47
  27.4 8.1 %collective-permute-start.10 = (bf16[256,512]{1,0:T(8,128)(2,1)S(1)}, bf16[256,512]{1,0:T(8,128)(2,1)S(1)}, u32[]{:S(2)}, u32[]{:S(2)}) collective-permute-start(bf16[256,512]{1,0:T(8,128)(2,1)S(1)} %collective-permute-done.9.refs_3_), channel_id=1, source_target_pairs={{0,14},{2,0},{4,2},{6,4},{8,6},{10,8},{12,10},{14,12},{16,18},{18,... | collective-permute-start | bytes 786440 | tf_op jit(solution)/shard_map/ppermute | solution.py:47
  27.5 9.2 %collective-permute-start.7 = (bf16[256,512]{1,0:T(8,128)(2,1)S(1)}, bf16[256,512]{1,0:T(8,128)(2,1)S(1)}, u32[]{:S(2)}, u32[]{:S(2)}) collective-permute-start(bf16[256,512]{1,0:T(8,128)(2,1)S(1)} %collective-permute-done.5.refs_4_), channel_id=1, source_target_pairs={{0,2},{2,4},{4,6},{6,8},{8,10},{10,12},{12,14},{14,0},{16,30},{18,... | collective-permute-start | bytes 786440 | tf_op jit(solution)/shard_map/ppermute | solution.py:47
  32.0 9.6 %collective-permute-start.13 = (bf16[1024,512]{1,0:T(8,128)(2,1)S(1)}, bf16[1024,512]{1,0:T(8,128)(2,1)S(1)}, u32[]{:S(2)}, u32[]{:S(2)}) collective-permute-start(bf16[1024,512]{1,0:T(8,128)(2,1)S(1)} %get-tuple-element.45), channel_id=1, source_target_pairs={{0,16},{16,0},{1,17},{17,1},{2,18},{18,2},{3,19},{19,3},{4,20},{20... | collective-permute-start | bytes 3145736 | tf_op jit(solution)/shard_map/ppermute | solution.py:51
  35.5 5.3 %collective-permute-start.12 = (bf16[256,512]{1,0:T(8,128)(2,1)S(1)}, bf16[256,512]{1,0:T(8,128)(2,1)S(1)}, u32[]{:S(2)}, u32[]{:S(2)}) collective-permute-start(bf16[256,512]{1,0:T(8,128)(2,1)S(1)} %collective-permute-done.10.refs_1_), channel_id=1, source_target_pairs={{0,16},{16,0},{1,17},{17,1},{2,18},{18,2},{3,19},{19,3},{4,20},{20... | collective-permute-start | bytes 786440 | tf_op jit(solution)/shard_map/ppermute | solution.py:51
  36.7 4.9 %collective-permute-start.8 = (bf16[256,512]{1,0:T(8,128)(2,1)S(1)}, bf16[256,512]{1,0:T(8,128)(2,1)S(1)}, u32[]{:S(2)}, u32[]{:S(2)}) collective-permute-start(bf16[256,512]{1,0:T(8,128)(2,1)S(1)} %collective-permute-done.7.refs_1_), channel_id=1, source_target_pairs={{0,16},{16,0},{1,17},{17,1},{2,18},{18,2},{3,19},{19,3},{4,20},{20... | collective-permute-start | bytes 786440 | tf_op jit(solution)/shard_map/ppermute | solution.py:51
  41.5 5.8 %copy-start.1 = (f32[512]{0:T(512)S(1)}, f32[512]{0:T(512)}, u32[]{:S(2)}) copy-start(f32[512]{0:T(512)} %param.11) | copy-start | bytes 6148
  41.5 15.9 %copy-start.2 = (s32[64]{0:T(128)S(1)}, s32[64]{0:T(128)}, u32[]{:S(2)}) copy-start(s32[64]{0:T(128)} %counts_ref.1) | copy-start | bytes 772
  42.0 9.2 %collective-permute-start.14 = (bf16[256,512]{1,0:T(8,128)(2,1)S(1)}, bf16[256,512]{1,0:T(8,128)(2,1)S(1)}, u32[]{:S(2)}, u32[]{:S(2)}) collective-permute-start(bf16[256,512]{1,0:T(8,128)(2,1)S(1)} %get-tuple-element.47), channel_id=1, source_target_pairs={{0,1},{1,0},{32,33},{33,32},{2,3},{3,2},{34,35},{35,34},{4,5},{5,4... | collective-permute-start | bytes 786440 | tf_op jit(solution)/shard_map/ppermute | solution.py:41
  44.7 12.8 %collective-permute-start.15 = (bf16[256,512]{1,0:T(8,128)(2,1)S(1)}, bf16[256,512]{1,0:T(8,128)(2,1)S(1)}, u32[]{:S(2)}, u32[]{:S(2)}) collective-permute-start(bf16[256,512]{1,0:T(8,128)(2,1)S(1)} %get-tuple-element.48), channel_id=1, source_target_pairs={{0,32},{1,33},{32,1},{33,0},{2,34},{3,35},{34,3},{35,2},{4,36},{5,... | collective-permute-start | bytes 786440 | tf_op jit(solution)/shard_map/ppermute | solution.py:41
  45.0 12.5 %collective-permute-start.16 = (bf16[256,512]{1,0:T(8,128)(2,1)S(1)}, bf16[256,512]{1,0:T(8,128)(2,1)S(1)}, u32[]{:S(2)}, u32[]{:S(2)}) collective-permute-start(bf16[256,512]{1,0:T(8,128)(2,1)S(1)} %get-tuple-element.49), channel_id=1, source_target_pairs={{0,33},{1,32},{32,0},{33,1},{2,35},{3,34},{34,2},{35,3},{4,37},{5,... | collective-permute-start | bytes 786440 | tf_op jit(solution)/shard_map/ppermute | solution.py:41

commit v12 on v11

--- a/solution.py
+++ b/solution.py
@@ -360,13 +360,13 @@
     table, factors = tables(
         hold(in_hbm(counts), near), in_hbm(poles.reshape(-1, LANES)), in_hbm(weights.reshape(-1, LANES))
     )
-    p4 = around(hold(p2, factors, *far), -1)
-    p5 = around(hold(p3, *far), 1)
+    p4 = around(hold(p2, factors, far[0]), -1)
+    p5 = around(hold(p3, far[0]), 1)
     c_other = cauchy(1, OTHER, me, table, factors, [hold(near, p3), *far])
     c_mine = cauchy(0, MINE, me, table, factors, [hold(near, c_other), *far])
-    p6 = around(hold(p4, c_mine), -1)
-    sums = stage(0, c_mine, c_other, (own, p2, p3), (), False)
-    p7 = around(hold(p5, sums[0]), 1)
+    p6 = around(hold(p4, *far), -1)
+    sums = stage(0, c_mine, c_other, (hold(own, p5), p2, p3), (), False)
+    p7 = around(hold(p5, *far), 1)
     mine, other = stage(3, c_mine, c_other, (p1, p4, p5), sums, True)
     other = cshift(other)
     p6 = hold(p6, mine)

time: 59.2 us -> 61 us (1.030)
  waiting for transfers between devices: 10.4 us -> 16.6 us
  starting transfers between devices: 32.1 us -> 27.7 us
    ppermute x4, starting transfers between devices: 8.38 us -> 2.7 us  [cshift(): return lax.ppermute(a, 'core', [(0, 1), (1, 0)])]
    ppermute x7, waiting for transfers between devices: 0.02 us -> 3.15 us  [around(): return lax.ppermute(a, ('core', 'z'), up + down)]
    ppermute x6, waiting for transfers between devices: 8.99 us -> 11 us  [xshift(): return lax.ppermute(a, ('xl', 'xh'), pairs)]
    ppermute x6, starting transfers between devices: 8.95 us -> 10.2 us  [xshift(): return lax.ppermute(a, ('xl', 'xh'), pairs)]
    ppermute x4, waiting for transfers between devices: 1.37 us -> 2.46 us  [cshift(): return lax.ppermute(a, 'core', [(0, 1), (1, 0)])]
  transfers between devices with their start and end apart: 17 -> 17, of which waited for: 5 -> 7; matrix products, arithmetic and copies ran while one was open for 0% -> 0% of each run, Pallas kernels for 20% -> 20%
where the time goes in v12:
time: 61 us; the launch traced here: 60.8 us
  starting transfers between devices  27.7 us (45%)
  waiting for transfers between devices  16.6 us (27%)
  Pallas kernels  15.6 us (26%)
  local copies, waits for them, and re-layouts  0.69 us (1%)
    ppermute x7, starting transfers between devices, around(): return lax.ppermute(a, ('core', 'z'), up + down)  14.8 us
    ppermute x6, waiting for transfers between devices, xshift(): return lax.ppermute(a, ('xl', 'xh'), pairs)  11 us
    ppermute x6, starting transfers between devices, xshift(): return lax.ppermute(a, ('xl', 'xh'), pairs)  10.2 us
    pallas_call x2, Pallas kernels, stage(): pl.pallas_call(lambda *refs: stage_kernel(first, len(pieces), *refs), in_...  3.61 us
    pallas_call x1, Pallas kernels, norms(): pl.pallas_call(norm_kernel, in_specs=[VM] * 4, out_specs=[VM, HB], out_sh...  3.38 us
    ppermute x7, waiting for transfers between devices, around(): return lax.ppermute(a, ('core', 'z'), up + down)  3.15 us
    pallas_call x2, Pallas kernels, cauchy(): pl.pallas_call(lambda *refs: cauchy_kernel(fc, pieces, *refs), in_specs=[...  2.72 us
    ppermute x4, starting transfers between devices, cshift(): return lax.ppermute(a, 'core', [(0, 1), (1, 0)])  2.7 us
  transfers between devices with their start and end apart: 17, of which 7 were waited for; matrix products, arithmetic and copies ran while one was open for 0% of the time, Pallas kernels for 20%

profile of v12, /device:TPU:1, one launch (start us, length us, event | category | flops | bytes accessed | tf_op | source)
XLA Modules:
  0.0 60.8 jit_solution(16539033319338372667)
XLA Ops:
  0.0 1.7 %permute.1 = (bf16[256,512]{1,0:T(8,128)(2,1)S(1)}, bf16[512,256]{1,0:T(8,128)(2,1)S(1)}, bf16[512,256]{1,0:T(8,128)(2,1)S(1)}) custom-call(bf16[512,512]{1,0:T(8,128)(2,1)} %e_hbm.1, s32[1,512]{1,0:T(1,128)} %bitcast.10), custom_call_target="tpu_custom_call" | custom-call | flops 1 | bytes 1 | tf_op jit(solution)/shard_map/permute/pallas_call | solution.py:86
  1.7 2.5 %collective-permute-start.8 = (bf16[256,512]{1,0:T(8,128)(2,1)S(1)}, bf16[256,512]{1,0:T(8,128)(2,1)S(1)}, u32[]{:S(2)}, u32[]{:S(2)}) collective-permute-start(bf16[256,512]{1,0:T(8,128)(2,1)S(1)} %get-tuple-element.42.refs_2_), channel_id=1, source_target_pairs={{0,14},{2,0},{4,2},{6,4},{8,6},{10,8},{12,10},{14,12},{16,18},{18,... | collective-permute-start | bytes 786440 | tf_op jit(solution)/shard_map/ppermute | solution.py:47
  4.3 5.1 %collective-permute-start.1 = (bf16[256,512]{1,0:T(8,128)(2,1)S(1)}, bf16[256,512]{1,0:T(8,128)(2,1)S(1)}, u32[]{:S(2)}, u32[]{:S(2)}) collective-permute-start(bf16[256,512]{1,0:T(8,128)(2,1)S(1)} %get-tuple-element.42.refs_2_), channel_id=1, source_target_pairs={{0,4},{2,6},{4,8},{6,10},{8,12},{10,14},{12,0},{14,2},{16,28},{18,... | collective-permute-start | bytes 786440 | tf_op jit(solution)/shard_map/ppermute | solution.py:47
  9.4 1.4 %collective-permute-done.b_ref = f32[1,512]{1,0:T(1,128)S(1)} collective-permute-done((f32[1,512]{1,0:T(1,128)}, f32[1,512]{1,0:T(1,128)S(1)}, u32[]{:S(2)}, u32[]{:S(2)}) %collective-permute-start) | collective-permute-done | bytes 2080 | tf_op jit(solution)/shard_map/ppermute | solution.py:51
  11.4 2.5 %collective-permute-start.2 = (f32[1,1024]{1,0:T(1,128)S(1)}, f32[1,1024]{1,0:T(1,128)S(1)}, u32[]{:S(2)}, u32[]{:S(2)}) collective-permute-start(f32[1,1024]{1,0:T(1,128)S(1)} %join.1.refs_3_), channel_id=1, source_target_pairs={{0,33},{1,32},{32,0},{33,1},{2,35},{3,34},{34,2},{35,3},{4,37},{5,... | collective-permute-start | bytes 12296 | tf_op jit(solution)/shard_map/ppermute | solution.py:41
  13.9 1.1 %tables.1 = (f32[128,128]{1,0:T(8,128)S(1)}, f32[128,128]{1,0:T(8,128)S(1)}) custom-call(s32[64]{0:T(128)} %counts_ref.1, f32[256,128]{1,0:T(8,128)} %bitcast.8, f32[256,128]{1,0:T(8,128)} %bitcast.9), custom_call_target="tpu_custom_call" | custom-call | flops 1 | bytes 1 | tf_op jit(solution)/shard_map/tables/pallas_call | solution.py:128
  15.2 3.1 %collective-permute-done.1.refs_4_ = bf16[256,512]{1,0:T(8,128)(2,1)S(1)} collective-permute-done((bf16[256,512]{1,0:T(8,128)(2,1)S(1)}, bf16[256,512]{1,0:T(8,128)(2,1)S(1)}, u32[]{:S(2)}, u32[]{:S(2)}) %collective-permute-start.1) | collective-permute-done | bytes 262176 | tf_op jit(solution)/shard_map/ppermute | solution.py:47
  18.8 3.7 %collective-permute-start.11 = (bf16[256,512]{1,0:T(8,128)(2,1)S(1)}, bf16[256,512]{1,0:T(8,128)(2,1)S(1)}, u32[]{:S(2)}, u32[]{:S(2)}) collective-permute-start(bf16[256,512]{1,0:T(8,128)(2,1)S(1)} %get-tuple-element.42.refs_2_), channel_id=1, source_target_pairs={{0,2},{2,4},{4,6},{6,8},{8,10},{10,12},{12,14},{14,0},{16,30},{18,... | collective-permute-start | bytes 786440 | tf_op jit(solution)/shard_map/ppermute | solution.py:47
  22.6 2.7 %collective-permute-start.3 = (f32[1,1024]{1,0:T(1,128)S(1)}, f32[1,1024]{1,0:T(1,128)S(1)}, u32[]{:S(2)}, u32[]{:S(2)}) collective-permute-start(f32[1,1024]{1,0:T(1,128)S(1)} %join.1.refs_3_), channel_id=1, source_target_pairs={{0,1},{1,0},{32,33},{33,32},{2,3},{3,2},{34,35},{35,34},{4,5},{5,4... | collective-permute-start | bytes 12296 | tf_op jit(solution)/shard_map/ppermute | solution.py:41
  26.5 2.7 %collective-permute-done.4.refs_6_ = f32[1,1024]{1,0:T(1,128)S(1)} collective-permute-done((f32[1,1024]{1,0:T(1,128)S(1)}, f32[1,1024]{1,0:T(1,128)S(1)}, u32[]{:S(2)}, u32[]{:S(2)}) %collective-permute-start.4) | collective-permute-done | bytes 4128 | tf_op jit(solution)/shard_map/ppermute | solution.py:41
  29.2 2.7 %collective-permute-start.6 = (bf16[256,512]{1,0:T(8,128)(2,1)S(1)}, bf16[256,512]{1,0:T(8,128)(2,1)S(1)}, u32[]{:S(2)}, u32[]{:S(2)}) collective-permute-start(bf16[256,512]{1,0:T(8,128)(2,1)S(1)} %collective-permute-done.5.refs_4_), channel_id=1, source_target_pairs={{0,2},{2,4},{4,6},{6,8},{8,10},{10,12},{12,14},{14,0},{16,30},{18,... | collective-permute-start | bytes 786440 | tf_op jit(solution)/shard_map/ppermute | solution.py:47
  31.9 1.1 %cauchy.2.refs_1_ = bf16[1024,1536]{1,0:T(8,128)(2,1)S(1)} custom-call(s32[1]{0:T(128)} %bitcast.refs_0_.me_ref, f32[128,128]{1,0:T(8,128)S(1)} %get-tuple-element.34.refs_1_.poles_ref, f32[128,128]{1,0:T(8,128)S(1)} %get-tuple-element.35.refs_2_.factors_ref, f32[1,1024]{1,0:T(1,128)S(1)} %join.1.refs_3_, f32[1,1024]{1,0:T(1,128)S(1)} %collective-permute-done.2.refs_4_, ...), custom_call_target="tpu_custom_call" | custom-call | flops 1 | bytes 1 | tf_op jit(solution)/shard_map/cauchy/pallas_call | solution.py:185
  33.0 1.7 %cauchy.3.refs_0_.c_ref = bf16[1024,2560]{1,0:T(8,128)(2,1)S(1)} custom-call(s32[1]{0:T(128)} %bitcast.refs_0_.me_ref, f32[128,128]{1,0:T(8,128)S(1)} %get-tuple-element.34.refs_1_.poles_ref, f32[128,128]{1,0:T(8,128)S(1)} %get-tuple-element.35.refs_2_.factors_ref, f32[1,1024]{1,0:T(1,128)S(1)} %join.1.refs_3_, ...), custom_call_target="tpu_custom_call" | custom-call | flops 1 | bytes 1 | tf_op jit(solution)/shard_map/cauchy/pallas_call | solution.py:185
  34.6 1.8 %stage.2 = (f32[1024,512]{1,0:T(8,128)S(1)}, f32[1024,512]{1,0:T(8,128)S(1)}) custom-call(bf16[1024,2560]{1,0:T(8,128)(2,1)S(1)} %cauchy.3.refs_0_.c_ref, bf16[1024,1536]{1,0:T(8,128)(2,1)S(1)} %cauchy.2.refs_1_, bf16[256,512]{1,0:T(8,128)(2,1)S(1)} %get-tuple-element.42.refs_2_, bf16[256,512]{1,0:T(8,128)(2,1)S(1)} %collective-permute-done.8.refs_3_, ...), custom_call_target="tpu_custom_call" | custom-call | flops 1 | bytes 1 | tf_op jit(solution)/shard_map/stage/pallas_call | solution.py:257
  36.4 1.8 %stage.3 = (f32[1024,512]{1,0:T(8,128)S(1)}, bf16[1024,512]{1,0:T(8,128)(2,1)S(1)}) custom-call(bf16[1024,2560]{1,0:T(8,128)(2,1)S(1)} %cauchy.3.refs_0_.c_ref, bf16[1024,1536]{1,0:T(8,128)(2,1)S(1)} %cauchy.2.refs_1_, bf16[256,512]{1,0:T(8,128)(2,1)S(1)} %collective-permute-done.11.refs_2_, bf16[256,512]{1,0:T(8,128)(2,1)S(1)} %collective-permute-done.9.refs_3_, ...), custom_call_target="tpu_custom_call" | custom-call | flops 1 | bytes 1 | tf_op jit(solution)/shard_map/stage/pallas_call | solution.py:257
  38.3 1.6 %collective-permute-start.13 = (bf16[1024,512]{1,0:T(8,128)(2,1)S(1)}, bf16[1024,512]{1,0:T(8,128)(2,1)S(1)}, u32[]{:S(2)}, u32[]{:S(2)}) collective-permute-start(bf16[1024,512]{1,0:T(8,128)(2,1)S(1)} %get-tuple-element.47), channel_id=1, source_target_pairs={{0,16},{16,0},{1,17},{17,1},{2,18},{18,2},{3,19},{19,3},{4,20},{20... | collective-permute-start | bytes 3145736 | tf_op jit(solution)/shard_map/ppermute | solution.py:51
  40.0 1.0 %collective-permute-start.7 = (bf16[256,512]{1,0:T(8,128)(2,1)S(1)}, bf16[256,512]{1,0:T(8,128)(2,1)S(1)}, u32[]{:S(2)}, u32[]{:S(2)}) collective-permute-start(bf16[256,512]{1,0:T(8,128)(2,1)S(1)} %collective-permute-done.6.refs_1_), channel_id=1, source_target_pairs={{0,16},{16,0},{1,17},{17,1},{2,18},{18,2},{3,19},{19,3},{4,20},{20... | collective-permute-start | bytes 786440 | tf_op jit(solution)/shard_map/ppermute | solution.py:51
  41.4 1.1 %collective-permute-done.12.refs_2_ = bf16[256,512]{1,0:T(8,128)(2,1)S(1)} collective-permute-done((bf16[256,512]{1,0:T(8,128)(2,1)S(1)}, bf16[256,512]{1,0:T(8,128)(2,1)S(1)}, u32[]{:S(2)}, u32[]{:S(2)}) %collective-permute-start.12) | collective-permute-done | bytes 262176 | tf_op jit(solution)/shard_map/ppermute | solution.py:51
  43.7 2.0 %collective-permute-start.14 = (bf16[256,512]{1,0:T(8,128)(2,1)S(1)}, bf16[256,512]{1,0:T(8,128)(2,1)S(1)}, u32[]{:S(2)}, u32[]{:S(2)}) collective-permute-start(bf16[256,512]{1,0:T(8,128)(2,1)S(1)} %get-tuple-element.49), channel_id=1, source_target_pairs={{0,1},{1,0},{32,33},{33,32},{2,3},{3,2},{34,35},{35,34},{4,5},{5,4... | collective-permute-start | bytes 786440 | tf_op jit(solution)/shard_map/ppermute | solution.py:41
  46.1 2.4 %collective-permute-start.16 = (bf16[256,512]{1,0:T(8,128)(2,1)S(1)}, bf16[256,512]{1,0:T(8,128)(2,1)S(1)}, u32[]{:S(2)}, u32[]{:S(2)}) collective-permute-start(bf16[256,512]{1,0:T(8,128)(2,1)S(1)} %get-tuple-element.51), channel_id=1, source_target_pairs={{0,33},{1,32},{32,0},{33,1},{2,35},{3,34},{34,2},{35,3},{4,37},{5,... | collective-permute-start | bytes 786440 | tf_op jit(solution)/shard_map/ppermute | solution.py:41
  48.4 3.4 %norms.1 = (f32[256,128]{1,0:T(8,128)S(1)}, bf16[512,512]{1,0:T(8,128)(2,1)}) custom-call(f32[128,128]{1,0:T(8,128)S(1)} %get-tuple-element.34.refs_1_.poles_ref, f32[128,128]{1,0:T(8,128)S(1)} %get-tuple-element.35.refs_2_.factors_ref, f32[1,512]{1,0:T(1,128)S(1)} %bitcast.7, bf16[512,256]{1,0:T(8,128)(2,1)S(1)} %get-tuple-element.53.rest_ref), custom_call_target="tpu_custom_call" | custom-call | flops 1 | bytes 1 | tf_op jit(solution)/shard_map/norms/pallas_call | solution.py:218
  51.8 1.0 %collective-permute-done.14.a_ref = bf16[256,512]{1,0:T(8,128)(2,1)S(1)} collective-permute-done((bf16[256,512]{1,0:T(8,128)(2,1)S(1)}, bf16[256,512]{1,0:T(8,128)(2,1)S(1)}, u32[]{:S(2)}, u32[]{:S(2)}) %collective-permute-start.14) | collective-permute-done | bytes 262176 | tf_op jit(solution)/shard_map/ppermute | solution.py:41
  52.9 6.3 %collective-permute-done.15.b_ref = bf16[256,512]{1,0:T(8,128)(2,1)S(1)} collective-permute-done((bf16[256,512]{1,0:T(8,128)(2,1)S(1)}, bf16[256,512]{1,0:T(8,128)(2,1)S(1)}, u32[]{:S(2)}, u32[]{:S(2)}) %collective-permute-start.15) | collective-permute-done | bytes 262176 | tf_op jit(solution)/shard_map/ppermute | solution.py:41
  59.2 1.5 %finish.1 = bf16[512,512]{1,0:T(8,128)(2,1)} custom-call(s32[1]{0:T(128)} %bitcast.refs_0_.me_ref, s32[64]{0:T(128)S(1)} %copy-done.2, f32[256,512]{1,0:T(8,128)S(1)} %get-tuple-element.48.own_ref, bf16[256,512]{1,0:T(8,128)(2,1)S(1)} %collective-permute-done.14.a_ref, ...), custom_call_target="tpu_custom_call", output_to_operand_aliasing={{}: (8, {})} | custom-call | flops 1 | bytes 1 | tf_op jit(solution)/shard_map/finish/pallas_call | solution.py:336
  (28 shorter events, 4.7 us)
Async XLA Ops:
  1.7 13.3 %collective-permute-start.8 = (bf16[256,512]{1,0:T(8,128)(2,1)S(1)}, bf16[256,512]{1,0:T(8,128)(2,1)S(1)}, u32[]{:S(2)}, u32[]{:S(2)}) collective-permute-start(bf16[256,512]{1,0:T(8,128)(2,1)S(1)} %get-tuple-element.42.refs_2_), channel_id=1, source_target_pairs={{0,14},{2,0},{4,2},{6,4},{8,6},{10,8},{12,10},{14,12},{16,18},{18,... | collective-permute-start | bytes 786440 | tf_op jit(solution)/shard_map/ppermute | solution.py:47
  4.3 14.0 %collective-permute-start.1 = (bf16[256,512]{1,0:T(8,128)(2,1)S(1)}, bf16[256,512]{1,0:T(8,128)(2,1)S(1)}, u32[]{:S(2)}, u32[]{:S(2)}) collective-permute-start(bf16[256,512]{1,0:T(8,128)(2,1)S(1)} %get-tuple-element.42.refs_2_), channel_id=1, source_target_pairs={{0,4},{2,6},{4,8},{6,10},{8,12},{10,14},{12,0},{14,2},{16,28},{18,... | collective-permute-start | bytes 786440 | tf_op jit(solution)/shard_map/ppermute | solution.py:47
  9.4 1.4 %collective-permute-start = (f32[1,512]{1,0:T(1,128)}, f32[1,512]{1,0:T(1,128)S(1)}, u32[]{:S(2)}, u32[]{:S(2)}) collective-permute-start(f32[1,512]{1,0:T(1,128)} %bitcast.5), channel_id=1, source_target_pairs={{0,16},{16,0},{1,17},{17,1},{2,18},{18,2},{3,19},{19,3},{4,20},{20... | collective-permute-start | bytes 6152 | tf_op jit(solution)/shard_map/ppermute | solution.py:51
  10.8 0.7 %copy-start = (f32[512]{0:T(512)S(1)}, f32[512]{0:T(512)}, u32[]{:S(2)}) copy-start(f32[512]{0:T(512)} %param.11) | copy-start | bytes 6148
  11.4 3.5 %collective-permute-start.2 = (f32[1,1024]{1,0:T(1,128)S(1)}, f32[1,1024]{1,0:T(1,128)S(1)}, u32[]{:S(2)}, u32[]{:S(2)}) collective-permute-start(f32[1,1024]{1,0:T(1,128)S(1)} %join.1.refs_3_), channel_id=1, source_target_pairs={{0,33},{1,32},{32,0},{33,1},{2,35},{3,34},{34,2},{35,3},{4,37},{5,... | collective-permute-start | bytes 12296 | tf_op jit(solution)/shard_map/ppermute | solution.py:41
  15.0 14.2 %collective-permute-start.9 = (bf16[256,512]{1,0:T(8,128)(2,1)S(1)}, bf16[256,512]{1,0:T(8,128)(2,1)S(1)}, u32[]{:S(2)}, u32[]{:S(2)}) collective-permute-start(bf16[256,512]{1,0:T(8,128)(2,1)S(1)} %collective-permute-done.8.refs_3_), channel_id=1, source_target_pairs={{0,14},{2,0},{4,2},{6,4},{8,6},{10,8},{12,10},{14,12},{16,18},{18,... | collective-permute-start | bytes 786440 | tf_op jit(solution)/shard_map/ppermute | solution.py:47
  18.3 10.9 %collective-permute-start.5 = (bf16[256,512]{1,0:T(8,128)(2,1)S(1)}, bf16[256,512]{1,0:T(8,128)(2,1)S(1)}, u32[]{:S(2)}, u32[]{:S(2)}) collective-permute-start(bf16[256,512]{1,0:T(8,128)(2,1)S(1)} %collective-permute-done.1.refs_4_), channel_id=1, source_target_pairs={{0,2},{2,4},{4,6},{6,8},{8,10},{10,12},{12,14},{14,0},{16,30},{18,... | collective-permute-start | bytes 786440 | tf_op jit(solution)/shard_map/ppermute | solution.py:47
  18.8 17.6 %collective-permute-start.11 = (bf16[256,512]{1,0:T(8,128)(2,1)S(1)}, bf16[256,512]{1,0:T(8,128)(2,1)S(1)}, u32[]{:S(2)}, u32[]{:S(2)}) collective-permute-start(bf16[256,512]{1,0:T(8,128)(2,1)S(1)} %get-tuple-element.42.refs_2_), channel_id=1, source_target_pairs={{0,2},{2,4},{4,6},{6,8},{8,10},{10,12},{12,14},{14,0},{16,30},{18,... | collective-permute-start | bytes 786440 | tf_op jit(solution)/shard_map/ppermute | solution.py:47
  22.6 4.0 %collective-permute-start.3 = (f32[1,1024]{1,0:T(1,128)S(1)}, f32[1,1024]{1,0:T(1,128)S(1)}, u32[]{:S(2)}, u32[]{:S(2)}) collective-permute-start(f32[1,1024]{1,0:T(1,128)S(1)} %join.1.refs_3_), channel_id=1, source_target_pairs={{0,1},{1,0},{32,33},{33,32},{2,3},{3,2},{34,35},{35,34},{4,5},{5,4... | collective-permute-start | bytes 12296 | tf_op jit(solution)/shard_map/ppermute | solution.py:41
  25.3 4.0 %collective-permute-start.4 = (f32[1,1024]{1,0:T(1,128)S(1)}, f32[1,1024]{1,0:T(1,128)S(1)}, u32[]{:S(2)}, u32[]{:S(2)}) collective-permute-start(f32[1,1024]{1,0:T(1,128)S(1)} %join.1.refs_3_), channel_id=1, source_target_pairs={{0,32},{1,33},{32,1},{33,0},{2,34},{3,35},{34,3},{35,2},{4,36},{5,... | collective-permute-start | bytes 12296 | tf_op jit(solution)/shard_map/ppermute | solution.py:41
  29.2 10.6 %collective-permute-start.10 = (bf16[256,512]{1,0:T(8,128)(2,1)S(1)}, bf16[256,512]{1,0:T(8,128)(2,1)S(1)}, u32[]{:S(2)}, u32[]{:S(2)}) collective-permute-start(bf16[256,512]{1,0:T(8,128)(2,1)S(1)} %collective-permute-done.9.refs_3_), channel_id=1, source_target_pairs={{0,14},{2,0},{4,2},{6,4},{8,6},{10,8},{12,10},{14,12},{16,18},{18,... | collective-permute-start | bytes 786440 | tf_op jit(solution)/shard_map/ppermute | solution.py:47
  29.2 10.7 %collective-permute-start.6 = (bf16[256,512]{1,0:T(8,128)(2,1)S(1)}, bf16[256,512]{1,0:T(8,128)(2,1)S(1)}, u32[]{:S(2)}, u32[]{:S(2)}) collective-permute-start(bf16[256,512]{1,0:T(8,128)(2,1)S(1)} %collective-permute-done.5.refs_4_), channel_id=1, source_target_pairs={{0,2},{2,4},{4,6},{6,8},{8,10},{10,12},{12,14},{14,0},{16,30},{18,... | collective-permute-start | bytes 786440 | tf_op jit(solution)/shard_map/ppermute | solution.py:47
  38.3 5.0 %collective-permute-start.13 = (bf16[1024,512]{1,0:T(8,128)(2,1)S(1)}, bf16[1024,512]{1,0:T(8,128)(2,1)S(1)}, u32[]{:S(2)}, u32[]{:S(2)}) collective-permute-start(bf16[1024,512]{1,0:T(8,128)(2,1)S(1)} %get-tuple-element.47), channel_id=1, source_target_pairs={{0,16},{16,0},{1,17},{17,1},{2,18},{18,2},{3,19},{19,3},{4,20},{20... | collective-permute-start | bytes 3145736 | tf_op jit(solution)/shard_map/ppermute | solution.py:51
  39.9 2.7 %collective-permute-start.12 = (bf16[256,512]{1,0:T(8,128)(2,1)S(1)}, bf16[256,512]{1,0:T(8,128)(2,1)S(1)}, u32[]{:S(2)}, u32[]{:S(2)}) collective-permute-start(bf16[256,512]{1,0:T(8,128)(2,1)S(1)} %collective-permute-done.10.refs_1_), channel_id=1, source_target_pairs={{0,16},{16,0},{1,17},{17,1},{2,18},{18,2},{3,19},{19,3},{4,20},{20... | collective-permute-start | bytes 786440 | tf_op jit(solution)/shard_map/ppermute | solution.py:51
  40.0 3.3 %collective-permute-start.7 = (bf16[256,512]{1,0:T(8,128)(2,1)S(1)}, bf16[256,512]{1,0:T(8,128)(2,1)S(1)}, u32[]{:S(2)}, u32[]{:S(2)}) collective-permute-start(bf16[256,512]{1,0:T(8,128)(2,1)S(1)} %collective-permute-done.6.refs_1_), channel_id=1, source_target_pairs={{0,16},{16,0},{1,17},{17,1},{2,18},{18,2},{3,19},{19,3},{4,20},{20... | collective-permute-start | bytes 786440 | tf_op jit(solution)/shard_map/ppermute | solution.py:51
  43.2 5.2 %copy-start.1 = (f32[512]{0:T(512)S(1)}, f32[512]{0:T(512)}, u32[]{:S(2)}) copy-start(f32[512]{0:T(512)} %param.11) | copy-start | bytes 6148
  43.2 15.9 %copy-start.2 = (s32[64]{0:T(128)S(1)}, s32[64]{0:T(128)}, u32[]{:S(2)}) copy-start(s32[64]{0:T(128)} %counts_ref.1) | copy-start | bytes 772
  43.7 9.1 %collective-permute-start.14 = (bf16[256,512]{1,0:T(8,128)(2,1)S(1)}, bf16[256,512]{1,0:T(8,128)(2,1)S(1)}, u32[]{:S(2)}, u32[]{:S(2)}) collective-permute-start(bf16[256,512]{1,0:T(8,128)(2,1)S(1)} %get-tuple-element.49), channel_id=1, source_target_pairs={{0,1},{1,0},{32,33},{33,32},{2,3},{3,2},{34,35},{35,34},{4,5},{5,4... | collective-permute-start | bytes 786440 | tf_op jit(solution)/shard_map/ppermute | solution.py:41
  45.8 13.4 %collective-permute-start.15 = (bf16[256,512]{1,0:T(8,128)(2,1)S(1)}, bf16[256,512]{1,0:T(8,128)(2,1)S(1)}, u32[]{:S(2)}, u32[]{:S(2)}) collective-permute-start(bf16[256,512]{1,0:T(8,128)(2,1)S(1)} %get-tuple-element.50), channel_id=1, source_target_pairs={{0,32},{1,33},{32,1},{33,0},{2,34},{3,35},{34,3},{35,2},{4,36},{5,... | collective-permute-start | bytes 786440 | tf_op jit(solution)/shard_map/ppermute | solution.py:41
  46.1 13.1 %collective-permute-start.16 = (bf16[256,512]{1,0:T(8,128)(2,1)S(1)}, bf16[256,512]{1,0:T(8,128)(2,1)S(1)}, u32[]{:S(2)}, u32[]{:S(2)}) collective-permute-start(bf16[256,512]{1,0:T(8,128)(2,1)S(1)} %get-tuple-element.51), channel_id=1, source_target_pairs={{0,33},{1,32},{32,0},{33,1},{2,35},{3,34},{34,2},{35,3},{4,37},{5,... | collective-permute-start | bytes 786440 | tf_op jit(solution)/shard_map/ppermute | solution.py:41

commit v13 on v11

--- a/solution.py
+++ b/solution.py
@@ -374,7 +374,7 @@
     mine = add((7,), c_mine, (p7,), (mine,), LONG)
     mine = add((6, 8), c_mine, (p6, cshift(p6)), (mine,), TINY)
     own_sum, *sent = totals(c_mine, sibling, mine, other)
-    received = [xshift(sent[i], k) for i, k in ((1, 2), (0, 1), (2, -1))]
+    received = [xshift(sent[i], k) for i, k in ((0, 1), (2, -1), (1, 2))]
     norm, out = norms(table, factors, hold(roots, own_sum), rest)
     return finish(me, counts, own_sum, received, norm, lead, out)
 

time: 59.2 us -> 59.1 us (level)
  starting transfers between devices: 32.1 us -> 30.9 us
  waiting for transfers between devices: 10.4 us -> 11.5 us
    ppermute x6, starting transfers between devices: 8.95 us -> 7.73 us  [xshift(): return lax.ppermute(a, ('xl', 'xh'), pairs)]
    ppermute x6, waiting for transfers between devices: 8.99 us -> 10.1 us  [xshift(): return lax.ppermute(a, ('xl', 'xh'), pairs)]
where the time goes in v13:
time: 59.1 us; the launch traced here: 59 us
  starting transfers between devices  30.9 us (52%)
  Pallas kernels  15.5 us (26%)
  waiting for transfers between devices  11.5 us (19%)
  local copies, waits for them, and re-layouts  0.69 us (1%)
    ppermute x7, starting transfers between devices, around(): return lax.ppermute(a, ('core', 'z'), up + down)  14.8 us
    ppermute x6, waiting for transfers between devices, xshift(): return lax.ppermute(a, ('xl', 'xh'), pairs)  10.1 us
    ppermute x4, starting transfers between devices, cshift(): return lax.ppermute(a, 'core', [(0, 1), (1, 0)])  8.38 us
    ppermute x6, starting transfers between devices, xshift(): return lax.ppermute(a, ('xl', 'xh'), pairs)  7.73 us
    pallas_call x2, Pallas kernels, stage(): pl.pallas_call(lambda *refs: stage_kernel(first, len(pieces), *refs), in_...  3.61 us
    pallas_call x1, Pallas kernels, norms(): pl.pallas_call(norm_kernel, in_specs=[VM] * 4, out_specs=[VM, HB], out_sh...  3.38 us
    pallas_call x2, Pallas kernels, cauchy(): pl.pallas_call(lambda *refs: cauchy_kernel(fc, pieces, *refs), in_specs=[...  2.72 us
    pallas_call x1, Pallas kernels, permute(): pl.pallas_call(permute_kernel, in_specs=[HB, HB], out_specs=[VM] * 3, out...  1.72 us
  transfers between devices with their start and end apart: 17, of which 5 were waited for; matrix products, arithmetic and copies ran while one was open for 0% of the time, Pallas kernels for 20%

profile of v13, /device:TPU:1, one launch (start us, length us, event | category | flops | bytes accessed | tf_op | source)
XLA Modules:
  0.0 59.0 jit_solution(7656669273357484733)
XLA Ops:
  0.0 1.7 %permute.1 = (bf16[256,512]{1,0:T(8,128)(2,1)S(1)}, bf16[512,256]{1,0:T(8,128)(2,1)S(1)}, bf16[512,256]{1,0:T(8,128)(2,1)S(1)}) custom-call(bf16[512,512]{1,0:T(8,128)(2,1)} %e_hbm.1, s32[1,512]{1,0:T(1,128)} %bitcast.10), custom_call_target="tpu_custom_call" | custom-call | flops 1 | bytes 1 | tf_op jit(solution)/shard_map/permute/pallas_call | solution.py:86
  1.7 2.5 %collective-permute-start.6 = (bf16[256,512]{1,0:T(8,128)(2,1)S(1)}, bf16[256,512]{1,0:T(8,128)(2,1)S(1)}, u32[]{:S(2)}, u32[]{:S(2)}) collective-permute-start(bf16[256,512]{1,0:T(8,128)(2,1)S(1)} %get-tuple-element.30.refs_2_), channel_id=1, source_target_pairs={{0,14},{2,0},{4,2},{6,4},{8,6},{10,8},{12,10},{14,12},{16,18},{18,... | collective-permute-start | bytes 786440 | tf_op jit(solution)/shard_map/ppermute | solution.py:47
  4.3 5.1 %collective-permute-start.1 = (bf16[256,512]{1,0:T(8,128)(2,1)S(1)}, bf16[256,512]{1,0:T(8,128)(2,1)S(1)}, u32[]{:S(2)}, u32[]{:S(2)}) collective-permute-start(bf16[256,512]{1,0:T(8,128)(2,1)S(1)} %get-tuple-element.30.refs_2_), channel_id=1, source_target_pairs={{0,4},{2,6},{4,8},{6,10},{8,12},{10,14},{12,0},{14,2},{16,28},{18,... | collective-permute-start | bytes 786440 | tf_op jit(solution)/shard_map/ppermute | solution.py:47
  9.4 1.4 %collective-permute-done.b_ref = f32[1,512]{1,0:T(1,128)S(1)} collective-permute-done((f32[1,512]{1,0:T(1,128)}, f32[1,512]{1,0:T(1,128)S(1)}, u32[]{:S(2)}, u32[]{:S(2)}) %collective-permute-start) | collective-permute-done | bytes 2080 | tf_op jit(solution)/shard_map/ppermute | solution.py:51
  11.4 2.5 %collective-permute-start.2 = (f32[1,1024]{1,0:T(1,128)S(1)}, f32[1,1024]{1,0:T(1,128)S(1)}, u32[]{:S(2)}, u32[]{:S(2)}) collective-permute-start(f32[1,1024]{1,0:T(1,128)S(1)} %join.1.refs_3_), channel_id=1, source_target_pairs={{0,33},{1,32},{32,0},{33,1},{2,35},{3,34},{34,2},{35,3},{4,37},{5,... | collective-permute-start | bytes 12296 | tf_op jit(solution)/shard_map/ppermute | solution.py:41
  15.1 1.1 %tables.1 = (f32[128,128]{1,0:T(8,128)S(1)}, f32[128,128]{1,0:T(8,128)S(1)}) custom-call(s32[64]{0:T(128)} %counts_ref.1, f32[256,128]{1,0:T(8,128)} %bitcast.8, f32[256,128]{1,0:T(8,128)} %bitcast.9), custom_call_target="tpu_custom_call" | custom-call | flops 1 | bytes 1 | tf_op jit(solution)/shard_map/tables/pallas_call | solution.py:128
  16.1 2.1 %collective-permute-done.3.refs_5_ = f32[1,1024]{1,0:T(1,128)S(1)} collective-permute-done((f32[1,1024]{1,0:T(1,128)S(1)}, f32[1,1024]{1,0:T(1,128)S(1)}, u32[]{:S(2)}, u32[]{:S(2)}) %collective-permute-start.3) | collective-permute-done | bytes 4128 | tf_op jit(solution)/shard_map/ppermute | solution.py:41
  18.4 2.7 %collective-permute-start.5 = (bf16[256,512]{1,0:T(8,128)(2,1)S(1)}, bf16[256,512]{1,0:T(8,128)(2,1)S(1)}, u32[]{:S(2)}, u32[]{:S(2)}) collective-permute-start(bf16[256,512]{1,0:T(8,128)(2,1)S(1)} %collective-permute-done.1.refs_4_), channel_id=1, source_target_pairs={{0,2},{2,4},{4,6},{6,8},{8,10},{10,12},{12,14},{14,0},{16,30},{18,... | collective-permute-start | bytes 786440 | tf_op jit(solution)/shard_map/ppermute | solution.py:47
  21.1 1.7 %collective-permute-start.11 = (bf16[256,512]{1,0:T(8,128)(2,1)S(1)}, bf16[256,512]{1,0:T(8,128)(2,1)S(1)}, u32[]{:S(2)}, u32[]{:S(2)}) collective-permute-start(bf16[256,512]{1,0:T(8,128)(2,1)S(1)} %get-tuple-element.30.refs_2_), channel_id=1, source_target_pairs={{0,2},{2,4},{4,6},{6,8},{8,10},{10,12},{12,14},{14,0},{16,30},{18,... | collective-permute-start | bytes 786440 | tf_op jit(solution)/shard_map/ppermute | solution.py:47
  22.8 1.1 %cauchy.2.refs_1_ = bf16[1024,1536]{1,0:T(8,128)(2,1)S(1)} custom-call(s32[1]{0:T(128)} %bitcast.refs_0_.me_ref, f32[128,128]{1,0:T(8,128)S(1)} %get-tuple-element.33.refs_1_.poles_ref, f32[128,128]{1,0:T(8,128)S(1)} %get-tuple-element.34.refs_2_.factors_ref, f32[1,1024]{1,0:T(1,128)S(1)} %join.1.refs_3_, f32[1,1024]{1,0:T(1,128)S(1)} %collective-permute-done.2.refs_4_, ...), custom_call_target="tpu_custom_call" | custom-call | flops 1 | bytes 1 | tf_op jit(solution)/shard_map/cauchy/pallas_call | solution.py:185
  23.9 1.7 %cauchy.3.refs_0_.c_ref = bf16[1024,2560]{1,0:T(8,128)(2,1)S(1)} custom-call(s32[1]{0:T(128)} %bitcast.refs_0_.me_ref, f32[128,128]{1,0:T(8,128)S(1)} %get-tuple-element.33.refs_1_.poles_ref, f32[128,128]{1,0:T(8,128)S(1)} %get-tuple-element.34.refs_2_.factors_ref, f32[1,1024]{1,0:T(1,128)S(1)} %join.1.refs_3_, ...), custom_call_target="tpu_custom_call" | custom-call | flops 1 | bytes 1 | tf_op jit(solution)/shard_map/cauchy/pallas_call | solution.py:185
  25.6 1.8 %stage.2 = (f32[1024,512]{1,0:T(8,128)S(1)}, f32[1024,512]{1,0:T(8,128)S(1)}) custom-call(bf16[1024,2560]{1,0:T(8,128)(2,1)S(1)} %cauchy.3.refs_0_.c_ref, bf16[1024,1536]{1,0:T(8,128)(2,1)S(1)} %cauchy.2.refs_1_, bf16[256,512]{1,0:T(8,128)(2,1)S(1)} %get-tuple-element.30.refs_2_, bf16[256,512]{1,0:T(8,128)(2,1)S(1)} %collective-permute-done.6.refs_3_, ...), custom_call_target="tpu_custom_call" | custom-call | flops 1 | bytes 1 | tf_op jit(solution)/shard_map/stage/pallas_call | solution.py:257
  27.5 2.7 %collective-permute-start.7 = (bf16[256,512]{1,0:T(8,128)(2,1)S(1)}, bf16[256,512]{1,0:T(8,128)(2,1)S(1)}, u32[]{:S(2)}, u32[]{:S(2)}) collective-permute-start(bf16[256,512]{1,0:T(8,128)(2,1)S(1)} %collective-permute-done.5.refs_4_), channel_id=1, source_target_pairs={{0,2},{2,4},{4,6},{6,8},{8,10},{10,12},{12,14},{14,0},{16,30},{18,... | collective-permute-start | bytes 786440 | tf_op jit(solution)/shard_map/ppermute | solution.py:47
  30.1 1.8 %stage.3 = (f32[1024,512]{1,0:T(8,128)S(1)}, bf16[1024,512]{1,0:T(8,128)(2,1)S(1)}) custom-call(bf16[1024,2560]{1,0:T(8,128)(2,1)S(1)} %cauchy.3.refs_0_.c_ref, bf16[1024,1536]{1,0:T(8,128)(2,1)S(1)} %cauchy.2.refs_1_, bf16[256,512]{1,0:T(8,128)(2,1)S(1)} %collective-permute-done.11.refs_2_, bf16[256,512]{1,0:T(8,128)(2,1)S(1)} %collective-permute-done.9.refs_3_, ...), custom_call_target="tpu_custom_call" | custom-call | flops 1 | bytes 1 | tf_op jit(solution)/shard_map/stage/pallas_call | solution.py:257
  32.0 3.5 %collective-permute-start.13 = (bf16[1024,512]{1,0:T(8,128)(2,1)S(1)}, bf16[1024,512]{1,0:T(8,128)(2,1)S(1)}, u32[]{:S(2)}, u32[]{:S(2)}) collective-permute-start(bf16[1024,512]{1,0:T(8,128)(2,1)S(1)} %get-tuple-element.45), channel_id=1, source_target_pairs={{0,16},{16,0},{1,17},{17,1},{2,18},{18,2},{3,19},{19,3},{4,20},{20... | collective-permute-start | bytes 3145736 | tf_op jit(solution)/shard_map/ppermute | solution.py:51
  35.5 1.1 %collective-permute-start.12 = (bf16[256,512]{1,0:T(8,128)(2,1)S(1)}, bf16[256,512]{1,0:T(8,128)(2,1)S(1)}, u32[]{:S(2)}, u32[]{:S(2)}) collective-permute-start(bf16[256,512]{1,0:T(8,128)(2,1)S(1)} %collective-permute-done.10.refs_1_), channel_id=1, source_target_pairs={{0,16},{16,0},{1,17},{17,1},{2,18},{18,2},{3,19},{19,3},{4,20},{20... | collective-permute-start | bytes 786440 | tf_op jit(solution)/shard_map/ppermute | solution.py:51
  36.7 3.7 %collective-permute-start.8 = (bf16[256,512]{1,0:T(8,128)(2,1)S(1)}, bf16[256,512]{1,0:T(8,128)(2,1)S(1)}, u32[]{:S(2)}, u32[]{:S(2)}) collective-permute-start(bf16[256,512]{1,0:T(8,128)(2,1)S(1)} %collective-permute-done.7.refs_1_), channel_id=1, source_target_pairs={{0,16},{16,0},{1,17},{17,1},{2,18},{18,2},{3,19},{19,3},{4,20},{20... | collective-permute-start | bytes 786440 | tf_op jit(solution)/shard_map/ppermute | solution.py:51
  42.0 1.1 %collective-permute-start.14 = (bf16[256,512]{1,0:T(8,128)(2,1)S(1)}, bf16[256,512]{1,0:T(8,128)(2,1)S(1)}, u32[]{:S(2)}, u32[]{:S(2)}) collective-permute-start(bf16[256,512]{1,0:T(8,128)(2,1)S(1)} %get-tuple-element.47), channel_id=1, source_target_pairs={{0,32},{1,33},{32,1},{33,0},{2,34},{3,35},{34,3},{35,2},{4,36},{5,... | collective-permute-start | bytes 786440 | tf_op jit(solution)/shard_map/ppermute | solution.py:41
  43.1 1.6 %collective-permute-start.15 = (bf16[256,512]{1,0:T(8,128)(2,1)S(1)}, bf16[256,512]{1,0:T(8,128)(2,1)S(1)}, u32[]{:S(2)}, u32[]{:S(2)}) collective-permute-start(bf16[256,512]{1,0:T(8,128)(2,1)S(1)} %get-tuple-element.48), channel_id=1, source_target_pairs={{0,33},{1,32},{32,0},{33,1},{2,35},{3,34},{34,2},{35,3},{4,37},{5,... | collective-permute-start | bytes 786440 | tf_op jit(solution)/shard_map/ppermute | solution.py:41
  44.8 1.4 %collective-permute-start.16 = (bf16[256,512]{1,0:T(8,128)(2,1)S(1)}, bf16[256,512]{1,0:T(8,128)(2,1)S(1)}, u32[]{:S(2)}, u32[]{:S(2)}) collective-permute-start(bf16[256,512]{1,0:T(8,128)(2,1)S(1)} %get-tuple-element.49), channel_id=1, source_target_pairs={{0,1},{1,0},{32,33},{33,32},{2,3},{3,2},{34,35},{35,34},{4,5},{5,4... | collective-permute-start | bytes 786440 | tf_op jit(solution)/shard_map/ppermute | solution.py:41
  46.1 3.4 %norms.1 = (f32[256,128]{1,0:T(8,128)S(1)}, bf16[512,512]{1,0:T(8,128)(2,1)}) custom-call(f32[128,128]{1,0:T(8,128)S(1)} %get-tuple-element.33.refs_1_.poles_ref, f32[128,128]{1,0:T(8,128)S(1)} %get-tuple-element.34.refs_2_.factors_ref, f32[1,512]{1,0:T(1,128)S(1)} %bitcast.7, bf16[512,256]{1,0:T(8,128)(2,1)S(1)} %get-tuple-element.51.rest_ref), custom_call_target="tpu_custom_call" | custom-call | flops 1 | bytes 1 | tf_op jit(solution)/shard_map/norms/pallas_call | solution.py:218
  49.5 1.3 %collective-permute-done.14.a_ref = bf16[256,512]{1,0:T(8,128)(2,1)S(1)} collective-permute-done((bf16[256,512]{1,0:T(8,128)(2,1)S(1)}, bf16[256,512]{1,0:T(8,128)(2,1)S(1)}, u32[]{:S(2)}, u32[]{:S(2)}) %collective-permute-start.14) | collective-permute-done | bytes 262176 | tf_op jit(solution)/shard_map/ppermute | solution.py:41
  50.9 6.4 %collective-permute-done.16.c_ref = bf16[256,512]{1,0:T(8,128)(2,1)S(1)} collective-permute-done((bf16[256,512]{1,0:T(8,128)(2,1)S(1)}, bf16[256,512]{1,0:T(8,128)(2,1)S(1)}, u32[]{:S(2)}, u32[]{:S(2)}) %collective-permute-start.16) | collective-permute-done | bytes 262176 | tf_op jit(solution)/shard_map/ppermute | solution.py:41
  57.3 1.5 %finish.1 = bf16[512,512]{1,0:T(8,128)(2,1)} custom-call(s32[1]{0:T(128)} %bitcast.refs_0_.me_ref, s32[64]{0:T(128)S(1)} %copy-done.2, f32[256,512]{1,0:T(8,128)S(1)} %get-tuple-element.46.own_ref, bf16[256,512]{1,0:T(8,128)(2,1)S(1)} %collective-permute-done.14.a_ref, ...), custom_call_target="tpu_custom_call", output_to_operand_aliasing={{}: (8, {})} | custom-call | flops 1 | bytes 1 | tf_op jit(solution)/shard_map/finish/pallas_call | solution.py:336
  (28 shorter events, 3.8 us)
Async XLA Ops:
  1.7 16.7 %collective-permute-start.6 = (bf16[256,512]{1,0:T(8,128)(2,1)S(1)}, bf16[256,512]{1,0:T(8,128)(2,1)S(1)}, u32[]{:S(2)}, u32[]{:S(2)}) collective-permute-start(bf16[256,512]{1,0:T(8,128)(2,1)S(1)} %get-tuple-element.30.refs_2_), channel_id=1, source_target_pairs={{0,14},{2,0},{4,2},{6,4},{8,6},{10,8},{12,10},{14,12},{16,18},{18,... | collective-permute-start | bytes 786440 | tf_op jit(solution)/shard_map/ppermute | solution.py:47
  4.3 14.1 %collective-permute-start.1 = (bf16[256,512]{1,0:T(8,128)(2,1)S(1)}, bf16[256,512]{1,0:T(8,128)(2,1)S(1)}, u32[]{:S(2)}, u32[]{:S(2)}) collective-permute-start(bf16[256,512]{1,0:T(8,128)(2,1)S(1)} %get-tuple-element.30.refs_2_), channel_id=1, source_target_pairs={{0,4},{2,6},{4,8},{6,10},{8,12},{10,14},{12,0},{14,2},{16,28},{18,... | collective-permute-start | bytes 786440 | tf_op jit(solution)/shard_map/ppermute | solution.py:47
  9.4 1.4 %collective-permute-start = (f32[1,512]{1,0:T(1,128)}, f32[1,512]{1,0:T(1,128)S(1)}, u32[]{:S(2)}, u32[]{:S(2)}) collective-permute-start(f32[1,512]{1,0:T(1,128)} %bitcast.5), channel_id=1, source_target_pairs={{0,16},{16,0},{1,17},{17,1},{2,18},{18,2},{3,19},{19,3},{4,20},{20... | collective-permute-start | bytes 6152 | tf_op jit(solution)/shard_map/ppermute | solution.py:51
  10.8 0.7 %copy-start = (f32[512]{0:T(512)S(1)}, f32[512]{0:T(512)}, u32[]{:S(2)}) copy-start(f32[512]{0:T(512)} %param.11) | copy-start | bytes 6148
  11.4 4.7 %collective-permute-start.2 = (f32[1,1024]{1,0:T(1,128)S(1)}, f32[1,1024]{1,0:T(1,128)S(1)}, u32[]{:S(2)}, u32[]{:S(2)}) collective-permute-start(f32[1,1024]{1,0:T(1,128)S(1)} %join.1.refs_3_), channel_id=1, source_target_pairs={{0,33},{1,32},{32,0},{33,1},{2,35},{3,34},{34,2},{35,3},{4,37},{5,... | collective-permute-start | bytes 12296 | tf_op jit(solution)/shard_map/ppermute | solution.py:41
  13.9 4.3 %collective-permute-start.3 = (f32[1,1024]{1,0:T(1,128)S(1)}, f32[1,1024]{1,0:T(1,128)S(1)}, u32[]{:S(2)}, u32[]{:S(2)}) collective-permute-start(f32[1,1024]{1,0:T(1,128)S(1)} %join.1.refs_3_), channel_id=1, source_target_pairs={{0,1},{1,0},{32,33},{33,32},{2,3},{3,2},{34,35},{35,34},{4,5},{5,4... | collective-permute-start | bytes 12296 | tf_op jit(solution)/shard_map/ppermute | solution.py:41
  14.4 4.0 %collective-permute-start.4 = (f32[1,1024]{1,0:T(1,128)S(1)}, f32[1,1024]{1,0:T(1,128)S(1)}, u32[]{:S(2)}, u32[]{:S(2)}) collective-permute-start(f32[1,1024]{1,0:T(1,128)S(1)} %join.1.refs_3_), channel_id=1, source_target_pairs={{0,32},{1,33},{32,1},{33,0},{2,34},{3,35},{34,3},{35,2},{4,36},{5,... | collective-permute-start | bytes 12296 | tf_op jit(solution)/shard_map/ppermute | solution.py:41
  18.4 9.0 %collective-permute-start.9 = (bf16[256,512]{1,0:T(8,128)(2,1)S(1)}, bf16[256,512]{1,0:T(8,128)(2,1)S(1)}, u32[]{:S(2)}, u32[]{:S(2)}) collective-permute-start(bf16[256,512]{1,0:T(8,128)(2,1)S(1)} %collective-permute-done.6.refs_3_), channel_id=1, source_target_pairs={{0,14},{2,0},{4,2},{6,4},{8,6},{10,8},{12,10},{14,12},{16,18},{18,... | collective-permute-start | bytes 786440 | tf_op jit(solution)/shard_map/ppermute | solution.py:47
  18.4 9.1 %collective-permute-start.5 = (bf16[256,512]{1,0:T(8,128)(2,1)S(1)}, bf16[256,512]{1,0:T(8,128)(2,1)S(1)}, u32[]{:S(2)}, u32[]{:S(2)}) collective-permute-start(bf16[256,512]{1,0:T(8,128)(2,1)S(1)} %collective-permute-done.1.refs_4_), channel_id=1, source_target_pairs={{0,2},{2,4},{4,6},{6,8},{8,10},{10,12},{12,14},{14,0},{16,30},{18,... | collective-permute-start | bytes 786440 | tf_op jit(solution)/shard_map/ppermute | solution.py:47
  21.1 9.0 %collective-permute-start.11 = (bf16[256,512]{1,0:T(8,128)(2,1)S(1)}, bf16[256,512]{1,0:T(8,128)(2,1)S(1)}, u32[]{:S(2)}, u32[]{:S(2)}) collective-permute-start(bf16[256,512]{1,0:T(8,128)(2,1)S(1)} %get-tuple-element.30.refs_2_), channel_id=1, source_target_pairs={{0,2},{2,4},{4,6},{6,8},{8,10},{10,12},{12,14},{14,0},{16,30},{18,... | collective-permute-start | bytes 786440 | tf_op jit(solution)/shard_map/ppermute | solution.py:47
  27.4 8.1 %collective-permute-start.10 = (bf16[256,512]{1,0:T(8,128)(2,1)S(1)}, bf16[256,512]{1,0:T(8,128)(2,1)S(1)}, u32[]{:S(2)}, u32[]{:S(2)}) collective-permute-start(bf16[256,512]{1,0:T(8,128)(2,1)S(1)} %collective-permute-done.9.refs_3_), channel_id=1, source_target_pairs={{0,14},{2,0},{4,2},{6,4},{8,6},{10,8},{12,10},{14,12},{16,18},{18,... | collective-permute-start | bytes 786440 | tf_op jit(solution)/shard_map/ppermute | solution.py:47
  27.5 9.2 %collective-permute-start.7 = (bf16[256,512]{1,0:T(8,128)(2,1)S(1)}, bf16[256,512]{1,0:T(8,128)(2,1)S(1)}, u32[]{:S(2)}, u32[]{:S(2)}) collective-permute-start(bf16[256,512]{1,0:T(8,128)(2,1)S(1)} %collective-permute-done.5.refs_4_), channel_id=1, source_target_pairs={{0,2},{2,4},{4,6},{6,8},{8,10},{10,12},{12,14},{14,0},{16,30},{18,... | collective-permute-start | bytes 786440 | tf_op jit(solution)/shard_map/ppermute | solution.py:47
  32.0 9.6 %collective-permute-start.13 = (bf16[1024,512]{1,0:T(8,128)(2,1)S(1)}, bf16[1024,512]{1,0:T(8,128)(2,1)S(1)}, u32[]{:S(2)}, u32[]{:S(2)}) collective-permute-start(bf16[1024,512]{1,0:T(8,128)(2,1)S(1)} %get-tuple-element.45), channel_id=1, source_target_pairs={{0,16},{16,0},{1,17},{17,1},{2,18},{18,2},{3,19},{19,3},{4,20},{20... | collective-permute-start | bytes 3145736 | tf_op jit(solution)/shard_map/ppermute | solution.py:51
  35.5 5.3 %collective-permute-start.12 = (bf16[256,512]{1,0:T(8,128)(2,1)S(1)}, bf16[256,512]{1,0:T(8,128)(2,1)S(1)}, u32[]{:S(2)}, u32[]{:S(2)}) collective-permute-start(bf16[256,512]{1,0:T(8,128)(2,1)S(1)} %collective-permute-done.10.refs_1_), channel_id=1, source_target_pairs={{0,16},{16,0},{1,17},{17,1},{2,18},{18,2},{3,19},{19,3},{4,20},{20... | collective-permute-start | bytes 786440 | tf_op jit(solution)/shard_map/ppermute | solution.py:51
  36.7 4.9 %collective-permute-start.8 = (bf16[256,512]{1,0:T(8,128)(2,1)S(1)}, bf16[256,512]{1,0:T(8,128)(2,1)S(1)}, u32[]{:S(2)}, u32[]{:S(2)}) collective-permute-start(bf16[256,512]{1,0:T(8,128)(2,1)S(1)} %collective-permute-done.7.refs_1_), channel_id=1, source_target_pairs={{0,16},{16,0},{1,17},{17,1},{2,18},{18,2},{3,19},{19,3},{4,20},{20... | collective-permute-start | bytes 786440 | tf_op jit(solution)/shard_map/ppermute | solution.py:51
  41.5 4.6 %copy-start.1 = (f32[512]{0:T(512)S(1)}, f32[512]{0:T(512)}, u32[]{:S(2)}) copy-start(f32[512]{0:T(512)} %param.11) | copy-start | bytes 6148
  41.5 15.8 %copy-start.2 = (s32[64]{0:T(128)S(1)}, s32[64]{0:T(128)}, u32[]{:S(2)}) copy-start(s32[64]{0:T(128)} %counts_ref.1) | copy-start | bytes 772
  42.0 8.9 %collective-permute-start.14 = (bf16[256,512]{1,0:T(8,128)(2,1)S(1)}, bf16[256,512]{1,0:T(8,128)(2,1)S(1)}, u32[]{:S(2)}, u32[]{:S(2)}) collective-permute-start(bf16[256,512]{1,0:T(8,128)(2,1)S(1)} %get-tuple-element.47), channel_id=1, source_target_pairs={{0,32},{1,33},{32,1},{33,0},{2,34},{3,35},{34,3},{35,2},{4,36},{5,... | collective-permute-start | bytes 786440 | tf_op jit(solution)/shard_map/ppermute | solution.py:41
  43.1 7.7 %collective-permute-start.15 = (bf16[256,512]{1,0:T(8,128)(2,1)S(1)}, bf16[256,512]{1,0:T(8,128)(2,1)S(1)}, u32[]{:S(2)}, u32[]{:S(2)}) collective-permute-start(bf16[256,512]{1,0:T(8,128)(2,1)S(1)} %get-tuple-element.48), channel_id=1, source_target_pairs={{0,33},{1,32},{32,0},{33,1},{2,35},{3,34},{34,2},{35,3},{4,37},{5,... | collective-permute-start | bytes 786440 | tf_op jit(solution)/shard_map/ppermute | solution.py:41
  44.8 12.5 %collective-permute-start.16 = (bf16[256,512]{1,0:T(8,128)(2,1)S(1)}, bf16[256,512]{1,0:T(8,128)(2,1)S(1)}, u32[]{:S(2)}, u32[]{:S(2)}) collective-permute-start(bf16[256,512]{1,0:T(8,128)(2,1)S(1)} %get-tuple-element.49), channel_id=1, source_target_pairs={{0,1},{1,0},{32,33},{33,32},{2,3},{3,2},{34,35},{35,34},{4,5},{5,4... | collective-permute-start | bytes 786440 | tf_op jit(solution)/shard_map/ppermute | solution.py:41

commit v14 on v13

--- a/solution.py
+++ b/solution.py
@@ -193,9 +193,11 @@
     )(me, poles, factors, *roots)
 
 
-def norm_kernel(poles_ref, factors_ref, r_ref, rest_ref, n_ref, o_hbm, sem):
+def norm_kernel(me_ref, counts_ref, poles_ref, factors_ref, r_ref, rest_ref, n_ref, live_ref, o_hbm, sem):
     copy = pltpu.make_async_copy(rest_ref, o_hbm.at[:, pl.ds(LIVE, COLS - LIVE)], sem.at[0])
     copy.start()
+    within = lax.broadcasted_iota(jnp.int32, (8, LIVE), 1)
+    live_ref[...] = jnp.where(within < counts_ref[me_ref[0]], 1.0, 0.0)
     roots = column(r_ref[:, :LIVE])
     group = 16
     for t in range(LIVE // TILE):
@@ -214,20 +216,21 @@
     copy.wait()
 
 
-def norms(poles, factors, roots, rest):
+def norms(me, counts, poles, factors, roots, rest):
     return pl.pallas_call(
         norm_kernel,
-        in_specs=[VM] * 4,
-        out_specs=[VM, HB],
+        in_specs=[SM, SM] + [VM] * 4,
+        out_specs=[VM, VM, HB],
         out_shape=[
             pltpu.VMEM((LIVE, LANES), F32),
+            pltpu.VMEM((8, LIVE), F32),
             jax.ShapeDtypeStruct((rest.shape[0], COLS), BF16),
         ],
         scratch_shapes=[pltpu.SemaphoreType.DMA((1,))],
         name="norms",
         compiler_params=params(4),
         cost_estimate=TINY,
-    )(poles, factors, roots, rest)
+    )(me, counts, poles, factors, roots, rest)
 
 
 def product(c_ref, j, first, x_refs):
@@ -310,9 +313,8 @@
     )(c_mine, sibling, mine, other)
 
 
-def finish_kernel(me_ref, counts_ref, own_ref, a_ref, b_ref, c_ref, n_ref, lead_ref, _, o_hbm, buffer, sem):
-    within = lax.broadcasted_iota(jnp.int32, (1, LIVE), 1)
-    retain = within < counts_ref[me_ref[0]]
+def finish_kernel(own_ref, a_ref, b_ref, c_ref, n_ref, live_ref, lead_ref, _, o_hbm, buffer, sem):
+    retain = live_ref[:1, :] > 0.5
     norm = n_ref[:, :1]
     size = buffer.shape[0] // 4
     copies = []
@@ -332,18 +334,18 @@
         copy.wait()
 
 
-def finish(me, counts, own, received, norm, lead, out):
+def finish(own, received, norm, live, lead, out):
     return pl.pallas_call(
         finish_kernel,
-        in_specs=[SM, SM] + [VM] * (XS + 2) + [HB],
+        in_specs=[VM] * (XS + 3) + [HB],
         out_specs=HB,
         out_shape=jax.ShapeDtypeStruct(out.shape, BF16),
         scratch_shapes=[pltpu.VMEM(lead.shape, BF16), pltpu.SemaphoreType.DMA((4,))],
-        input_output_aliases={4 + XS: 0},
+        input_output_aliases={XS + 3: 0},
         name="finish",
         compiler_params=params(4),
         cost_estimate=TINY,
-    )(me, counts, own, *received, norm, lead, out)
+    )(own, *received, norm, live, lead, out)
 
 
 def per_device(eigvecs, perm, counts, poles, weights, roots):
@@ -375,8 +377,8 @@
     mine = add((6, 8), c_mine, (p6, cshift(p6)), (mine,), TINY)
     own_sum, *sent = totals(c_mine, sibling, mine, other)
     received = [xshift(sent[i], k) for i, k in ((0, 1), (2, -1), (1, 2))]
-    norm, out = norms(table, factors, hold(roots, own_sum), rest)
-    return finish(me, counts, own_sum, received, norm, lead, out)
+    norm, live, out = norms(me, counts, table, factors, hold(roots, own_sum), rest)
+    return finish(own_sum, received, norm, live, lead, out)
 
 
 def solution(mesh):

time: 59.1 us -> 58.6 us (level)
  waiting for transfers between devices: 11.5 us -> 10.9 us
  transfers between devices with their start and end apart: 17 -> 17, of which waited for: 5 -> 5; matrix products, arithmetic and copies ran while one was open for 0% -> 0% of each run, Pallas kernels for 20% -> 21%
where the time goes in v14:
time: 58.6 us; the launch traced here: 58.4 us
  starting transfers between devices  30.9 us (53%)
  Pallas kernels  15.6 us (27%)
  waiting for transfers between devices  10.9 us (19%)
  local copies, waits for them, and re-layouts  0.69 us (1%)
    ppermute x7, starting transfers between devices, around(): return lax.ppermute(a, ('core', 'z'), up + down)  14.8 us
    ppermute x6, waiting for transfers between devices, xshift(): return lax.ppermute(a, ('xl', 'xh'), pairs)  9.53 us
    ppermute x4, starting transfers between devices, cshift(): return lax.ppermute(a, 'core', [(0, 1), (1, 0)])  8.38 us
    ppermute x6, starting transfers between devices, xshift(): return lax.ppermute(a, ('xl', 'xh'), pairs)  7.73 us
    pallas_call x1, Pallas kernels, norms(): pl.pallas_call(norm_kernel, in_specs=[SM, SM] + [VM] * 4, out_specs=[VM,...  3.92 us
    pallas_call x2, Pallas kernels, stage(): pl.pallas_call(lambda *refs: stage_kernel(first, len(pieces), *refs), in_...  3.61 us
    pallas_call x2, Pallas kernels, cauchy(): pl.pallas_call(lambda *refs: cauchy_kernel(fc, pieces, *refs), in_specs=[...  2.72 us
    pallas_call x1, Pallas kernels, permute(): pl.pallas_call(permute_kernel, in_specs=[HB, HB], out_specs=[VM] * 3, out...  1.72 us
  transfers between devices with their start and end apart: 17, of which 5 were waited for; matrix products, arithmetic and copies ran while one was open for 0% of the time, Pallas kernels for 21%

profile of v14, /device:TPU:1, one launch (start us, length us, event | category | flops | bytes accessed | tf_op | source)
XLA Modules:
  0.0 58.4 jit_solution(8595839361839046265)
XLA Ops:
  0.0 1.7 %permute.1 = (bf16[256,512]{1,0:T(8,128)(2,1)S(1)}, bf16[512,256]{1,0:T(8,128)(2,1)S(1)}, bf16[512,256]{1,0:T(8,128)(2,1)S(1)}) custom-call(bf16[512,512]{1,0:T(8,128)(2,1)} %e_hbm.1, s32[1,512]{1,0:T(1,128)} %bitcast.10), custom_call_target="tpu_custom_call" | custom-call | flops 1 | bytes 1 | tf_op jit(solution)/shard_map/permute/pallas_call | solution.py:86
  1.7 2.5 %collective-permute-start.6 = (bf16[256,512]{1,0:T(8,128)(2,1)S(1)}, bf16[256,512]{1,0:T(8,128)(2,1)S(1)}, u32[]{:S(2)}, u32[]{:S(2)}) collective-permute-start(bf16[256,512]{1,0:T(8,128)(2,1)S(1)} %get-tuple-element.31.refs_2_), channel_id=1, source_target_pairs={{0,14},{2,0},{4,2},{6,4},{8,6},{10,8},{12,10},{14,12},{16,18},{18,... | collective-permute-start | bytes 786440 | tf_op jit(solution)/shard_map/ppermute | solution.py:47
  4.3 5.1 %collective-permute-start.1 = (bf16[256,512]{1,0:T(8,128)(2,1)S(1)}, bf16[256,512]{1,0:T(8,128)(2,1)S(1)}, u32[]{:S(2)}, u32[]{:S(2)}) collective-permute-start(bf16[256,512]{1,0:T(8,128)(2,1)S(1)} %get-tuple-element.31.refs_2_), channel_id=1, source_target_pairs={{0,4},{2,6},{4,8},{6,10},{8,12},{10,14},{12,0},{14,2},{16,28},{18,... | collective-permute-start | bytes 786440 | tf_op jit(solution)/shard_map/ppermute | solution.py:47
  9.4 1.4 %collective-permute-done.b_ref = f32[1,512]{1,0:T(1,128)S(1)} collective-permute-done((f32[1,512]{1,0:T(1,128)}, f32[1,512]{1,0:T(1,128)S(1)}, u32[]{:S(2)}, u32[]{:S(2)}) %collective-permute-start) | collective-permute-done | bytes 2080 | tf_op jit(solution)/shard_map/ppermute | solution.py:51
  11.4 2.5 %collective-permute-start.2 = (f32[1,1024]{1,0:T(1,128)S(1)}, f32[1,1024]{1,0:T(1,128)S(1)}, u32[]{:S(2)}, u32[]{:S(2)}) collective-permute-start(f32[1,1024]{1,0:T(1,128)S(1)} %join.1.refs_3_), channel_id=1, source_target_pairs={{0,33},{1,32},{32,0},{33,1},{2,35},{3,34},{34,2},{35,3},{4,37},{5,... | collective-permute-start | bytes 12296 | tf_op jit(solution)/shard_map/ppermute | solution.py:41
  15.1 1.1 %tables.1 = (f32[128,128]{1,0:T(8,128)S(1)}, f32[128,128]{1,0:T(8,128)S(1)}) custom-call(s32[64]{0:T(128)} %counts_ref.1, f32[256,128]{1,0:T(8,128)} %bitcast.8, f32[256,128]{1,0:T(8,128)} %bitcast.9), custom_call_target="tpu_custom_call" | custom-call | flops 1 | bytes 1 | tf_op jit(solution)/shard_map/tables/pallas_call | solution.py:128
  16.1 2.1 %collective-permute-done.3.refs_5_ = f32[1,1024]{1,0:T(1,128)S(1)} collective-permute-done((f32[1,1024]{1,0:T(1,128)S(1)}, f32[1,1024]{1,0:T(1,128)S(1)}, u32[]{:S(2)}, u32[]{:S(2)}) %collective-permute-start.3) | collective-permute-done | bytes 4128 | tf_op jit(solution)/shard_map/ppermute | solution.py:41
  18.4 2.7 %collective-permute-start.5 = (bf16[256,512]{1,0:T(8,128)(2,1)S(1)}, bf16[256,512]{1,0:T(8,128)(2,1)S(1)}, u32[]{:S(2)}, u32[]{:S(2)}) collective-permute-start(bf16[256,512]{1,0:T(8,128)(2,1)S(1)} %collective-permute-done.1.refs_4_), channel_id=1, source_target_pairs={{0,2},{2,4},{4,6},{6,8},{8,10},{10,12},{12,14},{14,0},{16,30},{18,... | collective-permute-start | bytes 786440 | tf_op jit(solution)/shard_map/ppermute | solution.py:47
  21.1 1.7 %collective-permute-start.11 = (bf16[256,512]{1,0:T(8,128)(2,1)S(1)}, bf16[256,512]{1,0:T(8,128)(2,1)S(1)}, u32[]{:S(2)}, u32[]{:S(2)}) collective-permute-start(bf16[256,512]{1,0:T(8,128)(2,1)S(1)} %get-tuple-element.31.refs_2_), channel_id=1, source_target_pairs={{0,2},{2,4},{4,6},{6,8},{8,10},{10,12},{12,14},{14,0},{16,30},{18,... | collective-permute-start | bytes 786440 | tf_op jit(solution)/shard_map/ppermute | solution.py:47
  22.8 1.1 %cauchy.2.refs_1_ = bf16[1024,1536]{1,0:T(8,128)(2,1)S(1)} custom-call(s32[1]{0:T(128)} %bitcast.refs_0_.me_ref, f32[128,128]{1,0:T(8,128)S(1)} %get-tuple-element.34.refs_1_.poles_ref, f32[128,128]{1,0:T(8,128)S(1)} %get-tuple-element.35.refs_2_.factors_ref, f32[1,1024]{1,0:T(1,128)S(1)} %join.1.refs_3_, f32[1,1024]{1,0:T(1,128)S(1)} %collective-permute-done.2.refs_4_, ...), custom_call_target="tpu_custom_call" | custom-call | flops 1 | bytes 1 | tf_op jit(solution)/shard_map/cauchy/pallas_call | solution.py:185
  23.9 1.7 %cauchy.3.refs_0_.c_ref = bf16[1024,2560]{1,0:T(8,128)(2,1)S(1)} custom-call(s32[1]{0:T(128)} %bitcast.refs_0_.me_ref, f32[128,128]{1,0:T(8,128)S(1)} %get-tuple-element.34.refs_1_.poles_ref, f32[128,128]{1,0:T(8,128)S(1)} %get-tuple-element.35.refs_2_.factors_ref, f32[1,1024]{1,0:T(1,128)S(1)} %join.1.refs_3_, ...), custom_call_target="tpu_custom_call" | custom-call | flops 1 | bytes 1 | tf_op jit(solution)/shard_map/cauchy/pallas_call | solution.py:185
  25.6 1.8 %stage.2 = (f32[1024,512]{1,0:T(8,128)S(1)}, f32[1024,512]{1,0:T(8,128)S(1)}) custom-call(bf16[1024,2560]{1,0:T(8,128)(2,1)S(1)} %cauchy.3.refs_0_.c_ref, bf16[1024,1536]{1,0:T(8,128)(2,1)S(1)} %cauchy.2.refs_1_, bf16[256,512]{1,0:T(8,128)(2,1)S(1)} %get-tuple-element.31.refs_2_, bf16[256,512]{1,0:T(8,128)(2,1)S(1)} %collective-permute-done.6.refs_3_, ...), custom_call_target="tpu_custom_call" | custom-call | flops 1 | bytes 1 | tf_op jit(solution)/shard_map/stage/pallas_call | solution.py:260
  27.5 2.7 %collective-permute-start.7 = (bf16[256,512]{1,0:T(8,128)(2,1)S(1)}, bf16[256,512]{1,0:T(8,128)(2,1)S(1)}, u32[]{:S(2)}, u32[]{:S(2)}) collective-permute-start(bf16[256,512]{1,0:T(8,128)(2,1)S(1)} %collective-permute-done.5.refs_4_), channel_id=1, source_target_pairs={{0,2},{2,4},{4,6},{6,8},{8,10},{10,12},{12,14},{14,0},{16,30},{18,... | collective-permute-start | bytes 786440 | tf_op jit(solution)/shard_map/ppermute | solution.py:47
  30.1 1.8 %stage.3 = (f32[1024,512]{1,0:T(8,128)S(1)}, bf16[1024,512]{1,0:T(8,128)(2,1)S(1)}) custom-call(bf16[1024,2560]{1,0:T(8,128)(2,1)S(1)} %cauchy.3.refs_0_.c_ref, bf16[1024,1536]{1,0:T(8,128)(2,1)S(1)} %cauchy.2.refs_1_, bf16[256,512]{1,0:T(8,128)(2,1)S(1)} %collective-permute-done.11.refs_2_, bf16[256,512]{1,0:T(8,128)(2,1)S(1)} %collective-permute-done.9.refs_3_, ...), custom_call_target="tpu_custom_call" | custom-call | flops 1 | bytes 1 | tf_op jit(solution)/shard_map/stage/pallas_call | solution.py:260
  32.0 3.5 %collective-permute-start.13 = (bf16[1024,512]{1,0:T(8,128)(2,1)S(1)}, bf16[1024,512]{1,0:T(8,128)(2,1)S(1)}, u32[]{:S(2)}, u32[]{:S(2)}) collective-permute-start(bf16[1024,512]{1,0:T(8,128)(2,1)S(1)} %get-tuple-element.46), channel_id=1, source_target_pairs={{0,16},{16,0},{1,17},{17,1},{2,18},{18,2},{3,19},{19,3},{4,20},{20... | collective-permute-start | bytes 3145736 | tf_op jit(solution)/shard_map/ppermute | solution.py:51
  35.5 1.1 %collective-permute-start.12 = (bf16[256,512]{1,0:T(8,128)(2,1)S(1)}, bf16[256,512]{1,0:T(8,128)(2,1)S(1)}, u32[]{:S(2)}, u32[]{:S(2)}) collective-permute-start(bf16[256,512]{1,0:T(8,128)(2,1)S(1)} %collective-permute-done.10.refs_1_), channel_id=1, source_target_pairs={{0,16},{16,0},{1,17},{17,1},{2,18},{18,2},{3,19},{19,3},{4,20},{20... | collective-permute-start | bytes 786440 | tf_op jit(solution)/shard_map/ppermute | solution.py:51
  36.7 3.7 %collective-permute-start.8 = (bf16[256,512]{1,0:T(8,128)(2,1)S(1)}, bf16[256,512]{1,0:T(8,128)(2,1)S(1)}, u32[]{:S(2)}, u32[]{:S(2)}) collective-permute-start(bf16[256,512]{1,0:T(8,128)(2,1)S(1)} %collective-permute-done.7.refs_1_), channel_id=1, source_target_pairs={{0,16},{16,0},{1,17},{17,1},{2,18},{18,2},{3,19},{19,3},{4,20},{20... | collective-permute-start | bytes 786440 | tf_op jit(solution)/shard_map/ppermute | solution.py:51
  42.0 1.1 %collective-permute-start.14 = (bf16[256,512]{1,0:T(8,128)(2,1)S(1)}, bf16[256,512]{1,0:T(8,128)(2,1)S(1)}, u32[]{:S(2)}, u32[]{:S(2)}) collective-permute-start(bf16[256,512]{1,0:T(8,128)(2,1)S(1)} %get-tuple-element.48), channel_id=1, source_target_pairs={{0,32},{1,33},{32,1},{33,0},{2,34},{3,35},{34,3},{35,2},{4,36},{5,... | collective-permute-start | bytes 786440 | tf_op jit(solution)/shard_map/ppermute | solution.py:41
  43.1 1.6 %collective-permute-start.15 = (bf16[256,512]{1,0:T(8,128)(2,1)S(1)}, bf16[256,512]{1,0:T(8,128)(2,1)S(1)}, u32[]{:S(2)}, u32[]{:S(2)}) collective-permute-start(bf16[256,512]{1,0:T(8,128)(2,1)S(1)} %get-tuple-element.49), channel_id=1, source_target_pairs={{0,33},{1,32},{32,0},{33,1},{2,35},{3,34},{34,2},{35,3},{4,37},{5,... | collective-permute-start | bytes 786440 | tf_op jit(solution)/shard_map/ppermute | solution.py:41
  44.8 1.4 %collective-permute-start.16 = (bf16[256,512]{1,0:T(8,128)(2,1)S(1)}, bf16[256,512]{1,0:T(8,128)(2,1)S(1)}, u32[]{:S(2)}, u32[]{:S(2)}) collective-permute-start(bf16[256,512]{1,0:T(8,128)(2,1)S(1)} %get-tuple-element.50), channel_id=1, source_target_pairs={{0,1},{1,0},{32,33},{33,32},{2,3},{3,2},{34,35},{35,34},{4,5},{5,4... | collective-permute-start | bytes 786440 | tf_op jit(solution)/shard_map/ppermute | solution.py:41
  46.1 3.9 %norms.1 = (f32[256,128]{1,0:T(8,128)S(1)}, f32[8,256]{1,0:T(8,128)S(1)}, bf16[512,512]{1,0:T(8,128)(2,1)}) custom-call(s32[1]{0:T(128)} %bitcast.refs_0_.me_ref, s32[64]{0:T(128)S(1)} %copy-done.2, f32[128,128]{1,0:T(8,128)S(1)} %get-tuple-element.34.refs_1_.poles_ref, f32[128,128]{1,0:T(8,128)S(1)} %get-tuple-element.35.refs_2_.factors_ref, ...), custom_call_target="tpu_custom_call" | custom-call | flops 1 | bytes 1 | tf_op jit(solution)/shard_map/norms/pallas_call | solution.py:220
  50.1 0.8 %collective-permute-done.14.a_ref = bf16[256,512]{1,0:T(8,128)(2,1)S(1)} collective-permute-done((bf16[256,512]{1,0:T(8,128)(2,1)S(1)}, bf16[256,512]{1,0:T(8,128)(2,1)S(1)}, u32[]{:S(2)}, u32[]{:S(2)}) %collective-permute-start.14) | collective-permute-done | bytes 262176 | tf_op jit(solution)/shard_map/ppermute | solution.py:41
  50.9 6.4 %collective-permute-done.16.c_ref = bf16[256,512]{1,0:T(8,128)(2,1)S(1)} collective-permute-done((bf16[256,512]{1,0:T(8,128)(2,1)S(1)}, bf16[256,512]{1,0:T(8,128)(2,1)S(1)}, u32[]{:S(2)}, u32[]{:S(2)}) %collective-permute-start.16) | collective-permute-done | bytes 262176 | tf_op jit(solution)/shard_map/ppermute | solution.py:41
  57.3 1.0 %finish.1 = bf16[512,512]{1,0:T(8,128)(2,1)} custom-call(f32[256,512]{1,0:T(8,128)S(1)} %get-tuple-element.47.own_ref, bf16[256,512]{1,0:T(8,128)(2,1)S(1)} %collective-permute-done.14.a_ref, bf16[256,512]{1,0:T(8,128)(2,1)S(1)} %collective-permute-done.15.b_ref, bf16[256,512]{1,0:T(8,128)(2,1)S(1)} %collective-permute-done.16.c_ref, ...), custom_call_target="tpu_custom_call", output_to_operand_aliasing={{}: (7, {})} | custom-call | flops 1 | bytes 1 | tf_op jit(solution)/shard_map/finish/pallas_call | solution.py:338
  (28 shorter events, 3.8 us)
Async XLA Ops:
  1.7 16.7 %collective-permute-start.6 = (bf16[256,512]{1,0:T(8,128)(2,1)S(1)}, bf16[256,512]{1,0:T(8,128)(2,1)S(1)}, u32[]{:S(2)}, u32[]{:S(2)}) collective-permute-start(bf16[256,512]{1,0:T(8,128)(2,1)S(1)} %get-tuple-element.31.refs_2_), channel_id=1, source_target_pairs={{0,14},{2,0},{4,2},{6,4},{8,6},{10,8},{12,10},{14,12},{16,18},{18,... | collective-permute-start | bytes 786440 | tf_op jit(solution)/shard_map/ppermute | solution.py:47
  4.3 14.1 %collective-permute-start.1 = (bf16[256,512]{1,0:T(8,128)(2,1)S(1)}, bf16[256,512]{1,0:T(8,128)(2,1)S(1)}, u32[]{:S(2)}, u32[]{:S(2)}) collective-permute-start(bf16[256,512]{1,0:T(8,128)(2,1)S(1)} %get-tuple-element.31.refs_2_), channel_id=1, source_target_pairs={{0,4},{2,6},{4,8},{6,10},{8,12},{10,14},{12,0},{14,2},{16,28},{18,... | collective-permute-start | bytes 786440 | tf_op jit(solution)/shard_map/ppermute | solution.py:47
  9.4 1.4 %collective-permute-start = (f32[1,512]{1,0:T(1,128)}, f32[1,512]{1,0:T(1,128)S(1)}, u32[]{:S(2)}, u32[]{:S(2)}) collective-permute-start(f32[1,512]{1,0:T(1,128)} %bitcast.5), channel_id=1, source_target_pairs={{0,16},{16,0},{1,17},{17,1},{2,18},{18,2},{3,19},{19,3},{4,20},{20... | collective-permute-start | bytes 6152 | tf_op jit(solution)/shard_map/ppermute | solution.py:51
  10.8 0.7 %copy-start = (f32[512]{0:T(512)S(1)}, f32[512]{0:T(512)}, u32[]{:S(2)}) copy-start(f32[512]{0:T(512)} %param.11) | copy-start | bytes 6148
  11.4 4.7 %collective-permute-start.2 = (f32[1,1024]{1,0:T(1,128)S(1)}, f32[1,1024]{1,0:T(1,128)S(1)}, u32[]{:S(2)}, u32[]{:S(2)}) collective-permute-start(f32[1,1024]{1,0:T(1,128)S(1)} %join.1.refs_3_), channel_id=1, source_target_pairs={{0,33},{1,32},{32,0},{33,1},{2,35},{3,34},{34,2},{35,3},{4,37},{5,... | collective-permute-start | bytes 12296 | tf_op jit(solution)/shard_map/ppermute | solution.py:41
  13.9 4.3 %collective-permute-start.3 = (f32[1,1024]{1,0:T(1,128)S(1)}, f32[1,1024]{1,0:T(1,128)S(1)}, u32[]{:S(2)}, u32[]{:S(2)}) collective-permute-start(f32[1,1024]{1,0:T(1,128)S(1)} %join.1.refs_3_), channel_id=1, source_target_pairs={{0,1},{1,0},{32,33},{33,32},{2,3},{3,2},{34,35},{35,34},{4,5},{5,4... | collective-permute-start | bytes 12296 | tf_op jit(solution)/shard_map/ppermute | solution.py:41
  14.4 4.0 %collective-permute-start.4 = (f32[1,1024]{1,0:T(1,128)S(1)}, f32[1,1024]{1,0:T(1,128)S(1)}, u32[]{:S(2)}, u32[]{:S(2)}) collective-permute-start(f32[1,1024]{1,0:T(1,128)S(1)} %join.1.refs_3_), channel_id=1, source_target_pairs={{0,32},{1,33},{32,1},{33,0},{2,34},{3,35},{34,3},{35,2},{4,36},{5,... | collective-permute-start | bytes 12296 | tf_op jit(solution)/shard_map/ppermute | solution.py:41
  18.4 9.0 %collective-permute-start.9 = (bf16[256,512]{1,0:T(8,128)(2,1)S(1)}, bf16[256,512]{1,0:T(8,128)(2,1)S(1)}, u32[]{:S(2)}, u32[]{:S(2)}) collective-permute-start(bf16[256,512]{1,0:T(8,128)(2,1)S(1)} %collective-permute-done.6.refs_3_), channel_id=1, source_target_pairs={{0,14},{2,0},{4,2},{6,4},{8,6},{10,8},{12,10},{14,12},{16,18},{18,... | collective-permute-start | bytes 786440 | tf_op jit(solution)/shard_map/ppermute | solution.py:47
  18.4 9.1 %collective-permute-start.5 = (bf16[256,512]{1,0:T(8,128)(2,1)S(1)}, bf16[256,512]{1,0:T(8,128)(2,1)S(1)}, u32[]{:S(2)}, u32[]{:S(2)}) collective-permute-start(bf16[256,512]{1,0:T(8,128)(2,1)S(1)} %collective-permute-done.1.refs_4_), channel_id=1, source_target_pairs={{0,2},{2,4},{4,6},{6,8},{8,10},{10,12},{12,14},{14,0},{16,30},{18,... | collective-permute-start | bytes 786440 | tf_op jit(solution)/shard_map/ppermute | solution.py:47
  21.1 9.0 %collective-permute-start.11 = (bf16[256,512]{1,0:T(8,128)(2,1)S(1)}, bf16[256,512]{1,0:T(8,128)(2,1)S(1)}, u32[]{:S(2)}, u32[]{:S(2)}) collective-permute-start(bf16[256,512]{1,0:T(8,128)(2,1)S(1)} %get-tuple-element.31.refs_2_), channel_id=1, source_target_pairs={{0,2},{2,4},{4,6},{6,8},{8,10},{10,12},{12,14},{14,0},{16,30},{18,... | collective-permute-start | bytes 786440 | tf_op jit(solution)/shard_map/ppermute | solution.py:47
  27.4 8.1 %collective-permute-start.10 = (bf16[256,512]{1,0:T(8,128)(2,1)S(1)}, bf16[256,512]{1,0:T(8,128)(2,1)S(1)}, u32[]{:S(2)}, u32[]{:S(2)}) collective-permute-start(bf16[256,512]{1,0:T(8,128)(2,1)S(1)} %collective-permute-done.9.refs_3_), channel_id=1, source_target_pairs={{0,14},{2,0},{4,2},{6,4},{8,6},{10,8},{12,10},{14,12},{16,18},{18,... | collective-permute-start | bytes 786440 | tf_op jit(solution)/shard_map/ppermute | solution.py:47
  27.5 9.2 %collective-permute-start.7 = (bf16[256,512]{1,0:T(8,128)(2,1)S(1)}, bf16[256,512]{1,0:T(8,128)(2,1)S(1)}, u32[]{:S(2)}, u32[]{:S(2)}) collective-permute-start(bf16[256,512]{1,0:T(8,128)(2,1)S(1)} %collective-permute-done.5.refs_4_), channel_id=1, source_target_pairs={{0,2},{2,4},{4,6},{6,8},{8,10},{10,12},{12,14},{14,0},{16,30},{18,... | collective-permute-start | bytes 786440 | tf_op jit(solution)/shard_map/ppermute | solution.py:47
  32.0 9.6 %collective-permute-start.13 = (bf16[1024,512]{1,0:T(8,128)(2,1)S(1)}, bf16[1024,512]{1,0:T(8,128)(2,1)S(1)}, u32[]{:S(2)}, u32[]{:S(2)}) collective-permute-start(bf16[1024,512]{1,0:T(8,128)(2,1)S(1)} %get-tuple-element.46), channel_id=1, source_target_pairs={{0,16},{16,0},{1,17},{17,1},{2,18},{18,2},{3,19},{19,3},{4,20},{20... | collective-permute-start | bytes 3145736 | tf_op jit(solution)/shard_map/ppermute | solution.py:51
  35.5 5.3 %collective-permute-start.12 = (bf16[256,512]{1,0:T(8,128)(2,1)S(1)}, bf16[256,512]{1,0:T(8,128)(2,1)S(1)}, u32[]{:S(2)}, u32[]{:S(2)}) collective-permute-start(bf16[256,512]{1,0:T(8,128)(2,1)S(1)} %collective-permute-done.10.refs_1_), channel_id=1, source_target_pairs={{0,16},{16,0},{1,17},{17,1},{2,18},{18,2},{3,19},{19,3},{4,20},{20... | collective-permute-start | bytes 786440 | tf_op jit(solution)/shard_map/ppermute | solution.py:51
  36.7 4.9 %collective-permute-start.8 = (bf16[256,512]{1,0:T(8,128)(2,1)S(1)}, bf16[256,512]{1,0:T(8,128)(2,1)S(1)}, u32[]{:S(2)}, u32[]{:S(2)}) collective-permute-start(bf16[256,512]{1,0:T(8,128)(2,1)S(1)} %collective-permute-done.7.refs_1_), channel_id=1, source_target_pairs={{0,16},{16,0},{1,17},{17,1},{2,18},{18,2},{3,19},{19,3},{4,20},{20... | collective-permute-start | bytes 786440 | tf_op jit(solution)/shard_map/ppermute | solution.py:51
  41.5 4.6 %copy-start.1 = (f32[512]{0:T(512)S(1)}, f32[512]{0:T(512)}, u32[]{:S(2)}) copy-start(f32[512]{0:T(512)} %param.11) | copy-start | bytes 6148
  41.5 4.6 %copy-start.2 = (s32[64]{0:T(128)S(1)}, s32[64]{0:T(128)}, u32[]{:S(2)}) copy-start(s32[64]{0:T(128)} %counts_ref.1) | copy-start | bytes 772
  42.0 8.9 %collective-permute-start.14 = (bf16[256,512]{1,0:T(8,128)(2,1)S(1)}, bf16[256,512]{1,0:T(8,128)(2,1)S(1)}, u32[]{:S(2)}, u32[]{:S(2)}) collective-permute-start(bf16[256,512]{1,0:T(8,128)(2,1)S(1)} %get-tuple-element.48), channel_id=1, source_target_pairs={{0,32},{1,33},{32,1},{33,0},{2,34},{3,35},{34,3},{35,2},{4,36},{5,... | collective-permute-start | bytes 786440 | tf_op jit(solution)/shard_map/ppermute | solution.py:41
  43.1 7.7 %collective-permute-start.15 = (bf16[256,512]{1,0:T(8,128)(2,1)S(1)}, bf16[256,512]{1,0:T(8,128)(2,1)S(1)}, u32[]{:S(2)}, u32[]{:S(2)}) collective-permute-start(bf16[256,512]{1,0:T(8,128)(2,1)S(1)} %get-tuple-element.49), channel_id=1, source_target_pairs={{0,33},{1,32},{32,0},{33,1},{2,35},{3,34},{34,2},{35,3},{4,37},{5,... | collective-permute-start | bytes 786440 | tf_op jit(solution)/shard_map/ppermute | solution.py:41
  44.8 12.5 %collective-permute-start.16 = (bf16[256,512]{1,0:T(8,128)(2,1)S(1)}, bf16[256,512]{1,0:T(8,128)(2,1)S(1)}, u32[]{:S(2)}, u32[]{:S(2)}) collective-permute-start(bf16[256,512]{1,0:T(8,128)(2,1)S(1)} %get-tuple-element.50), channel_id=1, source_target_pairs={{0,1},{1,0},{32,33},{33,32},{2,3},{3,2},{34,35},{35,34},{4,5},{5,4... | collective-permute-start | bytes 786440 | tf_op jit(solution)/shard_map/ppermute | solution.py:41

commit v15 on v14

--- a/solution.py
+++ b/solution.py
@@ -313,16 +313,30 @@
     )(c_mine, sibling, mine, other)
 
 
-def finish_kernel(own_ref, a_ref, b_ref, c_ref, n_ref, live_ref, lead_ref, _, o_hbm, buffer, sem):
+def gather_kernel(own_ref, a_ref, b_ref, n_ref, o_ref):
+    o_ref[...] = (own_ref[...] + a_ref[...].astype(F32) + b_ref[...].astype(F32)) / n_ref[:, :1]
+
+
+def add_near(own, a, b, norm):
+    return pl.pallas_call(
+        gather_kernel,
+        in_specs=[VM] * 4,
+        out_specs=VM,
+        out_shape=pltpu.VMEM(own.shape, F32),
+        name="add_near",
+        compiler_params=params(4),
+        cost_estimate=TINY,
+    )(own, a, b, norm)
+
+
+def finish_kernel(own_ref, c_ref, n_ref, live_ref, lead_ref, _, o_hbm, buffer, sem):
     retain = live_ref[:1, :] > 0.5
     norm = n_ref[:, :1]
     size = buffer.shape[0] // 4
     copies = []
     for i in range(4):
         part = slice(i * size, (i + 1) * size)
-        total = own_ref[:, part] + a_ref[:, part].astype(F32)
-        total = total + b_ref[:, part].astype(F32) + c_ref[:, part].astype(F32)
-        updated = jnp.transpose(total / norm)
+        updated = jnp.transpose(own_ref[:, part] + c_ref[:, part].astype(F32) / norm)
         lead = lead_ref[part, :].astype(F32)
         buffer[part, :] = jnp.where(retain, updated, lead).astype(BF16)
         rows = pl.ds(i * size, size)
@@ -334,18 +348,18 @@
         copy.wait()
 
 
-def finish(own, received, norm, live, lead, out):
+def finish(own, last, norm, live, lead, out):
     return pl.pallas_call(
         finish_kernel,
-        in_specs=[VM] * (XS + 3) + [HB],
+        in_specs=[VM] * 5 + [HB],
         out_specs=HB,
         out_shape=jax.ShapeDtypeStruct(out.shape, BF16),
         scratch_shapes=[pltpu.VMEM(lead.shape, BF16), pltpu.SemaphoreType.DMA((4,))],
-        input_output_aliases={XS + 3: 0},
+        input_output_aliases={5: 0},
         name="finish",
         compiler_params=params(4),
         cost_estimate=TINY,
-    )(own, *received, norm, live, lead, out)
+    )(own, last, norm, live, lead, out)
 
 
 def per_device(eigvecs, perm, counts, poles, weights, roots):
@@ -378,7 +392,8 @@
     own_sum, *sent = totals(c_mine, sibling, mine, other)
     received = [xshift(sent[i], k) for i, k in ((0, 1), (2, -1), (1, 2))]
     norm, live, out = norms(me, counts, table, factors, hold(roots, own_sum), rest)
-    return finish(own_sum, received, norm, live, lead, out)
+    own_sum = add_near(own_sum, received[0], received[1], norm)
+    return finish(own_sum, received[2], norm, live, lead, out)
 
 
 def solution(mesh):

time: 58.6 us -> 58.5 us (level)
  transfers between devices with their start and end apart: 17 -> 17, of which waited for: 5 -> 5; matrix products, arithmetic and copies ran while one was open for 0% -> 0% of each run, Pallas kernels for 21% -> 22%
where the time goes in v15:
time: 58.5 us; the launch traced here: 58.4 us
  starting transfers between devices  30.9 us (53%)
  Pallas kernels  15.7 us (27%)
  waiting for transfers between devices  10.8 us (18%)
  local copies, waits for them, and re-layouts  0.69 us (1%)
    ppermute x7, starting transfers between devices, around(): return lax.ppermute(a, ('core', 'z'), up + down)  14.8 us
    ppermute x6, waiting for transfers between devices, xshift(): return lax.ppermute(a, ('xl', 'xh'), pairs)  9.39 us
    ppermute x4, starting transfers between devices, cshift(): return lax.ppermute(a, 'core', [(0, 1), (1, 0)])  8.38 us
    ppermute x6, starting transfers between devices, xshift(): return lax.ppermute(a, ('xl', 'xh'), pairs)  7.73 us
    pallas_call x1, Pallas kernels, norms(): pl.pallas_call(norm_kernel, in_specs=[SM, SM] + [VM] * 4, out_specs=[VM,...  3.92 us
    pallas_call x2, Pallas kernels, stage(): pl.pallas_call(lambda *refs: stage_kernel(first, len(pieces), *refs), in_...  3.61 us
    pallas_call x2, Pallas kernels, cauchy(): pl.pallas_call(lambda *refs: cauchy_kernel(fc, pieces, *refs), in_specs=[...  2.72 us
    pallas_call x1, Pallas kernels, permute(): pl.pallas_call(permute_kernel, in_specs=[HB, HB], out_specs=[VM] * 3, out...  1.72 us
  transfers between devices with their start and end apart: 17, of which 5 were waited for; matrix products, arithmetic and copies ran while one was open for 0% of the time, Pallas kernels for 22%

profile of v15, /device:TPU:1, one launch (start us, length us, event | category | flops | bytes accessed | tf_op | source)
XLA Modules:
  0.0 58.4 jit_solution(1479297289133311174)
XLA Ops:
  0.0 1.7 %permute.1 = (bf16[256,512]{1,0:T(8,128)(2,1)S(1)}, bf16[512,256]{1,0:T(8,128)(2,1)S(1)}, bf16[512,256]{1,0:T(8,128)(2,1)S(1)}) custom-call(bf16[512,512]{1,0:T(8,128)(2,1)} %e_hbm.1, s32[1,512]{1,0:T(1,128)} %bitcast.10), custom_call_target="tpu_custom_call" | custom-call | flops 1 | bytes 1 | tf_op jit(solution)/shard_map/permute/pallas_call | solution.py:86
  1.7 2.5 %collective-permute-start.6 = (bf16[256,512]{1,0:T(8,128)(2,1)S(1)}, bf16[256,512]{1,0:T(8,128)(2,1)S(1)}, u32[]{:S(2)}, u32[]{:S(2)}) collective-permute-start(bf16[256,512]{1,0:T(8,128)(2,1)S(1)} %get-tuple-element.31.refs_2_), channel_id=1, source_target_pairs={{0,14},{2,0},{4,2},{6,4},{8,6},{10,8},{12,10},{14,12},{16,18},{18,... | collective-permute-start | bytes 786440 | tf_op jit(solution)/shard_map/ppermute | solution.py:47
  4.3 5.1 %collective-permute-start.1 = (bf16[256,512]{1,0:T(8,128)(2,1)S(1)}, bf16[256,512]{1,0:T(8,128)(2,1)S(1)}, u32[]{:S(2)}, u32[]{:S(2)}) collective-permute-start(bf16[256,512]{1,0:T(8,128)(2,1)S(1)} %get-tuple-element.31.refs_2_), channel_id=1, source_target_pairs={{0,4},{2,6},{4,8},{6,10},{8,12},{10,14},{12,0},{14,2},{16,28},{18,... | collective-permute-start | bytes 786440 | tf_op jit(solution)/shard_map/ppermute | solution.py:47
  9.4 1.4 %collective-permute-done.b_ref = f32[1,512]{1,0:T(1,128)S(1)} collective-permute-done((f32[1,512]{1,0:T(1,128)}, f32[1,512]{1,0:T(1,128)S(1)}, u32[]{:S(2)}, u32[]{:S(2)}) %collective-permute-start) | collective-permute-done | bytes 2080 | tf_op jit(solution)/shard_map/ppermute | solution.py:51
  11.4 2.5 %collective-permute-start.2 = (f32[1,1024]{1,0:T(1,128)S(1)}, f32[1,1024]{1,0:T(1,128)S(1)}, u32[]{:S(2)}, u32[]{:S(2)}) collective-permute-start(f32[1,1024]{1,0:T(1,128)S(1)} %join.1.refs_3_), channel_id=1, source_target_pairs={{0,33},{1,32},{32,0},{33,1},{2,35},{3,34},{34,2},{35,3},{4,37},{5,... | collective-permute-start | bytes 12296 | tf_op jit(solution)/shard_map/ppermute | solution.py:41
  15.1 1.1 %tables.1 = (f32[128,128]{1,0:T(8,128)S(1)}, f32[128,128]{1,0:T(8,128)S(1)}) custom-call(s32[64]{0:T(128)} %counts_ref.1, f32[256,128]{1,0:T(8,128)} %bitcast.8, f32[256,128]{1,0:T(8,128)} %bitcast.9), custom_call_target="tpu_custom_call" | custom-call | flops 1 | bytes 1 | tf_op jit(solution)/shard_map/tables/pallas_call | solution.py:128
  16.1 2.1 %collective-permute-done.3.refs_5_ = f32[1,1024]{1,0:T(1,128)S(1)} collective-permute-done((f32[1,1024]{1,0:T(1,128)S(1)}, f32[1,1024]{1,0:T(1,128)S(1)}, u32[]{:S(2)}, u32[]{:S(2)}) %collective-permute-start.3) | collective-permute-done | bytes 4128 | tf_op jit(solution)/shard_map/ppermute | solution.py:41
  18.4 2.7 %collective-permute-start.5 = (bf16[256,512]{1,0:T(8,128)(2,1)S(1)}, bf16[256,512]{1,0:T(8,128)(2,1)S(1)}, u32[]{:S(2)}, u32[]{:S(2)}) collective-permute-start(bf16[256,512]{1,0:T(8,128)(2,1)S(1)} %collective-permute-done.1.refs_4_), channel_id=1, source_target_pairs={{0,2},{2,4},{4,6},{6,8},{8,10},{10,12},{12,14},{14,0},{16,30},{18,... | collective-permute-start | bytes 786440 | tf_op jit(solution)/shard_map/ppermute | solution.py:47
  21.1 1.7 %collective-permute-start.11 = (bf16[256,512]{1,0:T(8,128)(2,1)S(1)}, bf16[256,512]{1,0:T(8,128)(2,1)S(1)}, u32[]{:S(2)}, u32[]{:S(2)}) collective-permute-start(bf16[256,512]{1,0:T(8,128)(2,1)S(1)} %get-tuple-element.31.refs_2_), channel_id=1, source_target_pairs={{0,2},{2,4},{4,6},{6,8},{8,10},{10,12},{12,14},{14,0},{16,30},{18,... | collective-permute-start | bytes 786440 | tf_op jit(solution)/shard_map/ppermute | solution.py:47
  22.8 1.1 %cauchy.2.refs_1_ = bf16[1024,1536]{1,0:T(8,128)(2,1)S(1)} custom-call(s32[1]{0:T(128)} %bitcast.refs_0_.me_ref, f32[128,128]{1,0:T(8,128)S(1)} %get-tuple-element.34.refs_1_.poles_ref, f32[128,128]{1,0:T(8,128)S(1)} %get-tuple-element.35.refs_2_.factors_ref, f32[1,1024]{1,0:T(1,128)S(1)} %join.1.refs_3_, f32[1,1024]{1,0:T(1,128)S(1)} %collective-permute-done.2.refs_4_, ...), custom_call_target="tpu_custom_call" | custom-call | flops 1 | bytes 1 | tf_op jit(solution)/shard_map/cauchy/pallas_call | solution.py:185
  23.9 1.7 %cauchy.3.refs_0_.c_ref = bf16[1024,2560]{1,0:T(8,128)(2,1)S(1)} custom-call(s32[1]{0:T(128)} %bitcast.refs_0_.me_ref, f32[128,128]{1,0:T(8,128)S(1)} %get-tuple-element.34.refs_1_.poles_ref, f32[128,128]{1,0:T(8,128)S(1)} %get-tuple-element.35.refs_2_.factors_ref, f32[1,1024]{1,0:T(1,128)S(1)} %join.1.refs_3_, ...), custom_call_target="tpu_custom_call" | custom-call | flops 1 | bytes 1 | tf_op jit(solution)/shard_map/cauchy/pallas_call | solution.py:185
  25.6 1.8 %stage.2 = (f32[1024,512]{1,0:T(8,128)S(1)}, f32[1024,512]{1,0:T(8,128)S(1)}) custom-call(bf16[1024,2560]{1,0:T(8,128)(2,1)S(1)} %cauchy.3.refs_0_.c_ref, bf16[1024,1536]{1,0:T(8,128)(2,1)S(1)} %cauchy.2.refs_1_, bf16[256,512]{1,0:T(8,128)(2,1)S(1)} %get-tuple-element.31.refs_2_, bf16[256,512]{1,0:T(8,128)(2,1)S(1)} %collective-permute-done.6.refs_3_, ...), custom_call_target="tpu_custom_call" | custom-call | flops 1 | bytes 1 | tf_op jit(solution)/shard_map/stage/pallas_call | solution.py:260
  27.5 2.7 %collective-permute-start.7 = (bf16[256,512]{1,0:T(8,128)(2,1)S(1)}, bf16[256,512]{1,0:T(8,128)(2,1)S(1)}, u32[]{:S(2)}, u32[]{:S(2)}) collective-permute-start(bf16[256,512]{1,0:T(8,128)(2,1)S(1)} %collective-permute-done.5.refs_4_), channel_id=1, source_target_pairs={{0,2},{2,4},{4,6},{6,8},{8,10},{10,12},{12,14},{14,0},{16,30},{18,... | collective-permute-start | bytes 786440 | tf_op jit(solution)/shard_map/ppermute | solution.py:47
  30.1 1.8 %stage.3 = (f32[1024,512]{1,0:T(8,128)S(1)}, bf16[1024,512]{1,0:T(8,128)(2,1)S(1)}) custom-call(bf16[1024,2560]{1,0:T(8,128)(2,1)S(1)} %cauchy.3.refs_0_.c_ref, bf16[1024,1536]{1,0:T(8,128)(2,1)S(1)} %cauchy.2.refs_1_, bf16[256,512]{1,0:T(8,128)(2,1)S(1)} %collective-permute-done.11.refs_2_, bf16[256,512]{1,0:T(8,128)(2,1)S(1)} %collective-permute-done.9.refs_3_, ...), custom_call_target="tpu_custom_call" | custom-call | flops 1 | bytes 1 | tf_op jit(solution)/shard_map/stage/pallas_call | solution.py:260
  32.0 3.5 %collective-permute-start.13 = (bf16[1024,512]{1,0:T(8,128)(2,1)S(1)}, bf16[1024,512]{1,0:T(8,128)(2,1)S(1)}, u32[]{:S(2)}, u32[]{:S(2)}) collective-permute-start(bf16[1024,512]{1,0:T(8,128)(2,1)S(1)} %get-tuple-element.46), channel_id=1, source_target_pairs={{0,16},{16,0},{1,17},{17,1},{2,18},{18,2},{3,19},{19,3},{4,20},{20... | collective-permute-start | bytes 3145736 | tf_op jit(solution)/shard_map/ppermute | solution.py:51
  35.5 1.1 %collective-permute-start.12 = (bf16[256,512]{1,0:T(8,128)(2,1)S(1)}, bf16[256,512]{1,0:T(8,128)(2,1)S(1)}, u32[]{:S(2)}, u32[]{:S(2)}) collective-permute-start(bf16[256,512]{1,0:T(8,128)(2,1)S(1)} %collective-permute-done.10.refs_1_), channel_id=1, source_target_pairs={{0,16},{16,0},{1,17},{17,1},{2,18},{18,2},{3,19},{19,3},{4,20},{20... | collective-permute-start | bytes 786440 | tf_op jit(solution)/shard_map/ppermute | solution.py:51
  36.7 3.7 %collective-permute-start.8 = (bf16[256,512]{1,0:T(8,128)(2,1)S(1)}, bf16[256,512]{1,0:T(8,128)(2,1)S(1)}, u32[]{:S(2)}, u32[]{:S(2)}) collective-permute-start(bf16[256,512]{1,0:T(8,128)(2,1)S(1)} %collective-permute-done.7.refs_1_), channel_id=1, source_target_pairs={{0,16},{16,0},{1,17},{17,1},{2,18},{18,2},{3,19},{19,3},{4,20},{20... | collective-permute-start | bytes 786440 | tf_op jit(solution)/shard_map/ppermute | solution.py:51
  42.0 1.1 %collective-permute-start.14 = (bf16[256,512]{1,0:T(8,128)(2,1)S(1)}, bf16[256,512]{1,0:T(8,128)(2,1)S(1)}, u32[]{:S(2)}, u32[]{:S(2)}) collective-permute-start(bf16[256,512]{1,0:T(8,128)(2,1)S(1)} %get-tuple-element.48), channel_id=1, source_target_pairs={{0,32},{1,33},{32,1},{33,0},{2,34},{3,35},{34,3},{35,2},{4,36},{5,... | collective-permute-start | bytes 786440 | tf_op jit(solution)/shard_map/ppermute | solution.py:41
  43.1 1.6 %collective-permute-start.15 = (bf16[256,512]{1,0:T(8,128)(2,1)S(1)}, bf16[256,512]{1,0:T(8,128)(2,1)S(1)}, u32[]{:S(2)}, u32[]{:S(2)}) collective-permute-start(bf16[256,512]{1,0:T(8,128)(2,1)S(1)} %get-tuple-element.49), channel_id=1, source_target_pairs={{0,33},{1,32},{32,0},{33,1},{2,35},{3,34},{34,2},{35,3},{4,37},{5,... | collective-permute-start | bytes 786440 | tf_op jit(solution)/shard_map/ppermute | solution.py:41
  44.8 1.4 %collective-permute-start.16 = (bf16[256,512]{1,0:T(8,128)(2,1)S(1)}, bf16[256,512]{1,0:T(8,128)(2,1)S(1)}, u32[]{:S(2)}, u32[]{:S(2)}) collective-permute-start(bf16[256,512]{1,0:T(8,128)(2,1)S(1)} %get-tuple-element.53), channel_id=1, source_target_pairs={{0,1},{1,0},{32,33},{33,32},{2,3},{3,2},{34,35},{35,34},{4,5},{5,4... | collective-permute-start | bytes 786440 | tf_op jit(solution)/shard_map/ppermute | solution.py:41
  46.1 3.9 %norms.1 = (f32[256,128]{1,0:T(8,128)S(1)}, f32[8,256]{1,0:T(8,128)S(1)}, bf16[512,512]{1,0:T(8,128)(2,1)}) custom-call(s32[1]{0:T(128)} %bitcast.refs_0_.me_ref, s32[64]{0:T(128)S(1)} %copy-done.2, f32[128,128]{1,0:T(8,128)S(1)} %get-tuple-element.34.refs_1_.poles_ref, f32[128,128]{1,0:T(8,128)S(1)} %get-tuple-element.35.refs_2_.factors_ref, ...), custom_call_target="tpu_custom_call" | custom-call | flops 1 | bytes 1 | tf_op jit(solution)/shard_map/norms/pallas_call | solution.py:220
  50.1 0.8 %collective-permute-done.14.a_ref = bf16[256,512]{1,0:T(8,128)(2,1)S(1)} collective-permute-done((bf16[256,512]{1,0:T(8,128)(2,1)S(1)}, bf16[256,512]{1,0:T(8,128)(2,1)S(1)}, u32[]{:S(2)}, u32[]{:S(2)}) %collective-permute-start.14) | collective-permute-done | bytes 262176 | tf_op jit(solution)/shard_map/ppermute | solution.py:41
  51.0 6.3 %collective-permute-done.16.c_ref = bf16[256,512]{1,0:T(8,128)(2,1)S(1)} collective-permute-done((bf16[256,512]{1,0:T(8,128)(2,1)S(1)}, bf16[256,512]{1,0:T(8,128)(2,1)S(1)}, u32[]{:S(2)}, u32[]{:S(2)}) %collective-permute-start.16) | collective-permute-done | bytes 262176 | tf_op jit(solution)/shard_map/ppermute | solution.py:41
  57.3 0.9 %finish.1 = bf16[512,512]{1,0:T(8,128)(2,1)} custom-call(f32[256,512]{1,0:T(8,128)S(1)} %add_near.1.own_ref, bf16[256,512]{1,0:T(8,128)(2,1)S(1)} %collective-permute-done.16.c_ref, f32[256,128]{1,0:T(8,128)S(1)} %get-tuple-element.52.n_ref, f32[8,256]{1,0:T(8,128)S(1)} %get-tuple-element.54.live_ref, ...), custom_call_target="tpu_custom_call", output_to_operand_aliasing={{}: (5, {})} | custom-call | flops 1 | bytes 1 | tf_op jit(solution)/shard_map/finish/pallas_call | solution.py:352
  (29 shorter events, 3.9 us)
Async XLA Ops:
  1.7 16.7 %collective-permute-start.6 = (bf16[256,512]{1,0:T(8,128)(2,1)S(1)}, bf16[256,512]{1,0:T(8,128)(2,1)S(1)}, u32[]{:S(2)}, u32[]{:S(2)}) collective-permute-start(bf16[256,512]{1,0:T(8,128)(2,1)S(1)} %get-tuple-element.31.refs_2_), channel_id=1, source_target_pairs={{0,14},{2,0},{4,2},{6,4},{8,6},{10,8},{12,10},{14,12},{16,18},{18,... | collective-permute-start | bytes 786440 | tf_op jit(solution)/shard_map/ppermute | solution.py:47
  4.3 14.1 %collective-permute-start.1 = (bf16[256,512]{1,0:T(8,128)(2,1)S(1)}, bf16[256,512]{1,0:T(8,128)(2,1)S(1)}, u32[]{:S(2)}, u32[]{:S(2)}) collective-permute-start(bf16[256,512]{1,0:T(8,128)(2,1)S(1)} %get-tuple-element.31.refs_2_), channel_id=1, source_target_pairs={{0,4},{2,6},{4,8},{6,10},{8,12},{10,14},{12,0},{14,2},{16,28},{18,... | collective-permute-start | bytes 786440 | tf_op jit(solution)/shard_map/ppermute | solution.py:47
  9.4 1.4 %collective-permute-start = (f32[1,512]{1,0:T(1,128)}, f32[1,512]{1,0:T(1,128)S(1)}, u32[]{:S(2)}, u32[]{:S(2)}) collective-permute-start(f32[1,512]{1,0:T(1,128)} %bitcast.5), channel_id=1, source_target_pairs={{0,16},{16,0},{1,17},{17,1},{2,18},{18,2},{3,19},{19,3},{4,20},{20... | collective-permute-start | bytes 6152 | tf_op jit(solution)/shard_map/ppermute | solution.py:51
  10.8 0.7 %copy-start = (f32[512]{0:T(512)S(1)}, f32[512]{0:T(512)}, u32[]{:S(2)}) copy-start(f32[512]{0:T(512)} %param.11) | copy-start | bytes 6148
  11.4 4.7 %collective-permute-start.2 = (f32[1,1024]{1,0:T(1,128)S(1)}, f32[1,1024]{1,0:T(1,128)S(1)}, u32[]{:S(2)}, u32[]{:S(2)}) collective-permute-start(f32[1,1024]{1,0:T(1,128)S(1)} %join.1.refs_3_), channel_id=1, source_target_pairs={{0,33},{1,32},{32,0},{33,1},{2,35},{3,34},{34,2},{35,3},{4,37},{5,... | collective-permute-start | bytes 12296 | tf_op jit(solution)/shard_map/ppermute | solution.py:41
  13.9 4.3 %collective-permute-start.3 = (f32[1,1024]{1,0:T(1,128)S(1)}, f32[1,1024]{1,0:T(1,128)S(1)}, u32[]{:S(2)}, u32[]{:S(2)}) collective-permute-start(f32[1,1024]{1,0:T(1,128)S(1)} %join.1.refs_3_), channel_id=1, source_target_pairs={{0,1},{1,0},{32,33},{33,32},{2,3},{3,2},{34,35},{35,34},{4,5},{5,4... | collective-permute-start | bytes 12296 | tf_op jit(solution)/shard_map/ppermute | solution.py:41
  14.4 4.0 %collective-permute-start.4 = (f32[1,1024]{1,0:T(1,128)S(1)}, f32[1,1024]{1,0:T(1,128)S(1)}, u32[]{:S(2)}, u32[]{:S(2)}) collective-permute-start(f32[1,1024]{1,0:T(1,128)S(1)} %join.1.refs_3_), channel_id=1, source_target_pairs={{0,32},{1,33},{32,1},{33,0},{2,34},{3,35},{34,3},{35,2},{4,36},{5,... | collective-permute-start | bytes 12296 | tf_op jit(solution)/shard_map/ppermute | solution.py:41
  18.4 9.0 %collective-permute-start.9 = (bf16[256,512]{1,0:T(8,128)(2,1)S(1)}, bf16[256,512]{1,0:T(8,128)(2,1)S(1)}, u32[]{:S(2)}, u32[]{:S(2)}) collective-permute-start(bf16[256,512]{1,0:T(8,128)(2,1)S(1)} %collective-permute-done.6.refs_3_), channel_id=1, source_target_pairs={{0,14},{2,0},{4,2},{6,4},{8,6},{10,8},{12,10},{14,12},{16,18},{18,... | collective-permute-start | bytes 786440 | tf_op jit(solution)/shard_map/ppermute | solution.py:47
  18.4 9.1 %collective-permute-start.5 = (bf16[256,512]{1,0:T(8,128)(2,1)S(1)}, bf16[256,512]{1,0:T(8,128)(2,1)S(1)}, u32[]{:S(2)}, u32[]{:S(2)}) collective-permute-start(bf16[256,512]{1,0:T(8,128)(2,1)S(1)} %collective-permute-done.1.refs_4_), channel_id=1, source_target_pairs={{0,2},{2,4},{4,6},{6,8},{8,10},{10,12},{12,14},{14,0},{16,30},{18,... | collective-permute-start | bytes 786440 | tf_op jit(solution)/shard_map/ppermute | solution.py:47
  21.1 9.0 %collective-permute-start.11 = (bf16[256,512]{1,0:T(8,128)(2,1)S(1)}, bf16[256,512]{1,0:T(8,128)(2,1)S(1)}, u32[]{:S(2)}, u32[]{:S(2)}) collective-permute-start(bf16[256,512]{1,0:T(8,128)(2,1)S(1)} %get-tuple-element.31.refs_2_), channel_id=1, source_target_pairs={{0,2},{2,4},{4,6},{6,8},{8,10},{10,12},{12,14},{14,0},{16,30},{18,... | collective-permute-start | bytes 786440 | tf_op jit(solution)/shard_map/ppermute | solution.py:47
  27.4 8.1 %collective-permute-start.10 = (bf16[256,512]{1,0:T(8,128)(2,1)S(1)}, bf16[256,512]{1,0:T(8,128)(2,1)S(1)}, u32[]{:S(2)}, u32[]{:S(2)}) collective-permute-start(bf16[256,512]{1,0:T(8,128)(2,1)S(1)} %collective-permute-done.9.refs_3_), channel_id=1, source_target_pairs={{0,14},{2,0},{4,2},{6,4},{8,6},{10,8},{12,10},{14,12},{16,18},{18,... | collective-permute-start | bytes 786440 | tf_op jit(solution)/shard_map/ppermute | solution.py:47
  27.5 9.2 %collective-permute-start.7 = (bf16[256,512]{1,0:T(8,128)(2,1)S(1)}, bf16[256,512]{1,0:T(8,128)(2,1)S(1)}, u32[]{:S(2)}, u32[]{:S(2)}) collective-permute-start(bf16[256,512]{1,0:T(8,128)(2,1)S(1)} %collective-permute-done.5.refs_4_), channel_id=1, source_target_pairs={{0,2},{2,4},{4,6},{6,8},{8,10},{10,12},{12,14},{14,0},{16,30},{18,... | collective-permute-start | bytes 786440 | tf_op jit(solution)/shard_map/ppermute | solution.py:47
  32.0 9.6 %collective-permute-start.13 = (bf16[1024,512]{1,0:T(8,128)(2,1)S(1)}, bf16[1024,512]{1,0:T(8,128)(2,1)S(1)}, u32[]{:S(2)}, u32[]{:S(2)}) collective-permute-start(bf16[1024,512]{1,0:T(8,128)(2,1)S(1)} %get-tuple-element.46), channel_id=1, source_target_pairs={{0,16},{16,0},{1,17},{17,1},{2,18},{18,2},{3,19},{19,3},{4,20},{20... | collective-permute-start | bytes 3145736 | tf_op jit(solution)/shard_map/ppermute | solution.py:51
  35.5 5.3 %collective-permute-start.12 = (bf16[256,512]{1,0:T(8,128)(2,1)S(1)}, bf16[256,512]{1,0:T(8,128)(2,1)S(1)}, u32[]{:S(2)}, u32[]{:S(2)}) collective-permute-start(bf16[256,512]{1,0:T(8,128)(2,1)S(1)} %collective-permute-done.10.refs_1_), channel_id=1, source_target_pairs={{0,16},{16,0},{1,17},{17,1},{2,18},{18,2},{3,19},{19,3},{4,20},{20... | collective-permute-start | bytes 786440 | tf_op jit(solution)/shard_map/ppermute | solution.py:51
  36.7 4.9 %collective-permute-start.8 = (bf16[256,512]{1,0:T(8,128)(2,1)S(1)}, bf16[256,512]{1,0:T(8,128)(2,1)S(1)}, u32[]{:S(2)}, u32[]{:S(2)}) collective-permute-start(bf16[256,512]{1,0:T(8,128)(2,1)S(1)} %collective-permute-done.7.refs_1_), channel_id=1, source_target_pairs={{0,16},{16,0},{1,17},{17,1},{2,18},{18,2},{3,19},{19,3},{4,20},{20... | collective-permute-start | bytes 786440 | tf_op jit(solution)/shard_map/ppermute | solution.py:51
  41.5 4.6 %copy-start.1 = (f32[512]{0:T(512)S(1)}, f32[512]{0:T(512)}, u32[]{:S(2)}) copy-start(f32[512]{0:T(512)} %param.11) | copy-start | bytes 6148
  41.5 4.6 %copy-start.2 = (s32[64]{0:T(128)S(1)}, s32[64]{0:T(128)}, u32[]{:S(2)}) copy-start(s32[64]{0:T(128)} %counts_ref.1) | copy-start | bytes 772
  42.0 8.9 %collective-permute-start.14 = (bf16[256,512]{1,0:T(8,128)(2,1)S(1)}, bf16[256,512]{1,0:T(8,128)(2,1)S(1)}, u32[]{:S(2)}, u32[]{:S(2)}) collective-permute-start(bf16[256,512]{1,0:T(8,128)(2,1)S(1)} %get-tuple-element.48), channel_id=1, source_target_pairs={{0,32},{1,33},{32,1},{33,0},{2,34},{3,35},{34,3},{35,2},{4,36},{5,... | collective-permute-start | bytes 786440 | tf_op jit(solution)/shard_map/ppermute | solution.py:41
  43.1 7.7 %collective-permute-start.15 = (bf16[256,512]{1,0:T(8,128)(2,1)S(1)}, bf16[256,512]{1,0:T(8,128)(2,1)S(1)}, u32[]{:S(2)}, u32[]{:S(2)}) collective-permute-start(bf16[256,512]{1,0:T(8,128)(2,1)S(1)} %get-tuple-element.49), channel_id=1, source_target_pairs={{0,33},{1,32},{32,0},{33,1},{2,35},{3,34},{34,2},{35,3},{4,37},{5,... | collective-permute-start | bytes 786440 | tf_op jit(solution)/shard_map/ppermute | solution.py:41
  44.8 12.5 %collective-permute-start.16 = (bf16[256,512]{1,0:T(8,128)(2,1)S(1)}, bf16[256,512]{1,0:T(8,128)(2,1)S(1)}, u32[]{:S(2)}, u32[]{:S(2)}) collective-permute-start(bf16[256,512]{1,0:T(8,128)(2,1)S(1)} %get-tuple-element.53), channel_id=1, source_target_pairs={{0,1},{1,0},{32,33},{33,32},{2,3},{3,2},{34,35},{35,34},{4,5},{5,4... | collective-permute-start | bytes 786440 | tf_op jit(solution)/shard_map/ppermute | solution.py:41
